TPU v7x, 128 devices: a whole 4x4x4 slice. The times are simulated.
128 devices in a mesh: vel: 8 (over y, z_lo), space: 16 (over x, z_hi, core).
Axes of the slice: x: 4, y: 4, z: 4 (z_hi: 2, z_lo: 2; z = z_hi * 2 + z_lo), core: 2. Of those that a mesh axis runs over, the one named last changes fastest.
Arguments:
- density: float32 [1024, 64, 8, 128], P('vel', 'space'), may hold values from -6 to 6
- limiter: int32 [64, 8, 128], P('space'), may hold values from 0 to 2
- heading: int32 [1024], P('vel'), may hold values from 0 to 1
- courant: float32 [1024], P('vel'), may hold values from 0.1 to 0.9
- kernel_slices: bfloat16 [16, 1024, 1024], P('space', None, 'vel'), may hold values from -0.046875 to 0.046875
Outputs:
- transported: float32 [1024, 64, 8, 128], P('vel', 'space')
- collision: float32 [1024, 64, 8, 128], P('vel', 'space')
Inputs may be any that keep to these rules, and one draw needn't show every extreme that they name: `limiter`: 0 no slope, 1 minmod slope, 2 central slope.
All inputs are finite; a program needn't handle non-finite values.
Results may differ from a plain program's by a relative error of at most 0.0041.
Values may be sent and summed in bfloat16 or wider, within the bound.
No kernel may reach another device: no remote copies, remote signals or barrier semaphores. Data moves between devices by JAX's collectives and lax.ppermute only.
A program may use at most 128 MiB of HBM per device.

v0:
```python
import jax
import jax.numpy as jnp
from jax import lax
from jax.sharding import PartitionSpec as P

V = 1024
SLICES = 16


def extended(shard, sides, width):
    for axis, dim in sides:
        size, length = (lax.axis_size(axis), shard.shape[dim])
        up = [(i, (i + 1) % size) for i in range(size - 1)]
        down = [(j, i) for i, j in up]
        last = lax.slice_in_dim(shard, length - width, length, axis=dim)
        first = lax.slice_in_dim(shard, 0, width, axis=dim)
        before = lax.ppermute(last, axis, up)
        after = lax.ppermute(first, axis, down)
        shard = jnp.concatenate([before, shard, after], axis=dim)
    return shard


def limited_slopes(left_diff, right_diff, limiter):
    minmod_slope = jnp.where(
        left_diff * right_diff > 0,
        jnp.sign(left_diff) * jnp.minimum(jnp.abs(left_diff), jnp.abs(right_diff)),
        jnp.zeros_like(left_diff),
    )
    central = 0.5 * (left_diff + right_diff)
    codes = limiter[None]
    return jnp.where(
        codes == 1, minmod_slope, jnp.where(codes == 2, central, jnp.zeros_like(central))
    )


def make_fold(source, totals, pieces):
    stride = V // SLICES

    def one_slice(counter, running):
        matrix = lax.dynamic_index_in_dim(pieces, counter, 0, keepdims=False)
        projected = lax.dot_general(
            matrix, source, (((0,), (0,)), ((), ())), preferred_element_type=jnp.float32
        )
        weight = lax.dynamic_index_in_dim(source, counter * stride, 0, keepdims=True).astype(
            jnp.float32
        )
        return running + weight * projected

    return lax.fori_loop(0, pieces.shape[0], one_slice, totals)


def local(density, limiter, heading, courant, kernel_slices):
    padded = extended(density, (("space", 1),), 1)
    left_diff = density - padded[:, :-2]
    right_diff = padded[:, 2:] - density
    slopes = limited_slopes(left_diff, right_diff, limiter)
    upwind = (2 * heading - 1).astype(jnp.float32)[:, None, None, None]
    rebuilt = density + 0.5 * upwind * slopes
    rebuilt_pad = extended(rebuilt, (("space", 1),), 1)
    forward = (heading == 1)[:, None, None, None]
    upstream = jnp.where(forward, rebuilt_pad[:, :-2], rebuilt_pad[:, 2:])
    transported = density - courant[:, None, None, None] * (rebuilt - upstream)
    flattened = transported.astype(jnp.bfloat16).reshape(density.shape[0], -1)
    columns = lax.all_to_all(flattened, "vel", split_axis=1, concat_axis=0, tiled=True)
    full_slices = lax.all_gather(kernel_slices, "vel", axis=2, tiled=True)
    initial = jnp.zeros(columns.shape, jnp.float32)
    summed = make_fold(columns, initial, lax.all_gather(full_slices, "space", axis=0, tiled=True))
    restored = lax.all_to_all(summed, "vel", split_axis=0, concat_axis=1, tiled=True)
    return (transported, restored.reshape(density.shape))


def solution(mesh):
    return jax.shard_map(
        local,
        mesh=mesh,
        in_specs=(
            P("vel", "space", None, None),
            P("space", None, None),
            P("vel"),
            P("vel"),
            P("space", None, "vel"),
        ),
        out_specs=(P("vel", "space", None, None), P("vel", "space", None, None)),
        check_vma=False,
    )
```

profile of v0, /device:TPU:0, one launch (start us, length us, event | category | flops | bytes accessed | tf_op | source)
XLA Modules:
  0.0 379.6 jit_solution(10808552207556664224)
XLA Ops:
  7.2 0.0 all-gather.3.cloned.1.call-start
  7.2 0.7 all-gather.3.cloned.1.call-update
  7.9 0.0 all-gather.5.cloned.1.call-start
  7.9 61.7 %all-gather.3.cloned.1.call-done = bf16[1,1024,1024]{2,1,0:T(8,128)(2,1)} async-done(((bf16[1,1024,128]{2,1,0:T(8,128)(2,1)}), bf16[1,1024,1024]{2,1,0:T(8,128)(2,1)}) %all-gather.3.cloned.1.call-update) | async-done | bytes 2097168 | tf_op jit(solution)/shard_map/all_gather | solution.py:65
  69.6 0.0 all-gather.5.cloned.1.call-update
  69.7 2.0 copy.16
  71.7 0.0 copy-start.4
  71.7 0.0 copy-start.2
  71.7 0.1 fusion.18
  71.8 1.3 collective-permute-start
  73.1 1.3 collective-permute-start.1
  74.5 0.1 collective-permute-done
  74.6 6.0 %collective-permute-done.1 = f32[128,1,8,128]{0,3,2,1:T(8,128)S(1)} collective-permute-done((f32[128,1,8,128]{0,3,2,1:T(8,128)S(1)}, f32[128,1,8,128]{0,3,2,1:T(8,128)S(1)}, u32[]{:S(2)}, u32[]{:S(2)}) %collective-permute-start.1) | collective-permute-done | bytes 524320 | tf_op jit(solution)/shard_map/ppermute | solution.py:18
  80.6 1.9 multiply_add_fusion
  82.5 0.0 copy-start.3
  82.5 0.1 fusion.17
  82.6 12.2 %collective-permute-start.2 = (f32[128,1,8,128]{0,3,2,1:T(8,128)S(1)}, f32[128,1,8,128]{0,3,2,1:T(8,128)S(1)}, u32[]{:S(2)}, u32[]{:S(2)}) collective-permute-start(f32[128,1,8,128]{0,3,2,1:T(8,128)S(1)} %get-tuple-element.109), channel_id=1, source_target_pairs={{0,1},{1,2},{2,3},{3,4},{4,5},{5,6},{6,7},{7,8},{8,9},{9,10},{10,1... | collective-permute-start | bytes 1572872 | tf_op jit(solution)/shard_map/ppermute | solution.py:17
  94.8 1.3 collective-permute-start.3
  96.1 0.2 collective-permute-done.2
  96.3 5.8 %collective-permute-done.3 = f32[128,1,8,128]{0,3,2,1:T(8,128)S(1)} collective-permute-done((f32[128,1,8,128]{0,3,2,1:T(8,128)S(1)}, f32[128,1,8,128]{0,3,2,1:T(8,128)S(1)}, u32[]{:S(2)}, u32[]{:S(2)}) %collective-permute-start.3) | collective-permute-done | bytes 524320 | tf_op jit(solution)/shard_map/ppermute | solution.py:18
  102.1 1.9 fusion.15
  104.0 1.3 copy.17
  105.3 3.6 all-to-all-start
  108.8 15.1 %all-to-all-done = bf16[128,8,512]{2,0,1:T(8,128)(2,1)S(1)} async-done(((bf16[128,8,512]{2,0,1:T(8,128)(2,1)}), bf16[128,8,512]{2,0,1:T(8,128)(2,1)S(1)}, u32[]{:S(2)}, u32[]{:S(2)}) %all-to-all-start) | async-done | bytes 1048608 | tf_op jit(solution)/shard_map/all_to_all | solution.py:64
  123.9 155.6 %all-gather.5.cloned.1.call-done = bf16[16,1024,1024]{2,1,0:T(8,128)(2,1)} async-done(((bf16[1,1024,1024]{2,1,0:T(8,128)(2,1)}), bf16[16,1024,1024]{2,1,0:T(8,128)(2,1)}) %all-gather.5.cloned.1.call-update) | async-done | bytes 33554448 | tf_op jit(solution)/shard_map/all_gather | solution.py:67
  279.5 51.4 %while.14 = (s32[]{:T(128)}, f32[1024,512]{1,0:T(8,128)S(1)}, bf16[1024,512]{1,0:T(8,128)(2,1)S(1)}, bf16[16,1024,1024]{2,1,0:T(8,128)(2,1)}, s32[]{:T(128)}, /*index=5*/s32[]{:T(128)}, s32[]{:T(128)}, s32[]{:T(128)}) while((s32[]{:T(128)}, f32[1024,512]{1,0:T(8,128)S(1)}, bf16[1024,512]{1,0:T(8,128)(2,1)S(1)}, ...), condition=%wide.region_1.2_spmd.clone, body=%wide.region_0.1_spmd.clone.sunk | while | flops 1075315200 | bytes 7345809 | solution.py:49
  279.5 3.2 select_add_fusion.2
  282.8 3.2 select_add_fusion.2
  286.0 3.2 select_add_fusion.2
  289.2 3.2 select_add_fusion.2
  292.4 3.2 select_add_fusion.2
  295.6 3.2 select_add_fusion.2
  298.8 3.2 select_add_fusion.2
  302.1 3.2 select_add_fusion.2
  305.3 3.2 select_add_fusion.2
  308.5 3.2 select_add_fusion.2
  311.7 3.2 select_add_fusion.2
  314.9 3.2 select_add_fusion.2
  318.1 3.2 select_add_fusion.2
  321.4 3.2 select_add_fusion.2
  324.6 3.2 select_add_fusion.2
  327.8 3.2 select_add_fusion.2
  331.0 1.3 copy-done.1
  332.3 4.5 %all-to-all-start.1 = ((f32[8,128,512]{2,1,0:T(8,128)}), f32[8,128,512]{2,1,0:T(8,128)}, u32[]{:S(2)}, u32[]{:S(2)}) async-start(f32[8,128,512]{2,1,0:T(8,128)} %bitcast.23), calls=%async_computation.1 | async-start | bytes 4194304 | tf_op jit(solution)/shard_map/all_to_all | solution.py:68
  336.8 2.0 copy.19
  338.8 30.1 %all-to-all-done.1 = f32[8,128,512]{2,1,0:T(8,128)} async-done(((f32[8,128,512]{2,1,0:T(8,128)}), f32[8,128,512]{2,1,0:T(8,128)}, u32[]{:S(2)}, u32[]{:S(2)}) %all-to-all-start.1) | async-done | bytes 2097184 | tf_op jit(solution)/shard_map/all_to_all | solution.py:68
  368.9 1.9 copy.18
  370.8 2.0 copy.20
  (26 shorter events, 0.2 us)
Async XLA Ops:
  7.2 62.5 %all-gather.3.cloned.1.call-start = ((), (), s32[]{:S(2)}) async-start(), calls=%async_computation.2 | async-start | bytes 2359296 | tf_op jit(solution)/shard_map/all_gather | solution.py:65
  7.9 271.6 %all-gather.5.cloned.1.call-start = ((), (), s32[]{:S(2)}) async-start(), calls=%async_computation.3 | async-start | bytes 35651584 | tf_op jit(solution)/shard_map/all_gather | solution.py:67
  71.7 2.7 copy-start.4
  71.7 2.7 copy-start.2
  71.8 2.8 collective-permute-start
  73.1 7.5 %collective-permute-start.1 = (f32[128,1,8,128]{0,3,2,1:T(8,128)S(1)}, f32[128,1,8,128]{0,3,2,1:T(8,128)S(1)}, u32[]{:S(2)}, u32[]{:S(2)}) collective-permute-start(f32[128,1,8,128]{0,3,2,1:T(8,128)S(1)} %get-tuple-element.112), channel_id=1, source_target_pairs={{1,0},{2,1},{3,2},{4,3},{5,4},{6,5},{7,6},{8,7},{9,8},{10,9},{11,1... | collective-permute-start | bytes 1572872 | tf_op jit(solution)/shard_map/ppermute | solution.py:18
  82.5 19.6 %copy-start.3 = (f32[128]{0:T(128)S(1)}, f32[128]{0:T(128)}, u32[]{:S(2)}) copy-start(f32[128]{0:T(128)} %param.10) | copy-start | bytes 1540
  82.6 13.7 %collective-permute-start.2 = (f32[128,1,8,128]{0,3,2,1:T(8,128)S(1)}, f32[128,1,8,128]{0,3,2,1:T(8,128)S(1)}, u32[]{:S(2)}, u32[]{:S(2)}) collective-permute-start(f32[128,1,8,128]{0,3,2,1:T(8,128)S(1)} %get-tuple-element.109), channel_id=1, source_target_pairs={{0,1},{1,2},{2,3},{3,4},{4,5},{5,6},{6,7},{7,8},{8,9},{9,10},{10,1... | collective-permute-start | bytes 1572872 | tf_op jit(solution)/shard_map/ppermute | solution.py:17
  94.8 7.3 %collective-permute-start.3 = (f32[128,1,8,128]{0,3,2,1:T(8,128)S(1)}, f32[128,1,8,128]{0,3,2,1:T(8,128)S(1)}, u32[]{:S(2)}, u32[]{:S(2)}) collective-permute-start(f32[128,1,8,128]{0,3,2,1:T(8,128)S(1)} %get-tuple-element.110), channel_id=1, source_target_pairs={{1,0},{2,1},{3,2},{4,3},{5,4},{6,5},{7,6},{8,7},{9,8},{10,9},{11,1... | collective-permute-start | bytes 1572872 | tf_op jit(solution)/shard_map/ppermute | solution.py:18
  105.3 18.6 %all-to-all-start = ((bf16[128,8,512]{2,0,1:T(8,128)(2,1)}), bf16[128,8,512]{2,0,1:T(8,128)(2,1)S(1)}, u32[]{:S(2)}, u32[]{:S(2)}) async-start(bf16[128,8,512]{2,0,1:T(8,128)(2,1)} %copy.17), calls=%async_computation | async-start | bytes 2097152 | tf_op jit(solution)/shard_map/all_to_all | solution.py:64
  331.0 1.3 copy-start.1
  332.3 4.5 %copy-start = (f32[128,4,8,128]{0,3,2,1:T(8,128)S(1)}, f32[128,4,8,128]{0,3,2,1:T(8,128)}, u32[]{:S(2)}) copy-start(f32[128,4,8,128]{0,3,2,1:T(8,128)} %get-tuple-element.108) | copy-start | bytes 6291460
  332.3 36.6 %all-to-all-start.1 = ((f32[8,128,512]{2,1,0:T(8,128)}), f32[8,128,512]{2,1,0:T(8,128)}, u32[]{:S(2)}, u32[]{:S(2)}) async-start(f32[8,128,512]{2,1,0:T(8,128)} %bitcast.23), calls=%async_computation.1 | async-start | bytes 4194304 | tf_op jit(solution)/shard_map/all_to_all | solution.py:68
Sparse Core Ops, SparseCore 0:
  9.6 60.0 all-gather.2
  72.0 207.4 all-gather.4
where the time goes:
time: 381 us; the launch traced here: 380 us
  waiting for transfers between devices  275 us (72%)
  matrix products  50.7 us (13%)
  starting transfers between devices  24.2 us (6%)
  between operations  14.2 us (4%)
  local copies, waits for them, and re-layouts  10.6 us (3%)
  other arithmetic  3.97 us (1%)
    all_gather x1, waiting for transfers between devices, local(): lax.all_gather(full_slices, 'space', axis=0, tiled=True)  156 us
    all_gather x1, waiting for transfers between devices, local(): full_slices = lax.all_gather(kernel_slices, 'vel', axis=2, tiled=True)  61.7 us
    dot_general x16, matrix products, one_slice(): lax.dot_general(matrix, source, (((0,), (0,)), ((), ())), preferred_eleme...  50.7 us
    all_to_all x1, waiting for transfers between devices, local(): lax.all_to_all(summed, 'vel', split_axis=0, concat_axis=1, tiled=True)  30.1 us
    all_to_all x1, waiting for transfers between devices, local(): lax.all_to_all(flattened, 'vel', split_axis=1, concat_axis=0, tiled=True)  15.1 us
    ppermute x2, starting transfers between devices, extended(): before = lax.ppermute(last, axis, up)  13.5 us
    ppermute x2, waiting for transfers between devices, extended(): after = lax.ppermute(first, axis, down)  11.8 us
  transfers between devices with their start and end apart: 8, of which 8 were waited for; matrix products, arithmetic and copies ran while one was open for 2% of the time, Pallas kernels for 0%

commit v1 on v0

v1 whole, which is shorter than its diff:
```python
import jax
import jax.numpy as jnp
from jax import lax
from jax.experimental import pallas as pl
from jax.experimental.pallas import tpu as pltpu
from jax.sharding import PartitionSpec as P

SLICES = 16
LAYERS = 4
BOTH = ("vel", "space")
FLAT = [
    (y, z, x, h, c)
    for y in range(4)
    for z in range(2)
    for x in range(4)
    for h in range(2)
    for c in range(2)
]


def rank(y, z, x, h, c):
    return ((y % 4) * 2 + z) * 16 + (x % 4) * 4 + h * 2 + c


def shift(value, dy=0, dz=0, dx=0, dh=0, dc=0):
    pairs = [
        (rank(y, z, x, h, c), rank(y + dy, z ^ dz, x + dx, h ^ dh, c ^ dc)) for y, z, x, h, c in FLAT
    ]
    return lax.ppermute(value, BOTH, pairs)


def halos(density, limiter):
    codes = limiter.astype(jnp.bfloat16)[None]
    upper = jnp.concatenate([density[:, 2:].astype(jnp.bfloat16), codes[:, 2:]], 0)
    lower = jnp.concatenate([density[:, :2].astype(jnp.bfloat16), codes[:, :2]], 0)
    size = lax.axis_size("space")
    up = [(i, i + 1) for i in range(size - 1)]
    below = lax.ppermute(upper, "space", up)
    above = lax.ppermute(lower, "space", [(j, i) for i, j in up])
    return below, above


def transport(density, limiter, heading, courant, below, above):
    rows = density.shape[0]
    f32 = jnp.float32
    padded = jnp.concatenate([below[:rows].astype(f32), density, above[:rows].astype(f32)], 1)
    codes = jnp.concatenate(
        [below[rows:, 1:], limiter[None].astype(jnp.bfloat16), above[rows:, :1]], 1
    ).astype(f32)
    middle = padded[:, 1:-1]
    left = middle - padded[:, :-2]
    right = padded[:, 2:] - middle
    minmod = jnp.where(
        left * right > 0, jnp.sign(left) * jnp.minimum(jnp.abs(left), jnp.abs(right)), 0.0
    )
    slope = jnp.where(codes == 1, minmod, jnp.where(codes == 2, 0.5 * (left + right), 0.0))
    upwind = (2 * heading - 1).astype(f32)[:, None, None, None]
    rebuilt = middle + 0.5 * upwind * slope
    forward = (heading == 1)[:, None, None, None]
    upstream = jnp.where(forward, rebuilt[:, :-2], rebuilt[:, 2:])
    return density - courant[:, None, None, None] * (rebuilt[:, 1:-1] - upstream)


def gather_slices(kernel_slices):
    z = lax.axis_index("vel") % 2
    own = kernel_slices[0].reshape(4, 2, 128, 128)
    keep = lax.dynamic_index_in_dim(own, z, 1, keepdims=False).reshape(512, 128).T
    send = lax.dynamic_index_in_dim(own, 1 - z, 1, keepdims=False).reshape(512, 128).T
    here = shift(send, dz=1)
    far = shift(keep, dh=1)
    cross = shift(send, dz=1, dh=1)
    base = jnp.concatenate([keep, here, far, cross], 0)
    one = shift(base, dx=1)
    three = shift(base, dx=-1)
    two_a = shift(one[:512 // 2], dx=1)
    two_b = shift(three[512 // 2 :], dx=-1)
    pieces = [base, one, three, two_a, two_b]
    return pieces + [shift(p, dc=1) for p in pieces]


ORDER = [(0, 0), (0, 1), (3, 0), (3, 1), (1, 0), (1, 1), (2, 0), (2, 1)]


def weight_rows():
    vel, space = lax.axis_index("vel"), lax.axis_index("space")
    y, z = vel // 2, vel % 2
    x, h, c = space // 4, (space // 2) % 2, space % 2
    rows = []
    for dc in range(2):
        for dx, dh in ORDER:
            s = ((x + dx) % 4) * 4 + (h ^ dh) * 2 + (c ^ dc)
            v = s // 2
            rows.append(((v // 2 - y) % 4) * 4 + ((v % 2) ^ z) * 2 + s % 2)
    return jnp.stack(rows + [y] + [y] * 15).astype(jnp.int32)


def collide(table, pieces, blocks, weights):
    cells = blocks[0].shape[1]
    tile = 512

    def kernel(table_ref, w_ref, *refs):
        slabs = refs[:10]
        parts = refs[10:14]
        mine_ref, other_ref, k_ref, m_ref, sem_k, sem_m = refs[14:]
        y = table_ref[SLICES]
        loads = []
        for d in range(4):
            at = pl.multiple_of(((y + d) % 4) * 128, 128)
            loads.append(pltpu.make_async_copy(parts[d], m_ref.at[pl.ds(at, 128)], sem_m.at[d]))
        row, starts = 0, []
        for i in range(10):
            n = slabs[i].shape[0]
            loads.append(
                pltpu.make_async_copy(slabs[i], k_ref.at[pl.ds(row, n)], sem_k.at[i])
            )
            starts.append(row // 256)
            row += n
        for load in loads:
            load.start()
        for load in loads[:4]:
            load.wait()
        for t in range(cells // tile):
            cols = pl.ds(t * tile, tile)
            moved = m_ref[:, cols]
            total = jnp.zeros((256, tile), jnp.float32)
            for s in range(SLICES):
                if t == 0 and s in starts:
                    loads[4 + starts.index(s)].wait()
                product = jnp.dot(
                    k_ref[s * 256 : (s + 1) * 256], moved, preferred_element_type=jnp.float32
                )
                total = total + w_ref[pl.ds(table_ref[s], 1), cols] * product
            mine_ref[:, cols] = total[:128]
            other_ref[:, cols] = total[128:].astype(jnp.bfloat16)

    anywhere = pl.BlockSpec(memory_space=pl.ANY)
    vmem = pl.BlockSpec(memory_space=pltpu.VMEM)
    return pl.pallas_call(
        kernel,
        out_shape=(
            jax.ShapeDtypeStruct((128, cells), jnp.float32),
            jax.ShapeDtypeStruct((128, cells), jnp.bfloat16),
        ),
        in_specs=[pl.BlockSpec(memory_space=pltpu.SMEM), vmem] + [anywhere] * 14,
        out_specs=(vmem, vmem),
        scratch_shapes=[
            pltpu.VMEM((SLICES * 256, 512), jnp.bfloat16),
            pltpu.VMEM((512, cells), jnp.bfloat16),
            pltpu.SemaphoreType.DMA((10,)),
            pltpu.SemaphoreType.DMA((4,)),
        ],
        compiler_params=pltpu.CompilerParams(vmem_limit_bytes=24 << 20),
        cost_estimate=pl.CostEstimate(
            flops=2 * SLICES * 256 * 512 * cells, bytes_accessed=6 << 20, transcendentals=0
        ),
        name="collide",
    )(table, weights, *pieces, *blocks)


def local(density, limiter, heading, courant, kernel_slices):
    below, above = halos(density, limiter)
    pieces = gather_slices(kernel_slices)
    transported = transport(density, limiter, heading, courant, below, above)
    cells = density.shape[2] * density.shape[3]
    moved = transported.astype(jnp.bfloat16)
    chunks = [moved[:, i].reshape(-1, cells) for i in range(LAYERS)]
    own = moved.reshape(2, 64, -1)[:, 0]
    rows = jnp.concatenate([own, shift(own, dz=1)], 0)
    weights = jnp.concatenate(
        [rows, shift(rows, dy=-1), shift(rows, dy=2), shift(rows, dy=1)], 0
    ).astype(jnp.float32)
    table = weight_rows()
    results = []
    for i, block in enumerate(chunks):
        before = shift(block, dy=1)
        after = shift(block, dy=-1)
        across = shift(before, dy=1) if i % 2 == 0 else shift(after, dy=-1)
        mine, other = collide(
            table, pieces, [block, after, across, before], weights[:, i * cells : (i + 1) * cells]
        )
        got = shift(other, dz=1)
        results.append((mine + got.astype(jnp.float32)).reshape(-1, 1, *density.shape[2:]))
    return transported, jnp.concatenate(results, 1)


def solution(mesh):
    return jax.shard_map(
        local,
        mesh=mesh,
        in_specs=(
            P("vel", "space", None, None),
            P("space", None, None),
            P("vel"),
            P("vel"),
            P("space", None, "vel"),
        ),
        out_specs=(P("vel", "space", None, None), P("vel", "space", None, None)),
        check_vma=False,
    )
```

time: 381 us -> 134 us (0.35)
  waiting for transfers between devices: 275 us -> 27.5 us
  matrix products: 50.7 us -> 0 us
  Pallas kernels: 0 us -> 28.9 us
  starting transfers between devices: 24.2 us -> 52.3 us
  between operations: 14.2 us -> 1.14 us
  other arithmetic: 3.97 us -> 11.6 us
    all_gather x2 -> x0, waiting for transfers between devices: 217 us -> none  [the longest x1 156 us: local(): lax.all_gather(full_slices, 'space', axis=0, tiled=True)]
    dot_general x16 -> x0, matrix products: 50.7 us -> none  [one_slice(): lax.dot_general(matrix, source, (((0,), (0,)), ((), ())), preferred_eleme...]
    all_to_all x2 -> x0, waiting for transfers between devices: 45.2 us -> none  [the longest x1 30.1 us: local(): lax.all_to_all(summed, 'vel', split_axis=0, concat_axis=1, tiled=True)]
    ppermute x4 -> x34, starting transfers between devices: 16.1 us -> 52.3 us  [the longest x32 47.8 us: shift(): return lax.ppermute(value, BOTH, pairs)]
    pallas_call x0 -> x4, Pallas kernels: none -> 28.9 us  [collide(): pl.pallas_call(kernel, out_shape=(jax.ShapeDtypeStruct((128, cells), jnp....]
    ppermute x4 -> x34, waiting for transfers between devices: 12.1 us -> 27.5 us  [the longest x32 26.6 us: shift(): return lax.ppermute(value, BOTH, pairs)]
    all_to_all x2 -> x0, starting transfers between devices: 8.07 us -> none  [the longest x1 4.51 us: local(): lax.all_to_all(summed, 'vel', split_axis=0, concat_axis=1, tiled=True)]
  transfers between devices with their start and end apart: 8 -> 34, of which waited for: 8 -> 10; matrix products, arithmetic and copies ran while one was open for 2% -> 7% of each run, Pallas kernels for 0% -> 22%
where the time goes in v1:
time: 134 us
  starting transfers between devices  52.3 us (39%)
  Pallas kernels  28.9 us (22%)
  waiting for transfers between devices  27.5 us (21%)
  local copies, waits for them, and re-layouts  12.1 us (9%)
  other arithmetic  11.6 us (9%)
    ppermute x32, starting transfers between devices, shift(): return lax.ppermute(value, BOTH, pairs)  47.8 us
    pallas_call x4, Pallas kernels, collide(): pl.pallas_call(kernel, out_shape=(jax.ShapeDtypeStruct((128, cells), jnp....  28.9 us
    ppermute x32, waiting for transfers between devices, shift(): return lax.ppermute(value, BOTH, pairs)  26.6 us
    unnamed x37, local copies, waits for them, and re-layouts  4.8 us
    ppermute x1, starting transfers between devices, halos(): below = lax.ppermute(upper, 'space', up)  3.05 us
  transfers between devices with their start and end apart: 34, of which 10 were waited for; matrix products, arithmetic and copies ran while one was open for 7% of the time, Pallas kernels for 22%

profile of v1, /device:TPU:0, one launch (start us, length us, event | category | flops | bytes accessed | tf_op | source)
XLA Modules:
  0.0 133.5 jit_solution(3214678454677854509)
XLA Ops:
  0.6 0.7 convert_bitcast_fusion
  1.4 1.8 %convert.4 = bf16[128,4,8,128]{3,2,1,0:T(8,128)(2,1)S(1)} convert(f32[128,4,8,128]{3,2,1,0:T(8,128)} %param.5) | non-fusion elementwise | flops 524288 | bytes 3145728 | tf_op jit(solution)/shard_map/convert.1
  3.5 1.4 %collective-permute-start.1 = (bf16[129,2,8,128]{3,2,1,0:T(8,128)(2,1)S(1)}, bf16[129,2,8,128]{3,2,1,0:T(8,128)(2,1)}, u32[]{:S(2)}, u32[]{:S(2)}) collective-permute-start(bf16[129,2,8,128]{3,2,1,0:T(8,128)(2,1)S(1)} %pad_maximum_fusion.4), channel_id=1, source_target_pairs={{1,0},{2,1},{3,2},{4,3},{5,4},{6,5},{7,6},{8,7},{9,8},{10,9},{11,1... | collective-permute-start | bytes 1585160 | tf_op jit(solution)/shard_map/ppermute | solution.py:39
  4.9 0.8 pad_maximum_fusion.3
  5.7 3.1 %collective-permute-start = (bf16[129,2,8,128]{3,2,1,0:T(8,128)(2,1)}, bf16[129,2,8,128]{3,2,1,0:T(8,128)(2,1)S(1)}, u32[]{:S(2)}, u32[]{:S(2)}) collective-permute-start(bf16[129,2,8,128]{3,2,1,0:T(8,128)(2,1)} %pad_maximum_fusion.3), channel_id=1, source_target_pairs={{0,1},{1,2},{2,3},{3,4},{4,5},{5,6},{6,7},{7,8},{8,9},{9,10},{10,1... | collective-permute-start | bytes 1585160 | tf_op jit(solution)/shard_map/ppermute | solution.py:38
  9.6 0.9 collective-permute-done
  10.5 1.1 slice_convert_fusion
  11.7 2.6 %multiply_add_fusion = f32[128,6,8,128]{3,2,1,0:T(8,128)S(1)} fusion(f32[128,2,8,128]{3,2,1,0:T(8,128)S(1)} %slice_convert_fusion, f32[128,4,8,128]{3,2,1,0:T(8,128)S(1)} %copy-done.4, f32[128,2,8,128]{3,2,1,0:T(8,128)S(1)} %slice_convert_fusion.1, f32[128]{0:T(128)S(1)} %convert_multiply_fusion, pred[6,8,128]{2,1,0:T(8,128)(4,1)S(1)} %get-tuple-element.33, ...), kind=kLoop, calls=%fused_computation.4 | loop fusion | flops 15728640 | bytes 7352832 | tf_op jit(solution)/shard_map/add | solution.py:58
  14.3 2.6 %fusion.3 = (bf16[128,4,8,128]{3,2,1,0:T(8,128)(2,1)}, f32[128,4,8,128]{3,2,1,0:T(8,128)}) fusion(f32[128,4,8,128]{3,2,1,0:T(8,128)S(1)} %copy-done.4, f32[128,6,8,128]{3,2,1,0:T(8,128)S(1)} %multiply_add_fusion, pred[128]{0:T(512)(128)(4,1)S(1)} %broadcast_compare_fusion, f32[128]{0:T(128)S(1)} %copy-done.12), kind=kLoop, calls=%fused_computation.35 | loop fusion | flops 2621440 | bytes 11534976 | tf_op jit(solution)/shard_map/convert_element_type | solution.py:165
  17.0 1.5 %reshape.80 = bf16[2,64,4096]{2,1,0:T(8,128)(2,1)S(1)} reshape(bf16[128,4,8,128]{3,2,1,0:T(8,128)(2,1)} %get-tuple-element.18) | data formatting | bytes 2097152 | tf_op jit(solution)/shard_map/reshape | solution.py:167
  18.6 2.1 %collective-permute-start.2 = (bf16[2,4096]{1,0:T(2,128)(2,1)S(1)}, bf16[2,4096]{1,0:T(2,128)(2,1)S(1)}, u32[]{:S(2)}, u32[]{:S(2)}) collective-permute-start(bf16[2,4096]{1,0:T(2,128)(2,1)S(1)} %bitcast.106), channel_id=1, source_target_pairs={{0,16},{1,17},{2,18},{3,19},{4,20},{5,21},{6,22},{7,23},{8,24},{9,... | collective-permute-start | bytes 49160 | tf_op jit(solution)/shard_map/ppermute | solution.py:29
  20.8 14.5 %collective-permute-start.8 = (bf16[128,512]{1,0:T(8,128)(2,1)S(1)}, bf16[128,512]{1,0:T(8,128)(2,1)S(1)}, u32[]{:S(2)}, u32[]{:S(2)}) collective-permute-start(bf16[128,512]{1,0:T(8,128)(2,1)S(1)} %bitcast.109), channel_id=1, source_target_pairs={{0,18},{1,19},{2,16},{3,17},{4,22},{5,23},{6,20},{7,21},{8,26},{9,... | collective-permute-start | bytes 393224 | tf_op jit(solution)/shard_map/ppermute | solution.py:29
  35.3 1.0 collective-permute-start.6
  37.1 3.1 %collective-permute-start.3 = (bf16[4,4096]{1,0:T(4,128)(2,1)S(1)}, bf16[4,4096]{1,0:T(4,128)(2,1)S(1)}, u32[]{:S(2)}, u32[]{:S(2)}) collective-permute-start(bf16[4,4096]{1,0:T(4,128)(2,1)S(1)} %pad_maximum_fusion.6), channel_id=1, source_target_pairs={{0,96},{1,97},{2,98},{3,99},{4,100},{5,101},{6,102},{7,103},{8,104... | collective-permute-start | bytes 98312 | tf_op jit(solution)/shard_map/ppermute | solution.py:29
  40.2 2.8 %collective-permute-done.7 = bf16[128,512]{1,0:T(8,128)(2,1)S(1)} collective-permute-done((bf16[128,512]{1,0:T(8,128)(2,1)S(1)}, bf16[128,512]{1,0:T(8,128)(2,1)S(1)}, u32[]{:S(2)}, u32[]{:S(2)}) %collective-permute-start.7) | collective-permute-done | bytes 131104 | tf_op jit(solution)/shard_map/ppermute | solution.py:29
  43.0 1.4 %collective-permute-start.9 = (bf16[512,512]{1,0:T(8,128)(2,1)S(1)}, bf16[512,512]{1,0:T(8,128)(2,1)S(1)}, u32[]{:S(2)}, u32[]{:S(2)}) collective-permute-start(bf16[512,512]{1,0:T(8,128)(2,1)S(1)} %pad_maximum_fusion.5.refs_0_), channel_id=1, source_target_pairs={{0,4},{1,5},{2,6},{3,7},{4,8},{5,9},{6,10},{7,11},{8,12},{9,13},{1... | collective-permute-start | bytes 1572872 | tf_op jit(solution)/shard_map/ppermute | solution.py:29
  44.4 1.9 %collective-permute-start.10 = (bf16[512,512]{1,0:T(8,128)(2,1)S(1)}, bf16[512,512]{1,0:T(8,128)(2,1)S(1)}, u32[]{:S(2)}, u32[]{:S(2)}) collective-permute-start(bf16[512,512]{1,0:T(8,128)(2,1)S(1)} %pad_maximum_fusion.5.refs_0_), channel_id=1, source_target_pairs={{0,12},{1,13},{2,14},{3,15},{4,0},{5,1},{6,2},{7,3},{8,4},{9,5},{1... | collective-permute-start | bytes 1572872 | tf_op jit(solution)/shard_map/ppermute | solution.py:29
  46.3 3.2 %collective-permute-start.4 = (bf16[4,4096]{1,0:T(4,128)(2,1)S(1)}, bf16[4,4096]{1,0:T(4,128)(2,1)S(1)}, u32[]{:S(2)}, u32[]{:S(2)}) collective-permute-start(bf16[4,4096]{1,0:T(4,128)(2,1)S(1)} %pad_maximum_fusion.6), channel_id=1, source_target_pairs={{0,64},{1,65},{2,66},{3,67},{4,68},{5,69},{6,70},{7,71},{8,72},{9,... | collective-permute-start | bytes 98312 | tf_op jit(solution)/shard_map/ppermute | solution.py:29
  50.1 0.7 collective-permute-start.5
  50.8 2.1 %fusion.5 = (bf16[128,1,8,128]{3,2,1,0:T(8,128)(2,1)}, bf16[128,1,8,128]{3,2,1,0:T(8,128)(2,1)S(1)}, bf16[128,1,8,128]{3,2,1,0:T(8,128)(2,1)S(1)}, bf16[128,1,8,128]{3,2,1,0:T(8,128)(2,1)}) fusion(bf16[128,4,8,128]{3,2,1,0:T(8,128)(2,1)} %get-tuple-element.18), kind=kLoop, calls=%fused_computation.36 | loop fusion | bytes 2097152 | tf_op jit(solution)/shard_map/slice | solution.py:166
  53.0 2.6 %collective-permute-start.30 = (bf16[128,1024]{1,0:T(8,128)(2,1)S(1)}, bf16[128,1024]{1,0:T(8,128)(2,1)}, u32[]{:S(2)}, u32[]{:S(2)}) collective-permute-start(bf16[128,1024]{1,0:T(8,128)(2,1)S(1)} %bitcast.84), channel_id=1, source_target_pairs={{0,96},{1,97},{2,98},{3,99},{4,100},{5,101},{6,102},{7,103},{8,104... | collective-permute-start | bytes 786440 | tf_op jit(solution)/shard_map/ppermute | solution.py:29
  55.9 1.6 %collective-permute-start.27 = (bf16[128,1024]{1,0:T(8,128)(2,1)S(1)}, bf16[128,1024]{1,0:T(8,128)(2,1)S(1)}, u32[]{:S(2)}, u32[]{:S(2)}) collective-permute-start(bf16[128,1024]{1,0:T(8,128)(2,1)S(1)} %bitcast.81), channel_id=1, source_target_pairs={{0,32},{1,33},{2,34},{3,35},{4,36},{5,37},{6,38},{7,39},{8,40},{9,... | collective-permute-start | bytes 786440 | tf_op jit(solution)/shard_map/ppermute | solution.py:29
  58.1 3.2 %collective-permute-done.30.refs_11_ = bf16[128,1024]{1,0:T(8,128)(2,1)} collective-permute-done((bf16[128,1024]{1,0:T(8,128)(2,1)S(1)}, bf16[128,1024]{1,0:T(8,128)(2,1)}, u32[]{:S(2)}, u32[]{:S(2)}) %collective-permute-start.30) | collective-permute-done | bytes 262176 | tf_op jit(solution)/shard_map/ppermute | solution.py:29
  61.4 0.7 slice.112
  62.1 3.9 %collective-permute-done.32.refs_13_ = bf16[128,1024]{1,0:T(8,128)(2,1)S(1)} collective-permute-done((bf16[128,1024]{1,0:T(8,128)(2,1)S(1)}, bf16[128,1024]{1,0:T(8,128)(2,1)S(1)}, u32[]{:S(2)}, u32[]{:S(2)}) %collective-permute-start.32) | collective-permute-done | bytes 262176 | tf_op jit(solution)/shard_map/ppermute | solution.py:29
  66.0 0.7 copy-done.2
  67.0 3.3 %collective-permute-done.27.refs_13_ = bf16[128,1024]{1,0:T(8,128)(2,1)S(1)} collective-permute-done((bf16[128,1024]{1,0:T(8,128)(2,1)S(1)}, bf16[128,1024]{1,0:T(8,128)(2,1)S(1)}, u32[]{:S(2)}, u32[]{:S(2)}) %collective-permute-start.27) | collective-permute-done | bytes 262176 | tf_op jit(solution)/shard_map/ppermute | solution.py:29
  70.4 3.0 %collective-permute-done.12.refs_4_ = bf16[256,512]{1,0:T(8,128)(2,1)} collective-permute-done((bf16[256,512]{1,0:T(8,128)(2,1)}, bf16[256,512]{1,0:T(8,128)(2,1)}, u32[]{:S(2)}, u32[]{:S(2)}) %collective-permute-start.12) | collective-permute-done | bytes 262176 | tf_op jit(solution)/shard_map/ppermute | solution.py:29
  73.6 1.0 copy.40
  74.6 1.0 copy.41
  75.6 1.7 %concatenate.52 = bf16[16,4096]{1,0:T(8,128)(2,1)S(1)} concatenate(bf16[2,4096]{1,0:T(2,128)(2,1)} %bitcast.108, bf16[2,4096]{1,0:T(2,128)(2,1)} %copy-done.8, bf16[4,4096]{1,0:T(4,128)(2,1)} %copy-done.9, bf16[4,4096]{1,0:T(4,128)(2,1)} %copy-done.10, bf16[4,4096]{1,0:T(4,128)(2,1)} %copy-done.11), dimensions={0} | concatenate | bytes 262144 | tf_op jit(solution)/shard_map/concatenate | solution.py:169
  77.6 1.5 %collective-permute-start.26 = (bf16[128,1024]{1,0:T(8,128)(2,1)S(1)}, bf16[128,1024]{1,0:T(8,128)(2,1)S(1)}, u32[]{:S(2)}, u32[]{:S(2)}) collective-permute-start(bf16[128,1024]{1,0:T(8,128)(2,1)S(1)} %bitcast.82), channel_id=1, source_target_pairs={{0,96},{1,97},{2,98},{3,99},{4,100},{5,101},{6,102},{7,103},{8,104... | collective-permute-start | bytes 786440 | tf_op jit(solution)/shard_map/ppermute | solution.py:29
  79.1 2.0 %collective-permute-start.24 = (bf16[128,1024]{1,0:T(8,128)(2,1)S(1)}, bf16[128,1024]{1,0:T(8,128)(2,1)S(1)}, u32[]{:S(2)}, u32[]{:S(2)}) collective-permute-start(bf16[128,1024]{1,0:T(8,128)(2,1)S(1)} %bitcast.91), channel_id=1, source_target_pairs={{0,32},{1,33},{2,34},{3,35},{4,36},{5,37},{6,38},{7,39},{8,40},{9,... | collective-permute-start | bytes 786440 | tf_op jit(solution)/shard_map/ppermute | solution.py:29
  81.8 0.9 copy-done.3
  82.7 7.8 %collide.7 = (f32[128,1024]{1,0:T(8,128)S(1)}, bf16[128,1024]{1,0:T(8,128)(2,1)S(1)}) custom-call(s32[32]{0:T(128)S(1)} %stack.86.table_ref, f32[16,1024]{1,0:T(8,128)S(1)} %get-tuple-element.31.w_ref, bf16[512,512]{1,0:T(8,128)(2,1)S(1)} %pad_maximum_fusion.5.refs_0_, bf16[512,512]{1,0:T(8,128)(2,1)S(1)} %collective-permute-done.9.refs_1_, ...), custom_call_target="tpu_custom_call" | custom-call | flops 4294967296 | bytes 6291456 | tf_op jit(solution)/shard_map/collide/pallas_call | solution.py:138
  90.5 3.2 %collective-permute-start.18 = (bf16[128,1024]{1,0:T(8,128)(2,1)S(1)}, bf16[128,1024]{1,0:T(8,128)(2,1)S(1)}, u32[]{:S(2)}, u32[]{:S(2)}) collective-permute-start(bf16[128,1024]{1,0:T(8,128)(2,1)S(1)} %bitcast.88), channel_id=1, source_target_pairs={{0,96},{1,97},{2,98},{3,99},{4,100},{5,101},{6,102},{7,103},{8,104... | collective-permute-start | bytes 786440 | tf_op jit(solution)/shard_map/ppermute | solution.py:29
  93.8 1.5 %collective-permute-start.23 = (bf16[128,1024]{1,0:T(8,128)(2,1)S(1)}, bf16[128,1024]{1,0:T(8,128)(2,1)S(1)}, u32[]{:S(2)}, u32[]{:S(2)}) collective-permute-start(bf16[128,1024]{1,0:T(8,128)(2,1)S(1)} %collective-permute-done.22.refs_11_), channel_id=1, source_target_pairs={{0,96},{1,97},{2,98},{3,99},{4,100},{5,101},{6,102},{7,103},{8,104... | collective-permute-start | bytes 786440 | tf_op jit(solution)/shard_map/ppermute | solution.py:29
  95.3 0.7 collective-permute-start.20
  96.0 4.9 %collective-permute-done.28.refs_12_ = bf16[128,1024]{1,0:T(8,128)(2,1)S(1)} collective-permute-done((bf16[128,1024]{1,0:T(8,128)(2,1)}, bf16[128,1024]{1,0:T(8,128)(2,1)S(1)}, u32[]{:S(2)}, u32[]{:S(2)}) %collective-permute-start.28) | collective-permute-done | bytes 262176 | tf_op jit(solution)/shard_map/ppermute | solution.py:29
  100.9 1.0 collective-permute-start.33
  101.9 7.0 %collide.6 = (f32[128,1024]{1,0:T(8,128)S(1)}, bf16[128,1024]{1,0:T(8,128)(2,1)S(1)}) custom-call(s32[32]{0:T(128)S(1)} %stack.86.table_ref, f32[16,1024]{1,0:T(8,128)S(1)} %get-tuple-element.30.w_ref, bf16[512,512]{1,0:T(8,128)(2,1)S(1)} %pad_maximum_fusion.5.refs_0_, bf16[512,512]{1,0:T(8,128)(2,1)S(1)} %collective-permute-done.9.refs_1_, ...), custom_call_target="tpu_custom_call" | custom-call | flops 4294967296 | bytes 6291456 | tf_op jit(solution)/shard_map/collide/pallas_call | solution.py:138
  108.9 1.1 collective-permute-start.29
  110.0 7.0 %collide.5 = (f32[128,1024]{1,0:T(8,128)S(1)}, bf16[128,1024]{1,0:T(8,128)(2,1)S(1)}) custom-call(s32[32]{0:T(128)S(1)} %stack.86.table_ref, f32[16,1024]{1,0:T(8,128)S(1)} %get-tuple-element.29.w_ref, bf16[512,512]{1,0:T(8,128)(2,1)S(1)} %pad_maximum_fusion.5.refs_0_, bf16[512,512]{1,0:T(8,128)(2,1)S(1)} %collective-permute-done.9.refs_1_, ...), custom_call_target="tpu_custom_call" | custom-call | flops 4294967296 | bytes 6291456 | tf_op jit(solution)/shard_map/collide/pallas_call | solution.py:138
  117.1 1.3 %collective-permute-start.25 = (bf16[128,1024]{1,0:T(8,128)(2,1)S(1)}, bf16[128,1024]{1,0:T(8,128)(2,1)S(1)}, u32[]{:S(2)}, u32[]{:S(2)}) collective-permute-start(bf16[128,1024]{1,0:T(8,128)(2,1)S(1)} %get-tuple-element.13), channel_id=1, source_target_pairs={{0,16},{1,17},{2,18},{3,19},{4,20},{5,21},{6,22},{7,23},{8,24},{9,... | collective-permute-start | bytes 786440 | tf_op jit(solution)/shard_map/ppermute | solution.py:29
  118.4 7.0 %collide.4 = (f32[128,1024]{1,0:T(8,128)S(1)}, bf16[128,1024]{1,0:T(8,128)(2,1)S(1)}) custom-call(s32[32]{0:T(128)S(1)} %stack.86.table_ref, f32[16,1024]{1,0:T(8,128)S(1)} %get-tuple-element.28.w_ref, bf16[512,512]{1,0:T(8,128)(2,1)S(1)} %pad_maximum_fusion.5.refs_0_, bf16[512,512]{1,0:T(8,128)(2,1)S(1)} %collective-permute-done.9.refs_1_, ...), custom_call_target="tpu_custom_call" | custom-call | flops 4294967296 | bytes 6291456 | tf_op jit(solution)/shard_map/collide/pallas_call | solution.py:138
  125.4 1.1 collective-permute-start.21
  127.1 4.8 %collective-permute-done.21 = bf16[128,1024]{1,0:T(8,128)(2,1)S(1)} collective-permute-done((bf16[128,1024]{1,0:T(8,128)(2,1)S(1)}, bf16[128,1024]{1,0:T(8,128)(2,1)S(1)}, u32[]{:S(2)}, u32[]{:S(2)}) %collective-permute-start.21) | collective-permute-done | bytes 262176 | tf_op jit(solution)/shard_map/ppermute | solution.py:29
  132.1 1.5 %pad_maximum_fusion.2 = f32[128,4,8,128]{3,2,1,0:T(8,128)} fusion(f32[128,1,8,128]{3,2,1,0:T(8,128)S(1)} %bitcast.93, f32[128,1,8,128]{3,2,1,0:T(8,128)S(1)} %bitcast.94, f32[128,1,8,128]{3,2,1,0:T(8,128)S(1)} %bitcast.95, f32[128,1,8,128]{3,2,1,0:T(8,128)S(1)} %bitcast.96), kind=kLoop, calls=%fused_computation.10 | loop fusion | flops 1572864 | bytes 4194304 | tf_op jit(solution)/shard_map/concatenate | solution.py:183
  (95 shorter events, 5.8 us)
Async XLA Ops:
  1.4 7.4 %copy-start.13 = (s32[128]{0:T(128)S(1)}, s32[128]{0:T(128)}, u32[]{:S(2)}) copy-start(s32[128]{0:T(128)} %param.7) | copy-start | bytes 1540
  1.4 7.5 %copy-start.7 = (s32[4,8,128]{2,1,0:T(8,128)S(1)}, s32[4,8,128]{2,1,0:T(8,128)}, u32[]{:S(2)}) copy-start(s32[4,8,128]{2,1,0:T(8,128)} %param.6) | copy-start | bytes 49156
  3.4 8.3 %copy-start.4 = (f32[128,4,8,128]{3,2,1,0:T(8,128)S(1)}, f32[128,4,8,128]{3,2,1,0:T(8,128)}, u32[]{:S(2)}) copy-start(f32[128,4,8,128]{3,2,1,0:T(8,128)} %param.5) | copy-start | bytes 6291460
  3.5 5.4 %collective-permute-start.1 = (bf16[129,2,8,128]{3,2,1,0:T(8,128)(2,1)S(1)}, bf16[129,2,8,128]{3,2,1,0:T(8,128)(2,1)}, u32[]{:S(2)}, u32[]{:S(2)}) collective-permute-start(bf16[129,2,8,128]{3,2,1,0:T(8,128)(2,1)S(1)} %pad_maximum_fusion.4), channel_id=1, source_target_pairs={{1,0},{2,1},{3,2},{4,3},{5,4},{6,5},{7,6},{8,7},{9,8},{10,9},{11,1... | collective-permute-start | bytes 1585160 | tf_op jit(solution)/shard_map/ppermute | solution.py:39
  5.7 4.8 %collective-permute-start = (bf16[129,2,8,128]{3,2,1,0:T(8,128)(2,1)}, bf16[129,2,8,128]{3,2,1,0:T(8,128)(2,1)S(1)}, u32[]{:S(2)}, u32[]{:S(2)}) collective-permute-start(bf16[129,2,8,128]{3,2,1,0:T(8,128)(2,1)} %pad_maximum_fusion.3), channel_id=1, source_target_pairs={{0,1},{1,2},{2,3},{3,4},{4,5},{5,6},{6,7},{7,8},{8,9},{9,10},{10,1... | collective-permute-start | bytes 1585160 | tf_op jit(solution)/shard_map/ppermute | solution.py:38
  11.7 2.6 %copy-start.12 = (f32[128]{0:T(128)S(1)}, f32[128]{0:T(128)}, u32[]{:S(2)}) copy-start(f32[128]{0:T(128)} %param.8) | copy-start | bytes 1540
  14.3 6.3 %copy-start.5 = (bf16[1,1024,128]{2,1,0:T(8,128)(2,1)S(1)}, bf16[1,1024,128]{2,1,0:T(8,128)(2,1)}, u32[]{:S(2)}) copy-start(bf16[1,1024,128]{2,1,0:T(8,128)(2,1)} %param.9) | copy-start | bytes 786436
  18.6 24.4 %copy-start.6 = (bf16[2,1,4096]{2,0,1:T(2,128)(2,1)}, bf16[2,1,4096]{2,0,1:T(2,128)(2,1)S(1)}, u32[]{:S(2)}) copy-start(bf16[2,1,4096]{2,0,1:T(2,128)(2,1)S(1)} %copy.42) | copy-start | bytes 49156
  18.6 18.5 %collective-permute-start.2 = (bf16[2,4096]{1,0:T(2,128)(2,1)S(1)}, bf16[2,4096]{1,0:T(2,128)(2,1)S(1)}, u32[]{:S(2)}, u32[]{:S(2)}) collective-permute-start(bf16[2,4096]{1,0:T(2,128)(2,1)S(1)} %bitcast.106), channel_id=1, source_target_pairs={{0,16},{1,17},{2,18},{3,19},{4,20},{5,21},{6,22},{7,23},{8,24},{9,... | collective-permute-start | bytes 49160 | tf_op jit(solution)/shard_map/ppermute | solution.py:29
  20.8 19.4 %collective-permute-start.8 = (bf16[128,512]{1,0:T(8,128)(2,1)S(1)}, bf16[128,512]{1,0:T(8,128)(2,1)S(1)}, u32[]{:S(2)}, u32[]{:S(2)}) collective-permute-start(bf16[128,512]{1,0:T(8,128)(2,1)S(1)} %bitcast.109), channel_id=1, source_target_pairs={{0,18},{1,19},{2,16},{3,17},{4,22},{5,23},{6,20},{7,21},{8,26},{9,... | collective-permute-start | bytes 393224 | tf_op jit(solution)/shard_map/ppermute | solution.py:29
  35.3 7.7 %collective-permute-start.6 = (bf16[128,512]{1,0:T(8,128)(2,1)S(1)}, bf16[128,512]{1,0:T(8,128)(2,1)S(1)}, u32[]{:S(2)}, u32[]{:S(2)}) collective-permute-start(bf16[128,512]{1,0:T(8,128)(2,1)S(1)} %bitcast.110), channel_id=1, source_target_pairs={{0,16},{1,17},{2,18},{3,19},{4,20},{5,21},{6,22},{7,23},{8,24},{9,... | collective-permute-start | bytes 393224 | tf_op jit(solution)/shard_map/ppermute | solution.py:29
  36.4 6.6 %collective-permute-start.7 = (bf16[128,512]{1,0:T(8,128)(2,1)S(1)}, bf16[128,512]{1,0:T(8,128)(2,1)S(1)}, u32[]{:S(2)}, u32[]{:S(2)}) collective-permute-start(bf16[128,512]{1,0:T(8,128)(2,1)S(1)} %bitcast.103), channel_id=1, source_target_pairs={{0,2},{1,3},{2,0},{3,1},{4,6},{5,7},{6,4},{7,5},{8,10},{9,11},{10,... | collective-permute-start | bytes 393224 | tf_op jit(solution)/shard_map/ppermute | solution.py:29
  37.0 5.9 %copy-start.8 = (bf16[2,4096]{1,0:T(2,128)(2,1)}, bf16[2,4096]{1,0:T(2,128)(2,1)S(1)}, u32[]{:S(2)}) copy-start(bf16[2,4096]{1,0:T(2,128)(2,1)S(1)} %collective-permute-done.2) | copy-start | bytes 49156
  37.1 12.5 %collective-permute-start.3 = (bf16[4,4096]{1,0:T(4,128)(2,1)S(1)}, bf16[4,4096]{1,0:T(4,128)(2,1)S(1)}, u32[]{:S(2)}, u32[]{:S(2)}) collective-permute-start(bf16[4,4096]{1,0:T(4,128)(2,1)S(1)} %pad_maximum_fusion.6), channel_id=1, source_target_pairs={{0,96},{1,97},{2,98},{3,99},{4,100},{5,101},{6,102},{7,103},{8,104... | collective-permute-start | bytes 98312 | tf_op jit(solution)/shard_map/ppermute | solution.py:29
  43.0 12.8 %collective-permute-start.9 = (bf16[512,512]{1,0:T(8,128)(2,1)S(1)}, bf16[512,512]{1,0:T(8,128)(2,1)S(1)}, u32[]{:S(2)}, u32[]{:S(2)}) collective-permute-start(bf16[512,512]{1,0:T(8,128)(2,1)S(1)} %pad_maximum_fusion.5.refs_0_), channel_id=1, source_target_pairs={{0,4},{1,5},{2,6},{3,7},{4,8},{5,9},{6,10},{7,11},{8,12},{9,13},{1... | collective-permute-start | bytes 1572872 | tf_op jit(solution)/shard_map/ppermute | solution.py:29
  44.4 13.1 %collective-permute-start.10 = (bf16[512,512]{1,0:T(8,128)(2,1)S(1)}, bf16[512,512]{1,0:T(8,128)(2,1)S(1)}, u32[]{:S(2)}, u32[]{:S(2)}) collective-permute-start(bf16[512,512]{1,0:T(8,128)(2,1)S(1)} %pad_maximum_fusion.5.refs_0_), channel_id=1, source_target_pairs={{0,12},{1,13},{2,14},{3,15},{4,0},{5,1},{6,2},{7,3},{8,4},{9,5},{1... | collective-permute-start | bytes 1572872 | tf_op jit(solution)/shard_map/ppermute | solution.py:29
  46.3 11.2 %collective-permute-start.13 = (bf16[512,512]{1,0:T(8,128)(2,1)S(1)}, bf16[512,512]{1,0:T(8,128)(2,1)S(1)}, u32[]{:S(2)}, u32[]{:S(2)}) collective-permute-start(bf16[512,512]{1,0:T(8,128)(2,1)S(1)} %pad_maximum_fusion.5.refs_0_), channel_id=1, source_target_pairs={{0,1},{1,0},{2,3},{3,2},{4,5},{5,4},{6,7},{7,6},{8,9},{9,8},{10,11... | collective-permute-start | bytes 1572872 | tf_op jit(solution)/shard_map/ppermute | solution.py:29
  46.3 6.6 %collective-permute-start.4 = (bf16[4,4096]{1,0:T(4,128)(2,1)S(1)}, bf16[4,4096]{1,0:T(4,128)(2,1)S(1)}, u32[]{:S(2)}, u32[]{:S(2)}) collective-permute-start(bf16[4,4096]{1,0:T(4,128)(2,1)S(1)} %pad_maximum_fusion.6), channel_id=1, source_target_pairs={{0,64},{1,65},{2,66},{3,67},{4,68},{5,69},{6,70},{7,71},{8,72},{9,... | collective-permute-start | bytes 98312 | tf_op jit(solution)/shard_map/ppermute | solution.py:29
  49.5 0.6 copy-start.9
  50.1 5.5 %collective-permute-start.5 = (bf16[4,4096]{1,0:T(4,128)(2,1)S(1)}, bf16[4,4096]{1,0:T(4,128)(2,1)S(1)}, u32[]{:S(2)}, u32[]{:S(2)}) collective-permute-start(bf16[4,4096]{1,0:T(4,128)(2,1)S(1)} %pad_maximum_fusion.6), channel_id=1, source_target_pairs={{0,32},{1,33},{2,34},{3,35},{4,36},{5,37},{6,38},{7,39},{8,40},{9,... | collective-permute-start | bytes 98312 | tf_op jit(solution)/shard_map/ppermute | solution.py:29
  53.0 13.1 %copy-start.10 = (bf16[4,4096]{1,0:T(4,128)(2,1)}, bf16[4,4096]{1,0:T(4,128)(2,1)S(1)}, u32[]{:S(2)}) copy-start(bf16[4,4096]{1,0:T(4,128)(2,1)S(1)} %collective-permute-done.4) | copy-start | bytes 98308
  53.0 8.3 %collective-permute-start.30 = (bf16[128,1024]{1,0:T(8,128)(2,1)S(1)}, bf16[128,1024]{1,0:T(8,128)(2,1)}, u32[]{:S(2)}, u32[]{:S(2)}) collective-permute-start(bf16[128,1024]{1,0:T(8,128)(2,1)S(1)} %bitcast.84), channel_id=1, source_target_pairs={{0,96},{1,97},{2,98},{3,99},{4,100},{5,101},{6,102},{7,103},{8,104... | collective-permute-start | bytes 786440 | tf_op jit(solution)/shard_map/ppermute | solution.py:29
  55.6 10.4 %copy-start.11 = (bf16[4,4096]{1,0:T(4,128)(2,1)}, bf16[4,4096]{1,0:T(4,128)(2,1)S(1)}, u32[]{:S(2)}) copy-start(bf16[4,4096]{1,0:T(4,128)(2,1)S(1)} %collective-permute-done.5) | copy-start | bytes 98308
  55.6 10.4 %collective-permute-start.32 = (bf16[128,1024]{1,0:T(8,128)(2,1)S(1)}, bf16[128,1024]{1,0:T(8,128)(2,1)S(1)}, u32[]{:S(2)}, u32[]{:S(2)}) collective-permute-start(bf16[128,1024]{1,0:T(8,128)(2,1)S(1)} %bitcast.85), channel_id=1, source_target_pairs={{0,32},{1,33},{2,34},{3,35},{4,36},{5,37},{6,38},{7,39},{8,40},{9,... | collective-permute-start | bytes 786440 | tf_op jit(solution)/shard_map/ppermute | solution.py:29
  55.9 14.4 %collective-permute-start.27 = (bf16[128,1024]{1,0:T(8,128)(2,1)S(1)}, bf16[128,1024]{1,0:T(8,128)(2,1)S(1)}, u32[]{:S(2)}, u32[]{:S(2)}) collective-permute-start(bf16[128,1024]{1,0:T(8,128)(2,1)S(1)} %bitcast.81), channel_id=1, source_target_pairs={{0,32},{1,33},{2,34},{3,35},{4,36},{5,37},{6,38},{7,39},{8,40},{9,... | collective-permute-start | bytes 786440 | tf_op jit(solution)/shard_map/ppermute | solution.py:29
  57.5 21.6 %collective-permute-start.14 = (bf16[512,512]{1,0:T(8,128)(2,1)S(1)}, bf16[512,512]{1,0:T(8,128)(2,1)}, u32[]{:S(2)}, u32[]{:S(2)}) collective-permute-start(bf16[512,512]{1,0:T(8,128)(2,1)S(1)} %collective-permute-done.9.refs_1_), channel_id=1, source_target_pairs={{0,1},{1,0},{2,3},{3,2},{4,5},{5,4},{6,7},{7,6},{8,9},{9,8},{10,11... | collective-permute-start | bytes 1572872 | tf_op jit(solution)/shard_map/ppermute | solution.py:29
  57.6 21.6 %collective-permute-start.15 = (bf16[512,512]{1,0:T(8,128)(2,1)S(1)}, bf16[512,512]{1,0:T(8,128)(2,1)}, u32[]{:S(2)}, u32[]{:S(2)}) collective-permute-start(bf16[512,512]{1,0:T(8,128)(2,1)S(1)} %collective-permute-done.10.refs_2_), channel_id=1, source_target_pairs={{0,1},{1,0},{2,3},{3,2},{4,5},{5,4},{6,7},{7,6},{8,9},{9,8},{10,11... | collective-permute-start | bytes 1572872 | tf_op jit(solution)/shard_map/ppermute | solution.py:29
  61.3 9.0 %collective-permute-start.11 = (bf16[256,512]{1,0:T(8,128)(2,1)S(1)}, bf16[256,512]{1,0:T(8,128)(2,1)S(1)}, u32[]{:S(2)}, u32[]{:S(2)}) collective-permute-start(bf16[256,512]{1,0:T(8,128)(2,1)S(1)} %slice.111), channel_id=1, source_target_pairs={{0,4},{1,5},{2,6},{3,7},{4,8},{5,9},{6,10},{7,11},{8,12},{9,13},{1... | collective-permute-start | bytes 786440 | tf_op jit(solution)/shard_map/ppermute | solution.py:29
  66.0 0.7 copy-start.2
  66.7 6.7 %collective-permute-start.12 = (bf16[256,512]{1,0:T(8,128)(2,1)}, bf16[256,512]{1,0:T(8,128)(2,1)}, u32[]{:S(2)}, u32[]{:S(2)}) collective-permute-start(bf16[256,512]{1,0:T(8,128)(2,1)} %slice.112), channel_id=1, source_target_pairs={{0,12},{1,13},{2,14},{3,15},{4,0},{5,1},{6,2},{7,3},{8,4},{9,5},{1... | collective-permute-start | bytes 786440 | tf_op jit(solution)/shard_map/ppermute | solution.py:29
  70.3 3.1 %copy-start = (bf16[128,1024]{1,0:T(8,128)(2,1)}, bf16[128,1024]{1,0:T(8,128)(2,1)S(1)}, u32[]{:S(2)}) copy-start(bf16[128,1024]{1,0:T(8,128)(2,1)S(1)} %collective-permute-done.27.refs_13_) | copy-start | bytes 786436
  70.3 7.3 %collective-permute-start.31 = (bf16[128,1024]{1,0:T(8,128)(2,1)}, bf16[128,1024]{1,0:T(8,128)(2,1)}, u32[]{:S(2)}, u32[]{:S(2)}) collective-permute-start(bf16[128,1024]{1,0:T(8,128)(2,1)} %collective-permute-done.30.refs_11_), channel_id=1, source_target_pairs={{0,96},{1,97},{2,98},{3,99},{4,100},{5,101},{6,102},{7,103},{8,104... | collective-permute-start | bytes 786440 | tf_op jit(solution)/shard_map/ppermute | solution.py:29
  70.3 10.8 %collective-permute-start.16 = (bf16[256,512]{1,0:T(8,128)(2,1)S(1)}, bf16[256,512]{1,0:T(8,128)(2,1)}, u32[]{:S(2)}, u32[]{:S(2)}) collective-permute-start(bf16[256,512]{1,0:T(8,128)(2,1)S(1)} %collective-permute-done.11.refs_3_), channel_id=1, source_target_pairs={{0,1},{1,0},{2,3},{3,2},{4,5},{5,4},{6,7},{7,6},{8,9},{9,8},{10,11... | collective-permute-start | bytes 786440 | tf_op jit(solution)/shard_map/ppermute | solution.py:29
  73.4 8.2 %collective-permute-start.17 = (bf16[256,512]{1,0:T(8,128)(2,1)}, bf16[256,512]{1,0:T(8,128)(2,1)}, u32[]{:S(2)}, u32[]{:S(2)}) collective-permute-start(bf16[256,512]{1,0:T(8,128)(2,1)} %collective-permute-done.12.refs_4_), channel_id=1, source_target_pairs={{0,1},{1,0},{2,3},{3,2},{4,5},{5,4},{6,7},{7,6},{8,9},{9,8},{10,11... | collective-permute-start | bytes 786440 | tf_op jit(solution)/shard_map/ppermute | solution.py:29
  77.6 12.9 %collective-permute-start.26 = (bf16[128,1024]{1,0:T(8,128)(2,1)S(1)}, bf16[128,1024]{1,0:T(8,128)(2,1)S(1)}, u32[]{:S(2)}, u32[]{:S(2)}) collective-permute-start(bf16[128,1024]{1,0:T(8,128)(2,1)S(1)} %bitcast.82), channel_id=1, source_target_pairs={{0,96},{1,97},{2,98},{3,99},{4,100},{5,101},{6,102},{7,103},{8,104... | collective-permute-start | bytes 786440 | tf_op jit(solution)/shard_map/ppermute | solution.py:29
  79.1 14.7 %collective-permute-start.22 = (bf16[128,1024]{1,0:T(8,128)(2,1)S(1)}, bf16[128,1024]{1,0:T(8,128)(2,1)S(1)}, u32[]{:S(2)}, u32[]{:S(2)}) collective-permute-start(bf16[128,1024]{1,0:T(8,128)(2,1)S(1)} %bitcast.90), channel_id=1, source_target_pairs={{0,96},{1,97},{2,98},{3,99},{4,100},{5,101},{6,102},{7,103},{8,104... | collective-permute-start | bytes 786440 | tf_op jit(solution)/shard_map/ppermute | solution.py:29
  79.1 29.8 %collective-permute-start.24 = (bf16[128,1024]{1,0:T(8,128)(2,1)S(1)}, bf16[128,1024]{1,0:T(8,128)(2,1)S(1)}, u32[]{:S(2)}, u32[]{:S(2)}) collective-permute-start(bf16[128,1024]{1,0:T(8,128)(2,1)S(1)} %bitcast.91), channel_id=1, source_target_pairs={{0,32},{1,33},{2,34},{3,35},{4,36},{5,37},{6,38},{7,39},{8,40},{9,... | collective-permute-start | bytes 786440 | tf_op jit(solution)/shard_map/ppermute | solution.py:29
  81.1 14.1 %collective-permute-start.19 = (bf16[128,1024]{1,0:T(8,128)(2,1)S(1)}, bf16[128,1024]{1,0:T(8,128)(2,1)S(1)}, u32[]{:S(2)}, u32[]{:S(2)}) collective-permute-start(bf16[128,1024]{1,0:T(8,128)(2,1)S(1)} %bitcast.87), channel_id=1, source_target_pairs={{0,32},{1,33},{2,34},{3,35},{4,36},{5,37},{6,38},{7,39},{8,40},{9,... | collective-permute-start | bytes 786440 | tf_op jit(solution)/shard_map/ppermute | solution.py:29
  81.7 19.2 %collective-permute-start.28 = (bf16[128,1024]{1,0:T(8,128)(2,1)}, bf16[128,1024]{1,0:T(8,128)(2,1)S(1)}, u32[]{:S(2)}, u32[]{:S(2)}) collective-permute-start(bf16[128,1024]{1,0:T(8,128)(2,1)} %copy-done), channel_id=1, source_target_pairs={{0,32},{1,33},{2,34},{3,35},{4,36},{5,37},{6,38},{7,39},{8,40},{9,... | collective-permute-start | bytes 786440 | tf_op jit(solution)/shard_map/ppermute | solution.py:29
  81.8 0.9 copy-start.3
  82.7 19.2 %copy-start.1 = (bf16[128,1024]{1,0:T(8,128)(2,1)S(1)}, bf16[128,1024]{1,0:T(8,128)(2,1)}, u32[]{:S(2)}) copy-start(bf16[128,1024]{1,0:T(8,128)(2,1)} %copy-done) | copy-start | bytes 786436
  90.5 27.9 %collective-permute-start.18 = (bf16[128,1024]{1,0:T(8,128)(2,1)S(1)}, bf16[128,1024]{1,0:T(8,128)(2,1)S(1)}, u32[]{:S(2)}, u32[]{:S(2)}) collective-permute-start(bf16[128,1024]{1,0:T(8,128)(2,1)S(1)} %bitcast.88), channel_id=1, source_target_pairs={{0,96},{1,97},{2,98},{3,99},{4,100},{5,101},{6,102},{7,103},{8,104... | collective-permute-start | bytes 786440 | tf_op jit(solution)/shard_map/ppermute | solution.py:29
  93.8 16.2 %collective-permute-start.23 = (bf16[128,1024]{1,0:T(8,128)(2,1)S(1)}, bf16[128,1024]{1,0:T(8,128)(2,1)S(1)}, u32[]{:S(2)}, u32[]{:S(2)}) collective-permute-start(bf16[128,1024]{1,0:T(8,128)(2,1)S(1)} %collective-permute-done.22.refs_11_), channel_id=1, source_target_pairs={{0,96},{1,97},{2,98},{3,99},{4,100},{5,101},{6,102},{7,103},{8,104... | collective-permute-start | bytes 786440 | tf_op jit(solution)/shard_map/ppermute | solution.py:29
  95.3 23.1 %collective-permute-start.20 = (bf16[128,1024]{1,0:T(8,128)(2,1)S(1)}, bf16[128,1024]{1,0:T(8,128)(2,1)S(1)}, u32[]{:S(2)}, u32[]{:S(2)}) collective-permute-start(bf16[128,1024]{1,0:T(8,128)(2,1)S(1)} %collective-permute-done.19.refs_13_), channel_id=1, source_target_pairs={{0,32},{1,33},{2,34},{3,35},{4,36},{5,37},{6,38},{7,39},{8,40},{9,... | collective-permute-start | bytes 786440 | tf_op jit(solution)/shard_map/ppermute | solution.py:29
  100.9 25.7 %collective-permute-start.33 = (bf16[128,1024]{1,0:T(8,128)(2,1)S(1)}, bf16[128,1024]{1,0:T(8,128)(2,1)S(1)}, u32[]{:S(2)}, u32[]{:S(2)}) collective-permute-start(bf16[128,1024]{1,0:T(8,128)(2,1)S(1)} %get-tuple-element.17), channel_id=1, source_target_pairs={{0,16},{1,17},{2,18},{3,19},{4,20},{5,21},{6,22},{7,23},{8,24},{9,... | collective-permute-start | bytes 786440 | tf_op jit(solution)/shard_map/ppermute | solution.py:29
  108.9 17.7 %collective-permute-start.29 = (bf16[128,1024]{1,0:T(8,128)(2,1)S(1)}, bf16[128,1024]{1,0:T(8,128)(2,1)S(1)}, u32[]{:S(2)}, u32[]{:S(2)}) collective-permute-start(bf16[128,1024]{1,0:T(8,128)(2,1)S(1)} %get-tuple-element.15), channel_id=1, source_target_pairs={{0,16},{1,17},{2,18},{3,19},{4,20},{5,21},{6,22},{7,23},{8,24},{9,... | collective-permute-start | bytes 786440 | tf_op jit(solution)/shard_map/ppermute | solution.py:29
  117.1 9.8 %collective-permute-start.25 = (bf16[128,1024]{1,0:T(8,128)(2,1)S(1)}, bf16[128,1024]{1,0:T(8,128)(2,1)S(1)}, u32[]{:S(2)}, u32[]{:S(2)}) collective-permute-start(bf16[128,1024]{1,0:T(8,128)(2,1)S(1)} %get-tuple-element.13), channel_id=1, source_target_pairs={{0,16},{1,17},{2,18},{3,19},{4,20},{5,21},{6,22},{7,23},{8,24},{9,... | collective-permute-start | bytes 786440 | tf_op jit(solution)/shard_map/ppermute | solution.py:29
  125.4 6.5 %collective-permute-start.21 = (bf16[128,1024]{1,0:T(8,128)(2,1)S(1)}, bf16[128,1024]{1,0:T(8,128)(2,1)S(1)}, u32[]{:S(2)}, u32[]{:S(2)}) collective-permute-start(bf16[128,1024]{1,0:T(8,128)(2,1)S(1)} %get-tuple-element.11), channel_id=1, source_target_pairs={{0,16},{1,17},{2,18},{3,19},{4,20},{5,21},{6,22},{7,23},{8,24},{9,... | collective-permute-start | bytes 786440 | tf_op jit(solution)/shard_map/ppermute | solution.py:29

commit v2 on v1

v2 whole, which is shorter than its diff:
```python
import jax
import jax.numpy as jnp
from jax import lax
from jax.experimental import pallas as pl
from jax.experimental.pallas import tpu as pltpu
from jax.sharding import PartitionSpec as P

SLICES = 16
CHUNKS = ((0,), (1,), (2,), (3,))
BOTH = ("vel", "space")
FLAT = [
    (y, z, x, h, c)
    for y in range(4)
    for z in range(2)
    for x in range(4)
    for h in range(2)
    for c in range(2)
]
BF16, F32 = jnp.bfloat16, jnp.float32
ANY = pl.BlockSpec(memory_space=pl.ANY)
VMEM = pl.BlockSpec(memory_space=pltpu.VMEM)
SMEM = pl.BlockSpec(memory_space=pltpu.SMEM)


def rank(y, z, x, h, c):
    return ((y % 4) * 2 + z) * 16 + (x % 4) * 4 + h * 2 + c


def shift(value, dy=0, dz=0, dx=0, dh=0, dc=0):
    pairs = [
        (rank(y, z, x, h, c), rank(y + dy, z ^ dz, x + dx, h ^ dh, c ^ dc)) for y, z, x, h, c in FLAT
    ]
    return lax.ppermute(value, BOTH, pairs)


def after(value, *earlier):
    return lax.optimization_barrier((value, earlier))[0]


def shape(dims, dtype):
    return jax.ShapeDtypeStruct(dims, dtype)


def pack(density, limiter):
    rows = density.shape[0]

    def kernel(d_ref, l_ref, up_ref, down_ref):
        up_ref[:rows] = d_ref[:, 2:].astype(BF16)
        down_ref[:rows] = d_ref[:, :2].astype(BF16)
        codes = l_ref[...].astype(F32).astype(BF16)
        up_ref[rows] = codes[2:]
        down_ref[rows] = codes[:2]

    out = shape((rows + 1, 2, *density.shape[2:]), BF16)
    return pl.pallas_call(
        kernel, out_shape=(out, out), in_specs=[VMEM, VMEM], out_specs=(VMEM, VMEM), name="pack"
    )(density, limiter)


def split_slice(kernel_slice):
    def kernel(k_ref, keep_ref, send_ref):
        z = lax.axis_index("vel") & 1
        for y in range(4):
            cols = pl.ds(y * 128, 128)
            keep_ref[:, cols] = k_ref[y, z].astype(F32).T.astype(BF16)
            send_ref[:, cols] = k_ref[y, 1 - z].astype(F32).T.astype(BF16)

    out = shape((128, 512), BF16)
    return pl.pallas_call(
        kernel, out_shape=(out, out), in_specs=[VMEM], out_specs=(VMEM, VMEM), name="split_slice"
    )(kernel_slice.reshape(4, 2, 128, 128))


def transport(density, limiter, heading, courant, below, above):
    rows = density.shape[0]
    step = 32

    def kernel(h_ref, c_ref, d_ref, lo_ref, hi_ref, lo_code, hi_code, l_ref, t_ref, w_ref, *m_refs):
        first = pl.program_id(0) * step
        codes = [lo_code[0, 1].astype(F32)] + [l_ref[i].astype(F32) for i in range(4)]
        codes.append(hi_code[0, 0].astype(F32))
        minmod = [code == 1 for code in codes]
        central = [code == 2 for code in codes]

        def one(j, _):
            cell = [lo_ref[j, 0].astype(F32), lo_ref[j, 1].astype(F32)]
            cell += [d_ref[pl.ds(pl.multiple_of(j * 32 + 8 * i, 8), 8), :] for i in range(4)]
            cell += [hi_ref[j, 0].astype(F32), hi_ref[j, 1].astype(F32)]
            ahead = h_ref[first + j]
            half = 0.5 * (2 * ahead - 1).astype(F32)
            number = c_ref[first + j]
            diff = [cell[i + 1] - cell[i] for i in range(7)]
            rebuilt = []
            for i in range(6):
                left, right = diff[i], diff[i + 1]
                small = jnp.where(left > 0, jnp.minimum(left, right), jnp.maximum(left, right))
                small = jnp.where(left * right > 0, small, 0.0)
                slope = jnp.where(
                    minmod[i], small, jnp.where(central[i], 0.5 * (left + right), 0.0)
                )
                rebuilt.append(cell[i + 1] + half * slope)
            forward = jnp.full((8, 128), ahead, jnp.int32) == 1
            for i in range(4):
                upstream = jnp.where(forward, rebuilt[i], rebuilt[i + 2])
                value = cell[i + 2] - number * (rebuilt[i + 1] - upstream)
                t_ref[pl.ds(pl.multiple_of(j * 32 + 8 * i, 8), 8), :] = value
            return 0

        lax.fori_loop(0, step, one, 0, unroll=4)
        for m_ref, layers in zip(m_refs, CHUNKS, strict=True):
            for place, i in enumerate(layers):
                for y in range(8):
                    cols = pl.ds(place * 1024 + y * 128, 128)
                    m_ref[:, cols] = t_ref[pl.ds(8 * i + y, step, stride=32), :].astype(BF16)

        @pl.when(pl.program_id(0) % 2 == 0)
        def _():
            for i in range(4):
                w_ref[0, i] = t_ref[8 * i : 8 * i + 8, :].astype(BF16)

    halo = pl.BlockSpec((step, 2, 8, 128), lambda i: (i, 0, 0, 0))
    code = pl.BlockSpec((1, 2, 8, 128), lambda i: (rows, 0, 0, 0))
    flat = pl.BlockSpec((step * 32, 128), lambda i: (i, 0))
    outs = pl.pallas_call(
        kernel,
        grid=(rows // step,),
        out_shape=(shape((rows * 32, 128), F32), shape((2, 4, 8, 128), BF16))
        + tuple(shape((rows, 1024 * len(layers)), BF16) for layers in CHUNKS),
        in_specs=[
            SMEM,
            SMEM,
            flat,
            halo,
            halo,
            code,
            code,
            pl.BlockSpec((4, 8, 128), lambda i: (0, 0, 0)),
        ],
        out_specs=(flat, pl.BlockSpec((1, 4, 8, 128), lambda i: (i // 2, 0, 0, 0)))
        + tuple(pl.BlockSpec((step, 1024 * len(layers)), lambda i: (i, 0)) for layers in CHUNKS),
        cost_estimate=pl.CostEstimate(flops=2 << 20, bytes_accessed=6 << 20, transcendentals=0),
        name="transport",
    )(heading, courant, density.reshape(rows * 32, 128), below, above, below, above, limiter)
    return outs[0].reshape(density.shape), outs[1], outs[2:]


ORDER = [(0, 0), (0, 1), (3, 0), (3, 1), (1, 0), (1, 1), (2, 0), (2, 1)]


def weight_rows():
    vel, space = lax.axis_index("vel"), lax.axis_index("space")
    y, z = vel >> 1, vel & 1
    x, h, c = space >> 2, (space >> 1) & 1, space & 1
    rows = []
    for dc in range(2):
        for dx, dh in ORDER:
            v = (((x + dx) & 3) << 1) + (h ^ dh)
            rows.append(((((v >> 1) - y) & 3) << 2) + (((v & 1) ^ z) << 1) + (c ^ dc))
    return y, rows


def collide(layers, pieces, blocks, weights):
    cells = blocks[0].shape[1]
    tile = 512

    def kernel(*refs):
        w_parts = refs[:4]
        slabs = refs[4:14]
        parts = refs[14:18]
        mine_ref, other_ref, k_ref, m_ref, w_ref, sem_k, sem_m = refs[18:]
        y, places = weight_rows()
        loads = []
        for d in range(4):
            at = pl.multiple_of(((y + d) & 3) * 128, 128)
            loads.append(pltpu.make_async_copy(parts[d], m_ref.at[pl.ds(at, 128)], sem_m.at[d]))
        row, starts = 0, []
        for i in range(10):
            n = slabs[i].shape[0]
            loads.append(pltpu.make_async_copy(slabs[i], k_ref.at[pl.ds(row, n)], sem_k.at[i]))
            starts.append(row // 256)
            row += n
        for load in loads:
            load.start()
        for d in range(4):
            for i, layer in enumerate(layers):
                w_ref[4 * d : 4 * d + 4, i] = w_parts[d][:, layer].astype(F32)
        for load in loads[:4]:
            load.wait()
        for t in range(cells // tile):
            cols = pl.ds(t * tile, tile)
            moved = m_ref[:, cols]
            total = jnp.zeros((256, tile), F32)
            for s in range(SLICES):
                if t == 0 and s in starts:
                    loads[4 + starts.index(s)].wait()
                product = jnp.dot(
                    k_ref[s * 256 : (s + 1) * 256], moved, preferred_element_type=F32
                )
                lines = [
                    w_ref[places[s], t // 2, pl.ds((t % 2) * 4 + i, 1), :] for i in range(tile // 128)
                ]
                total = total + jnp.concatenate(lines, 1) * product
            mine_ref[:, cols] = total[:128]
            other_ref[:, cols] = total[128:].astype(BF16)

    return pl.pallas_call(
        kernel,
        out_shape=(shape((128, cells), F32), shape((128, cells), BF16)),
        in_specs=[VMEM] * 4 + [ANY] * 14,
        out_specs=(VMEM, VMEM),
        scratch_shapes=[
            pltpu.VMEM((SLICES * 256, 512), BF16),
            pltpu.VMEM((512, cells), BF16),
            pltpu.VMEM((SLICES, len(layers), 8, 128), F32),
            pltpu.SemaphoreType.DMA((10,)),
            pltpu.SemaphoreType.DMA((4,)),
        ],
        compiler_params=pltpu.CompilerParams(vmem_limit_bytes=24 << 20),
        cost_estimate=pl.CostEstimate(
            flops=2 * SLICES * 256 * 512 * cells, bytes_accessed=6 << 20, transcendentals=0
        ),
        name="collide",
    )(*weights, *pieces, *blocks)


def combine(mine, got):
    step = 32
    n = len(CHUNKS)

    def kernel(*refs):
        o_ref = refs[-1]
        for a_ref, b_ref, layers in zip(refs[:n], refs[n : 2 * n], CHUNKS, strict=True):
            for place, i in enumerate(layers):
                for y in range(8):
                    cols = pl.ds(place * 1024 + y * 128, 128)
                    o_ref[pl.ds(8 * i + y, step, stride=32), :] = a_ref[:, cols] + b_ref[
                        :, cols
                    ].astype(F32)

    blocks = [pl.BlockSpec((step, 1024 * len(layers)), lambda i: (i, 0)) for layers in CHUNKS]
    return pl.pallas_call(
        kernel,
        grid=(128 // step,),
        out_shape=shape((128 * 32, 128), F32),
        in_specs=blocks + blocks,
        out_specs=pl.BlockSpec((step * 32, 128), lambda i: (i, 0)),
        cost_estimate=pl.CostEstimate(flops=1 << 19, bytes_accessed=5 << 20, transcendentals=0),
        name="combine",
    )(*mine, *got)


def local(density, limiter, heading, courant, kernel_slices):
    size = lax.axis_size("space")
    up = [(i, i + 1) for i in range(size - 1)]

    upper, lower = pack(density, limiter)
    below = lax.ppermute(upper, "space", up)
    above = lax.ppermute(lower, "space", [(j, i) for i, j in up])

    keep, send = split_slice(after(kernel_slices[0], upper))
    here = shift(send, dz=1)
    far = shift(keep, dh=1)
    cross = shift(send, dz=1, dh=1)
    base = jnp.concatenate([keep, here, far, cross], 0)
    one = shift(base, dx=1)
    three = shift(base, dx=-1)

    below, above = after((below, above), base)
    transported, own, chunks = transport(density, limiter, heading, courant, below, above)

    gathered, done = [], None
    for i, block in enumerate(chunks):
        if done is not None:
            block = after(block, *done)
        done = before, behind = shift(block, dy=1), shift(block, dy=-1)
        across = shift(before, dy=1) if i % 2 else shift(behind, dy=-1)
        gathered.append([block, behind, across, before])

    own = after(own, one, three)
    rows = jnp.concatenate([own, shift(own, dz=1)], 0)
    weights = [rows, shift(rows, dy=-1), shift(rows, dy=2), shift(rows, dy=1)]

    pieces = [base, one, three, shift(one[:256], dx=1), shift(three[256:], dx=-1)]
    pieces = pieces + [shift(p, dc=1) for p in pieces]

    mine, got = [], []
    for layers, blocks in zip(CHUNKS, gathered, strict=True):
        m, other = collide(layers, pieces, blocks, weights)
        mine.append(m)
        got.append(shift(other, dz=1))
    return transported, combine(mine, got).reshape(density.shape)


def solution(mesh):
    return jax.shard_map(
        local,
        mesh=mesh,
        in_specs=(
            P("vel", "space", None, None),
            P("space", None, None),
            P("vel"),
            P("vel"),
            P("space", None, "vel"),
        ),
        out_specs=(P("vel", "space", None, None), P("vel", "space", None, None)),
        check_vma=False,
    )
```

time: 134 us -> 125 us (0.933)
  Pallas kernels: 28.9 us -> 41.8 us
  other arithmetic: 11.6 us -> 0 us
  local copies, waits for them, and re-layouts: 12.1 us -> 7.52 us
  waiting for transfers between devices: 27.5 us -> 24.4 us
  starting transfers between devices: 52.3 us -> 49.3 us
    pallas_call x4 -> x8, Pallas kernels: 28.9 us -> 41.8 us  [the longest x4 26.4 us: collide(): pl.pallas_call(kernel, out_shape=(shape((128, cells), F32), shape((128, c...]
    convert_element_type x4 -> x0, other arithmetic: 3.81 us -> none  [the longest x1 2.62 us: local(): moved = transported.astype(jnp.bfloat16)]
    slice x7 -> x2, local copies, waits for them, and re-layouts: 3.04 us -> 0.04 us  [the longest x1 0.02 us: local(): one[:256]]
    unnamed x37 -> x32, local copies, waits for them, and re-layouts: 4.8 us -> 7.47 us
    add x1 -> x0, other arithmetic: 2.57 us -> none  [transport(): rebuilt = middle + 0.5 * upwind * slope]
    concatenate x5 -> x0, other arithmetic: 2.42 us -> none  [the longest x1 1.46 us: local(): return (transported, jnp.concatenate(results, 1))]
    concatenate x3 -> x2, local copies, waits for them, and re-layouts: 2.34 us -> 0.02 us  [the longest x1 0.01 us: local(): base = jnp.concatenate([keep, here, far, cross], 0)]
    ppermute x32, waiting for transfers between devices: 26.6 us -> 24.4 us  [shift(): return lax.ppermute(value, BOTH, pairs)]
  transfers between devices with their start and end apart: 34 -> 34, of which waited for: 10 -> 9; matrix products, arithmetic and copies ran while one was open for 7% -> 1% of each run, Pallas kernels for 22% -> 26%
where the time goes in v2:
time: 125 us; the launch traced here: 124 us
  starting transfers between devices  49.3 us (39%)
  Pallas kernels  41.8 us (33%)
  waiting for transfers between devices  24.4 us (20%)
  local copies, waits for them, and re-layouts  7.52 us (6%)
    ppermute x32, starting transfers between devices, shift(): return lax.ppermute(value, BOTH, pairs)  46.7 us
    pallas_call x4, Pallas kernels, collide(): pl.pallas_call(kernel, out_shape=(shape((128, cells), F32), shape((128, c...  26.4 us
    ppermute x32, waiting for transfers between devices, shift(): return lax.ppermute(value, BOTH, pairs)  24.4 us
    unnamed x32, local copies, waits for them, and re-layouts  7.47 us
    pallas_call x1, Pallas kernels, transport(): pl.pallas_call(kernel, grid=(rows // step,), out_shape=(shape((rows * 32,...  6.13 us
    pallas_call x1, Pallas kernels, combine(): pl.pallas_call(kernel, grid=(128 // step,), out_shape=shape((128 * 32, 12...  4.8 us
    pallas_call x1, Pallas kernels, pack(): pl.pallas_call(kernel, out_shape=(out, out), in_specs=[VMEM, VMEM], out_s...  2.69 us
  transfers between devices with their start and end apart: 34, of which 9 were waited for; matrix products, arithmetic and copies ran while one was open for 1% of the time, Pallas kernels for 26%

profile of v2, /device:TPU:0, one launch (start us, length us, event | category | flops | bytes accessed | tf_op | source)
XLA Modules:
  0.0 123.9 jit_solution(14173561867696659681)
XLA Ops:
  0.6 2.7 %pack.1 = (bf16[129,2,8,128]{3,2,1,0:T(8,128)(2,1)}, bf16[129,2,8,128]{3,2,1,0:T(8,128)(2,1)}) custom-call(f32[128,4,8,128]{3,2,1,0:T(8,128)} %d_ref.1, s32[4,8,128]{2,1,0:T(8,128)} %l_ref.3), custom_call_target="tpu_custom_call" | custom-call | tf_op jit(solution)/shard_map/pack/pallas_call | solution.py:55
  3.3 1.8 %split_slice.1 = (bf16[128,512]{1,0:T(8,128)(2,1)}, bf16[128,512]{1,0:T(8,128)(2,1)}) custom-call(bf16[4,2,128,128]{3,2,1,0:T(8,128)(2,1)} %bitcast.7), custom_call_target="tpu_custom_call" | custom-call | tf_op jit(solution)/shard_map/split_slice/pallas_call | solution.py:69
  5.1 2.0 %collective-permute-start.2 = (bf16[128,512]{1,0:T(8,128)(2,1)}, bf16[128,512]{1,0:T(8,128)(2,1)S(1)}, u32[]{:S(2)}, u32[]{:S(2)}) collective-permute-start(bf16[128,512]{1,0:T(8,128)(2,1)} %get-tuple-element.31), channel_id=1, source_target_pairs={{0,16},{1,17},{2,18},{3,19},{4,20},{5,21},{6,22},{7,23},{8,24},{9,... | collective-permute-start | bytes 393224 | tf_op jit(solution)/shard_map/ppermute | solution.py:33
  7.1 2.5 %collective-permute-start.4 = (bf16[128,512]{1,0:T(8,128)(2,1)}, bf16[128,512]{1,0:T(8,128)(2,1)S(1)}, u32[]{:S(2)}, u32[]{:S(2)}) collective-permute-start(bf16[128,512]{1,0:T(8,128)(2,1)} %get-tuple-element.31), channel_id=1, source_target_pairs={{0,18},{1,19},{2,16},{3,17},{4,22},{5,23},{6,20},{7,21},{8,26},{9,... | collective-permute-start | bytes 393224 | tf_op jit(solution)/shard_map/ppermute | solution.py:33
  9.6 1.3 %collective-permute-start = (bf16[129,2,8,128]{3,2,1,0:T(8,128)(2,1)}, bf16[129,2,8,128]{3,2,1,0:T(8,128)(2,1)S(1)}, u32[]{:S(2)}, u32[]{:S(2)}) collective-permute-start(bf16[129,2,8,128]{3,2,1,0:T(8,128)(2,1)} %get-tuple-element.27), channel_id=1, source_target_pairs={{0,1},{1,2},{2,3},{3,4},{4,5},{5,6},{6,7},{7,8},{8,9},{9,10},{10,1... | collective-permute-start | bytes 1585160 | tf_op jit(solution)/shard_map/ppermute | solution.py:257
  10.9 1.7 %collective-permute-start.3 = (bf16[128,512]{1,0:T(8,128)(2,1)}, bf16[128,512]{1,0:T(8,128)(2,1)S(1)}, u32[]{:S(2)}, u32[]{:S(2)}) collective-permute-start(bf16[128,512]{1,0:T(8,128)(2,1)} %get-tuple-element.30), channel_id=1, source_target_pairs={{0,2},{1,3},{2,0},{3,1},{4,6},{5,7},{6,4},{7,5},{8,10},{9,11},{10,... | collective-permute-start | bytes 393224 | tf_op jit(solution)/shard_map/ppermute | solution.py:33
  12.7 1.3 %collective-permute-start.1 = (bf16[129,2,8,128]{3,2,1,0:T(8,128)(2,1)}, bf16[129,2,8,128]{3,2,1,0:T(8,128)(2,1)S(1)}, u32[]{:S(2)}, u32[]{:S(2)}) collective-permute-start(bf16[129,2,8,128]{3,2,1,0:T(8,128)(2,1)} %get-tuple-element.28), channel_id=1, source_target_pairs={{1,0},{2,1},{3,2},{4,3},{5,4},{6,5},{7,6},{8,7},{9,8},{10,9},{11,1... | collective-permute-start | bytes 1585160 | tf_op jit(solution)/shard_map/ppermute | solution.py:258
  14.0 0.9 constant_dynamic-update-slice_fusion.3
  14.9 3.3 %collective-permute-done.3 = bf16[128,512]{1,0:T(8,128)(2,1)S(1)} collective-permute-done((bf16[128,512]{1,0:T(8,128)(2,1)}, bf16[128,512]{1,0:T(8,128)(2,1)S(1)}, u32[]{:S(2)}, u32[]{:S(2)}) %collective-permute-start.3) | collective-permute-done | bytes 131104 | tf_op jit(solution)/shard_map/ppermute | solution.py:33
  18.2 9.8 %collective-permute-start.6 = (bf16[512,512]{1,0:T(8,128)(2,1)S(1)}, bf16[512,512]{1,0:T(8,128)(2,1)S(1)}, u32[]{:S(2)}, u32[]{:S(2)}) collective-permute-start(bf16[512,512]{1,0:T(8,128)(2,1)S(1)} %constant_dynamic-update-slice_fusion.refs_4_), channel_id=1, source_target_pairs={{0,12},{1,13},{2,14},{3,15},{4,0},{5,1},{6,2},{7,3},{8,4},{9,5},{1... | collective-permute-start | bytes 1572872 | tf_op jit(solution)/shard_map/ppermute | solution.py:33
  28.0 1.2 collective-permute-start.13
  29.2 0.8 copy-done.9
  30.2 6.1 %transport.1 = (f32[4096,128]{1,0:T(8,128)}, bf16[2,4,8,128]{3,2,1,0:T(8,128)(2,1)}, bf16[128,1024]{1,0:T(8,128)(2,1)}, bf16[128,1024]{1,0:T(8,128)(2,1)}, bf16[...) custom-call(s32[128]{0:T(128)} %h_ref.1, f32[128]{0:T(128)} %c_ref.1, f32[4096,128]{1,0:T(8,128)} %bitcast.5, ...), custom_call_target="tpu_custom_call" | custom-call | flops 2097152 | bytes 6291456 | tf_op jit(solution)/shard_map/transport/pallas_call | solution.py:124
  36.3 1.6 %collective-permute-start.20 = (bf16[128,1024]{1,0:T(8,128)(2,1)}, bf16[128,1024]{1,0:T(8,128)(2,1)S(1)}, u32[]{:S(2)}, u32[]{:S(2)}) collective-permute-start(bf16[128,1024]{1,0:T(8,128)(2,1)} %get-tuple-element.37.refs_14_), channel_id=1, source_target_pairs={{0,32},{1,33},{2,34},{3,35},{4,36},{5,37},{6,38},{7,39},{8,40},{9,... | collective-permute-start | bytes 786440 | tf_op jit(solution)/shard_map/ppermute | solution.py:33
  38.0 1.7 %collective-permute-start.18 = (bf16[128,1024]{1,0:T(8,128)(2,1)}, bf16[128,1024]{1,0:T(8,128)(2,1)S(1)}, u32[]{:S(2)}, u32[]{:S(2)}) collective-permute-start(bf16[128,1024]{1,0:T(8,128)(2,1)} %get-tuple-element.37.refs_14_), channel_id=1, source_target_pairs={{0,96},{1,97},{2,98},{3,99},{4,100},{5,101},{6,102},{7,103},{8,104... | collective-permute-start | bytes 786440 | tf_op jit(solution)/shard_map/ppermute | solution.py:33
  39.7 3.7 %collective-permute-start.12 = (bf16[256,512]{1,0:T(8,128)(2,1)S(1)}, bf16[256,512]{1,0:T(8,128)(2,1)S(1)}, u32[]{:S(2)}, u32[]{:S(2)}) collective-permute-start(bf16[256,512]{1,0:T(8,128)(2,1)S(1)} %slice.9), channel_id=1, source_target_pairs={{0,12},{1,13},{2,14},{3,15},{4,0},{5,1},{6,2},{7,3},{8,4},{9,5},{1... | collective-permute-start | bytes 786440 | tf_op jit(solution)/shard_map/ppermute | solution.py:33
  43.9 0.8 constant_dynamic-update-slice_fusion.5
  44.6 2.7 %collective-permute-done.7 = bf16[2,4,8,128]{3,2,1,0:T(8,128)(2,1)S(1)} collective-permute-done((bf16[2,4,8,128]{3,2,1,0:T(8,128)(2,1)}, bf16[2,4,8,128]{3,2,1,0:T(8,128)(2,1)S(1)}, u32[]{:S(2)}, u32[]{:S(2)}) %collective-permute-start.7) | collective-permute-done | bytes 16416 | tf_op jit(solution)/shard_map/ppermute | solution.py:33
  47.3 1.6 %collective-permute-start.10 = (bf16[4,4,8,128]{3,2,1,0:T(8,128)(2,1)S(1)}, bf16[4,4,8,128]{3,2,1,0:T(8,128)(2,1)S(1)}, u32[]{:S(2)}, u32[]{:S(2)}) collective-permute-start(bf16[4,4,8,128]{3,2,1,0:T(8,128)(2,1)S(1)} %constant_dynamic-update-slice_fusion.4.refs_0_), channel_id=1, source_target_pairs={{0,32},{1,33},{2,34},{3,35},{4,36},{5,37},{6,38},{7,39},{8,40},{9,... | collective-permute-start | bytes 98312 | tf_op jit(solution)/shard_map/ppermute | solution.py:33
  48.9 2.9 %collective-permute-start.9 = (bf16[4,4,8,128]{3,2,1,0:T(8,128)(2,1)S(1)}, bf16[4,4,8,128]{3,2,1,0:T(8,128)(2,1)S(1)}, u32[]{:S(2)}, u32[]{:S(2)}) collective-permute-start(bf16[4,4,8,128]{3,2,1,0:T(8,128)(2,1)S(1)} %constant_dynamic-update-slice_fusion.4.refs_0_), channel_id=1, source_target_pairs={{0,64},{1,65},{2,66},{3,67},{4,68},{5,69},{6,70},{7,71},{8,72},{9,... | collective-permute-start | bytes 98312 | tf_op jit(solution)/shard_map/ppermute | solution.py:33
  51.8 1.3 %collective-permute-start.8 = (bf16[4,4,8,128]{3,2,1,0:T(8,128)(2,1)S(1)}, bf16[4,4,8,128]{3,2,1,0:T(8,128)(2,1)S(1)}, u32[]{:S(2)}, u32[]{:S(2)}) collective-permute-start(bf16[4,4,8,128]{3,2,1,0:T(8,128)(2,1)S(1)} %constant_dynamic-update-slice_fusion.4.refs_0_), channel_id=1, source_target_pairs={{0,96},{1,97},{2,98},{3,99},{4,100},{5,101},{6,102},{7,103},{8,104... | collective-permute-start | bytes 98312 | tf_op jit(solution)/shard_map/ppermute | solution.py:33
  53.4 0.9 collective-permute-done.9.refs_2_
  54.4 1.4 %collective-permute-done.8.refs_1_ = bf16[4,4,8,128]{3,2,1,0:T(8,128)(2,1)S(1)} collective-permute-done((bf16[4,4,8,128]{3,2,1,0:T(8,128)(2,1)S(1)}, bf16[4,4,8,128]{3,2,1,0:T(8,128)(2,1)S(1)}, u32[]{:S(2)}, u32[]{:S(2)}) %collective-permute-start.8) | collective-permute-done | bytes 32800 | tf_op jit(solution)/shard_map/ppermute | solution.py:33
  55.9 3.1 %collective-permute-start.21 = (bf16[128,1024]{1,0:T(8,128)(2,1)}, bf16[128,1024]{1,0:T(8,128)(2,1)S(1)}, u32[]{:S(2)}, u32[]{:S(2)}) collective-permute-start(bf16[128,1024]{1,0:T(8,128)(2,1)} %get-tuple-element.40.refs_14_), channel_id=1, source_target_pairs={{0,96},{1,97},{2,98},{3,99},{4,100},{5,101},{6,102},{7,103},{8,104... | collective-permute-start | bytes 786440 | tf_op jit(solution)/shard_map/ppermute | solution.py:33
  59.0 1.9 %collective-permute-done.11.refs_7_ = bf16[256,512]{1,0:T(8,128)(2,1)S(1)} collective-permute-done((bf16[256,512]{1,0:T(8,128)(2,1)S(1)}, bf16[256,512]{1,0:T(8,128)(2,1)S(1)}, u32[]{:S(2)}, u32[]{:S(2)}) %collective-permute-start.11) | collective-permute-done | bytes 262176 | tf_op jit(solution)/shard_map/ppermute | solution.py:33
  60.9 3.6 %collective-permute-done.22.refs_17_ = bf16[128,1024]{1,0:T(8,128)(2,1)S(1)} collective-permute-done((bf16[128,1024]{1,0:T(8,128)(2,1)}, bf16[128,1024]{1,0:T(8,128)(2,1)S(1)}, u32[]{:S(2)}, u32[]{:S(2)}) %collective-permute-start.22) | collective-permute-done | bytes 262176 | tf_op jit(solution)/shard_map/ppermute | solution.py:33
  64.5 1.6 %collective-permute-done.21.refs_15_ = bf16[128,1024]{1,0:T(8,128)(2,1)S(1)} collective-permute-done((bf16[128,1024]{1,0:T(8,128)(2,1)}, bf16[128,1024]{1,0:T(8,128)(2,1)S(1)}, u32[]{:S(2)}, u32[]{:S(2)}) %collective-permute-start.21) | collective-permute-done | bytes 262176 | tf_op jit(solution)/shard_map/ppermute | solution.py:33
  66.1 4.1 %collective-permute-done.19.refs_16_ = bf16[128,1024]{1,0:T(8,128)(2,1)S(1)} collective-permute-done((bf16[128,1024]{1,0:T(8,128)(2,1)S(1)}, bf16[128,1024]{1,0:T(8,128)(2,1)S(1)}, u32[]{:S(2)}, u32[]{:S(2)}) %collective-permute-start.19) | collective-permute-done | bytes 262176 | tf_op jit(solution)/shard_map/ppermute | solution.py:33
  70.2 1.3 %collective-permute-start.26 = (bf16[128,1024]{1,0:T(8,128)(2,1)}, bf16[128,1024]{1,0:T(8,128)(2,1)S(1)}, u32[]{:S(2)}, u32[]{:S(2)}) collective-permute-start(bf16[128,1024]{1,0:T(8,128)(2,1)} %get-tuple-element.43.refs_14_), channel_id=1, source_target_pairs={{0,32},{1,33},{2,34},{3,35},{4,36},{5,37},{6,38},{7,39},{8,40},{9,... | collective-permute-start | bytes 786440 | tf_op jit(solution)/shard_map/ppermute | solution.py:33
  71.5 2.0 %collective-permute-start.24 = (bf16[128,1024]{1,0:T(8,128)(2,1)}, bf16[128,1024]{1,0:T(8,128)(2,1)S(1)}, u32[]{:S(2)}, u32[]{:S(2)}) collective-permute-start(bf16[128,1024]{1,0:T(8,128)(2,1)} %get-tuple-element.43.refs_14_), channel_id=1, source_target_pairs={{0,96},{1,97},{2,98},{3,99},{4,100},{5,101},{6,102},{7,103},{8,104... | collective-permute-start | bytes 786440 | tf_op jit(solution)/shard_map/ppermute | solution.py:33
  73.5 0.9 copy-done.7
  74.5 6.6 %collide.4 = (f32[128,1024]{1,0:T(8,128)S(1)}, bf16[128,1024]{1,0:T(8,128)(2,1)S(1)}) custom-call(bf16[4,4,8,128]{3,2,1,0:T(8,128)(2,1)S(1)} %constant_dynamic-update-slice_fusion.4.refs_0_, bf16[4,4,8,128]{3,2,1,0:T(8,128)(2,1)S(1)} %collective-permute-done.8.refs_1_, bf16[4,4,8,128]{3,2,1,0:T(8,128)(2,1)S(1)} %collective-permute-done.9.refs_2_, ...), custom_call_target="tpu_custom_call" | custom-call | flops 4294967296 | bytes 6291456 | tf_op jit(solution)/shard_map/collide/pallas_call | solution.py:206
  81.1 0.8 copy-done
  82.4 1.3 %collective-permute-start.28 = (bf16[128,1024]{1,0:T(8,128)(2,1)S(1)}, bf16[128,1024]{1,0:T(8,128)(2,1)S(1)}, u32[]{:S(2)}, u32[]{:S(2)}) collective-permute-start(bf16[128,1024]{1,0:T(8,128)(2,1)S(1)} %copy-done.4), channel_id=1, source_target_pairs={{0,32},{1,33},{2,34},{3,35},{4,36},{5,37},{6,38},{7,39},{8,40},{9,... | collective-permute-start | bytes 786440 | tf_op jit(solution)/shard_map/ppermute | solution.py:33
  83.7 2.0 %collective-permute-start.27 = (bf16[128,1024]{1,0:T(8,128)(2,1)S(1)}, bf16[128,1024]{1,0:T(8,128)(2,1)S(1)}, u32[]{:S(2)}, u32[]{:S(2)}) collective-permute-start(bf16[128,1024]{1,0:T(8,128)(2,1)S(1)} %copy-done.4), channel_id=1, source_target_pairs={{0,96},{1,97},{2,98},{3,99},{4,100},{5,101},{6,102},{7,103},{8,104... | collective-permute-start | bytes 786440 | tf_op jit(solution)/shard_map/ppermute | solution.py:33
  85.7 1.9 %collective-permute-start.25 = (bf16[128,1024]{1,0:T(8,128)(2,1)S(1)}, bf16[128,1024]{1,0:T(8,128)(2,1)S(1)}, u32[]{:S(2)}, u32[]{:S(2)}) collective-permute-start(bf16[128,1024]{1,0:T(8,128)(2,1)S(1)} %collective-permute-done.24.refs_15_), channel_id=1, source_target_pairs={{0,96},{1,97},{2,98},{3,99},{4,100},{5,101},{6,102},{7,103},{8,104... | collective-permute-start | bytes 786440 | tf_op jit(solution)/shard_map/ppermute | solution.py:33
  87.7 6.6 %collide.5 = (f32[128,1024]{1,0:T(8,128)S(1)}, bf16[128,1024]{1,0:T(8,128)(2,1)S(1)}) custom-call(bf16[4,4,8,128]{3,2,1,0:T(8,128)(2,1)S(1)} %constant_dynamic-update-slice_fusion.4.refs_0_, bf16[4,4,8,128]{3,2,1,0:T(8,128)(2,1)S(1)} %collective-permute-done.8.refs_1_, bf16[4,4,8,128]{3,2,1,0:T(8,128)(2,1)S(1)} %collective-permute-done.9.refs_2_, ...), custom_call_target="tpu_custom_call" | custom-call | flops 4294967296 | bytes 6291456 | tf_op jit(solution)/shard_map/collide/pallas_call | solution.py:206
  94.3 0.8 copy-done.1
  95.1 1.5 %collective-permute-start.31 = (bf16[128,1024]{1,0:T(8,128)(2,1)S(1)}, bf16[128,1024]{1,0:T(8,128)(2,1)S(1)}, u32[]{:S(2)}, u32[]{:S(2)}) collective-permute-start(bf16[128,1024]{1,0:T(8,128)(2,1)S(1)} %get-tuple-element.49), channel_id=1, source_target_pairs={{0,16},{1,17},{2,18},{3,19},{4,20},{5,21},{6,22},{7,23},{8,24},{9,... | collective-permute-start | bytes 786440 | tf_op jit(solution)/shard_map/ppermute | solution.py:33
  96.7 6.6 %collide.6 = (f32[128,1024]{1,0:T(8,128)S(1)}, bf16[128,1024]{1,0:T(8,128)(2,1)S(1)}) custom-call(bf16[4,4,8,128]{3,2,1,0:T(8,128)(2,1)S(1)} %constant_dynamic-update-slice_fusion.4.refs_0_, bf16[4,4,8,128]{3,2,1,0:T(8,128)(2,1)S(1)} %collective-permute-done.8.refs_1_, bf16[4,4,8,128]{3,2,1,0:T(8,128)(2,1)S(1)} %collective-permute-done.9.refs_2_, ...), custom_call_target="tpu_custom_call" | custom-call | flops 4294967296 | bytes 6291456 | tf_op jit(solution)/shard_map/collide/pallas_call | solution.py:206
  103.3 0.8 copy-done.2
  104.1 0.5 collective-permute-start.32
  104.6 6.6 %collide.7 = (f32[128,1024]{1,0:T(8,128)S(1)}, bf16[128,1024]{1,0:T(8,128)(2,1)S(1)}) custom-call(bf16[4,4,8,128]{3,2,1,0:T(8,128)(2,1)S(1)} %constant_dynamic-update-slice_fusion.4.refs_0_, bf16[4,4,8,128]{3,2,1,0:T(8,128)(2,1)S(1)} %collective-permute-done.8.refs_1_, bf16[4,4,8,128]{3,2,1,0:T(8,128)(2,1)S(1)} %collective-permute-done.9.refs_2_, ...), custom_call_target="tpu_custom_call" | custom-call | flops 4294967296 | bytes 6291456 | tf_op jit(solution)/shard_map/collide/pallas_call | solution.py:206
  111.2 0.8 copy-done.3
  112.0 1.5 %collective-permute-start.33 = (bf16[128,1024]{1,0:T(8,128)(2,1)S(1)}, bf16[128,1024]{1,0:T(8,128)(2,1)S(1)}, u32[]{:S(2)}, u32[]{:S(2)}) collective-permute-start(bf16[128,1024]{1,0:T(8,128)(2,1)S(1)} %get-tuple-element.51), channel_id=1, source_target_pairs={{0,16},{1,17},{2,18},{3,19},{4,20},{5,21},{6,22},{7,23},{8,24},{9,... | collective-permute-start | bytes 786440 | tf_op jit(solution)/shard_map/ppermute | solution.py:33
  113.6 4.8 %collective-permute-done.33.refs_7_ = bf16[128,1024]{1,0:T(8,128)(2,1)S(1)} collective-permute-done((bf16[128,1024]{1,0:T(8,128)(2,1)S(1)}, bf16[128,1024]{1,0:T(8,128)(2,1)S(1)}, u32[]{:S(2)}, u32[]{:S(2)}) %collective-permute-start.33) | collective-permute-done | bytes 262176 | tf_op jit(solution)/shard_map/ppermute | solution.py:33
  118.4 0.7 copy-done.13
  119.1 4.8 %combine.1 = f32[4096,128]{1,0:T(8,128)} custom-call(f32[128,1024]{1,0:T(8,128)} %copy-done, f32[128,1024]{1,0:T(8,128)} %copy-done.1, f32[128,1024]{1,0:T(8,128)} %copy-done.2, f32[128,1024]{1,0:T(8,128)} %copy-done.3, bf16[128,1024]{1,0:T(8,128)(2,1)} %copy-done.10, bf16[128,1024]{1,0:T(8,128)(2,1)} %copy-done.11, bf16[128,1024]{1,0:T(8,128)(2,1)} %copy-done.12, ...), custom_call_target="tpu_custom_call" | custom-call | flops 524288 | bytes 5242880 | tf_op jit(solution)/shard_map/combine/pallas_call | solution.py:241
  (64 shorter events, 1.8 us)
Async XLA Ops:
  5.1 9.8 %collective-permute-start.2 = (bf16[128,512]{1,0:T(8,128)(2,1)}, bf16[128,512]{1,0:T(8,128)(2,1)S(1)}, u32[]{:S(2)}, u32[]{:S(2)}) collective-permute-start(bf16[128,512]{1,0:T(8,128)(2,1)} %get-tuple-element.31), channel_id=1, source_target_pairs={{0,16},{1,17},{2,18},{3,19},{4,20},{5,21},{6,22},{7,23},{8,24},{9,... | collective-permute-start | bytes 393224 | tf_op jit(solution)/shard_map/ppermute | solution.py:33
  7.1 11.1 %collective-permute-start.4 = (bf16[128,512]{1,0:T(8,128)(2,1)}, bf16[128,512]{1,0:T(8,128)(2,1)S(1)}, u32[]{:S(2)}, u32[]{:S(2)}) collective-permute-start(bf16[128,512]{1,0:T(8,128)(2,1)} %get-tuple-element.31), channel_id=1, source_target_pairs={{0,18},{1,19},{2,16},{3,17},{4,22},{5,23},{6,20},{7,21},{8,26},{9,... | collective-permute-start | bytes 393224 | tf_op jit(solution)/shard_map/ppermute | solution.py:33
  9.6 19.6 %collective-permute-start = (bf16[129,2,8,128]{3,2,1,0:T(8,128)(2,1)}, bf16[129,2,8,128]{3,2,1,0:T(8,128)(2,1)S(1)}, u32[]{:S(2)}, u32[]{:S(2)}) collective-permute-start(bf16[129,2,8,128]{3,2,1,0:T(8,128)(2,1)} %get-tuple-element.27), channel_id=1, source_target_pairs={{0,1},{1,2},{2,3},{3,4},{4,5},{5,6},{6,7},{7,8},{8,9},{9,10},{10,1... | collective-permute-start | bytes 1585160 | tf_op jit(solution)/shard_map/ppermute | solution.py:257
  10.9 7.2 %collective-permute-start.3 = (bf16[128,512]{1,0:T(8,128)(2,1)}, bf16[128,512]{1,0:T(8,128)(2,1)S(1)}, u32[]{:S(2)}, u32[]{:S(2)}) collective-permute-start(bf16[128,512]{1,0:T(8,128)(2,1)} %get-tuple-element.30), channel_id=1, source_target_pairs={{0,2},{1,3},{2,0},{3,1},{4,6},{5,7},{6,4},{7,5},{8,10},{9,11},{10,... | collective-permute-start | bytes 393224 | tf_op jit(solution)/shard_map/ppermute | solution.py:33
  12.7 16.5 %collective-permute-start.1 = (bf16[129,2,8,128]{3,2,1,0:T(8,128)(2,1)}, bf16[129,2,8,128]{3,2,1,0:T(8,128)(2,1)S(1)}, u32[]{:S(2)}, u32[]{:S(2)}) collective-permute-start(bf16[129,2,8,128]{3,2,1,0:T(8,128)(2,1)} %get-tuple-element.28), channel_id=1, source_target_pairs={{1,0},{2,1},{3,2},{4,3},{5,4},{6,5},{7,6},{8,7},{9,8},{10,9},{11,1... | collective-permute-start | bytes 1585160 | tf_op jit(solution)/shard_map/ppermute | solution.py:258
  18.2 21.4 %collective-permute-start.6 = (bf16[512,512]{1,0:T(8,128)(2,1)S(1)}, bf16[512,512]{1,0:T(8,128)(2,1)S(1)}, u32[]{:S(2)}, u32[]{:S(2)}) collective-permute-start(bf16[512,512]{1,0:T(8,128)(2,1)S(1)} %constant_dynamic-update-slice_fusion.refs_4_), channel_id=1, source_target_pairs={{0,12},{1,13},{2,14},{3,15},{4,0},{5,1},{6,2},{7,3},{8,4},{9,5},{1... | collective-permute-start | bytes 1572872 | tf_op jit(solution)/shard_map/ppermute | solution.py:33
  28.0 15.3 %collective-permute-start.5 = (bf16[512,512]{1,0:T(8,128)(2,1)S(1)}, bf16[512,512]{1,0:T(8,128)(2,1)S(1)}, u32[]{:S(2)}, u32[]{:S(2)}) collective-permute-start(bf16[512,512]{1,0:T(8,128)(2,1)S(1)} %constant_dynamic-update-slice_fusion.refs_4_), channel_id=1, source_target_pairs={{0,4},{1,5},{2,6},{3,7},{4,8},{5,9},{6,10},{7,11},{8,12},{9,13},{1... | collective-permute-start | bytes 1572872 | tf_op jit(solution)/shard_map/ppermute | solution.py:33
  28.0 25.2 %collective-permute-start.13 = (bf16[512,512]{1,0:T(8,128)(2,1)S(1)}, bf16[512,512]{1,0:T(8,128)(2,1)S(1)}, u32[]{:S(2)}, u32[]{:S(2)}) collective-permute-start(bf16[512,512]{1,0:T(8,128)(2,1)S(1)} %constant_dynamic-update-slice_fusion.refs_4_), channel_id=1, source_target_pairs={{0,1},{1,0},{2,3},{3,2},{4,5},{5,4},{6,7},{7,6},{8,9},{9,8},{10,11... | collective-permute-start | bytes 1572872 | tf_op jit(solution)/shard_map/ppermute | solution.py:33
  29.2 0.8 copy-start.9
  29.2 1.0 copy-start.8
  36.3 12.6 %collective-permute-start.20 = (bf16[128,1024]{1,0:T(8,128)(2,1)}, bf16[128,1024]{1,0:T(8,128)(2,1)S(1)}, u32[]{:S(2)}, u32[]{:S(2)}) collective-permute-start(bf16[128,1024]{1,0:T(8,128)(2,1)} %get-tuple-element.37.refs_14_), channel_id=1, source_target_pairs={{0,32},{1,33},{2,34},{3,35},{4,36},{5,37},{6,38},{7,39},{8,40},{9,... | collective-permute-start | bytes 786440 | tf_op jit(solution)/shard_map/ppermute | solution.py:33
  38.0 13.9 %collective-permute-start.18 = (bf16[128,1024]{1,0:T(8,128)(2,1)}, bf16[128,1024]{1,0:T(8,128)(2,1)S(1)}, u32[]{:S(2)}, u32[]{:S(2)}) collective-permute-start(bf16[128,1024]{1,0:T(8,128)(2,1)} %get-tuple-element.37.refs_14_), channel_id=1, source_target_pairs={{0,96},{1,97},{2,98},{3,99},{4,100},{5,101},{6,102},{7,103},{8,104... | collective-permute-start | bytes 786440 | tf_op jit(solution)/shard_map/ppermute | solution.py:33
  39.7 16.3 %collective-permute-start.12 = (bf16[256,512]{1,0:T(8,128)(2,1)S(1)}, bf16[256,512]{1,0:T(8,128)(2,1)S(1)}, u32[]{:S(2)}, u32[]{:S(2)}) collective-permute-start(bf16[256,512]{1,0:T(8,128)(2,1)S(1)} %slice.9), channel_id=1, source_target_pairs={{0,12},{1,13},{2,14},{3,15},{4,0},{5,1},{6,2},{7,3},{8,4},{9,5},{1... | collective-permute-start | bytes 786440 | tf_op jit(solution)/shard_map/ppermute | solution.py:33
  43.4 4.0 %collective-permute-start.7 = (bf16[2,4,8,128]{3,2,1,0:T(8,128)(2,1)}, bf16[2,4,8,128]{3,2,1,0:T(8,128)(2,1)S(1)}, u32[]{:S(2)}, u32[]{:S(2)}) collective-permute-start(bf16[2,4,8,128]{3,2,1,0:T(8,128)(2,1)} %get-tuple-element.36), channel_id=1, source_target_pairs={{0,16},{1,17},{2,18},{3,19},{4,20},{5,21},{6,22},{7,23},{8,24},{9,... | collective-permute-start | bytes 49160 | tf_op jit(solution)/shard_map/ppermute | solution.py:33
  47.3 6.0 %collective-permute-start.10 = (bf16[4,4,8,128]{3,2,1,0:T(8,128)(2,1)S(1)}, bf16[4,4,8,128]{3,2,1,0:T(8,128)(2,1)S(1)}, u32[]{:S(2)}, u32[]{:S(2)}) collective-permute-start(bf16[4,4,8,128]{3,2,1,0:T(8,128)(2,1)S(1)} %constant_dynamic-update-slice_fusion.4.refs_0_), channel_id=1, source_target_pairs={{0,32},{1,33},{2,34},{3,35},{4,36},{5,37},{6,38},{7,39},{8,40},{9,... | collective-permute-start | bytes 98312 | tf_op jit(solution)/shard_map/ppermute | solution.py:33
  48.9 5.4 %collective-permute-start.9 = (bf16[4,4,8,128]{3,2,1,0:T(8,128)(2,1)S(1)}, bf16[4,4,8,128]{3,2,1,0:T(8,128)(2,1)S(1)}, u32[]{:S(2)}, u32[]{:S(2)}) collective-permute-start(bf16[4,4,8,128]{3,2,1,0:T(8,128)(2,1)S(1)} %constant_dynamic-update-slice_fusion.4.refs_0_), channel_id=1, source_target_pairs={{0,64},{1,65},{2,66},{3,67},{4,68},{5,69},{6,70},{7,71},{8,72},{9,... | collective-permute-start | bytes 98312 | tf_op jit(solution)/shard_map/ppermute | solution.py:33
  51.8 3.9 %collective-permute-start.8 = (bf16[4,4,8,128]{3,2,1,0:T(8,128)(2,1)S(1)}, bf16[4,4,8,128]{3,2,1,0:T(8,128)(2,1)S(1)}, u32[]{:S(2)}, u32[]{:S(2)}) collective-permute-start(bf16[4,4,8,128]{3,2,1,0:T(8,128)(2,1)S(1)} %constant_dynamic-update-slice_fusion.4.refs_0_), channel_id=1, source_target_pairs={{0,96},{1,97},{2,98},{3,99},{4,100},{5,101},{6,102},{7,103},{8,104... | collective-permute-start | bytes 98312 | tf_op jit(solution)/shard_map/ppermute | solution.py:33
  53.2 7.7 %collective-permute-start.11 = (bf16[256,512]{1,0:T(8,128)(2,1)S(1)}, bf16[256,512]{1,0:T(8,128)(2,1)S(1)}, u32[]{:S(2)}, u32[]{:S(2)}) collective-permute-start(bf16[256,512]{1,0:T(8,128)(2,1)S(1)} %slice.8), channel_id=1, source_target_pairs={{0,4},{1,5},{2,6},{3,7},{4,8},{5,9},{6,10},{7,11},{8,12},{9,13},{1... | collective-permute-start | bytes 786440 | tf_op jit(solution)/shard_map/ppermute | solution.py:33
  53.3 18.2 %collective-permute-start.15 = (bf16[512,512]{1,0:T(8,128)(2,1)S(1)}, bf16[512,512]{1,0:T(8,128)(2,1)S(1)}, u32[]{:S(2)}, u32[]{:S(2)}) collective-permute-start(bf16[512,512]{1,0:T(8,128)(2,1)S(1)} %collective-permute-done.6.refs_6_), channel_id=1, source_target_pairs={{0,1},{1,0},{2,3},{3,2},{4,5},{5,4},{6,7},{7,6},{8,9},{9,8},{10,11... | collective-permute-start | bytes 1572872 | tf_op jit(solution)/shard_map/ppermute | solution.py:33
  54.3 19.1 %collective-permute-start.14 = (bf16[512,512]{1,0:T(8,128)(2,1)S(1)}, bf16[512,512]{1,0:T(8,128)(2,1)S(1)}, u32[]{:S(2)}, u32[]{:S(2)}) collective-permute-start(bf16[512,512]{1,0:T(8,128)(2,1)S(1)} %collective-permute-done.5.refs_5_), channel_id=1, source_target_pairs={{0,1},{1,0},{2,3},{3,2},{4,5},{5,4},{6,7},{7,6},{8,9},{9,8},{10,11... | collective-permute-start | bytes 1572872 | tf_op jit(solution)/shard_map/ppermute | solution.py:33
  55.7 8.7 %collective-permute-start.22 = (bf16[128,1024]{1,0:T(8,128)(2,1)}, bf16[128,1024]{1,0:T(8,128)(2,1)S(1)}, u32[]{:S(2)}, u32[]{:S(2)}) collective-permute-start(bf16[128,1024]{1,0:T(8,128)(2,1)} %get-tuple-element.40.refs_14_), channel_id=1, source_target_pairs={{0,32},{1,33},{2,34},{3,35},{4,36},{5,37},{6,38},{7,39},{8,40},{9,... | collective-permute-start | bytes 786440 | tf_op jit(solution)/shard_map/ppermute | solution.py:33
  55.9 10.1 %collective-permute-start.21 = (bf16[128,1024]{1,0:T(8,128)(2,1)}, bf16[128,1024]{1,0:T(8,128)(2,1)S(1)}, u32[]{:S(2)}, u32[]{:S(2)}) collective-permute-start(bf16[128,1024]{1,0:T(8,128)(2,1)} %get-tuple-element.40.refs_14_), channel_id=1, source_target_pairs={{0,96},{1,97},{2,98},{3,99},{4,100},{5,101},{6,102},{7,103},{8,104... | collective-permute-start | bytes 786440 | tf_op jit(solution)/shard_map/ppermute | solution.py:33
  60.9 9.3 %collective-permute-start.19 = (bf16[128,1024]{1,0:T(8,128)(2,1)S(1)}, bf16[128,1024]{1,0:T(8,128)(2,1)S(1)}, u32[]{:S(2)}, u32[]{:S(2)}) collective-permute-start(bf16[128,1024]{1,0:T(8,128)(2,1)S(1)} %collective-permute-done.18.refs_15_), channel_id=1, source_target_pairs={{0,96},{1,97},{2,98},{3,99},{4,100},{5,101},{6,102},{7,103},{8,104... | collective-permute-start | bytes 786440 | tf_op jit(solution)/shard_map/ppermute | solution.py:33
  64.5 9.0 %collective-permute-start.17 = (bf16[256,512]{1,0:T(8,128)(2,1)S(1)}, bf16[256,512]{1,0:T(8,128)(2,1)S(1)}, u32[]{:S(2)}, u32[]{:S(2)}) collective-permute-start(bf16[256,512]{1,0:T(8,128)(2,1)S(1)} %collective-permute-done.12.refs_8_), channel_id=1, source_target_pairs={{0,1},{1,0},{2,3},{3,2},{4,5},{5,4},{6,7},{7,6},{8,9},{9,8},{10,11... | collective-permute-start | bytes 786440 | tf_op jit(solution)/shard_map/ppermute | solution.py:33
  66.1 7.5 %collective-permute-start.16 = (bf16[256,512]{1,0:T(8,128)(2,1)S(1)}, bf16[256,512]{1,0:T(8,128)(2,1)S(1)}, u32[]{:S(2)}, u32[]{:S(2)}) collective-permute-start(bf16[256,512]{1,0:T(8,128)(2,1)S(1)} %collective-permute-done.11.refs_7_), channel_id=1, source_target_pairs={{0,1},{1,0},{2,3},{3,2},{4,5},{5,4},{6,7},{7,6},{8,9},{9,8},{10,11... | collective-permute-start | bytes 786440 | tf_op jit(solution)/shard_map/ppermute | solution.py:33
  66.1 16.3 %copy-start.4 = (bf16[128,1024]{1,0:T(8,128)(2,1)S(1)}, bf16[128,1024]{1,0:T(8,128)(2,1)}, u32[]{:S(2)}) copy-start(bf16[128,1024]{1,0:T(8,128)(2,1)} %get-tuple-element.46.refs_14_) | copy-start | bytes 786436
  66.1 21.6 %copy-start.6 = (bf16[128,1024]{1,0:T(8,128)(2,1)S(1)}, bf16[128,1024]{1,0:T(8,128)(2,1)}, u32[]{:S(2)}) copy-start(bf16[128,1024]{1,0:T(8,128)(2,1)} %get-tuple-element.40.refs_14_) | copy-start | bytes 786436
  70.2 12.2 %collective-permute-start.26 = (bf16[128,1024]{1,0:T(8,128)(2,1)}, bf16[128,1024]{1,0:T(8,128)(2,1)S(1)}, u32[]{:S(2)}, u32[]{:S(2)}) collective-permute-start(bf16[128,1024]{1,0:T(8,128)(2,1)} %get-tuple-element.43.refs_14_), channel_id=1, source_target_pairs={{0,32},{1,33},{2,34},{3,35},{4,36},{5,37},{6,38},{7,39},{8,40},{9,... | collective-permute-start | bytes 786440 | tf_op jit(solution)/shard_map/ppermute | solution.py:33
  71.5 10.9 %collective-permute-start.24 = (bf16[128,1024]{1,0:T(8,128)(2,1)}, bf16[128,1024]{1,0:T(8,128)(2,1)S(1)}, u32[]{:S(2)}, u32[]{:S(2)}) collective-permute-start(bf16[128,1024]{1,0:T(8,128)(2,1)} %get-tuple-element.43.refs_14_), channel_id=1, source_target_pairs={{0,96},{1,97},{2,98},{3,99},{4,100},{5,101},{6,102},{7,103},{8,104... | collective-permute-start | bytes 786440 | tf_op jit(solution)/shard_map/ppermute | solution.py:33
  73.4 14.2 %collective-permute-start.23 = (bf16[128,1024]{1,0:T(8,128)(2,1)S(1)}, bf16[128,1024]{1,0:T(8,128)(2,1)S(1)}, u32[]{:S(2)}, u32[]{:S(2)}) collective-permute-start(bf16[128,1024]{1,0:T(8,128)(2,1)S(1)} %collective-permute-done.22.refs_17_), channel_id=1, source_target_pairs={{0,32},{1,33},{2,34},{3,35},{4,36},{5,37},{6,38},{7,39},{8,40},{9,... | collective-permute-start | bytes 786440 | tf_op jit(solution)/shard_map/ppermute | solution.py:33
  73.5 1.0 copy-start.7
  81.1 0.8 copy-start
  81.9 31.7 %collective-permute-start.30 = (bf16[128,1024]{1,0:T(8,128)(2,1)S(1)}, bf16[128,1024]{1,0:T(8,128)(2,1)S(1)}, u32[]{:S(2)}, u32[]{:S(2)}) collective-permute-start(bf16[128,1024]{1,0:T(8,128)(2,1)S(1)} %get-tuple-element.48), channel_id=1, source_target_pairs={{0,16},{1,17},{2,18},{3,19},{4,20},{5,21},{6,22},{7,23},{8,24},{9,... | collective-permute-start | bytes 786440 | tf_op jit(solution)/shard_map/ppermute | solution.py:33
  82.4 14.3 %copy-start.5 = (bf16[128,1024]{1,0:T(8,128)(2,1)S(1)}, bf16[128,1024]{1,0:T(8,128)(2,1)}, u32[]{:S(2)}) copy-start(bf16[128,1024]{1,0:T(8,128)(2,1)} %get-tuple-element.43.refs_14_) | copy-start | bytes 786436
  82.4 14.2 %collective-permute-start.28 = (bf16[128,1024]{1,0:T(8,128)(2,1)S(1)}, bf16[128,1024]{1,0:T(8,128)(2,1)S(1)}, u32[]{:S(2)}, u32[]{:S(2)}) collective-permute-start(bf16[128,1024]{1,0:T(8,128)(2,1)S(1)} %copy-done.4), channel_id=1, source_target_pairs={{0,32},{1,33},{2,34},{3,35},{4,36},{5,37},{6,38},{7,39},{8,40},{9,... | collective-permute-start | bytes 786440 | tf_op jit(solution)/shard_map/ppermute | solution.py:33
  83.7 20.9 %collective-permute-start.27 = (bf16[128,1024]{1,0:T(8,128)(2,1)S(1)}, bf16[128,1024]{1,0:T(8,128)(2,1)S(1)}, u32[]{:S(2)}, u32[]{:S(2)}) collective-permute-start(bf16[128,1024]{1,0:T(8,128)(2,1)S(1)} %copy-done.4), channel_id=1, source_target_pairs={{0,96},{1,97},{2,98},{3,99},{4,100},{5,101},{6,102},{7,103},{8,104... | collective-permute-start | bytes 786440 | tf_op jit(solution)/shard_map/ppermute | solution.py:33
  85.7 11.0 %collective-permute-start.25 = (bf16[128,1024]{1,0:T(8,128)(2,1)S(1)}, bf16[128,1024]{1,0:T(8,128)(2,1)S(1)}, u32[]{:S(2)}, u32[]{:S(2)}) collective-permute-start(bf16[128,1024]{1,0:T(8,128)(2,1)S(1)} %collective-permute-done.24.refs_15_), channel_id=1, source_target_pairs={{0,96},{1,97},{2,98},{3,99},{4,100},{5,101},{6,102},{7,103},{8,104... | collective-permute-start | bytes 786440 | tf_op jit(solution)/shard_map/ppermute | solution.py:33
  94.3 0.8 copy-start.1
  95.1 18.5 %collective-permute-start.31 = (bf16[128,1024]{1,0:T(8,128)(2,1)S(1)}, bf16[128,1024]{1,0:T(8,128)(2,1)S(1)}, u32[]{:S(2)}, u32[]{:S(2)}) collective-permute-start(bf16[128,1024]{1,0:T(8,128)(2,1)S(1)} %get-tuple-element.49), channel_id=1, source_target_pairs={{0,16},{1,17},{2,18},{3,19},{4,20},{5,21},{6,22},{7,23},{8,24},{9,... | collective-permute-start | bytes 786440 | tf_op jit(solution)/shard_map/ppermute | solution.py:33
  96.6 8.0 %collective-permute-start.29 = (bf16[128,1024]{1,0:T(8,128)(2,1)S(1)}, bf16[128,1024]{1,0:T(8,128)(2,1)S(1)}, u32[]{:S(2)}, u32[]{:S(2)}) collective-permute-start(bf16[128,1024]{1,0:T(8,128)(2,1)S(1)} %collective-permute-done.28.refs_17_), channel_id=1, source_target_pairs={{0,32},{1,33},{2,34},{3,35},{4,36},{5,37},{6,38},{7,39},{8,40},{9,... | collective-permute-start | bytes 786440 | tf_op jit(solution)/shard_map/ppermute | solution.py:33
  103.3 0.8 copy-start.2
  104.1 9.5 %collective-permute-start.32 = (bf16[128,1024]{1,0:T(8,128)(2,1)S(1)}, bf16[128,1024]{1,0:T(8,128)(2,1)S(1)}, u32[]{:S(2)}, u32[]{:S(2)}) collective-permute-start(bf16[128,1024]{1,0:T(8,128)(2,1)S(1)} %get-tuple-element.50), channel_id=1, source_target_pairs={{0,16},{1,17},{2,18},{3,19},{4,20},{5,21},{6,22},{7,23},{8,24},{9,... | collective-permute-start | bytes 786440 | tf_op jit(solution)/shard_map/ppermute | solution.py:33
  111.2 0.8 copy-start.3
  112.0 6.4 %collective-permute-start.33 = (bf16[128,1024]{1,0:T(8,128)(2,1)S(1)}, bf16[128,1024]{1,0:T(8,128)(2,1)S(1)}, u32[]{:S(2)}, u32[]{:S(2)}) collective-permute-start(bf16[128,1024]{1,0:T(8,128)(2,1)S(1)} %get-tuple-element.51), channel_id=1, source_target_pairs={{0,16},{1,17},{2,18},{3,19},{4,20},{5,21},{6,22},{7,23},{8,24},{9,... | collective-permute-start | bytes 786440 | tf_op jit(solution)/shard_map/ppermute | solution.py:33
  113.5 4.8 %copy-start.10 = (bf16[128,1024]{1,0:T(8,128)(2,1)}, bf16[128,1024]{1,0:T(8,128)(2,1)S(1)}, u32[]{:S(2)}) copy-start(bf16[128,1024]{1,0:T(8,128)(2,1)S(1)} %collective-permute-done.30.refs_4_) | copy-start | bytes 786436
  113.6 4.8 %copy-start.11 = (bf16[128,1024]{1,0:T(8,128)(2,1)}, bf16[128,1024]{1,0:T(8,128)(2,1)S(1)}, u32[]{:S(2)}) copy-start(bf16[128,1024]{1,0:T(8,128)(2,1)S(1)} %collective-permute-done.31.refs_5_) | copy-start | bytes 786436
  113.6 4.8 %copy-start.12 = (bf16[128,1024]{1,0:T(8,128)(2,1)}, bf16[128,1024]{1,0:T(8,128)(2,1)S(1)}, u32[]{:S(2)}) copy-start(bf16[128,1024]{1,0:T(8,128)(2,1)S(1)} %collective-permute-done.32.refs_6_) | copy-start | bytes 786436
  118.4 0.7 copy-start.13

commit v3 on v2

v3 whole, which is shorter than its diff:
```python
import jax
import jax.numpy as jnp
from jax import lax
from jax.experimental import pallas as pl
from jax.experimental.pallas import tpu as pltpu
from jax.sharding import PartitionSpec as P

SLICES = 16
BLOCKS = ((1, 2), (0, 3))
BOTH = ("vel", "space")
FLAT = [
    (y, z, x, h, c)
    for y in range(4)
    for z in range(2)
    for x in range(4)
    for h in range(2)
    for c in range(2)
]
BF16, F32 = jnp.bfloat16, jnp.float32
ANY = pl.BlockSpec(memory_space=pl.ANY)
VMEM = pl.BlockSpec(memory_space=pltpu.VMEM)
SMEM = pl.BlockSpec(memory_space=pltpu.SMEM)


def rank(y, z, x, h, c):
    return ((y % 4) * 2 + z) * 16 + (x % 4) * 4 + h * 2 + c


def shift(value, dy=0, dz=0, dx=0, dh=0, dc=0):
    pairs = [
        (rank(y, z, x, h, c), rank(y + dy, z ^ dz, x + dx, h ^ dh, c ^ dc)) for y, z, x, h, c in FLAT
    ]
    return lax.ppermute(value, BOTH, pairs)


def after(value, *earlier):
    return lax.optimization_barrier((value, earlier))[0]


def shape(dims, dtype):
    return jax.ShapeDtypeStruct(dims, dtype)


def pack(density, limiter):
    rows = density.shape[0]

    def kernel(d_ref, l_ref, first_ref, second_ref, inner_ref):
        core = lax.axis_index("space") & 1

        def fill(outer, following, pair):
            first_ref[:rows] = d_ref[:, outer].astype(BF16)
            first_ref[rows] = l_ref[outer].astype(F32).astype(BF16)
            for i in range(2):
                first_ref[rows + 1 + i] = d_ref[64 * i, following].astype(BF16)
            second_ref[...] = d_ref[:, following].astype(BF16)
            inner_ref[:rows] = d_ref[:, pair : pair + 2].astype(BF16)
            inner_ref[rows] = l_ref[pair : pair + 2].astype(F32).astype(BF16)

        @pl.when(core == 1)
        def _():
            fill(3, 2, 0)

        @pl.when(core == 0)
        def _():
            fill(0, 1, 2)

    dims = density.shape[2:]
    return pl.pallas_call(
        kernel,
        out_shape=(
            shape((rows + 3, *dims), BF16),
            shape((rows, *dims), BF16),
            shape((rows + 1, 2, *dims), BF16),
        ),
        in_specs=[VMEM, VMEM],
        out_specs=(VMEM, VMEM, VMEM),
        name="pack",
    )(density, limiter)


def split_slice(kernel_slice):
    def kernel(k_ref, o_ref):
        z = lax.axis_index("vel") & 1
        for y in range(4):
            cols = pl.ds(y * 128, 128)
            o_ref[:128, cols] = k_ref[y, 1 - z].astype(F32).T.astype(BF16)
            o_ref[128:, cols] = k_ref[y, z].astype(F32).T.astype(BF16)

    return pl.pallas_call(
        kernel, out_shape=shape((256, 512), BF16), in_specs=[VMEM], out_specs=VMEM, name="split_slice"
    )(kernel_slice.reshape(4, 2, 128, 128))


def update(cells, codes, ahead, number, layers):
    half = 0.5 * (2 * ahead - 1).astype(F32)
    forward = jnp.full((8, 128), ahead, jnp.int32) == 1
    rebuilt = {}
    for i in sorted({i + d for i in layers for d in (-1, 0, 1)}):
        left, right = cells[i] - cells[i - 1], cells[i + 1] - cells[i]
        small = jnp.where(left > 0, jnp.minimum(left, right), jnp.maximum(left, right))
        small = jnp.where(left * right > 0, small, 0.0)
        slope = jnp.where(
            codes[i] == 1, small, jnp.where(codes[i] == 2, 0.5 * (left + right), 0.0)
        )
        rebuilt[i] = cells[i] + half * slope
    return [
        cells[i] - number * (rebuilt[i] - jnp.where(forward, rebuilt[i - 1], rebuilt[i + 1]))
        for i in layers
    ]


STEP = 32


def transport_specs(rows):
    return [
        SMEM,
        SMEM,
        pl.BlockSpec((STEP, 4, 8, 128), lambda i: (i, 0, 0, 0)),
        pl.BlockSpec((4, 8, 128), lambda i: (0, 0, 0)),
        pl.BlockSpec((STEP, 8, 128), lambda i: (i, 0, 0)),
        pl.BlockSpec((1, 8, 128), lambda i: (rows, 0, 0)),
        pl.BlockSpec((STEP, 2, 8, 128), lambda i: (i, 0, 0, 0)),
        pl.BlockSpec((1, 2, 8, 128), lambda i: (rows, 0, 0, 0)),
    ]


def outer_codes(core, l_ref, first_code, inner_code):
    codes = {i: l_ref[i].astype(F32) for i in range(4)}
    codes[-1] = jnp.where(core == 0, first_code[0].astype(F32), inner_code[0, 1].astype(F32))
    codes[4] = jnp.where(core == 0, inner_code[0, 0].astype(F32), first_code[0].astype(F32))
    return codes


def neighbours(core, j, first_ref, inner_ref, second=None):
    a, b = inner_ref[j, 0].astype(F32), inner_ref[j, 1].astype(F32)
    first = first_ref[j].astype(F32)
    cells = {-1: jnp.where(core == 0, first, b), 4: jnp.where(core == 0, a, first)}
    if second is not None:
        second = second.astype(F32)
        cells[-2] = jnp.where(core == 0, second, a)
        cells[5] = jnp.where(core == 0, b, second)
    return cells


def flatten(m_ref, t_ref, places):
    for place, i in enumerate(places):
        turned = jnp.swapaxes(t_ref[:, i], 0, 1)
        for y in range(8):
            m_ref[:, pl.ds(place * 1024 + y * 128, 128)] = turned[y].astype(BF16)


def transport_inner(density, limiter, heading, courant, first, inner):
    rows = density.shape[0]

    def kernel(
        h_ref, c_ref, d_ref, l_ref, first_ref, first_code, inner_ref, inner_code, next_ref, m_ref, w_ref, t_ref
    ):
        core = lax.axis_index("space") & 1
        start = pl.program_id(0) * STEP
        codes = outer_codes(core, l_ref, first_code, inner_code)

        def one(j, _):
            cells = {i: d_ref[j, i] for i in range(4)}
            cells.update(neighbours(core, j, first_ref, inner_ref))
            values = update(cells, codes, h_ref[start + j], c_ref[start + j], (1, 2))
            for i, value in enumerate(values):
                t_ref[j, i] = value
            return 0

        lax.fori_loop(0, STEP, one, 0, unroll=4)
        flatten(m_ref, t_ref, (0, 1))

        @pl.when(pl.program_id(0) % 2 == 0)
        def _():
            cells = {i: d_ref[0, i] for i in range(4)}
            cells.update(neighbours(core, 0, first_ref, inner_ref, next_ref[0]))
            values = update(cells, codes, h_ref[start], c_ref[start], range(4))
            for i, value in enumerate(values):
                w_ref[0, i] = value.astype(BF16)

    return pl.pallas_call(
        kernel,
        grid=(rows // STEP,),
        out_shape=(shape((rows, 2048), BF16), shape((2, 4, 8, 128), BF16)),
        in_specs=transport_specs(rows)
        + [pl.BlockSpec((1, 8, 128), lambda i: (rows + 1 + i // 2, 0, 0))],
        out_specs=(
            pl.BlockSpec((STEP, 2048), lambda i: (i, 0)),
            pl.BlockSpec((1, 4, 8, 128), lambda i: (i // 2, 0, 0, 0)),
        ),
        scratch_shapes=[pltpu.VMEM((STEP, 2, 8, 128), F32)],
        cost_estimate=pl.CostEstimate(flops=2 << 20, bytes_accessed=3 << 20, transcendentals=0),
        name="transport_inner",
    )(heading, courant, density, limiter, first, first, inner, inner, first)


def transport(density, limiter, heading, courant, first, second, inner):
    rows = density.shape[0]

    def kernel(
        h_ref, c_ref, d_ref, l_ref, first_ref, first_code, inner_ref, inner_code, next_ref, t_ref, m_ref
    ):
        core = lax.axis_index("space") & 1
        start = pl.program_id(0) * STEP
        codes = outer_codes(core, l_ref, first_code, inner_code)

        def one(j, _):
            cells = {i: d_ref[j, i] for i in range(4)}
            cells.update(neighbours(core, j, first_ref, inner_ref, next_ref[j]))
            values = update(cells, codes, h_ref[start + j], c_ref[start + j], range(4))
            for i, value in enumerate(values):
                t_ref[j, i] = value
            return 0

        lax.fori_loop(0, STEP, one, 0, unroll=4)
        flatten(m_ref, t_ref, (0, 3))

    return pl.pallas_call(
        kernel,
        grid=(rows // STEP,),
        out_shape=(shape(density.shape, F32), shape((rows, 2048), BF16)),
        in_specs=transport_specs(rows) + [pl.BlockSpec((STEP, 8, 128), lambda i: (i, 0, 0))],
        out_specs=(
            pl.BlockSpec((STEP, 4, 8, 128), lambda i: (i, 0, 0, 0)),
            pl.BlockSpec((STEP, 2048), lambda i: (i, 0)),
        ),
        cost_estimate=pl.CostEstimate(flops=4 << 20, bytes_accessed=6 << 20, transcendentals=0),
        name="transport",
    )(heading, courant, density, limiter, first, first, inner, inner, second)


ORDER = [(0, 0), (0, 1), (3, 0), (3, 1), (1, 0), (1, 1), (2, 0), (2, 1)]


def weight_rows():
    vel, space = lax.axis_index("vel"), lax.axis_index("space")
    y, z = vel >> 1, vel & 1
    x, h, c = space >> 2, (space >> 1) & 1, space & 1
    rows = []
    for dc in range(2):
        for dx, dh in ORDER:
            v = (((x + dx) & 3) << 1) + (h ^ dh)
            rows.append(((((v >> 1) - y) & 3) << 2) + (((v & 1) ^ z) << 1) + (c ^ dc))
    return y, rows


def collide(layer, place, pieces, blocks, weights):
    cells = 1024
    tile = 512
    columns = pl.ds(place * cells, cells)
    targets = [(0, 0, 128), (1, 0, 128), (3, 0, 128), (2, 0, 64), (2, 64, 64)]

    def kernel(*refs):
        w_parts = refs[:4]
        slabs = refs[4:14]
        parts = refs[14:19]
        mine_ref, other_ref, k_ref, m_ref, w_ref, sem_k, sem_m = refs[19:]
        y, places = weight_rows()
        loads = []
        for i, (d, skip, n) in enumerate(targets):
            at = pl.multiple_of(((y + d) & 3) * 128 + skip, 64)
            loads.append(
                pltpu.make_async_copy(
                    parts[i].at[:, columns], m_ref.at[pl.ds(at, n)], sem_m.at[i]
                )
            )
        row, starts = 0, []
        for i in range(10):
            n = slabs[i].shape[0]
            loads.append(pltpu.make_async_copy(slabs[i], k_ref.at[pl.ds(row, n)], sem_k.at[i]))
            starts.append(row // 256)
            row += n
        for load in loads:
            load.start()
        for d in range(4):
            w_ref[4 * d : 4 * d + 4] = w_parts[d][:, layer].astype(F32)
        for load in loads[:5]:
            load.wait()
        for t in range(cells // tile):
            cols = pl.ds(t * tile, tile)
            moved = m_ref[:, cols]
            total = jnp.zeros((256, tile), F32)
            for s in range(SLICES):
                if t == 0 and s in starts:
                    loads[5 + starts.index(s)].wait()
                product = jnp.dot(
                    k_ref[s * 256 : (s + 1) * 256], moved, preferred_element_type=F32
                )
                lines = [w_ref[places[s], pl.ds(t * 4 + i, 1), :] for i in range(tile // 128)]
                total = total + jnp.concatenate(lines, 1) * product
            mine_ref[:, cols] = total[:128]
            other_ref[:, cols] = total[128:].astype(BF16)

    return pl.pallas_call(
        kernel,
        out_shape=(shape((128, cells), F32), shape((128, cells), BF16)),
        in_specs=[VMEM] * 4 + [ANY] * 15,
        out_specs=(VMEM, VMEM),
        scratch_shapes=[
            pltpu.VMEM((SLICES * 256, 512), BF16),
            pltpu.VMEM((512, cells), BF16),
            pltpu.VMEM((SLICES, 8, 128), F32),
            pltpu.SemaphoreType.DMA((10,)),
            pltpu.SemaphoreType.DMA((5,)),
        ],
        compiler_params=pltpu.CompilerParams(vmem_limit_bytes=24 << 20),
        cost_estimate=pl.CostEstimate(
            flops=2 * SLICES * 256 * 512 * cells, bytes_accessed=6 << 20, transcendentals=0
        ),
        name="collide",
    )(*weights, *pieces, *blocks)


def combine(layer, mine, got, result):
    step = 64

    def kernel(a_ref, b_ref, *refs):
        o_ref = refs[-1]
        total = a_ref[...] + b_ref[...].astype(F32)
        lines = jnp.stack([total[:, y * 128 : (y + 1) * 128] for y in range(8)], 0)
        o_ref[:, 0] = jnp.swapaxes(lines, 0, 1)

    block = pl.BlockSpec((step, 1024), lambda i: (i, 0))
    given = [] if result is None else [result]
    return pl.pallas_call(
        kernel,
        grid=(128 // step,),
        out_shape=shape((128, 4, 8, 128), F32),
        in_specs=[block, block] + [ANY] * len(given),
        out_specs=pl.BlockSpec((step, 1, 8, 128), lambda i: (i, layer, 0, 0)),
        input_output_aliases={2: 0} if given else {},
        cost_estimate=pl.CostEstimate(flops=1 << 17, bytes_accessed=5 << 18, transcendentals=0),
        name="combine",
    )(mine, got, *given)


def local(density, limiter, heading, courant, kernel_slices):
    size = lax.axis_size("space")
    beside = [(i, i + 1) for i in range(1, size - 1, 2)]
    beside = beside + [(j, i) for i, j in beside]

    own_slice = split_slice(kernel_slices[0])
    partner = shift(own_slice, dz=1)
    first, second, inner = pack(after(density, own_slice), limiter)
    first = lax.ppermute(first, "space", beside)
    inner = shift(inner, dc=1)

    crossing = jnp.concatenate([partner[128:], own_slice[:128]], 0)
    cross = shift(crossing, dz=1, dh=1)
    first = after(first, crossing)
    second = lax.ppermute(after(second, first), "space", beside)
    block, own = transport_inner(density, limiter, heading, courant, first, inner)

    base = jnp.concatenate([own_slice[128:], partner[:128], after(cross, block)], 0)
    one = shift(base, dx=1)
    three = shift(base, dx=-1)
    pieces = [base, one, three, shift(one[:256], dx=1), shift(three[256:], dx=-1)]
    swapped = [shift(p, dc=1) for p in pieces]
    pieces = pieces + swapped

    def gather(block, *earlier):
        before, behind = after((shift(block, dy=1), shift(block, dy=-1)), *earlier)
        return [block, behind, before, shift(before[:64], dy=1), shift(behind[64:], dy=-1)]

    inside = gather(after(block, swapped[0]), second)
    rows = jnp.concatenate([own, shift(own, dz=1)], 0)
    second = after(second, inside[1], inside[2])
    transported, block = transport(density, limiter, heading, courant, first, second, inner)
    rows = after(rows, block, swapped[1], swapped[2])
    block = after(block, inside[3], inside[4])
    weights = [rows, shift(rows, dy=-1), shift(rows, dy=2), shift(rows, dy=1)]
    outside = gather(block)

    result, got = None, []
    for layers, blocks in zip(BLOCKS, (inside, outside), strict=True):
        for place, layer in enumerate(layers):
            mine, other = collide(layer, place, pieces, blocks, weights)
            weights = after(weights, mine, *got[-1:])
            got.append(shift(other, dz=1))
            result = combine(layer, mine, got[-1], result)
    return transported, result


def solution(mesh):
    return jax.shard_map(
        local,
        mesh=mesh,
        in_specs=(
            P("vel", "space", None, None),
            P("space", None, None),
            P("vel"),
            P("vel"),
            P("space", None, "vel"),
        ),
        out_specs=(P("vel", "space", None, None), P("vel", "space", None, None)),
        check_vma=False,
    )
```

time: 125 us -> 130 us (1.040)
  Pallas kernels: 41.8 us -> 47.8 us
  starting transfers between devices: 49.3 us -> 43.8 us
  waiting for transfers between devices: 24.4 us -> 27.1 us
  local copies, waits for them, and re-layouts: 7.52 us -> 9.84 us
    pallas_call x4 -> x8, Pallas kernels: 15.4 us -> 21.7 us  [the longest x4 7.57 us: combine(): pl.pallas_call(kernel, grid=(128 // step,), out_shape=shape((128, 4, 8, 1...]
    ppermute x32 -> x28, starting transfers between devices: 46.7 us -> 42.4 us  [shift(): return lax.ppermute(value, BOTH, pairs)]
    ppermute x32 -> x28, waiting for transfers between devices: 24.4 us -> 27.1 us  [shift(): return lax.ppermute(value, BOTH, pairs)]
    unnamed x32 -> x40, local copies, waits for them, and re-layouts: 7.47 us -> 9.7 us
  transfers between devices with their start and end apart: 34 -> 30, of which waited for: 9 -> 8; matrix products, arithmetic and copies ran while one was open for 1% -> 0% of each run, Pallas kernels for 26% -> 34%
where the time goes in v3:
time: 130 us
  Pallas kernels  47.8 us (37%)
  starting transfers between devices  43.8 us (34%)
  waiting for transfers between devices  27.1 us (21%)
  local copies, waits for them, and re-layouts  9.84 us (8%)
    ppermute x28, starting transfers between devices, shift(): return lax.ppermute(value, BOTH, pairs)  42.4 us
    ppermute x28, waiting for transfers between devices, shift(): return lax.ppermute(value, BOTH, pairs)  27.1 us
    pallas_call x4, Pallas kernels, collide(): pl.pallas_call(kernel, out_shape=(shape((128, cells), F32), shape((128, c...  26.1 us
    unnamed x40, local copies, waits for them, and re-layouts  9.7 us
    pallas_call x4, Pallas kernels, combine(): pl.pallas_call(kernel, grid=(128 // step,), out_shape=shape((128, 4, 8, 1...  7.57 us
    pallas_call x1, Pallas kernels, transport(): pl.pallas_call(kernel, grid=(rows // STEP,), out_shape=(shape(density.sha...  5.17 us
    pallas_call x1, Pallas kernels, transport_inner(): pl.pallas_call(kernel, grid=(rows // STEP,), out_shape=(shape((rows, 2048...  4.47 us
    pallas_call x1, Pallas kernels, pack(): pl.pallas_call(kernel, out_shape=(shape((rows + 3, *dims), BF16), shape((...  2.73 us
  transfers between devices with their start and end apart: 30, of which 8 were waited for; matrix products, arithmetic and copies ran while one was open for 0% of the time, Pallas kernels for 34%

profile of v3, /device:TPU:0, one launch (start us, length us, event | category | flops | bytes accessed | tf_op | source)
XLA Modules:
  0.0 129.5 jit_solution(10257415959920171331)
XLA Ops:
  0.6 1.8 %split_slice.1 = bf16[256,512]{1,0:T(8,128)(2,1)} custom-call(bf16[4,2,128,128]{3,2,1,0:T(8,128)(2,1)} %bitcast.1), custom_call_target="tpu_custom_call" | custom-call | tf_op jit(solution)/shard_map/split_slice/pallas_call | solution.py:89
  2.4 2.0 %collective-permute-start.1 = (bf16[256,512]{1,0:T(8,128)(2,1)}, bf16[256,512]{1,0:T(8,128)(2,1)S(1)}, u32[]{:S(2)}, u32[]{:S(2)}) collective-permute-start(bf16[256,512]{1,0:T(8,128)(2,1)} %split_slice.1), channel_id=1, source_target_pairs={{0,16},{1,17},{2,18},{3,19},{4,20},{5,21},{6,22},{7,23},{8,24},{9,... | collective-permute-start | bytes 786440 | tf_op jit(solution)/shard_map/ppermute | solution.py:33
  4.4 2.7 %pack.1 = (bf16[131,8,128]{2,1,0:T(8,128)(2,1)}, bf16[128,8,128]{2,1,0:T(8,128)(2,1)}, bf16[129,2,8,128]{3,2,1,0:T(8,128)(2,1)}) custom-call(f32[128,4,8,128]{3,2,1,0:T(8,128)} %d_ref.4, s32[4,8,128]{2,1,0:T(8,128)} %l_ref.5), custom_call_target="tpu_custom_call" | custom-call | tf_op jit(solution)/shard_map/pack/pallas_call | solution.py:68
  7.8 5.0 %collective-permute-start.2 = (bf16[129,2,8,128]{3,2,1,0:T(8,128)(2,1)}, bf16[129,2,8,128]{3,2,1,0:T(8,128)(2,1)S(1)}, u32[]{:S(2)}, u32[]{:S(2)}) collective-permute-start(bf16[129,2,8,128]{3,2,1,0:T(8,128)(2,1)} %get-tuple-element.44), channel_id=1, source_target_pairs={{0,1},{1,0},{2,3},{3,2},{4,5},{5,4},{6,7},{7,6},{8,9},{9,8},{10,11... | collective-permute-start | bytes 1585160 | tf_op jit(solution)/shard_map/ppermute | solution.py:33
  12.9 2.0 %collective-permute-start.4 = (bf16[256,512]{1,0:T(8,128)(2,1)S(1)}, bf16[256,512]{1,0:T(8,128)(2,1)S(1)}, u32[]{:S(2)}, u32[]{:S(2)}) collective-permute-start(bf16[256,512]{1,0:T(8,128)(2,1)S(1)} %pad_maximum_fusion.1), channel_id=1, source_target_pairs={{0,18},{1,19},{2,16},{3,17},{4,22},{5,23},{6,20},{7,21},{8,26},{9,... | collective-permute-start | bytes 786440 | tf_op jit(solution)/shard_map/ppermute | solution.py:33
  15.6 0.8 copy-done.11
  16.4 4.5 %transport_inner.1 = (bf16[128,2048]{1,0:T(8,128)(2,1)}, bf16[2,4,8,128]{3,2,1,0:T(8,128)(2,1)}) custom-call(s32[128]{0:T(128)} %h_ref.3, f32[128]{0:T(128)} %c_ref.3, f32[128,4,8,128]{3,2,1,0:T(8,128)} %d_ref.4, s32[4,8,128]{2,1,0:T(8,128)} %l_ref.5, bf16[131,8,128]{2,1,0:T(8,128)(2,1)} %copy-done.12, bf16[131,8,128]{2,1,0:T(8,128)(2,1)} %copy-done.12, ...), custom_call_target="tpu_custom_call" | custom-call | flops 2097152 | bytes 3145728 | tf_op jit(solution)/shard_map/transport_inner/pallas_call | solution.py:182
  20.9 3.0 %collective-permute-done.4 = bf16[256,512]{1,0:T(8,128)(2,1)S(1)} collective-permute-done((bf16[256,512]{1,0:T(8,128)(2,1)S(1)}, bf16[256,512]{1,0:T(8,128)(2,1)S(1)}, u32[]{:S(2)}, u32[]{:S(2)}) %collective-permute-start.4) | collective-permute-done | bytes 262176 | tf_op jit(solution)/shard_map/ppermute | solution.py:33
  24.0 1.5 %collective-permute-start.5 = (bf16[512,512]{1,0:T(8,128)(2,1)S(1)}, bf16[512,512]{1,0:T(8,128)(2,1)S(1)}, u32[]{:S(2)}, u32[]{:S(2)}) collective-permute-start(bf16[512,512]{1,0:T(8,128)(2,1)S(1)} %pad_maximum_fusion.refs_4_), channel_id=1, source_target_pairs={{0,1},{1,0},{2,3},{3,2},{4,5},{5,4},{6,7},{7,6},{8,9},{9,8},{10,11... | collective-permute-start | bytes 1572872 | tf_op jit(solution)/shard_map/ppermute | solution.py:33
  25.5 2.2 %collective-permute-start.9 = (bf16[512,512]{1,0:T(8,128)(2,1)S(1)}, bf16[512,512]{1,0:T(8,128)(2,1)S(1)}, u32[]{:S(2)}, u32[]{:S(2)}) collective-permute-start(bf16[512,512]{1,0:T(8,128)(2,1)S(1)} %pad_maximum_fusion.refs_4_), channel_id=1, source_target_pairs={{0,4},{1,5},{2,6},{3,7},{4,8},{5,9},{6,10},{7,11},{8,12},{9,13},{1... | collective-permute-start | bytes 1572872 | tf_op jit(solution)/shard_map/ppermute | solution.py:33
  27.6 1.3 collective-permute-start.11
  28.9 1.6 %collective-permute-start.6 = (bf16[128,2048]{1,0:T(8,128)(2,1)}, bf16[128,2048]{1,0:T(8,128)(2,1)S(1)}, u32[]{:S(2)}, u32[]{:S(2)}) collective-permute-start(bf16[128,2048]{1,0:T(8,128)(2,1)} %get-tuple-element.49.refs_14_), channel_id=1, source_target_pairs={{0,32},{1,33},{2,34},{3,35},{4,36},{5,37},{6,38},{7,39},{8,40},{9,... | collective-permute-start | bytes 1572872 | tf_op jit(solution)/shard_map/ppermute | solution.py:33
  30.5 1.7 %collective-permute-start.7 = (bf16[128,2048]{1,0:T(8,128)(2,1)}, bf16[128,2048]{1,0:T(8,128)(2,1)S(1)}, u32[]{:S(2)}, u32[]{:S(2)}) collective-permute-start(bf16[128,2048]{1,0:T(8,128)(2,1)} %get-tuple-element.49.refs_14_), channel_id=1, source_target_pairs={{0,96},{1,97},{2,98},{3,99},{4,100},{5,101},{6,102},{7,103},{8,104... | collective-permute-start | bytes 1572872 | tf_op jit(solution)/shard_map/ppermute | solution.py:33
  32.8 8.4 %collective-permute-done.9.refs_5_ = bf16[512,512]{1,0:T(8,128)(2,1)S(1)} collective-permute-done((bf16[512,512]{1,0:T(8,128)(2,1)S(1)}, bf16[512,512]{1,0:T(8,128)(2,1)S(1)}, u32[]{:S(2)}, u32[]{:S(2)}) %collective-permute-start.9) | collective-permute-done | bytes 524320 | tf_op jit(solution)/shard_map/ppermute | solution.py:33
  41.8 2.5 %collective-permute-start.12 = (bf16[512,512]{1,0:T(8,128)(2,1)S(1)}, bf16[512,512]{1,0:T(8,128)(2,1)}, u32[]{:S(2)}, u32[]{:S(2)}) collective-permute-start(bf16[512,512]{1,0:T(8,128)(2,1)S(1)} %collective-permute-done.11.refs_6_), channel_id=1, source_target_pairs={{0,1},{1,0},{2,3},{3,2},{4,5},{5,4},{6,7},{7,6},{8,9},{9,8},{10,11... | collective-permute-start | bytes 1572872 | tf_op jit(solution)/shard_map/ppermute | solution.py:33
  44.3 3.5 %collective-permute-start.17 = (bf16[256,512]{1,0:T(8,128)(2,1)S(1)}, bf16[256,512]{1,0:T(8,128)(2,1)}, u32[]{:S(2)}, u32[]{:S(2)}) collective-permute-start(bf16[256,512]{1,0:T(8,128)(2,1)S(1)} %slice.45), channel_id=1, source_target_pairs={{0,12},{1,13},{2,14},{3,15},{4,0},{5,1},{6,2},{7,3},{8,4},{9,5},{1... | collective-permute-start | bytes 786440 | tf_op jit(solution)/shard_map/ppermute | solution.py:33
  47.8 1.6 %collective-permute-start.20 = (bf16[64,2048]{1,0:T(8,128)(2,1)S(1)}, bf16[64,2048]{1,0:T(8,128)(2,1)S(1)}, u32[]{:S(2)}, u32[]{:S(2)}) collective-permute-start(bf16[64,2048]{1,0:T(8,128)(2,1)S(1)} %slice.36), channel_id=1, source_target_pairs={{0,32},{1,33},{2,34},{3,35},{4,36},{5,37},{6,38},{7,39},{8,40},{9,... | collective-permute-start | bytes 786440 | tf_op jit(solution)/shard_map/ppermute | solution.py:33
  49.5 0.9 collective-permute-done.16.refs_7_
  50.4 3.0 %collective-permute-start.21 = (bf16[64,2048]{1,0:T(8,128)(2,1)S(1)}, bf16[64,2048]{1,0:T(8,128)(2,1)S(1)}, u32[]{:S(2)}, u32[]{:S(2)}) collective-permute-start(bf16[64,2048]{1,0:T(8,128)(2,1)S(1)} %slice.37), channel_id=1, source_target_pairs={{0,96},{1,97},{2,98},{3,99},{4,100},{5,101},{6,102},{7,103},{8,104... | collective-permute-start | bytes 786440 | tf_op jit(solution)/shard_map/ppermute | solution.py:33
  53.4 1.0 collective-permute-done.17.refs_8_
  54.5 3.1 %collective-permute-done.20.refs_17_ = bf16[64,2048]{1,0:T(8,128)(2,1)S(1)} collective-permute-done((bf16[64,2048]{1,0:T(8,128)(2,1)S(1)}, bf16[64,2048]{1,0:T(8,128)(2,1)S(1)}, u32[]{:S(2)}, u32[]{:S(2)}) %collective-permute-start.20) | collective-permute-done | bytes 262176 | tf_op jit(solution)/shard_map/ppermute | solution.py:33
  57.5 0.7 copy-done.7
  59.0 5.2 %transport.1 = (f32[128,4,8,128]{3,2,1,0:T(8,128)}, bf16[128,2048]{1,0:T(8,128)(2,1)}) custom-call(s32[128]{0:T(128)} %h_ref.3, f32[128]{0:T(128)} %c_ref.3, f32[128,4,8,128]{3,2,1,0:T(8,128)} %d_ref.4, s32[4,8,128]{2,1,0:T(8,128)} %l_ref.5, bf16[131,8,128]{2,1,0:T(8,128)(2,1)} %copy-done.12, bf16[131,8,128]{2,1,0:T(8,128)(2,1)} %copy-done.12, ...), custom_call_target="tpu_custom_call" | custom-call | flops 4194304 | bytes 6291456 | tf_op jit(solution)/shard_map/transport/pallas_call | solution.py:219
  64.2 1.0 collective-permute-start.23
  65.2 2.5 %collective-permute-start.24 = (bf16[128,2048]{1,0:T(8,128)(2,1)}, bf16[128,2048]{1,0:T(8,128)(2,1)S(1)}, u32[]{:S(2)}, u32[]{:S(2)}) collective-permute-start(bf16[128,2048]{1,0:T(8,128)(2,1)} %get-tuple-element.68.refs_14_), channel_id=1, source_target_pairs={{0,96},{1,97},{2,98},{3,99},{4,100},{5,101},{6,102},{7,103},{8,104... | collective-permute-start | bytes 1572872 | tf_op jit(solution)/shard_map/ppermute | solution.py:33
  67.8 2.0 %collective-permute-start.13 = (bf16[4,4,8,128]{3,2,1,0:T(8,128)(2,1)S(1)}, bf16[4,4,8,128]{3,2,1,0:T(8,128)(2,1)S(1)}, u32[]{:S(2)}, u32[]{:S(2)}) collective-permute-start(bf16[4,4,8,128]{3,2,1,0:T(8,128)(2,1)S(1)} %pad_maximum_fusion.2.refs_0_), channel_id=1, source_target_pairs={{0,96},{1,97},{2,98},{3,99},{4,100},{5,101},{6,102},{7,103},{8,104... | collective-permute-start | bytes 98312 | tf_op jit(solution)/shard_map/ppermute | solution.py:33
  69.8 1.0 collective-permute-start.15
  70.7 9.9 %collective-permute-done.13.refs_1_ = bf16[4,4,8,128]{3,2,1,0:T(8,128)(2,1)S(1)} collective-permute-done((bf16[4,4,8,128]{3,2,1,0:T(8,128)(2,1)S(1)}, bf16[4,4,8,128]{3,2,1,0:T(8,128)(2,1)S(1)}, u32[]{:S(2)}, u32[]{:S(2)}) %collective-permute-start.13) | collective-permute-done | bytes 32800 | tf_op jit(solution)/shard_map/ppermute | solution.py:33
  81.4 1.0 copy-done.4
  82.4 0.9 copy-done.8
  83.4 0.9 copy-done.10
  84.3 6.5 %collide.4 = (f32[128,1024]{1,0:T(8,128)S(1)}, bf16[128,1024]{1,0:T(8,128)(2,1)S(1)}) custom-call(bf16[4,4,8,128]{3,2,1,0:T(8,128)(2,1)S(1)} %pad_maximum_fusion.2.refs_0_, bf16[4,4,8,128]{3,2,1,0:T(8,128)(2,1)S(1)} %collective-permute-done.13.refs_1_, bf16[4,4,8,128]{3,2,1,0:T(8,128)(2,1)S(1)} %collective-permute-done.14.refs_2_, ...), custom_call_target="tpu_custom_call" | custom-call | flops 4294967296 | bytes 6291456 | tf_op jit(solution)/shard_map/collide/pallas_call | solution.py:295
  90.9 1.8 %collective-permute-start.22 = (bf16[128,1024]{1,0:T(8,128)(2,1)S(1)}, bf16[128,1024]{1,0:T(8,128)(2,1)S(1)}, u32[]{:S(2)}, u32[]{:S(2)}) collective-permute-start(bf16[128,1024]{1,0:T(8,128)(2,1)S(1)} %get-tuple-element.63), channel_id=1, source_target_pairs={{0,16},{1,17},{2,18},{3,19},{4,20},{5,21},{6,22},{7,23},{8,24},{9,... | collective-permute-start | bytes 786440 | tf_op jit(solution)/shard_map/ppermute | solution.py:33
  92.7 1.2 collective-permute-start.25
  93.9 2.2 %collective-permute-start.26 = (bf16[64,2048]{1,0:T(8,128)(2,1)S(1)}, bf16[64,2048]{1,0:T(8,128)(2,1)S(1)}, u32[]{:S(2)}, u32[]{:S(2)}) collective-permute-start(bf16[64,2048]{1,0:T(8,128)(2,1)S(1)} %slice.39), channel_id=1, source_target_pairs={{0,96},{1,97},{2,98},{3,99},{4,100},{5,101},{6,102},{7,103},{8,104... | collective-permute-start | bytes 786440 | tf_op jit(solution)/shard_map/ppermute | solution.py:33
  96.1 6.5 %collide.5 = (f32[128,1024]{1,0:T(8,128)S(1)}, bf16[128,1024]{1,0:T(8,128)(2,1)S(1)}) custom-call(bf16[4,4,8,128]{3,2,1,0:T(8,128)(2,1)S(1)} %pad_maximum_fusion.2.refs_0_, bf16[4,4,8,128]{3,2,1,0:T(8,128)(2,1)S(1)} %collective-permute-done.13.refs_1_, bf16[4,4,8,128]{3,2,1,0:T(8,128)(2,1)S(1)} %collective-permute-done.14.refs_2_, ...), custom_call_target="tpu_custom_call" | custom-call | flops 4294967296 | bytes 6291456 | tf_op jit(solution)/shard_map/collide/pallas_call | solution.py:295
  102.7 0.8 copy-done
  103.8 6.6 %collide.6 = (f32[128,1024]{1,0:T(8,128)S(1)}, bf16[128,1024]{1,0:T(8,128)(2,1)S(1)}) custom-call(bf16[4,4,8,128]{3,2,1,0:T(8,128)(2,1)S(1)} %pad_maximum_fusion.2.refs_0_, bf16[4,4,8,128]{3,2,1,0:T(8,128)(2,1)S(1)} %collective-permute-done.13.refs_1_, bf16[4,4,8,128]{3,2,1,0:T(8,128)(2,1)S(1)} %collective-permute-done.14.refs_2_, ...), custom_call_target="tpu_custom_call" | custom-call | flops 4294967296 | bytes 6291456 | tf_op jit(solution)/shard_map/collide/pallas_call | solution.py:295
  110.4 0.8 copy-done.1
  111.2 1.7 %collective-permute-start.29 = (bf16[128,1024]{1,0:T(8,128)(2,1)S(1)}, bf16[128,1024]{1,0:T(8,128)(2,1)S(1)}, u32[]{:S(2)}, u32[]{:S(2)}) collective-permute-start(bf16[128,1024]{1,0:T(8,128)(2,1)S(1)} %get-tuple-element.79), channel_id=1, source_target_pairs={{0,16},{1,17},{2,18},{3,19},{4,20},{5,21},{6,22},{7,23},{8,24},{9,... | collective-permute-start | bytes 786440 | tf_op jit(solution)/shard_map/ppermute | solution.py:33
  112.9 6.5 %collide.7 = (f32[128,1024]{1,0:T(8,128)S(1)}, bf16[128,1024]{1,0:T(8,128)(2,1)S(1)}) custom-call(bf16[4,4,8,128]{3,2,1,0:T(8,128)(2,1)S(1)} %pad_maximum_fusion.2.refs_0_, bf16[4,4,8,128]{3,2,1,0:T(8,128)(2,1)S(1)} %collective-permute-done.13.refs_1_, bf16[4,4,8,128]{3,2,1,0:T(8,128)(2,1)S(1)} %collective-permute-done.14.refs_2_, ...), custom_call_target="tpu_custom_call" | custom-call | flops 4294967296 | bytes 6291456 | tf_op jit(solution)/shard_map/collide/pallas_call | solution.py:295
  119.4 0.8 copy-done.2
  120.5 1.9 %combine.4.refs_0_ = f32[128,4,8,128]{3,2,1,0:T(8,128)} custom-call(f32[128,1024]{1,0:T(8,128)} %copy-done.3, bf16[128,1024]{1,0:T(8,128)(2,1)} %copy-done.18), custom_call_target="tpu_custom_call" | custom-call | flops 131072 | bytes 1310720 | tf_op jit(solution)/shard_map/combine/pallas_call | solution.py:326
  122.4 1.9 %combine.5.refs_0_ = f32[128,4,8,128]{3,2,1,0:T(8,128)} custom-call(f32[128,1024]{1,0:T(8,128)} %copy-done, bf16[128,1024]{1,0:T(8,128)(2,1)} %copy-done.15, f32[128,4,8,128]{3,2,1,0:T(8,128)} %combine.4.refs_0_), custom_call_target="tpu_custom_call", output_to_operand_aliasing={{}: (2, {})} | custom-call | flops 131072 | bytes 1310720 | tf_op jit(solution)/shard_map/combine/pallas_call | solution.py:326
  124.3 0.7 copy-done.16
  125.0 1.9 %combine.6.refs_0_ = f32[128,4,8,128]{3,2,1,0:T(8,128)} custom-call(f32[128,1024]{1,0:T(8,128)} %copy-done.1, bf16[128,1024]{1,0:T(8,128)(2,1)} %copy-done.16, f32[128,4,8,128]{3,2,1,0:T(8,128)} %combine.5.refs_0_), custom_call_target="tpu_custom_call", output_to_operand_aliasing={{}: (2, {})} | custom-call | flops 131072 | bytes 1310720 | tf_op jit(solution)/shard_map/combine/pallas_call | solution.py:326
  126.9 0.7 copy-done.17
  127.6 1.9 %combine.7 = f32[128,4,8,128]{3,2,1,0:T(8,128)} custom-call(f32[128,1024]{1,0:T(8,128)} %copy-done.2, bf16[128,1024]{1,0:T(8,128)(2,1)} %copy-done.17, f32[128,4,8,128]{3,2,1,0:T(8,128)} %combine.6.refs_0_), custom_call_target="tpu_custom_call", output_to_operand_aliasing={{}: (2, {})} | custom-call | flops 131072 | bytes 1310720 | tf_op jit(solution)/shard_map/combine/pallas_call | solution.py:326
  (75 shorter events, 4.9 us)
Async XLA Ops:
  2.4 10.4 %copy-start.13 = (bf16[256,512]{1,0:T(8,128)(2,1)S(1)}, bf16[256,512]{1,0:T(8,128)(2,1)}, u32[]{:S(2)}) copy-start(bf16[256,512]{1,0:T(8,128)(2,1)} %split_slice.1) | copy-start | bytes 786436
  2.4 10.4 %collective-permute-start.1 = (bf16[256,512]{1,0:T(8,128)(2,1)}, bf16[256,512]{1,0:T(8,128)(2,1)S(1)}, u32[]{:S(2)}, u32[]{:S(2)}) collective-permute-start(bf16[256,512]{1,0:T(8,128)(2,1)} %split_slice.1), channel_id=1, source_target_pairs={{0,16},{1,17},{2,18},{3,19},{4,20},{5,21},{6,22},{7,23},{8,24},{9,... | collective-permute-start | bytes 786440 | tf_op jit(solution)/shard_map/ppermute | solution.py:33
  7.1 7.8 %collective-permute-start = (bf16[131,8,128]{2,1,0:T(8,128)(2,1)}, bf16[131,8,128]{2,1,0:T(8,128)(2,1)S(1)}, u32[]{:S(2)}, u32[]{:S(2)}) collective-permute-start(bf16[131,8,128]{2,1,0:T(8,128)(2,1)} %get-tuple-element.42), channel_id=1, source_target_pairs={{1,2},{3,4},{5,6},{7,8},{9,10},{11,12},{13,14},{2,1},{4,3},{6,5},{... | collective-permute-start | bytes 804872 | tf_op jit(solution)/shard_map/ppermute | solution.py:346
  7.8 7.1 %collective-permute-start.2 = (bf16[129,2,8,128]{3,2,1,0:T(8,128)(2,1)}, bf16[129,2,8,128]{3,2,1,0:T(8,128)(2,1)S(1)}, u32[]{:S(2)}, u32[]{:S(2)}) collective-permute-start(bf16[129,2,8,128]{3,2,1,0:T(8,128)(2,1)} %get-tuple-element.44), channel_id=1, source_target_pairs={{0,1},{1,0},{2,3},{3,2},{4,5},{5,4},{6,7},{7,6},{8,9},{9,8},{10,11... | collective-permute-start | bytes 1585160 | tf_op jit(solution)/shard_map/ppermute | solution.py:33
  12.9 11.0 %collective-permute-start.4 = (bf16[256,512]{1,0:T(8,128)(2,1)S(1)}, bf16[256,512]{1,0:T(8,128)(2,1)S(1)}, u32[]{:S(2)}, u32[]{:S(2)}) collective-permute-start(bf16[256,512]{1,0:T(8,128)(2,1)S(1)} %pad_maximum_fusion.1), channel_id=1, source_target_pairs={{0,18},{1,19},{2,16},{3,17},{4,22},{5,23},{6,20},{7,21},{8,26},{9,... | collective-permute-start | bytes 786440 | tf_op jit(solution)/shard_map/ppermute | solution.py:33
  15.6 0.8 copy-start.11
  20.9 38.1 %copy-start.19 = (bf16[2,4,8,128]{3,2,1,0:T(8,128)(2,1)S(1)}, bf16[2,4,8,128]{3,2,1,0:T(8,128)(2,1)}, u32[]{:S(2)}) copy-start(bf16[2,4,8,128]{3,2,1,0:T(8,128)(2,1)} %get-tuple-element.54) | copy-start | bytes 49156
  24.0 5.0 %collective-permute-start.5 = (bf16[512,512]{1,0:T(8,128)(2,1)S(1)}, bf16[512,512]{1,0:T(8,128)(2,1)S(1)}, u32[]{:S(2)}, u32[]{:S(2)}) collective-permute-start(bf16[512,512]{1,0:T(8,128)(2,1)S(1)} %pad_maximum_fusion.refs_4_), channel_id=1, source_target_pairs={{0,1},{1,0},{2,3},{3,2},{4,5},{5,4},{6,7},{7,6},{8,9},{9,8},{10,11... | collective-permute-start | bytes 1572872 | tf_op jit(solution)/shard_map/ppermute | solution.py:33
  25.5 15.8 %collective-permute-start.9 = (bf16[512,512]{1,0:T(8,128)(2,1)S(1)}, bf16[512,512]{1,0:T(8,128)(2,1)S(1)}, u32[]{:S(2)}, u32[]{:S(2)}) collective-permute-start(bf16[512,512]{1,0:T(8,128)(2,1)S(1)} %pad_maximum_fusion.refs_4_), channel_id=1, source_target_pairs={{0,4},{1,5},{2,6},{3,7},{4,8},{5,9},{6,10},{7,11},{8,12},{9,13},{1... | collective-permute-start | bytes 1572872 | tf_op jit(solution)/shard_map/ppermute | solution.py:33
  27.6 14.1 %collective-permute-start.11 = (bf16[512,512]{1,0:T(8,128)(2,1)S(1)}, bf16[512,512]{1,0:T(8,128)(2,1)S(1)}, u32[]{:S(2)}, u32[]{:S(2)}) collective-permute-start(bf16[512,512]{1,0:T(8,128)(2,1)S(1)} %pad_maximum_fusion.refs_4_), channel_id=1, source_target_pairs={{0,12},{1,13},{2,14},{3,15},{4,0},{5,1},{6,2},{7,3},{8,4},{9,5},{1... | collective-permute-start | bytes 1572872 | tf_op jit(solution)/shard_map/ppermute | solution.py:33
  28.9 15.4 %collective-permute-start.6 = (bf16[128,2048]{1,0:T(8,128)(2,1)}, bf16[128,2048]{1,0:T(8,128)(2,1)S(1)}, u32[]{:S(2)}, u32[]{:S(2)}) collective-permute-start(bf16[128,2048]{1,0:T(8,128)(2,1)} %get-tuple-element.49.refs_14_), channel_id=1, source_target_pairs={{0,32},{1,33},{2,34},{3,35},{4,36},{5,37},{6,38},{7,39},{8,40},{9,... | collective-permute-start | bytes 1572872 | tf_op jit(solution)/shard_map/ppermute | solution.py:33
  30.5 17.3 %collective-permute-start.7 = (bf16[128,2048]{1,0:T(8,128)(2,1)}, bf16[128,2048]{1,0:T(8,128)(2,1)S(1)}, u32[]{:S(2)}, u32[]{:S(2)}) collective-permute-start(bf16[128,2048]{1,0:T(8,128)(2,1)} %get-tuple-element.49.refs_14_), channel_id=1, source_target_pairs={{0,96},{1,97},{2,98},{3,99},{4,100},{5,101},{6,102},{7,103},{8,104... | collective-permute-start | bytes 1572872 | tf_op jit(solution)/shard_map/ppermute | solution.py:33
  32.2 9.7 %collective-permute-start.3 = (bf16[128,8,128]{2,1,0:T(8,128)(2,1)}, bf16[128,8,128]{2,1,0:T(8,128)(2,1)S(1)}, u32[]{:S(2)}, u32[]{:S(2)}) collective-permute-start(bf16[128,8,128]{2,1,0:T(8,128)(2,1)} %get-tuple-element.46), channel_id=1, source_target_pairs={{1,2},{3,4},{5,6},{7,8},{9,10},{11,12},{13,14},{2,1},{4,3},{6,5},{... | collective-permute-start | bytes 786440 | tf_op jit(solution)/shard_map/ppermute | solution.py:352
  41.2 9.2 %collective-permute-start.16 = (bf16[256,512]{1,0:T(8,128)(2,1)S(1)}, bf16[256,512]{1,0:T(8,128)(2,1)S(1)}, u32[]{:S(2)}, u32[]{:S(2)}) collective-permute-start(bf16[256,512]{1,0:T(8,128)(2,1)S(1)} %slice.44), channel_id=1, source_target_pairs={{0,4},{1,5},{2,6},{3,7},{4,8},{5,9},{6,10},{7,11},{8,12},{9,13},{1... | collective-permute-start | bytes 786440 | tf_op jit(solution)/shard_map/ppermute | solution.py:33
  41.8 23.4 %collective-permute-start.10 = (bf16[512,512]{1,0:T(8,128)(2,1)S(1)}, bf16[512,512]{1,0:T(8,128)(2,1)}, u32[]{:S(2)}, u32[]{:S(2)}) collective-permute-start(bf16[512,512]{1,0:T(8,128)(2,1)S(1)} %collective-permute-done.9.refs_5_), channel_id=1, source_target_pairs={{0,1},{1,0},{2,3},{3,2},{4,5},{5,4},{6,7},{7,6},{8,9},{9,8},{10,11... | collective-permute-start | bytes 1572872 | tf_op jit(solution)/shard_map/ppermute | solution.py:33
  41.8 6.0 %copy-start.14 = (bf16[128,8,128]{2,1,0:T(8,128)(2,1)}, bf16[128,8,128]{2,1,0:T(8,128)(2,1)S(1)}, u32[]{:S(2)}) copy-start(bf16[128,8,128]{2,1,0:T(8,128)(2,1)S(1)} %collective-permute-done.3.next_ref) | copy-start | bytes 786436
  41.8 25.9 %collective-permute-start.12 = (bf16[512,512]{1,0:T(8,128)(2,1)S(1)}, bf16[512,512]{1,0:T(8,128)(2,1)}, u32[]{:S(2)}, u32[]{:S(2)}) collective-permute-start(bf16[512,512]{1,0:T(8,128)(2,1)S(1)} %collective-permute-done.11.refs_6_), channel_id=1, source_target_pairs={{0,1},{1,0},{2,3},{3,2},{4,5},{5,4},{6,7},{7,6},{8,9},{9,8},{10,11... | collective-permute-start | bytes 1572872 | tf_op jit(solution)/shard_map/ppermute | solution.py:33
  44.3 10.2 %collective-permute-start.17 = (bf16[256,512]{1,0:T(8,128)(2,1)S(1)}, bf16[256,512]{1,0:T(8,128)(2,1)}, u32[]{:S(2)}, u32[]{:S(2)}) collective-permute-start(bf16[256,512]{1,0:T(8,128)(2,1)S(1)} %slice.45), channel_id=1, source_target_pairs={{0,12},{1,13},{2,14},{3,15},{4,0},{5,1},{6,2},{7,3},{8,4},{9,5},{1... | collective-permute-start | bytes 786440 | tf_op jit(solution)/shard_map/ppermute | solution.py:33
  47.8 9.7 %collective-permute-start.20 = (bf16[64,2048]{1,0:T(8,128)(2,1)S(1)}, bf16[64,2048]{1,0:T(8,128)(2,1)S(1)}, u32[]{:S(2)}, u32[]{:S(2)}) collective-permute-start(bf16[64,2048]{1,0:T(8,128)(2,1)S(1)} %slice.36), channel_id=1, source_target_pairs={{0,32},{1,33},{2,34},{3,35},{4,36},{5,37},{6,38},{7,39},{8,40},{9,... | collective-permute-start | bytes 786440 | tf_op jit(solution)/shard_map/ppermute | solution.py:33
  50.4 7.8 %collective-permute-start.21 = (bf16[64,2048]{1,0:T(8,128)(2,1)S(1)}, bf16[64,2048]{1,0:T(8,128)(2,1)S(1)}, u32[]{:S(2)}, u32[]{:S(2)}) collective-permute-start(bf16[64,2048]{1,0:T(8,128)(2,1)S(1)} %slice.37), channel_id=1, source_target_pairs={{0,96},{1,97},{2,98},{3,99},{4,100},{5,101},{6,102},{7,103},{8,104... | collective-permute-start | bytes 786440 | tf_op jit(solution)/shard_map/ppermute | solution.py:33
  54.5 15.3 %collective-permute-start.18 = (bf16[256,512]{1,0:T(8,128)(2,1)S(1)}, bf16[256,512]{1,0:T(8,128)(2,1)}, u32[]{:S(2)}, u32[]{:S(2)}) collective-permute-start(bf16[256,512]{1,0:T(8,128)(2,1)S(1)} %collective-permute-done.16.refs_7_), channel_id=1, source_target_pairs={{0,1},{1,0},{2,3},{3,2},{4,5},{5,4},{6,7},{7,6},{8,9},{9,8},{10,11... | collective-permute-start | bytes 786440 | tf_op jit(solution)/shard_map/ppermute | solution.py:33
  57.5 0.7 copy-start.7
  58.3 11.5 %collective-permute-start.19 = (bf16[256,512]{1,0:T(8,128)(2,1)}, bf16[256,512]{1,0:T(8,128)(2,1)}, u32[]{:S(2)}, u32[]{:S(2)}) collective-permute-start(bf16[256,512]{1,0:T(8,128)(2,1)} %collective-permute-done.17.refs_8_), channel_id=1, source_target_pairs={{0,1},{1,0},{2,3},{3,2},{4,5},{5,4},{6,7},{7,6},{8,9},{9,8},{10,11... | collective-permute-start | bytes 786440 | tf_op jit(solution)/shard_map/ppermute | solution.py:33
  58.3 0.7 copy-start.9
  59.0 5.2 %collective-permute-start.8 = (bf16[2,4,8,128]{3,2,1,0:T(8,128)(2,1)S(1)}, bf16[2,4,8,128]{3,2,1,0:T(8,128)(2,1)S(1)}, u32[]{:S(2)}, u32[]{:S(2)}) collective-permute-start(bf16[2,4,8,128]{3,2,1,0:T(8,128)(2,1)S(1)} %copy-done.19), channel_id=1, source_target_pairs={{0,16},{1,17},{2,18},{3,19},{4,20},{5,21},{6,22},{7,23},{8,24},{9,... | collective-permute-start | bytes 49160 | tf_op jit(solution)/shard_map/ppermute | solution.py:33
  64.2 28.5 %collective-permute-start.23 = (bf16[128,2048]{1,0:T(8,128)(2,1)}, bf16[128,2048]{1,0:T(8,128)(2,1)S(1)}, u32[]{:S(2)}, u32[]{:S(2)}) collective-permute-start(bf16[128,2048]{1,0:T(8,128)(2,1)} %get-tuple-element.68.refs_14_), channel_id=1, source_target_pairs={{0,32},{1,33},{2,34},{3,35},{4,36},{5,37},{6,38},{7,39},{8,40},{9,... | collective-permute-start | bytes 1572872 | tf_op jit(solution)/shard_map/ppermute | solution.py:33
  65.2 27.5 %collective-permute-start.24 = (bf16[128,2048]{1,0:T(8,128)(2,1)}, bf16[128,2048]{1,0:T(8,128)(2,1)S(1)}, u32[]{:S(2)}, u32[]{:S(2)}) collective-permute-start(bf16[128,2048]{1,0:T(8,128)(2,1)} %get-tuple-element.68.refs_14_), channel_id=1, source_target_pairs={{0,96},{1,97},{2,98},{3,99},{4,100},{5,101},{6,102},{7,103},{8,104... | collective-permute-start | bytes 1572872 | tf_op jit(solution)/shard_map/ppermute | solution.py:33
  67.8 12.9 %collective-permute-start.13 = (bf16[4,4,8,128]{3,2,1,0:T(8,128)(2,1)S(1)}, bf16[4,4,8,128]{3,2,1,0:T(8,128)(2,1)S(1)}, u32[]{:S(2)}, u32[]{:S(2)}) collective-permute-start(bf16[4,4,8,128]{3,2,1,0:T(8,128)(2,1)S(1)} %pad_maximum_fusion.2.refs_0_), channel_id=1, source_target_pairs={{0,96},{1,97},{2,98},{3,99},{4,100},{5,101},{6,102},{7,103},{8,104... | collective-permute-start | bytes 98312 | tf_op jit(solution)/shard_map/ppermute | solution.py:33
  69.8 11.3 %collective-permute-start.14 = (bf16[4,4,8,128]{3,2,1,0:T(8,128)(2,1)S(1)}, bf16[4,4,8,128]{3,2,1,0:T(8,128)(2,1)S(1)}, u32[]{:S(2)}, u32[]{:S(2)}) collective-permute-start(bf16[4,4,8,128]{3,2,1,0:T(8,128)(2,1)S(1)} %pad_maximum_fusion.2.refs_0_), channel_id=1, source_target_pairs={{0,64},{1,65},{2,66},{3,67},{4,68},{5,69},{6,70},{7,71},{8,72},{9,... | collective-permute-start | bytes 98312 | tf_op jit(solution)/shard_map/ppermute | solution.py:33
  69.8 11.6 %collective-permute-start.15 = (bf16[4,4,8,128]{3,2,1,0:T(8,128)(2,1)S(1)}, bf16[4,4,8,128]{3,2,1,0:T(8,128)(2,1)S(1)}, u32[]{:S(2)}, u32[]{:S(2)}) collective-permute-start(bf16[4,4,8,128]{3,2,1,0:T(8,128)(2,1)S(1)} %pad_maximum_fusion.2.refs_0_), channel_id=1, source_target_pairs={{0,32},{1,33},{2,34},{3,35},{4,36},{5,37},{6,38},{7,39},{8,40},{9,... | collective-permute-start | bytes 98312 | tf_op jit(solution)/shard_map/ppermute | solution.py:33
  81.4 1.0 copy-start.4
  82.4 0.9 copy-start.8
  83.4 0.9 copy-start.10
  84.3 11.8 %copy-start.5 = (bf16[128,2048]{1,0:T(8,128)(2,1)S(1)}, bf16[128,2048]{1,0:T(8,128)(2,1)}, u32[]{:S(2)}) copy-start(bf16[128,2048]{1,0:T(8,128)(2,1)} %get-tuple-element.49.refs_14_) | copy-start | bytes 1572868
  90.9 11.8 %copy-start.3 = (f32[128,1024]{1,0:T(8,128)}, f32[128,1024]{1,0:T(8,128)S(1)}, u32[]{:S(2)}) copy-start(f32[128,1024]{1,0:T(8,128)S(1)} %get-tuple-element.57.a_ref) | copy-start | bytes 1572868
  90.9 12.9 %collective-permute-start.22 = (bf16[128,1024]{1,0:T(8,128)(2,1)S(1)}, bf16[128,1024]{1,0:T(8,128)(2,1)S(1)}, u32[]{:S(2)}, u32[]{:S(2)}) collective-permute-start(bf16[128,1024]{1,0:T(8,128)(2,1)S(1)} %get-tuple-element.63), channel_id=1, source_target_pairs={{0,16},{1,17},{2,18},{3,19},{4,20},{5,21},{6,22},{7,23},{8,24},{9,... | collective-permute-start | bytes 786440 | tf_op jit(solution)/shard_map/ppermute | solution.py:33
  92.7 11.1 %collective-permute-start.25 = (bf16[64,2048]{1,0:T(8,128)(2,1)S(1)}, bf16[64,2048]{1,0:T(8,128)(2,1)S(1)}, u32[]{:S(2)}, u32[]{:S(2)}) collective-permute-start(bf16[64,2048]{1,0:T(8,128)(2,1)S(1)} %slice.38), channel_id=1, source_target_pairs={{0,32},{1,33},{2,34},{3,35},{4,36},{5,37},{6,38},{7,39},{8,40},{9,... | collective-permute-start | bytes 786440 | tf_op jit(solution)/shard_map/ppermute | solution.py:33
  93.9 9.9 %copy-start.6 = (bf16[128,2048]{1,0:T(8,128)(2,1)S(1)}, bf16[128,2048]{1,0:T(8,128)(2,1)}, u32[]{:S(2)}) copy-start(bf16[128,2048]{1,0:T(8,128)(2,1)} %get-tuple-element.68.refs_14_) | copy-start | bytes 1572868
  93.9 9.8 %collective-permute-start.26 = (bf16[64,2048]{1,0:T(8,128)(2,1)S(1)}, bf16[64,2048]{1,0:T(8,128)(2,1)S(1)}, u32[]{:S(2)}, u32[]{:S(2)}) collective-permute-start(bf16[64,2048]{1,0:T(8,128)(2,1)S(1)} %slice.39), channel_id=1, source_target_pairs={{0,96},{1,97},{2,98},{3,99},{4,100},{5,101},{6,102},{7,103},{8,104... | collective-permute-start | bytes 786440 | tf_op jit(solution)/shard_map/ppermute | solution.py:33
  102.6 0.8 copy-start
  103.5 7.7 %collective-permute-start.27 = (bf16[128,1024]{1,0:T(8,128)(2,1)S(1)}, bf16[128,1024]{1,0:T(8,128)(2,1)S(1)}, u32[]{:S(2)}, u32[]{:S(2)}) collective-permute-start(bf16[128,1024]{1,0:T(8,128)(2,1)S(1)} %get-tuple-element.72), channel_id=1, source_target_pairs={{0,16},{1,17},{2,18},{3,19},{4,20},{5,21},{6,22},{7,23},{8,24},{9,... | collective-permute-start | bytes 786440 | tf_op jit(solution)/shard_map/ppermute | solution.py:33
  103.8 6.6 %copy-start.18 = (bf16[128,1024]{1,0:T(8,128)(2,1)}, bf16[128,1024]{1,0:T(8,128)(2,1)S(1)}, u32[]{:S(2)}) copy-start(bf16[128,1024]{1,0:T(8,128)(2,1)S(1)} %collective-permute-done.22.b_ref) | copy-start | bytes 786436
  110.4 0.8 copy-start.1
  111.2 8.3 %copy-start.15 = (bf16[128,1024]{1,0:T(8,128)(2,1)}, bf16[128,1024]{1,0:T(8,128)(2,1)S(1)}, u32[]{:S(2)}) copy-start(bf16[128,1024]{1,0:T(8,128)(2,1)S(1)} %collective-permute-done.27.b_ref) | copy-start | bytes 786436
  111.2 13.2 %collective-permute-start.29 = (bf16[128,1024]{1,0:T(8,128)(2,1)S(1)}, bf16[128,1024]{1,0:T(8,128)(2,1)S(1)}, u32[]{:S(2)}, u32[]{:S(2)}) collective-permute-start(bf16[128,1024]{1,0:T(8,128)(2,1)S(1)} %get-tuple-element.79), channel_id=1, source_target_pairs={{0,16},{1,17},{2,18},{3,19},{4,20},{5,21},{6,22},{7,23},{8,24},{9,... | collective-permute-start | bytes 786440 | tf_op jit(solution)/shard_map/ppermute | solution.py:33
  119.4 0.8 copy-start.2
  120.2 6.7 %collective-permute-start.28 = (bf16[128,1024]{1,0:T(8,128)(2,1)S(1)}, bf16[128,1024]{1,0:T(8,128)(2,1)S(1)}, u32[]{:S(2)}, u32[]{:S(2)}) collective-permute-start(bf16[128,1024]{1,0:T(8,128)(2,1)S(1)} %get-tuple-element.78), channel_id=1, source_target_pairs={{0,16},{1,17},{2,18},{3,19},{4,20},{5,21},{6,22},{7,23},{8,24},{9,... | collective-permute-start | bytes 786440 | tf_op jit(solution)/shard_map/ppermute | solution.py:33
  124.3 0.7 copy-start.16
  (2 other events, 1.4 us)

commit v4 on v3

--- a/solution.py
+++ b/solution.py
@@ -304,7 +304,7 @@
             pltpu.SemaphoreType.DMA((10,)),
             pltpu.SemaphoreType.DMA((5,)),
         ],
-        compiler_params=pltpu.CompilerParams(vmem_limit_bytes=24 << 20),
+        compiler_params=pltpu.CompilerParams(vmem_limit_bytes=56 << 20),
         cost_estimate=pl.CostEstimate(
             flops=2 * SLICES * 256 * 512 * cells, bytes_accessed=6 << 20, transcendentals=0
         ),
@@ -353,33 +353,31 @@
     block, own = transport_inner(density, limiter, heading, courant, first, inner)
 
     base = jnp.concatenate([own_slice[128:], partner[:128], after(cross, block)], 0)
-    one = shift(base, dx=1)
-    three = shift(base, dx=-1)
+    swapped = [shift(base, dc=1)]
+    block = after(block, swapped[0])
+    before, behind = shift(block, dy=1), shift(block, dy=-1)
+    one, three, before, behind = after(
+        (shift(base, dx=1), shift(base, dx=-1), before, behind)
+    )
     pieces = [base, one, three, shift(one[:256], dx=1), shift(three[256:], dx=-1)]
-    swapped = [shift(p, dc=1) for p in pieces]
-    pieces = pieces + swapped
-
-    def gather(block, *earlier):
-        before, behind = after((shift(block, dy=1), shift(block, dy=-1)), *earlier)
-        return [block, behind, before, shift(before[:64], dy=1), shift(behind[64:], dy=-1)]
-
-    inside = gather(after(block, swapped[0]), second)
-    rows = jnp.concatenate([own, shift(own, dz=1)], 0)
-    second = after(second, inside[1], inside[2])
+    pieces = pieces + swapped + [shift(p, dc=1) for p in pieces[1:]]
+    inside = [block, behind, before, shift(before[:64], dy=1), shift(behind[64:], dy=-1)]
+
+    rows = after(jnp.concatenate([own, shift(own, dz=1)], 0), before)
+    weights = [rows, shift(rows, dy=-1), shift(rows, dy=2), shift(rows, dy=1)]
+    second = after(second, before)
     transported, block = transport(density, limiter, heading, courant, first, second, inner)
-    rows = after(rows, block, swapped[1], swapped[2])
-    block = after(block, inside[3], inside[4])
-    weights = [rows, shift(rows, dy=-1), shift(rows, dy=2), shift(rows, dy=1)]
-    outside = gather(block)
-
-    result, got = None, []
+    before, behind = shift(block, dy=1), shift(block, dy=-1)
+    outside = [block, behind, before, shift(before[:64], dy=1), shift(behind[64:], dy=-1)]
+
+    results, got = [None], []
     for layers, blocks in zip(BLOCKS, (inside, outside), strict=True):
         for place, layer in enumerate(layers):
             mine, other = collide(layer, place, pieces, blocks, weights)
-            weights = after(weights, mine, *got[-1:])
+            weights = after(weights, mine, *got[-1:], *results[1:][-1:])
             got.append(shift(other, dz=1))
-            result = combine(layer, mine, got[-1], result)
-    return transported, result
+            results.append(combine(layer, mine, got[-1], results[-1]))
+    return transported, results[-1]
 
 
 def solution(mesh):

time: 130 us -> 135 us (1.038)
  Pallas kernels: 47.8 us -> 62.8 us
  waiting for transfers between devices: 27.1 us -> 20 us
  local copies, waits for them, and re-layouts: 9.84 us -> 6.69 us
    pallas_call x4, Pallas kernels: 26.1 us -> 41.1 us  [collide(): pl.pallas_call(kernel, out_shape=(shape((128, cells), F32), shape((128, c...]
    ppermute x28, waiting for transfers between devices: 27.1 us -> 20 us  [shift(): return lax.ppermute(value, BOTH, pairs)]
    unnamed x40 -> x50, local copies, waits for them, and re-layouts: 9.7 us -> 6.54 us
  transfers between devices with their start and end apart: 30 -> 30, of which waited for: 8 -> 9; matrix products, arithmetic and copies ran while one was open for 0% -> 1% of each run, Pallas kernels for 34% -> 36%
where the time goes in v4:
time: 135 us; the launch traced here: 134 us
  Pallas kernels  62.8 us (47%)
  starting transfers between devices  42.7 us (32%)
  waiting for transfers between devices  20 us (15%)
  local copies, waits for them, and re-layouts  6.69 us (5%)
    ppermute x28, starting transfers between devices, shift(): return lax.ppermute(value, BOTH, pairs)  41.4 us
    pallas_call x4, Pallas kernels, collide(): pl.pallas_call(kernel, out_shape=(shape((128, cells), F32), shape((128, c...  41.1 us
    ppermute x28, waiting for transfers between devices, shift(): return lax.ppermute(value, BOTH, pairs)  20 us
    pallas_call x4, Pallas kernels, combine(): pl.pallas_call(kernel, grid=(128 // step,), out_shape=shape((128, 4, 8, 1...  7.57 us
    unnamed x50, local copies, waits for them, and re-layouts  6.54 us
    pallas_call x1, Pallas kernels, transport(): pl.pallas_call(kernel, grid=(rows // STEP,), out_shape=(shape(density.sha...  5.16 us
    pallas_call x1, Pallas kernels, transport_inner(): pl.pallas_call(kernel, grid=(rows // STEP,), out_shape=(shape((rows, 2048...  4.48 us
    pallas_call x1, Pallas kernels, pack(): pl.pallas_call(kernel, out_shape=(shape((rows + 3, *dims), BF16), shape((...  2.73 us
  transfers between devices with their start and end apart: 30, of which 9 were waited for; matrix products, arithmetic and copies ran while one was open for 1% of the time, Pallas kernels for 36%

profile of v4, /device:TPU:0, one launch (start us, length us, event | category | flops | bytes accessed | tf_op | source)
XLA Modules:
  0.0 134.0 jit_solution(6409841128782761171)
XLA Ops:
  0.6 1.8 %split_slice.1 = bf16[256,512]{1,0:T(8,128)(2,1)} custom-call(bf16[4,2,128,128]{3,2,1,0:T(8,128)(2,1)} %bitcast.1), custom_call_target="tpu_custom_call" | custom-call | tf_op jit(solution)/shard_map/split_slice/pallas_call | solution.py:89
  2.4 2.0 %collective-permute-start.1 = (bf16[256,512]{1,0:T(8,128)(2,1)}, bf16[256,512]{1,0:T(8,128)(2,1)S(1)}, u32[]{:S(2)}, u32[]{:S(2)}) collective-permute-start(bf16[256,512]{1,0:T(8,128)(2,1)} %split_slice.1), channel_id=1, source_target_pairs={{0,16},{1,17},{2,18},{3,19},{4,20},{5,21},{6,22},{7,23},{8,24},{9,... | collective-permute-start | bytes 786440 | tf_op jit(solution)/shard_map/ppermute | solution.py:33
  4.4 2.7 %pack.1 = (bf16[131,8,128]{2,1,0:T(8,128)(2,1)}, bf16[128,8,128]{2,1,0:T(8,128)(2,1)}, bf16[129,2,8,128]{3,2,1,0:T(8,128)(2,1)}) custom-call(f32[128,4,8,128]{3,2,1,0:T(8,128)} %d_ref.4, s32[4,8,128]{2,1,0:T(8,128)} %l_ref.5), custom_call_target="tpu_custom_call" | custom-call | tf_op jit(solution)/shard_map/pack/pallas_call | solution.py:68
  7.8 5.0 %collective-permute-start.2 = (bf16[129,2,8,128]{3,2,1,0:T(8,128)(2,1)}, bf16[129,2,8,128]{3,2,1,0:T(8,128)(2,1)S(1)}, u32[]{:S(2)}, u32[]{:S(2)}) collective-permute-start(bf16[129,2,8,128]{3,2,1,0:T(8,128)(2,1)} %get-tuple-element.43), channel_id=1, source_target_pairs={{0,1},{1,0},{2,3},{3,2},{4,5},{5,4},{6,7},{7,6},{8,9},{9,8},{10,11... | collective-permute-start | bytes 1585160 | tf_op jit(solution)/shard_map/ppermute | solution.py:33
  13.0 2.0 %collective-permute-start.4 = (bf16[256,512]{1,0:T(8,128)(2,1)S(1)}, bf16[256,512]{1,0:T(8,128)(2,1)S(1)}, u32[]{:S(2)}, u32[]{:S(2)}) collective-permute-start(bf16[256,512]{1,0:T(8,128)(2,1)S(1)} %pad_maximum_fusion.1), channel_id=1, source_target_pairs={{0,18},{1,19},{2,16},{3,17},{4,22},{5,23},{6,20},{7,21},{8,26},{9,... | collective-permute-start | bytes 786440 | tf_op jit(solution)/shard_map/ppermute | solution.py:33
  15.0 0.7 copy-done.1
  15.7 0.8 copy-done
  16.5 4.5 %transport_inner.1 = (bf16[128,2048]{1,0:T(8,128)(2,1)}, bf16[2,4,8,128]{3,2,1,0:T(8,128)(2,1)}) custom-call(s32[128]{0:T(128)} %h_ref.3, f32[128]{0:T(128)} %c_ref.3, f32[128,4,8,128]{3,2,1,0:T(8,128)} %d_ref.4, s32[4,8,128]{2,1,0:T(8,128)} %l_ref.5, bf16[131,8,128]{2,1,0:T(8,128)(2,1)} %copy-done.1, bf16[131,8,128]{2,1,0:T(8,128)(2,1)} %copy-done.1, ...), custom_call_target="tpu_custom_call" | custom-call | flops 2097152 | bytes 3145728 | tf_op jit(solution)/shard_map/transport_inner/pallas_call | solution.py:182
  21.0 3.0 %collective-permute-done.4 = bf16[256,512]{1,0:T(8,128)(2,1)S(1)} collective-permute-done((bf16[256,512]{1,0:T(8,128)(2,1)S(1)}, bf16[256,512]{1,0:T(8,128)(2,1)S(1)}, u32[]{:S(2)}, u32[]{:S(2)}) %collective-permute-start.4) | collective-permute-done | bytes 262176 | tf_op jit(solution)/shard_map/ppermute | solution.py:33
  24.0 1.5 %collective-permute-start.7 = (bf16[512,512]{1,0:T(8,128)(2,1)S(1)}, bf16[512,512]{1,0:T(8,128)(2,1)S(1)}, u32[]{:S(2)}, u32[]{:S(2)}) collective-permute-start(bf16[512,512]{1,0:T(8,128)(2,1)S(1)} %pad_maximum_fusion.refs_4_), channel_id=1, source_target_pairs={{0,1},{1,0},{2,3},{3,2},{4,5},{5,4},{6,7},{7,6},{8,9},{9,8},{10,11... | collective-permute-start | bytes 1572872 | tf_op jit(solution)/shard_map/ppermute | solution.py:33
  25.5 2.2 %collective-permute-start.5 = (bf16[512,512]{1,0:T(8,128)(2,1)S(1)}, bf16[512,512]{1,0:T(8,128)(2,1)S(1)}, u32[]{:S(2)}, u32[]{:S(2)}) collective-permute-start(bf16[512,512]{1,0:T(8,128)(2,1)S(1)} %pad_maximum_fusion.refs_4_), channel_id=1, source_target_pairs={{0,4},{1,5},{2,6},{3,7},{4,8},{5,9},{6,10},{7,11},{8,12},{9,13},{1... | collective-permute-start | bytes 1572872 | tf_op jit(solution)/shard_map/ppermute | solution.py:33
  27.7 1.3 collective-permute-start.6
  29.0 1.6 %collective-permute-start.8 = (bf16[128,2048]{1,0:T(8,128)(2,1)}, bf16[128,2048]{1,0:T(8,128)(2,1)S(1)}, u32[]{:S(2)}, u32[]{:S(2)}) collective-permute-start(bf16[128,2048]{1,0:T(8,128)(2,1)} %get-tuple-element.48.refs_14_), channel_id=1, source_target_pairs={{0,32},{1,33},{2,34},{3,35},{4,36},{5,37},{6,38},{7,39},{8,40},{9,... | collective-permute-start | bytes 1572872 | tf_op jit(solution)/shard_map/ppermute | solution.py:33
  30.5 1.7 %collective-permute-start.9 = (bf16[128,2048]{1,0:T(8,128)(2,1)}, bf16[128,2048]{1,0:T(8,128)(2,1)S(1)}, u32[]{:S(2)}, u32[]{:S(2)}) collective-permute-start(bf16[128,2048]{1,0:T(8,128)(2,1)} %get-tuple-element.48.refs_14_), channel_id=1, source_target_pairs={{0,96},{1,97},{2,98},{3,99},{4,100},{5,101},{6,102},{7,103},{8,104... | collective-permute-start | bytes 1572872 | tf_op jit(solution)/shard_map/ppermute | solution.py:33
  32.2 3.9 %collective-permute-done.10 = bf16[2,4,8,128]{3,2,1,0:T(8,128)(2,1)S(1)} collective-permute-done((bf16[2,4,8,128]{3,2,1,0:T(8,128)(2,1)}, bf16[2,4,8,128]{3,2,1,0:T(8,128)(2,1)S(1)}, u32[]{:S(2)}, u32[]{:S(2)}) %collective-permute-start.10) | collective-permute-done | bytes 16416 | tf_op jit(solution)/shard_map/ppermute | solution.py:33
  36.8 0.7 pad_maximum_fusion.2.refs_0_
  37.6 3.7 %collective-permute-done.5.refs_5_ = bf16[512,512]{1,0:T(8,128)(2,1)S(1)} collective-permute-done((bf16[512,512]{1,0:T(8,128)(2,1)S(1)}, bf16[512,512]{1,0:T(8,128)(2,1)S(1)}, u32[]{:S(2)}, u32[]{:S(2)}) %collective-permute-start.5) | collective-permute-done | bytes 524320 | tf_op jit(solution)/shard_map/ppermute | solution.py:33
  41.4 2.8 %collective-permute-done.8.refs_16_ = bf16[128,2048]{1,0:T(8,128)(2,1)S(1)} collective-permute-done((bf16[128,2048]{1,0:T(8,128)(2,1)}, bf16[128,2048]{1,0:T(8,128)(2,1)S(1)}, u32[]{:S(2)}, u32[]{:S(2)}) %collective-permute-start.8) | collective-permute-done | bytes 524320 | tf_op jit(solution)/shard_map/ppermute | solution.py:33
  44.2 3.0 %collective-permute-start.11 = (bf16[4,4,8,128]{3,2,1,0:T(8,128)(2,1)S(1)}, bf16[4,4,8,128]{3,2,1,0:T(8,128)(2,1)S(1)}, u32[]{:S(2)}, u32[]{:S(2)}) collective-permute-start(bf16[4,4,8,128]{3,2,1,0:T(8,128)(2,1)S(1)} %pad_maximum_fusion.2.refs_0_), channel_id=1, source_target_pairs={{0,96},{1,97},{2,98},{3,99},{4,100},{5,101},{6,102},{7,103},{8,104... | collective-permute-start | bytes 98312 | tf_op jit(solution)/shard_map/ppermute | solution.py:33
  47.9 0.7 collective-permute-start.13
  48.6 0.8 collective-permute-start.14
  49.4 2.6 %collective-permute-start.15 = (bf16[256,512]{1,0:T(8,128)(2,1)S(1)}, bf16[256,512]{1,0:T(8,128)(2,1)}, u32[]{:S(2)}, u32[]{:S(2)}) collective-permute-start(bf16[256,512]{1,0:T(8,128)(2,1)S(1)} %slice.35), channel_id=1, source_target_pairs={{0,12},{1,13},{2,14},{3,15},{4,0},{5,1},{6,2},{7,3},{8,4},{9,5},{1... | collective-permute-start | bytes 786440 | tf_op jit(solution)/shard_map/ppermute | solution.py:33
  52.0 2.2 %collective-permute-start.20 = (bf16[64,2048]{1,0:T(8,128)(2,1)S(1)}, bf16[64,2048]{1,0:T(8,128)(2,1)S(1)}, u32[]{:S(2)}, u32[]{:S(2)}) collective-permute-start(bf16[64,2048]{1,0:T(8,128)(2,1)S(1)} %slice.36), channel_id=1, source_target_pairs={{0,32},{1,33},{2,34},{3,35},{4,36},{5,37},{6,38},{7,39},{8,40},{9,... | collective-permute-start | bytes 786440 | tf_op jit(solution)/shard_map/ppermute | solution.py:33
  54.7 1.5 %collective-permute-done.14.refs_7_ = bf16[256,512]{1,0:T(8,128)(2,1)S(1)} collective-permute-done((bf16[256,512]{1,0:T(8,128)(2,1)S(1)}, bf16[256,512]{1,0:T(8,128)(2,1)S(1)}, u32[]{:S(2)}, u32[]{:S(2)}) %collective-permute-start.14) | collective-permute-done | bytes 262176 | tf_op jit(solution)/shard_map/ppermute | solution.py:33
  56.3 2.6 %collective-permute-start.21 = (bf16[64,2048]{1,0:T(8,128)(2,1)S(1)}, bf16[64,2048]{1,0:T(8,128)(2,1)}, u32[]{:S(2)}, u32[]{:S(2)}) collective-permute-start(bf16[64,2048]{1,0:T(8,128)(2,1)S(1)} %slice.37), channel_id=1, source_target_pairs={{0,96},{1,97},{2,98},{3,99},{4,100},{5,101},{6,102},{7,103},{8,104... | collective-permute-start | bytes 786440 | tf_op jit(solution)/shard_map/ppermute | solution.py:33
  58.8 0.8 collective-permute-done.20.refs_17_
  59.6 0.7 copy-done.19
  60.3 5.2 %transport.1 = (f32[128,4,8,128]{3,2,1,0:T(8,128)}, bf16[128,2048]{1,0:T(8,128)(2,1)}) custom-call(s32[128]{0:T(128)} %h_ref.3, f32[128]{0:T(128)} %c_ref.3, f32[128,4,8,128]{3,2,1,0:T(8,128)} %d_ref.4, s32[4,8,128]{2,1,0:T(8,128)} %l_ref.5, bf16[131,8,128]{2,1,0:T(8,128)(2,1)} %copy-done.1, bf16[131,8,128]{2,1,0:T(8,128)(2,1)} %copy-done.1, ...), custom_call_target="tpu_custom_call" | custom-call | flops 4194304 | bytes 6291456 | tf_op jit(solution)/shard_map/transport/pallas_call | solution.py:219
  65.6 1.0 collective-permute-start.24
  66.6 2.3 %collective-permute-start.23 = (bf16[128,2048]{1,0:T(8,128)(2,1)}, bf16[128,2048]{1,0:T(8,128)(2,1)S(1)}, u32[]{:S(2)}, u32[]{:S(2)}) collective-permute-start(bf16[128,2048]{1,0:T(8,128)(2,1)} %get-tuple-element.68.refs_14_), channel_id=1, source_target_pairs={{0,96},{1,97},{2,98},{3,99},{4,100},{5,101},{6,102},{7,103},{8,104... | collective-permute-start | bytes 1572872 | tf_op jit(solution)/shard_map/ppermute | solution.py:33
  68.9 10.3 %collide.4 = (f32[128,1024]{1,0:T(8,128)}, bf16[128,1024]{1,0:T(8,128)(2,1)}) custom-call(bf16[4,4,8,128]{3,2,1,0:T(8,128)(2,1)} %copy-done.15, bf16[4,4,8,128]{3,2,1,0:T(8,128)(2,1)} %copy-done.22, bf16[4,4,8,128]{3,2,1,0:T(8,128)(2,1)} %copy-done.23, bf16[4,4,8,128]{3,2,1,0:T(8,128)(2,1)} %copy-done.24, bf16[512,512]{1,0:T(8,128)(2,1)} %copy-done.3, ...), custom_call_target="tpu_custom_call" | custom-call | flops 4294967296 | bytes 6291456 | tf_op jit(solution)/shard_map/collide/pallas_call | solution.py:295
  79.3 10.3 %collide.5 = (f32[128,1024]{1,0:T(8,128)}, bf16[128,1024]{1,0:T(8,128)(2,1)}) custom-call(bf16[4,4,8,128]{3,2,1,0:T(8,128)(2,1)} %copy-done.15, bf16[4,4,8,128]{3,2,1,0:T(8,128)(2,1)} %copy-done.22, bf16[4,4,8,128]{3,2,1,0:T(8,128)(2,1)} %copy-done.23, bf16[4,4,8,128]{3,2,1,0:T(8,128)(2,1)} %copy-done.24, bf16[512,512]{1,0:T(8,128)(2,1)} %copy-done.3, ...), custom_call_target="tpu_custom_call" | custom-call | flops 4294967296 | bytes 6291456 | tf_op jit(solution)/shard_map/collide/pallas_call | solution.py:295
  89.6 2.1 %collective-permute-start.27 = (bf16[128,1024]{1,0:T(8,128)(2,1)}, bf16[128,1024]{1,0:T(8,128)(2,1)S(1)}, u32[]{:S(2)}, u32[]{:S(2)}) collective-permute-start(bf16[128,1024]{1,0:T(8,128)(2,1)} %get-tuple-element.70), channel_id=1, source_target_pairs={{0,16},{1,17},{2,18},{3,19},{4,20},{5,21},{6,22},{7,23},{8,24},{9,... | collective-permute-start | bytes 786440 | tf_op jit(solution)/shard_map/ppermute | solution.py:33
  91.8 3.5 %collective-permute-start.26 = (bf16[64,2048]{1,0:T(8,128)(2,1)S(1)}, bf16[64,2048]{1,0:T(8,128)(2,1)S(1)}, u32[]{:S(2)}, u32[]{:S(2)}) collective-permute-start(bf16[64,2048]{1,0:T(8,128)(2,1)S(1)} %slice.45), channel_id=1, source_target_pairs={{0,96},{1,97},{2,98},{3,99},{4,100},{5,101},{6,102},{7,103},{8,104... | collective-permute-start | bytes 786440 | tf_op jit(solution)/shard_map/ppermute | solution.py:33
  95.3 0.7 copy-done.8
  96.0 1.9 %combine.4.refs_0_ = f32[128,4,8,128]{3,2,1,0:T(8,128)} custom-call(f32[128,1024]{1,0:T(8,128)} %get-tuple-element.57.a_ref, bf16[128,1024]{1,0:T(8,128)(2,1)} %copy-done.8), custom_call_target="tpu_custom_call" | custom-call | flops 131072 | bytes 1310720 | tf_op jit(solution)/shard_map/combine/pallas_call | solution.py:326
  98.0 0.7 copy-done.6
  98.7 1.9 %combine.5.refs_0_ = f32[128,4,8,128]{3,2,1,0:T(8,128)} custom-call(f32[128,1024]{1,0:T(8,128)} %get-tuple-element.62.a_ref, bf16[128,1024]{1,0:T(8,128)(2,1)} %copy-done.6, f32[128,4,8,128]{3,2,1,0:T(8,128)} %combine.4.refs_0_), custom_call_target="tpu_custom_call", output_to_operand_aliasing={{}: (2, {})} | custom-call | flops 131072 | bytes 1310720 | tf_op jit(solution)/shard_map/combine/pallas_call | solution.py:326
  100.6 0.7 copy-done.20
  101.3 0.7 copy-done.21
  102.0 10.3 %collide.6 = (f32[128,1024]{1,0:T(8,128)}, bf16[128,1024]{1,0:T(8,128)(2,1)}) custom-call(bf16[4,4,8,128]{3,2,1,0:T(8,128)(2,1)} %copy-done.15, bf16[4,4,8,128]{3,2,1,0:T(8,128)(2,1)} %copy-done.22, bf16[4,4,8,128]{3,2,1,0:T(8,128)(2,1)} %copy-done.23, bf16[4,4,8,128]{3,2,1,0:T(8,128)(2,1)} %copy-done.24, bf16[512,512]{1,0:T(8,128)(2,1)} %copy-done.3, ...), custom_call_target="tpu_custom_call" | custom-call | flops 4294967296 | bytes 6291456 | tf_op jit(solution)/shard_map/collide/pallas_call | solution.py:295
  112.3 1.8 %collective-permute-start.29 = (bf16[128,1024]{1,0:T(8,128)(2,1)}, bf16[128,1024]{1,0:T(8,128)(2,1)S(1)}, u32[]{:S(2)}, u32[]{:S(2)}) collective-permute-start(bf16[128,1024]{1,0:T(8,128)(2,1)} %get-tuple-element.77), channel_id=1, source_target_pairs={{0,16},{1,17},{2,18},{3,19},{4,20},{5,21},{6,22},{7,23},{8,24},{9,... | collective-permute-start | bytes 786440 | tf_op jit(solution)/shard_map/ppermute | solution.py:33
  114.1 10.2 %collide.7 = (f32[128,1024]{1,0:T(8,128)}, bf16[128,1024]{1,0:T(8,128)(2,1)}) custom-call(bf16[4,4,8,128]{3,2,1,0:T(8,128)(2,1)} %copy-done.15, bf16[4,4,8,128]{3,2,1,0:T(8,128)(2,1)} %copy-done.22, bf16[4,4,8,128]{3,2,1,0:T(8,128)(2,1)} %copy-done.23, bf16[4,4,8,128]{3,2,1,0:T(8,128)(2,1)} %copy-done.24, bf16[512,512]{1,0:T(8,128)(2,1)} %copy-done.3, ...), custom_call_target="tpu_custom_call" | custom-call | flops 4294967296 | bytes 6291456 | tf_op jit(solution)/shard_map/collide/pallas_call | solution.py:295
  124.8 0.7 copy-done.5
  125.5 1.9 %combine.6.refs_0_ = f32[128,4,8,128]{3,2,1,0:T(8,128)} custom-call(f32[128,1024]{1,0:T(8,128)} %get-tuple-element.69.a_ref, bf16[128,1024]{1,0:T(8,128)(2,1)} %copy-done.5, f32[128,4,8,128]{3,2,1,0:T(8,128)} %combine.5.refs_0_), custom_call_target="tpu_custom_call", output_to_operand_aliasing={{}: (2, {})} | custom-call | flops 131072 | bytes 1310720 | tf_op jit(solution)/shard_map/combine/pallas_call | solution.py:326
  127.4 4.0 %collective-permute-done.28.b_ref = bf16[128,1024]{1,0:T(8,128)(2,1)S(1)} collective-permute-done((bf16[128,1024]{1,0:T(8,128)(2,1)}, bf16[128,1024]{1,0:T(8,128)(2,1)S(1)}, u32[]{:S(2)}, u32[]{:S(2)}) %collective-permute-start.28) | collective-permute-done | bytes 262176 | tf_op jit(solution)/shard_map/ppermute | solution.py:33
  131.4 0.7 copy-done.7
  132.1 1.9 %combine.7 = f32[128,4,8,128]{3,2,1,0:T(8,128)} custom-call(f32[128,1024]{1,0:T(8,128)} %get-tuple-element.75.a_ref, bf16[128,1024]{1,0:T(8,128)(2,1)} %copy-done.7, f32[128,4,8,128]{3,2,1,0:T(8,128)} %combine.6.refs_0_), custom_call_target="tpu_custom_call", output_to_operand_aliasing={{}: (2, {})} | custom-call | flops 131072 | bytes 1310720 | tf_op jit(solution)/shard_map/combine/pallas_call | solution.py:326
  (85 shorter events, 3.7 us)
Async XLA Ops:
  2.4 10.4 %copy-start.2 = (bf16[256,512]{1,0:T(8,128)(2,1)S(1)}, bf16[256,512]{1,0:T(8,128)(2,1)}, u32[]{:S(2)}) copy-start(bf16[256,512]{1,0:T(8,128)(2,1)} %split_slice.1) | copy-start | bytes 786436
  2.4 10.4 %collective-permute-start.1 = (bf16[256,512]{1,0:T(8,128)(2,1)}, bf16[256,512]{1,0:T(8,128)(2,1)S(1)}, u32[]{:S(2)}, u32[]{:S(2)}) collective-permute-start(bf16[256,512]{1,0:T(8,128)(2,1)} %split_slice.1), channel_id=1, source_target_pairs={{0,16},{1,17},{2,18},{3,19},{4,20},{5,21},{6,22},{7,23},{8,24},{9,... | collective-permute-start | bytes 786440 | tf_op jit(solution)/shard_map/ppermute | solution.py:33
  7.2 7.8 %collective-permute-start = (bf16[131,8,128]{2,1,0:T(8,128)(2,1)}, bf16[131,8,128]{2,1,0:T(8,128)(2,1)S(1)}, u32[]{:S(2)}, u32[]{:S(2)}) collective-permute-start(bf16[131,8,128]{2,1,0:T(8,128)(2,1)} %get-tuple-element.41), channel_id=1, source_target_pairs={{1,2},{3,4},{5,6},{7,8},{9,10},{11,12},{13,14},{2,1},{4,3},{6,5},{... | collective-permute-start | bytes 804872 | tf_op jit(solution)/shard_map/ppermute | solution.py:346
  7.8 7.1 %collective-permute-start.2 = (bf16[129,2,8,128]{3,2,1,0:T(8,128)(2,1)}, bf16[129,2,8,128]{3,2,1,0:T(8,128)(2,1)S(1)}, u32[]{:S(2)}, u32[]{:S(2)}) collective-permute-start(bf16[129,2,8,128]{3,2,1,0:T(8,128)(2,1)} %get-tuple-element.43), channel_id=1, source_target_pairs={{0,1},{1,0},{2,3},{3,2},{4,5},{5,4},{6,7},{7,6},{8,9},{9,8},{10,11... | collective-permute-start | bytes 1585160 | tf_op jit(solution)/shard_map/ppermute | solution.py:33
  12.9 23.2 %copy-start.18 = (bf16[128,8,128]{2,1,0:T(8,128)(2,1)S(1)}, bf16[128,8,128]{2,1,0:T(8,128)(2,1)}, u32[]{:S(2)}) copy-start(bf16[128,8,128]{2,1,0:T(8,128)(2,1)} %get-tuple-element.45) | copy-start | bytes 786436
  13.0 11.0 %collective-permute-start.4 = (bf16[256,512]{1,0:T(8,128)(2,1)S(1)}, bf16[256,512]{1,0:T(8,128)(2,1)S(1)}, u32[]{:S(2)}, u32[]{:S(2)}) collective-permute-start(bf16[256,512]{1,0:T(8,128)(2,1)S(1)} %pad_maximum_fusion.1), channel_id=1, source_target_pairs={{0,18},{1,19},{2,16},{3,17},{4,22},{5,23},{6,20},{7,21},{8,26},{9,... | collective-permute-start | bytes 786440 | tf_op jit(solution)/shard_map/ppermute | solution.py:33
  15.0 0.7 copy-start.1
  15.7 0.8 copy-start
  24.0 41.5 %copy-start.3 = (bf16[512,512]{1,0:T(8,128)(2,1)}, bf16[512,512]{1,0:T(8,128)(2,1)S(1)}, u32[]{:S(2)}) copy-start(bf16[512,512]{1,0:T(8,128)(2,1)S(1)} %pad_maximum_fusion.refs_4_) | copy-start | bytes 1572868
  24.0 5.0 %collective-permute-start.7 = (bf16[512,512]{1,0:T(8,128)(2,1)S(1)}, bf16[512,512]{1,0:T(8,128)(2,1)S(1)}, u32[]{:S(2)}, u32[]{:S(2)}) collective-permute-start(bf16[512,512]{1,0:T(8,128)(2,1)S(1)} %pad_maximum_fusion.refs_4_), channel_id=1, source_target_pairs={{0,1},{1,0},{2,3},{3,2},{4,5},{5,4},{6,7},{7,6},{8,9},{9,8},{10,11... | collective-permute-start | bytes 1572872 | tf_op jit(solution)/shard_map/ppermute | solution.py:33
  25.5 15.7 %collective-permute-start.5 = (bf16[512,512]{1,0:T(8,128)(2,1)S(1)}, bf16[512,512]{1,0:T(8,128)(2,1)S(1)}, u32[]{:S(2)}, u32[]{:S(2)}) collective-permute-start(bf16[512,512]{1,0:T(8,128)(2,1)S(1)} %pad_maximum_fusion.refs_4_), channel_id=1, source_target_pairs={{0,4},{1,5},{2,6},{3,7},{4,8},{5,9},{6,10},{7,11},{8,12},{9,13},{1... | collective-permute-start | bytes 1572872 | tf_op jit(solution)/shard_map/ppermute | solution.py:33
  27.7 13.7 %collective-permute-start.6 = (bf16[512,512]{1,0:T(8,128)(2,1)S(1)}, bf16[512,512]{1,0:T(8,128)(2,1)S(1)}, u32[]{:S(2)}, u32[]{:S(2)}) collective-permute-start(bf16[512,512]{1,0:T(8,128)(2,1)S(1)} %pad_maximum_fusion.refs_4_), channel_id=1, source_target_pairs={{0,12},{1,13},{2,14},{3,15},{4,0},{5,1},{6,2},{7,3},{8,4},{9,5},{1... | collective-permute-start | bytes 1572872 | tf_op jit(solution)/shard_map/ppermute | solution.py:33
  29.0 3.2 %copy-start.16 = (bf16[512,512]{1,0:T(8,128)(2,1)}, bf16[512,512]{1,0:T(8,128)(2,1)S(1)}, u32[]{:S(2)}) copy-start(bf16[512,512]{1,0:T(8,128)(2,1)S(1)} %collective-permute-done.7.refs_9_) | copy-start | bytes 1572868
  29.0 15.2 %collective-permute-start.8 = (bf16[128,2048]{1,0:T(8,128)(2,1)}, bf16[128,2048]{1,0:T(8,128)(2,1)S(1)}, u32[]{:S(2)}, u32[]{:S(2)}) collective-permute-start(bf16[128,2048]{1,0:T(8,128)(2,1)} %get-tuple-element.48.refs_14_), channel_id=1, source_target_pairs={{0,32},{1,33},{2,34},{3,35},{4,36},{5,37},{6,38},{7,39},{8,40},{9,... | collective-permute-start | bytes 1572872 | tf_op jit(solution)/shard_map/ppermute | solution.py:33
  30.5 13.7 %collective-permute-start.9 = (bf16[128,2048]{1,0:T(8,128)(2,1)}, bf16[128,2048]{1,0:T(8,128)(2,1)S(1)}, u32[]{:S(2)}, u32[]{:S(2)}) collective-permute-start(bf16[128,2048]{1,0:T(8,128)(2,1)} %get-tuple-element.48.refs_14_), channel_id=1, source_target_pairs={{0,96},{1,97},{2,98},{3,99},{4,100},{5,101},{6,102},{7,103},{8,104... | collective-permute-start | bytes 1572872 | tf_op jit(solution)/shard_map/ppermute | solution.py:33
  32.2 3.9 %collective-permute-start.10 = (bf16[2,4,8,128]{3,2,1,0:T(8,128)(2,1)}, bf16[2,4,8,128]{3,2,1,0:T(8,128)(2,1)S(1)}, u32[]{:S(2)}, u32[]{:S(2)}) collective-permute-start(bf16[2,4,8,128]{3,2,1,0:T(8,128)(2,1)} %get-tuple-element.52), channel_id=1, source_target_pairs={{0,16},{1,17},{2,18},{3,19},{4,20},{5,21},{6,22},{7,23},{8,24},{9,... | collective-permute-start | bytes 49160 | tf_op jit(solution)/shard_map/ppermute | solution.py:33
  36.2 13.2 %collective-permute-start.3 = (bf16[128,8,128]{2,1,0:T(8,128)(2,1)S(1)}, bf16[128,8,128]{2,1,0:T(8,128)(2,1)S(1)}, u32[]{:S(2)}, u32[]{:S(2)}) collective-permute-start(bf16[128,8,128]{2,1,0:T(8,128)(2,1)S(1)} %copy-done.18), channel_id=1, source_target_pairs={{1,2},{3,4},{5,6},{7,8},{9,10},{11,12},{13,14},{2,1},{4,3},{6,5},{... | collective-permute-start | bytes 786440 | tf_op jit(solution)/shard_map/ppermute | solution.py:352
  37.6 27.9 %copy-start.15 = (bf16[4,4,8,128]{3,2,1,0:T(8,128)(2,1)}, bf16[4,4,8,128]{3,2,1,0:T(8,128)(2,1)S(1)}, u32[]{:S(2)}) copy-start(bf16[4,4,8,128]{3,2,1,0:T(8,128)(2,1)S(1)} %pad_maximum_fusion.2.refs_0_) | copy-start | bytes 98308
  41.2 24.2 %copy-start.9 = (bf16[512,512]{1,0:T(8,128)(2,1)}, bf16[512,512]{1,0:T(8,128)(2,1)S(1)}, u32[]{:S(2)}) copy-start(bf16[512,512]{1,0:T(8,128)(2,1)S(1)} %collective-permute-done.5.refs_5_) | copy-start | bytes 1572868
  41.4 24.1 %copy-start.10 = (bf16[512,512]{1,0:T(8,128)(2,1)}, bf16[512,512]{1,0:T(8,128)(2,1)S(1)}, u32[]{:S(2)}) copy-start(bf16[512,512]{1,0:T(8,128)(2,1)S(1)} %collective-permute-done.6.refs_6_) | copy-start | bytes 1572868
  44.2 24.7 %copy-start.11 = (bf16[128,2048]{1,0:T(8,128)(2,1)}, bf16[128,2048]{1,0:T(8,128)(2,1)S(1)}, u32[]{:S(2)}) copy-start(bf16[128,2048]{1,0:T(8,128)(2,1)S(1)} %collective-permute-done.8.refs_16_) | copy-start | bytes 1572868
  44.2 24.7 %copy-start.12 = (bf16[128,2048]{1,0:T(8,128)(2,1)}, bf16[128,2048]{1,0:T(8,128)(2,1)S(1)}, u32[]{:S(2)}) copy-start(bf16[128,2048]{1,0:T(8,128)(2,1)S(1)} %collective-permute-done.9.refs_15_) | copy-start | bytes 1572868
  44.2 7.8 %collective-permute-start.11 = (bf16[4,4,8,128]{3,2,1,0:T(8,128)(2,1)S(1)}, bf16[4,4,8,128]{3,2,1,0:T(8,128)(2,1)S(1)}, u32[]{:S(2)}, u32[]{:S(2)}) collective-permute-start(bf16[4,4,8,128]{3,2,1,0:T(8,128)(2,1)S(1)} %pad_maximum_fusion.2.refs_0_), channel_id=1, source_target_pairs={{0,96},{1,97},{2,98},{3,99},{4,100},{5,101},{6,102},{7,103},{8,104... | collective-permute-start | bytes 98312 | tf_op jit(solution)/shard_map/ppermute | solution.py:33
  47.2 7.0 %collective-permute-start.12 = (bf16[4,4,8,128]{3,2,1,0:T(8,128)(2,1)S(1)}, bf16[4,4,8,128]{3,2,1,0:T(8,128)(2,1)S(1)}, u32[]{:S(2)}, u32[]{:S(2)}) collective-permute-start(bf16[4,4,8,128]{3,2,1,0:T(8,128)(2,1)S(1)} %pad_maximum_fusion.2.refs_0_), channel_id=1, source_target_pairs={{0,64},{1,65},{2,66},{3,67},{4,68},{5,69},{6,70},{7,71},{8,72},{9,... | collective-permute-start | bytes 98312 | tf_op jit(solution)/shard_map/ppermute | solution.py:33
  47.9 6.3 %collective-permute-start.13 = (bf16[4,4,8,128]{3,2,1,0:T(8,128)(2,1)S(1)}, bf16[4,4,8,128]{3,2,1,0:T(8,128)(2,1)S(1)}, u32[]{:S(2)}, u32[]{:S(2)}) collective-permute-start(bf16[4,4,8,128]{3,2,1,0:T(8,128)(2,1)S(1)} %pad_maximum_fusion.2.refs_0_), channel_id=1, source_target_pairs={{0,32},{1,33},{2,34},{3,35},{4,36},{5,37},{6,38},{7,39},{8,40},{9,... | collective-permute-start | bytes 98312 | tf_op jit(solution)/shard_map/ppermute | solution.py:33
  48.6 7.7 %collective-permute-start.14 = (bf16[256,512]{1,0:T(8,128)(2,1)S(1)}, bf16[256,512]{1,0:T(8,128)(2,1)S(1)}, u32[]{:S(2)}, u32[]{:S(2)}) collective-permute-start(bf16[256,512]{1,0:T(8,128)(2,1)S(1)} %slice.34), channel_id=1, source_target_pairs={{0,4},{1,5},{2,6},{3,7},{4,8},{5,9},{6,10},{7,11},{8,12},{9,13},{1... | collective-permute-start | bytes 786440 | tf_op jit(solution)/shard_map/ppermute | solution.py:33
  49.4 10.9 %copy-start.4 = (bf16[128,8,128]{2,1,0:T(8,128)(2,1)}, bf16[128,8,128]{2,1,0:T(8,128)(2,1)S(1)}, u32[]{:S(2)}) copy-start(bf16[128,8,128]{2,1,0:T(8,128)(2,1)S(1)} %collective-permute-done.3.next_ref) | copy-start | bytes 786436
  49.4 9.4 %collective-permute-start.15 = (bf16[256,512]{1,0:T(8,128)(2,1)S(1)}, bf16[256,512]{1,0:T(8,128)(2,1)}, u32[]{:S(2)}, u32[]{:S(2)}) collective-permute-start(bf16[256,512]{1,0:T(8,128)(2,1)S(1)} %slice.35), channel_id=1, source_target_pairs={{0,12},{1,13},{2,14},{3,15},{4,0},{5,1},{6,2},{7,3},{8,4},{9,5},{1... | collective-permute-start | bytes 786440 | tf_op jit(solution)/shard_map/ppermute | solution.py:33
  52.0 13.5 %copy-start.22 = (bf16[4,4,8,128]{3,2,1,0:T(8,128)(2,1)}, bf16[4,4,8,128]{3,2,1,0:T(8,128)(2,1)S(1)}, u32[]{:S(2)}) copy-start(bf16[4,4,8,128]{3,2,1,0:T(8,128)(2,1)S(1)} %collective-permute-done.11.refs_1_) | copy-start | bytes 98308
  52.0 7.6 %collective-permute-start.20 = (bf16[64,2048]{1,0:T(8,128)(2,1)S(1)}, bf16[64,2048]{1,0:T(8,128)(2,1)S(1)}, u32[]{:S(2)}, u32[]{:S(2)}) collective-permute-start(bf16[64,2048]{1,0:T(8,128)(2,1)S(1)} %slice.36), channel_id=1, source_target_pairs={{0,32},{1,33},{2,34},{3,35},{4,36},{5,37},{6,38},{7,39},{8,40},{9,... | collective-permute-start | bytes 786440 | tf_op jit(solution)/shard_map/ppermute | solution.py:33
  54.2 11.3 %copy-start.23 = (bf16[4,4,8,128]{3,2,1,0:T(8,128)(2,1)}, bf16[4,4,8,128]{3,2,1,0:T(8,128)(2,1)S(1)}, u32[]{:S(2)}) copy-start(bf16[4,4,8,128]{3,2,1,0:T(8,128)(2,1)S(1)} %collective-permute-done.12.refs_2_) | copy-start | bytes 98308
  54.2 14.7 %collective-permute-start.16 = (bf16[512,512]{1,0:T(8,128)(2,1)S(1)}, bf16[512,512]{1,0:T(8,128)(2,1)}, u32[]{:S(2)}, u32[]{:S(2)}) collective-permute-start(bf16[512,512]{1,0:T(8,128)(2,1)S(1)} %collective-permute-done.5.refs_5_), channel_id=1, source_target_pairs={{0,1},{1,0},{2,3},{3,2},{4,5},{5,4},{6,7},{7,6},{8,9},{9,8},{10,11... | collective-permute-start | bytes 1572872 | tf_op jit(solution)/shard_map/ppermute | solution.py:33
  54.2 11.3 %copy-start.24 = (bf16[4,4,8,128]{3,2,1,0:T(8,128)(2,1)}, bf16[4,4,8,128]{3,2,1,0:T(8,128)(2,1)S(1)}, u32[]{:S(2)}) copy-start(bf16[4,4,8,128]{3,2,1,0:T(8,128)(2,1)S(1)} %collective-permute-done.13.refs_3_) | copy-start | bytes 98308
  54.2 14.6 %collective-permute-start.17 = (bf16[512,512]{1,0:T(8,128)(2,1)S(1)}, bf16[512,512]{1,0:T(8,128)(2,1)}, u32[]{:S(2)}, u32[]{:S(2)}) collective-permute-start(bf16[512,512]{1,0:T(8,128)(2,1)S(1)} %collective-permute-done.6.refs_6_), channel_id=1, source_target_pairs={{0,1},{1,0},{2,3},{3,2},{4,5},{5,4},{6,7},{7,6},{8,9},{9,8},{10,11... | collective-permute-start | bytes 1572872 | tf_op jit(solution)/shard_map/ppermute | solution.py:33
  56.3 12.6 %copy-start.17 = (bf16[256,512]{1,0:T(8,128)(2,1)}, bf16[256,512]{1,0:T(8,128)(2,1)S(1)}, u32[]{:S(2)}) copy-start(bf16[256,512]{1,0:T(8,128)(2,1)S(1)} %collective-permute-done.14.refs_7_) | copy-start | bytes 786436
  56.3 9.3 %collective-permute-start.21 = (bf16[64,2048]{1,0:T(8,128)(2,1)S(1)}, bf16[64,2048]{1,0:T(8,128)(2,1)}, u32[]{:S(2)}, u32[]{:S(2)}) collective-permute-start(bf16[64,2048]{1,0:T(8,128)(2,1)S(1)} %slice.37), channel_id=1, source_target_pairs={{0,96},{1,97},{2,98},{3,99},{4,100},{5,101},{6,102},{7,103},{8,104... | collective-permute-start | bytes 786440 | tf_op jit(solution)/shard_map/ppermute | solution.py:33
  58.8 7.8 %collective-permute-start.18 = (bf16[256,512]{1,0:T(8,128)(2,1)S(1)}, bf16[256,512]{1,0:T(8,128)(2,1)}, u32[]{:S(2)}, u32[]{:S(2)}) collective-permute-start(bf16[256,512]{1,0:T(8,128)(2,1)S(1)} %collective-permute-done.14.refs_7_), channel_id=1, source_target_pairs={{0,1},{1,0},{2,3},{3,2},{4,5},{5,4},{6,7},{7,6},{8,9},{9,8},{10,11... | collective-permute-start | bytes 786440 | tf_op jit(solution)/shard_map/ppermute | solution.py:33
  60.3 8.6 %collective-permute-start.19 = (bf16[256,512]{1,0:T(8,128)(2,1)}, bf16[256,512]{1,0:T(8,128)(2,1)}, u32[]{:S(2)}, u32[]{:S(2)}) collective-permute-start(bf16[256,512]{1,0:T(8,128)(2,1)} %collective-permute-done.15.refs_8_), channel_id=1, source_target_pairs={{0,1},{1,0},{2,3},{3,2},{4,5},{5,4},{6,7},{7,6},{8,9},{9,8},{10,11... | collective-permute-start | bytes 786440 | tf_op jit(solution)/shard_map/ppermute | solution.py:33
  65.6 26.1 %collective-permute-start.24 = (bf16[128,2048]{1,0:T(8,128)(2,1)}, bf16[128,2048]{1,0:T(8,128)(2,1)S(1)}, u32[]{:S(2)}, u32[]{:S(2)}) collective-permute-start(bf16[128,2048]{1,0:T(8,128)(2,1)} %get-tuple-element.68.refs_14_), channel_id=1, source_target_pairs={{0,32},{1,33},{2,34},{3,35},{4,36},{5,37},{6,38},{7,39},{8,40},{9,... | collective-permute-start | bytes 1572872 | tf_op jit(solution)/shard_map/ppermute | solution.py:33
  66.6 25.2 %collective-permute-start.23 = (bf16[128,2048]{1,0:T(8,128)(2,1)}, bf16[128,2048]{1,0:T(8,128)(2,1)S(1)}, u32[]{:S(2)}, u32[]{:S(2)}) collective-permute-start(bf16[128,2048]{1,0:T(8,128)(2,1)} %get-tuple-element.68.refs_14_), channel_id=1, source_target_pairs={{0,96},{1,97},{2,98},{3,99},{4,100},{5,101},{6,102},{7,103},{8,104... | collective-permute-start | bytes 1572872 | tf_op jit(solution)/shard_map/ppermute | solution.py:33
  79.2 16.1 %collective-permute-start.22 = (bf16[128,1024]{1,0:T(8,128)(2,1)}, bf16[128,1024]{1,0:T(8,128)(2,1)S(1)}, u32[]{:S(2)}, u32[]{:S(2)}) collective-permute-start(bf16[128,1024]{1,0:T(8,128)(2,1)} %get-tuple-element.63), channel_id=1, source_target_pairs={{0,16},{1,17},{2,18},{3,19},{4,20},{5,21},{6,22},{7,23},{8,24},{9,... | collective-permute-start | bytes 786440 | tf_op jit(solution)/shard_map/ppermute | solution.py:33
  89.6 8.4 %collective-permute-start.27 = (bf16[128,1024]{1,0:T(8,128)(2,1)}, bf16[128,1024]{1,0:T(8,128)(2,1)S(1)}, u32[]{:S(2)}, u32[]{:S(2)}) collective-permute-start(bf16[128,1024]{1,0:T(8,128)(2,1)} %get-tuple-element.70), channel_id=1, source_target_pairs={{0,16},{1,17},{2,18},{3,19},{4,20},{5,21},{6,22},{7,23},{8,24},{9,... | collective-permute-start | bytes 786440 | tf_op jit(solution)/shard_map/ppermute | solution.py:33
  91.6 3.6 %copy-start.13 = (bf16[128,2048]{1,0:T(8,128)(2,1)}, bf16[128,2048]{1,0:T(8,128)(2,1)S(1)}, u32[]{:S(2)}) copy-start(bf16[128,2048]{1,0:T(8,128)(2,1)S(1)} %collective-permute-done.24.refs_16_) | copy-start | bytes 1572868
  91.7 8.9 %collective-permute-start.25 = (bf16[64,2048]{1,0:T(8,128)(2,1)S(1)}, bf16[64,2048]{1,0:T(8,128)(2,1)S(1)}, u32[]{:S(2)}, u32[]{:S(2)}) collective-permute-start(bf16[64,2048]{1,0:T(8,128)(2,1)S(1)} %slice.44), channel_id=1, source_target_pairs={{0,32},{1,33},{2,34},{3,35},{4,36},{5,37},{6,38},{7,39},{8,40},{9,... | collective-permute-start | bytes 786440 | tf_op jit(solution)/shard_map/ppermute | solution.py:33
  91.7 3.5 %copy-start.14 = (bf16[128,2048]{1,0:T(8,128)(2,1)}, bf16[128,2048]{1,0:T(8,128)(2,1)S(1)}, u32[]{:S(2)}) copy-start(bf16[128,2048]{1,0:T(8,128)(2,1)S(1)} %collective-permute-done.23.refs_15_) | copy-start | bytes 1572868
  91.8 8.8 %collective-permute-start.26 = (bf16[64,2048]{1,0:T(8,128)(2,1)S(1)}, bf16[64,2048]{1,0:T(8,128)(2,1)S(1)}, u32[]{:S(2)}, u32[]{:S(2)}) collective-permute-start(bf16[64,2048]{1,0:T(8,128)(2,1)S(1)} %slice.45), channel_id=1, source_target_pairs={{0,96},{1,97},{2,98},{3,99},{4,100},{5,101},{6,102},{7,103},{8,104... | collective-permute-start | bytes 786440 | tf_op jit(solution)/shard_map/ppermute | solution.py:33
  112.3 12.4 %collective-permute-start.29 = (bf16[128,1024]{1,0:T(8,128)(2,1)}, bf16[128,1024]{1,0:T(8,128)(2,1)S(1)}, u32[]{:S(2)}, u32[]{:S(2)}) collective-permute-start(bf16[128,1024]{1,0:T(8,128)(2,1)} %get-tuple-element.77), channel_id=1, source_target_pairs={{0,16},{1,17},{2,18},{3,19},{4,20},{5,21},{6,22},{7,23},{8,24},{9,... | collective-permute-start | bytes 786440 | tf_op jit(solution)/shard_map/ppermute | solution.py:33
  124.4 7.0 %collective-permute-start.28 = (bf16[128,1024]{1,0:T(8,128)(2,1)}, bf16[128,1024]{1,0:T(8,128)(2,1)S(1)}, u32[]{:S(2)}, u32[]{:S(2)}) collective-permute-start(bf16[128,1024]{1,0:T(8,128)(2,1)} %get-tuple-element.76), channel_id=1, source_target_pairs={{0,16},{1,17},{2,18},{3,19},{4,20},{5,21},{6,22},{7,23},{8,24},{9,... | collective-permute-start | bytes 786440 | tf_op jit(solution)/shard_map/ppermute | solution.py:33
  (7 other events, 5.0 us)

commit v5 on v4

v5 whole, which is shorter than its diff:
```python
import jax
import jax.numpy as jnp
from jax import lax
from jax.experimental import pallas as pl
from jax.experimental.pallas import tpu as pltpu
from jax.sharding import PartitionSpec as P

SLICES = 16
BLOCKS = ((0, 1), (2, 3))
BOTH = ("vel", "space")
FLAT = [
    (y, z, x, h, c)
    for y in range(4)
    for z in range(2)
    for x in range(4)
    for h in range(2)
    for c in range(2)
]
BF16, F32 = jnp.bfloat16, jnp.float32
ANY = pl.BlockSpec(memory_space=pl.ANY)
VMEM = pl.BlockSpec(memory_space=pltpu.VMEM)
SMEM = pl.BlockSpec(memory_space=pltpu.SMEM)


def rank(y, z, x, h, c):
    return ((y % 4) * 2 + z) * 16 + (x % 4) * 4 + h * 2 + c


def shift(value, dy=0, dz=0, dx=0, dh=0, dc=0):
    pairs = [
        (rank(y, z, x, h, c), rank(y + dy, z ^ dz, x + dx, h ^ dh, c ^ dc)) for y, z, x, h, c in FLAT
    ]
    return lax.ppermute(value, BOTH, pairs)


def after(value, *earlier):
    return lax.optimization_barrier((value, earlier))[0]


def shape(dims, dtype):
    return jax.ShapeDtypeStruct(dims, dtype)


def pack(density, limiter):
    rows = density.shape[0]

    def kernel(d_ref, l_ref, away_ref, inner_ref):
        core = lax.axis_index("space") & 1

        def fill(o_ref, start):
            o_ref[:rows] = d_ref[:, start : start + 2].astype(BF16)
            o_ref[rows] = l_ref[start : start + 2].astype(F32).astype(BF16)

        @pl.when(core == 1)
        def _():
            fill(away_ref, 2)
            fill(inner_ref, 0)

        @pl.when(core == 0)
        def _():
            fill(away_ref, 0)
            fill(inner_ref, 2)

    out = shape((rows + 1, 2, *density.shape[2:]), BF16)
    return pl.pallas_call(
        kernel, out_shape=(out, out), in_specs=[VMEM, VMEM], out_specs=(VMEM, VMEM), name="pack"
    )(density, limiter)


def split_slice(kernel_slice):
    def kernel(k_ref, o_ref):
        z = lax.axis_index("vel") & 1
        for y in range(4):
            cols = pl.ds(y * 128, 128)
            o_ref[:128, cols] = k_ref[y, 1 - z].astype(F32).T.astype(BF16)
            o_ref[128:, cols] = k_ref[y, z].astype(F32).T.astype(BF16)

    return pl.pallas_call(
        kernel, out_shape=shape((256, 512), BF16), in_specs=[VMEM], out_specs=VMEM, name="split_slice"
    )(kernel_slice.reshape(4, 2, 128, 128))


def update(cells, codes, ahead, number, layers):
    half = 0.5 * (2 * ahead - 1).astype(F32)
    forward = jnp.full((8, 128), ahead, jnp.int32) == 1
    rebuilt = {}
    for i in sorted({i + d for i in layers for d in (-1, 0, 1)}):
        left, right = cells[i] - cells[i - 1], cells[i + 1] - cells[i]
        small = jnp.where(left > 0, jnp.minimum(left, right), jnp.maximum(left, right))
        small = jnp.where(left * right > 0, small, 0.0)
        slope = jnp.where(
            codes[i] == 1, small, jnp.where(codes[i] == 2, 0.5 * (left + right), 0.0)
        )
        rebuilt[i] = cells[i] + half * slope
    return [
        cells[i] - number * (rebuilt[i] - jnp.where(forward, rebuilt[i - 1], rebuilt[i + 1]))
        for i in layers
    ]


STEP = 32


def transport(density, limiter, heading, courant, away, inner):
    rows = density.shape[0]

    def kernel(
        h_ref, c_ref, d_ref, l_ref, away_ref, away_code, inner_ref, inner_code, t_ref, w_ref, *m_refs
    ):
        core = lax.axis_index("space") & 1
        start = pl.program_id(0) * STEP

        def beside(a_ref, b_ref, j):
            a = [a_ref[j, i].astype(F32) for i in range(2)]
            b = [b_ref[j, i].astype(F32) for i in range(2)]
            below = [jnp.where(core == 0, a[i], b[i]) for i in range(2)]
            above = [jnp.where(core == 0, b[i], a[i]) for i in range(2)]
            return {-2: below[0], -1: below[1], 4: above[0], 5: above[1]}

        codes = beside(away_code, inner_code, 0)
        codes.update({i: l_ref[i].astype(F32) for i in range(4)})

        def one(j, _):
            cells = beside(away_ref, inner_ref, j)
            cells.update({i: d_ref[j, i] for i in range(4)})
            values = update(cells, codes, h_ref[start + j], c_ref[start + j], range(4))
            for i, value in enumerate(values):
                t_ref[j, i] = value
            return 0

        lax.fori_loop(0, STEP, one, 0, unroll=4)
        for m_ref, layers in zip(m_refs, BLOCKS, strict=True):
            for place, i in enumerate(layers):
                turned = jnp.swapaxes(t_ref[:, i], 0, 1)
                for y in range(8):
                    m_ref[:, pl.ds(place * 1024 + y * 128, 128)] = turned[y].astype(BF16)

        @pl.when(pl.program_id(0) % 2 == 0)
        def _():
            w_ref[0] = t_ref[0].astype(BF16)

    halo = pl.BlockSpec((STEP, 2, 8, 128), lambda i: (i, 0, 0, 0))
    code = pl.BlockSpec((1, 2, 8, 128), lambda i: (rows, 0, 0, 0))
    full = pl.BlockSpec((STEP, 4, 8, 128), lambda i: (i, 0, 0, 0))
    outs = pl.pallas_call(
        kernel,
        grid=(rows // STEP,),
        out_shape=(shape(density.shape, F32), shape((2, 4, 8, 128), BF16))
        + tuple(shape((rows, 1024 * len(layers)), BF16) for layers in BLOCKS),
        in_specs=[
            SMEM,
            SMEM,
            full,
            pl.BlockSpec((4, 8, 128), lambda i: (0, 0, 0)),
            halo,
            code,
            halo,
            code,
        ],
        out_specs=(full, pl.BlockSpec((1, 4, 8, 128), lambda i: (i // 2, 0, 0, 0)))
        + tuple(pl.BlockSpec((STEP, 1024 * len(layers)), lambda i: (i, 0)) for layers in BLOCKS),
        cost_estimate=pl.CostEstimate(flops=4 << 20, bytes_accessed=6 << 20, transcendentals=0),
        name="transport",
    )(heading, courant, density, limiter, away, away, inner, inner)
    return outs[0], outs[1], outs[2:]


ORDER = [(0, 0), (0, 1), (3, 0), (3, 1), (1, 0), (1, 1), (2, 0), (2, 1)]


def weight_rows():
    vel, space = lax.axis_index("vel"), lax.axis_index("space")
    y, z = vel >> 1, vel & 1
    x, h, c = space >> 2, (space >> 1) & 1, space & 1
    rows = []
    for dc in range(2):
        for dx, dh in ORDER:
            v = (((x + dx) & 3) << 1) + (h ^ dh)
            rows.append(((((v >> 1) - y) & 3) << 2) + (((v & 1) ^ z) << 1) + (c ^ dc))
    return y, rows


def collide(layer, place, pieces, blocks, weights):
    cells = 1024
    tile = 512
    columns = pl.ds(place * cells, cells)
    def kernel(*refs):
        w_parts = refs[:4]
        slabs = refs[4:12]
        parts = refs[12:16]
        mine_ref, other_ref, k_ref, m_ref, w_ref, sem_k, sem_m = refs[16:]
        y, places = weight_rows()
        loads = []
        for d in range(4):
            at = pl.multiple_of(((y + d) & 3) * 128, 128)
            loads.append(
                pltpu.make_async_copy(
                    parts[d].at[:, columns], m_ref.at[pl.ds(at, 128)], sem_m.at[d]
                )
            )
        for i in range(8):
            loads.append(
                pltpu.make_async_copy(slabs[i], k_ref.at[pl.ds(512 * i, 512)], sem_k.at[i])
            )
        for load in loads:
            load.start()
        for d in range(4):
            w_ref[4 * d : 4 * d + 4] = w_parts[d][:, layer].astype(F32)
        for load in loads[:4]:
            load.wait()
        for t in range(cells // tile):
            cols = pl.ds(t * tile, tile)
            moved = m_ref[:, cols]
            total = jnp.zeros((256, tile), F32)
            for s in range(SLICES):
                if t == 0 and s % 2 == 0:
                    loads[4 + s // 2].wait()
                product = jnp.dot(
                    k_ref[s * 256 : (s + 1) * 256], moved, preferred_element_type=F32
                )
                lines = [w_ref[places[s], pl.ds(t * 4 + i, 1), :] for i in range(tile // 128)]
                total = total + jnp.concatenate(lines, 1) * product
            mine_ref[:, cols] = total[:128]
            other_ref[:, cols] = total[128:].astype(BF16)

    return pl.pallas_call(
        kernel,
        out_shape=(shape((128, cells), F32), shape((128, cells), BF16)),
        in_specs=[VMEM] * 4 + [ANY] * 12,
        out_specs=(VMEM, VMEM),
        scratch_shapes=[
            pltpu.VMEM((SLICES * 256, 512), BF16),
            pltpu.VMEM((512, cells), BF16),
            pltpu.VMEM((SLICES, 8, 128), F32),
            pltpu.SemaphoreType.DMA((8,)),
            pltpu.SemaphoreType.DMA((4,)),
        ],
        compiler_params=pltpu.CompilerParams(vmem_limit_bytes=28 << 20),
        cost_estimate=pl.CostEstimate(
            flops=2 * SLICES * 256 * 512 * cells, bytes_accessed=6 << 20, transcendentals=0
        ),
        name="collide",
    )(*weights, *pieces, *blocks)


def combine(layer, mine, got, result):
    step = 64

    def kernel(a_ref, b_ref, *refs):
        o_ref = refs[-1]
        total = a_ref[...] + b_ref[...].astype(F32)
        lines = jnp.stack([total[:, y * 128 : (y + 1) * 128] for y in range(8)], 0)
        o_ref[:, 0] = jnp.swapaxes(lines, 0, 1)

    block = pl.BlockSpec((step, 1024), lambda i: (i, 0))
    given = [] if result is None else [result]
    return pl.pallas_call(
        kernel,
        grid=(128 // step,),
        out_shape=shape((128, 4, 8, 128), F32),
        in_specs=[block, block] + [ANY] * len(given),
        out_specs=pl.BlockSpec((step, 1, 8, 128), lambda i: (i, layer, 0, 0)),
        input_output_aliases={2: 0} if given else {},
        cost_estimate=pl.CostEstimate(flops=1 << 17, bytes_accessed=5 << 18, transcendentals=0),
        name="combine",
    )(mine, got, *given)


def local(density, limiter, heading, courant, kernel_slices):
    size = lax.axis_size("space")
    beside = [(i, i + 1) for i in range(1, size - 1, 2)]
    beside = beside + [(j, i) for i, j in beside]

    own_slice = split_slice(kernel_slices[0])
    partner = shift(own_slice, dz=1)
    payload, inner = pack(after(density, own_slice), limiter)
    away = lax.ppermute(payload, "space", beside)
    inner = shift(inner, dc=1)

    crossing = jnp.concatenate([partner[128:], own_slice[:128]], 0)
    cross = shift(after(crossing, payload), dz=1, dh=1)
    base = jnp.concatenate([own_slice[128:], partner[:128], after(cross, inner)], 0)
    pieces = [base, shift(base, dx=1), shift(base, dx=-1), shift(base, dx=2)]
    pieces = pieces + [shift(p, dc=1) for p in pieces]

    away = after(away, pieces[4])
    transported, own, blocks = transport(density, limiter, heading, courant, away, inner)
    rows = jnp.concatenate([own, shift(own, dz=1)], 0)
    weights = [rows, shift(rows, dy=-1), shift(rows, dy=2), shift(rows, dy=1)]

    results, got, column = [None], [], ()
    for layers, block in zip(BLOCKS, blocks, strict=True):
        block = after(block, *column[1:])
        column = [block, shift(block, dy=-1), shift(block, dy=2), shift(block, dy=1)]
        for place, layer in enumerate(layers):
            mine, other = collide(layer, place, pieces, column, weights)
            weights = after(weights, mine, *got[-1:], *results[1:][-1:])
            got.append(shift(other, dz=1))
            results.append(combine(layer, mine, got[-1], results[-1]))
    return transported, results[-1]


def solution(mesh):
    return jax.shard_map(
        local,
        mesh=mesh,
        in_specs=(
            P("vel", "space", None, None),
            P("space", None, None),
            P("vel"),
            P("vel"),
            P("space", None, "vel"),
        ),
        out_specs=(P("vel", "space", None, None), P("vel", "space", None, None)),
        check_vma=False,
    )
```

time: 135 us -> 135 us (level)
  waiting for transfers between devices: 20 us -> 44.6 us
  Pallas kernels: 62.8 us -> 44.5 us
  starting transfers between devices: 42.7 us -> 35.4 us
  local copies, waits for them, and re-layouts: 6.69 us -> 8.47 us
    ppermute x28 -> x24, waiting for transfers between devices: 20 us -> 44.6 us  [shift(): return lax.ppermute(value, BOTH, pairs)]
    pallas_call x4, Pallas kernels: 41.1 us -> 26.7 us  [collide(): pl.pallas_call(kernel, out_shape=(shape((128, cells), F32), shape((128, c...]
    ppermute x28 -> x24, starting transfers between devices: 41.4 us -> 33.9 us  [shift(): return lax.ppermute(value, BOTH, pairs)]
    pallas_call x2 -> x1, Pallas kernels: 7.2 us -> 2.7 us  [pack(): pl.pallas_call(kernel, out_shape=(out, out), in_specs=[VMEM, VMEM], out_s...]
    unnamed x50 -> x33, local copies, waits for them, and re-layouts: 6.54 us -> 8.43 us
  transfers between devices with their start and end apart: 30 -> 25, of which waited for: 9 -> 10; matrix products, arithmetic and copies ran while one was open for 1% -> 1% of each run, Pallas kernels for 36% -> 25%
where the time goes in v5:
time: 135 us; the launch traced here: 134 us
  waiting for transfers between devices  44.6 us (33%)
  Pallas kernels  44.5 us (33%)
  starting transfers between devices  35.4 us (26%)
  local copies, waits for them, and re-layouts  8.47 us (6%)
    ppermute x24, waiting for transfers between devices, shift(): return lax.ppermute(value, BOTH, pairs)  44.6 us
    ppermute x24, starting transfers between devices, shift(): return lax.ppermute(value, BOTH, pairs)  33.9 us
    pallas_call x4, Pallas kernels, collide(): pl.pallas_call(kernel, out_shape=(shape((128, cells), F32), shape((128, c...  26.7 us
    unnamed x33, local copies, waits for them, and re-layouts  8.43 us
    pallas_call x4, Pallas kernels, combine(): pl.pallas_call(kernel, grid=(128 // step,), out_shape=shape((128, 4, 8, 1...  7.58 us
    pallas_call x1, Pallas kernels, transport(): pl.pallas_call(kernel, grid=(rows // STEP,), out_shape=(shape(density.sha...  5.68 us
  transfers between devices with their start and end apart: 25, of which 10 were waited for; matrix products, arithmetic and copies ran while one was open for 1% of the time, Pallas kernels for 25%

profile of v5, /device:TPU:0, one launch (start us, length us, event | category | flops | bytes accessed | tf_op | source)
XLA Modules:
  0.0 133.8 jit_solution(8863983984860231797)
XLA Ops:
  0.6 1.8 %split_slice.1 = bf16[256,512]{1,0:T(8,128)(2,1)} custom-call(bf16[4,2,128,128]{3,2,1,0:T(8,128)(2,1)} %bitcast.1), custom_call_target="tpu_custom_call" | custom-call | tf_op jit(solution)/shard_map/split_slice/pallas_call | solution.py:78
  2.4 2.0 %collective-permute-start.1 = (bf16[256,512]{1,0:T(8,128)(2,1)}, bf16[256,512]{1,0:T(8,128)(2,1)S(1)}, u32[]{:S(2)}, u32[]{:S(2)}) collective-permute-start(bf16[256,512]{1,0:T(8,128)(2,1)} %split_slice.1), channel_id=1, source_target_pairs={{0,16},{1,17},{2,18},{3,19},{4,20},{5,21},{6,22},{7,23},{8,24},{9,... | collective-permute-start | bytes 786440 | tf_op jit(solution)/shard_map/ppermute | solution.py:33
  4.4 2.7 %pack.1 = (bf16[129,2,8,128]{3,2,1,0:T(8,128)(2,1)}, bf16[129,2,8,128]{3,2,1,0:T(8,128)(2,1)}) custom-call(f32[128,4,8,128]{3,2,1,0:T(8,128)} %d_ref.2, s32[4,8,128]{2,1,0:T(8,128)} %l_ref.3), custom_call_target="tpu_custom_call" | custom-call | tf_op jit(solution)/shard_map/pack/pallas_call | solution.py:65
  7.2 3.9 %collective-permute-done.1 = bf16[256,512]{1,0:T(8,128)(2,1)S(1)} collective-permute-done((bf16[256,512]{1,0:T(8,128)(2,1)}, bf16[256,512]{1,0:T(8,128)(2,1)S(1)}, u32[]{:S(2)}, u32[]{:S(2)}) %collective-permute-start.1) | collective-permute-done | bytes 262176 | tf_op jit(solution)/shard_map/ppermute | solution.py:33
  11.1 3.9 %collective-permute-start.2 = (bf16[256,512]{1,0:T(8,128)(2,1)S(1)}, bf16[256,512]{1,0:T(8,128)(2,1)S(1)}, u32[]{:S(2)}, u32[]{:S(2)}) collective-permute-start(bf16[256,512]{1,0:T(8,128)(2,1)S(1)} %pad_maximum_fusion.1), channel_id=1, source_target_pairs={{0,18},{1,19},{2,16},{3,17},{4,22},{5,23},{6,20},{7,21},{8,26},{9,... | collective-permute-start | bytes 786440 | tf_op jit(solution)/shard_map/ppermute | solution.py:33
  14.9 1.5 %collective-permute-start = (bf16[129,2,8,128]{3,2,1,0:T(8,128)(2,1)}, bf16[129,2,8,128]{3,2,1,0:T(8,128)(2,1)}, u32[]{:S(2)}, u32[]{:S(2)}) collective-permute-start(bf16[129,2,8,128]{3,2,1,0:T(8,128)(2,1)} %get-tuple-element.34), channel_id=1, source_target_pairs={{1,2},{3,4},{5,6},{7,8},{9,10},{11,12},{13,14},{2,1},{4,3},{6,5},{... | collective-permute-start | bytes 1585160 | tf_op jit(solution)/shard_map/ppermute | solution.py:277
  16.4 14.6 %collective-permute-done.2 = bf16[256,512]{1,0:T(8,128)(2,1)S(1)} collective-permute-done((bf16[256,512]{1,0:T(8,128)(2,1)S(1)}, bf16[256,512]{1,0:T(8,128)(2,1)S(1)}, u32[]{:S(2)}, u32[]{:S(2)}) %collective-permute-start.2) | collective-permute-done | bytes 262176 | tf_op jit(solution)/shard_map/ppermute | solution.py:33
  31.1 1.6 %collective-permute-start.9 = (bf16[512,512]{1,0:T(8,128)(2,1)S(1)}, bf16[512,512]{1,0:T(8,128)(2,1)S(1)}, u32[]{:S(2)}, u32[]{:S(2)}) collective-permute-start(bf16[512,512]{1,0:T(8,128)(2,1)S(1)} %pad_maximum_fusion.refs_4_), channel_id=1, source_target_pairs={{0,4},{1,5},{2,6},{3,7},{4,8},{5,9},{6,10},{7,11},{8,12},{9,13},{1... | collective-permute-start | bytes 1572872 | tf_op jit(solution)/shard_map/ppermute | solution.py:33
  32.6 1.7 %collective-permute-start.10 = (bf16[512,512]{1,0:T(8,128)(2,1)S(1)}, bf16[512,512]{1,0:T(8,128)(2,1)S(1)}, u32[]{:S(2)}, u32[]{:S(2)}) collective-permute-start(bf16[512,512]{1,0:T(8,128)(2,1)S(1)} %pad_maximum_fusion.refs_4_), channel_id=1, source_target_pairs={{0,12},{1,13},{2,14},{3,15},{4,0},{5,1},{6,2},{7,3},{8,4},{9,5},{1... | collective-permute-start | bytes 1572872 | tf_op jit(solution)/shard_map/ppermute | solution.py:33
  34.4 1.8 %collective-permute-start.11 = (bf16[512,512]{1,0:T(8,128)(2,1)S(1)}, bf16[512,512]{1,0:T(8,128)(2,1)S(1)}, u32[]{:S(2)}, u32[]{:S(2)}) collective-permute-start(bf16[512,512]{1,0:T(8,128)(2,1)S(1)} %pad_maximum_fusion.refs_4_), channel_id=1, source_target_pairs={{0,8},{1,9},{2,10},{3,11},{4,12},{5,13},{6,14},{7,15},{8,0},{9,1},... | collective-permute-start | bytes 1572872 | tf_op jit(solution)/shard_map/ppermute | solution.py:33
  36.2 5.7 %transport.1 = (f32[128,4,8,128]{3,2,1,0:T(8,128)}, bf16[2,4,8,128]{3,2,1,0:T(8,128)(2,1)}, bf16[128,2048]{1,0:T(8,128)(2,1)}, bf16[128,2048]{1,0:T(8,128)(2,1)}) custom-call(s32[128]{0:T(128)} %h_ref.1, f32[128]{0:T(128)} %c_ref.1, f32[128,4,8,128]{3,2,1,0:T(8,128)} %d_ref.2, s32[4,8,128]{2,1,0:T(8,128)} %l_ref.3, ...), custom_call_target="tpu_custom_call" | custom-call | flops 4194304 | bytes 6291456 | tf_op jit(solution)/shard_map/transport/pallas_call | solution.py:145
  41.9 3.1 %collective-permute-start.15 = (bf16[128,2048]{1,0:T(8,128)(2,1)}, bf16[128,2048]{1,0:T(8,128)(2,1)S(1)}, u32[]{:S(2)}, u32[]{:S(2)}) collective-permute-start(bf16[128,2048]{1,0:T(8,128)(2,1)} %get-tuple-element.41.refs_12_), channel_id=1, source_target_pairs={{0,96},{1,97},{2,98},{3,99},{4,100},{5,101},{6,102},{7,103},{8,104... | collective-permute-start | bytes 1572872 | tf_op jit(solution)/shard_map/ppermute | solution.py:33
  45.0 0.8 constant_dynamic-update-slice_fusion.1
  45.7 1.1 collective-permute-done.9.refs_5_
  46.8 3.2 %collective-permute-start.16 = (bf16[128,2048]{1,0:T(8,128)(2,1)}, bf16[128,2048]{1,0:T(8,128)(2,1)S(1)}, u32[]{:S(2)}, u32[]{:S(2)}) collective-permute-start(bf16[128,2048]{1,0:T(8,128)(2,1)} %get-tuple-element.41.refs_12_), channel_id=1, source_target_pairs={{0,64},{1,65},{2,66},{3,67},{4,68},{5,69},{6,70},{7,71},{8,72},{9,... | collective-permute-start | bytes 1572872 | tf_op jit(solution)/shard_map/ppermute | solution.py:33
  50.0 0.7 collective-permute-start.17
  50.7 6.4 %collective-permute-done.10.refs_6_ = bf16[512,512]{1,0:T(8,128)(2,1)S(1)} collective-permute-done((bf16[512,512]{1,0:T(8,128)(2,1)S(1)}, bf16[512,512]{1,0:T(8,128)(2,1)S(1)}, u32[]{:S(2)}, u32[]{:S(2)}) %collective-permute-start.10) | collective-permute-done | bytes 524320 | tf_op jit(solution)/shard_map/ppermute | solution.py:33
  57.2 3.0 %collective-permute-start.6 = (bf16[4,4,8,128]{3,2,1,0:T(8,128)(2,1)S(1)}, bf16[4,4,8,128]{3,2,1,0:T(8,128)(2,1)S(1)}, u32[]{:S(2)}, u32[]{:S(2)}) collective-permute-start(bf16[4,4,8,128]{3,2,1,0:T(8,128)(2,1)S(1)} %constant_dynamic-update-slice_fusion.refs_0_), channel_id=1, source_target_pairs={{0,96},{1,97},{2,98},{3,99},{4,100},{5,101},{6,102},{7,103},{8,104... | collective-permute-start | bytes 98312 | tf_op jit(solution)/shard_map/ppermute | solution.py:33
  60.2 7.9 %collective-permute-done.6.refs_1_ = bf16[4,4,8,128]{3,2,1,0:T(8,128)(2,1)S(1)} collective-permute-done((bf16[4,4,8,128]{3,2,1,0:T(8,128)(2,1)S(1)}, bf16[4,4,8,128]{3,2,1,0:T(8,128)(2,1)S(1)}, u32[]{:S(2)}, u32[]{:S(2)}) %collective-permute-start.6) | collective-permute-done | bytes 32800 | tf_op jit(solution)/shard_map/ppermute | solution.py:33
  68.1 0.5 collective-permute-start.14
  68.6 2.7 %collective-permute-start.7 = (bf16[4,4,8,128]{3,2,1,0:T(8,128)(2,1)S(1)}, bf16[4,4,8,128]{3,2,1,0:T(8,128)(2,1)S(1)}, u32[]{:S(2)}, u32[]{:S(2)}) collective-permute-start(bf16[4,4,8,128]{3,2,1,0:T(8,128)(2,1)S(1)} %constant_dynamic-update-slice_fusion.refs_0_), channel_id=1, source_target_pairs={{0,64},{1,65},{2,66},{3,67},{4,68},{5,69},{6,70},{7,71},{8,72},{9,... | collective-permute-start | bytes 98312 | tf_op jit(solution)/shard_map/ppermute | solution.py:33
  71.3 2.0 %collective-permute-done.17.refs_15_ = bf16[128,2048]{1,0:T(8,128)(2,1)S(1)} collective-permute-done((bf16[128,2048]{1,0:T(8,128)(2,1)}, bf16[128,2048]{1,0:T(8,128)(2,1)S(1)}, u32[]{:S(2)}, u32[]{:S(2)}) %collective-permute-start.17) | collective-permute-done | bytes 524320 | tf_op jit(solution)/shard_map/ppermute | solution.py:33
  73.3 1.9 %collective-permute-start.8 = (bf16[4,4,8,128]{3,2,1,0:T(8,128)(2,1)S(1)}, bf16[4,4,8,128]{3,2,1,0:T(8,128)(2,1)S(1)}, u32[]{:S(2)}, u32[]{:S(2)}) collective-permute-start(bf16[4,4,8,128]{3,2,1,0:T(8,128)(2,1)S(1)} %constant_dynamic-update-slice_fusion.refs_0_), channel_id=1, source_target_pairs={{0,32},{1,33},{2,34},{3,35},{4,36},{5,37},{6,38},{7,39},{8,40},{9,... | collective-permute-start | bytes 98312 | tf_op jit(solution)/shard_map/ppermute | solution.py:33
  75.2 2.5 %collective-permute-start.19 = (bf16[128,2048]{1,0:T(8,128)(2,1)}, bf16[128,2048]{1,0:T(8,128)(2,1)}, u32[]{:S(2)}, u32[]{:S(2)}) collective-permute-start(bf16[128,2048]{1,0:T(8,128)(2,1)} %get-tuple-element.54.refs_12_), channel_id=1, source_target_pairs={{0,96},{1,97},{2,98},{3,99},{4,100},{5,101},{6,102},{7,103},{8,104... | collective-permute-start | bytes 1572872 | tf_op jit(solution)/shard_map/ppermute | solution.py:33
  77.7 0.7 collective-permute-done.8.refs_3_
  78.4 1.0 collective-permute-start.20
  79.5 1.4 %copy-done.7 = bf16[128,2048]{1,0:T(8,128)(2,1)S(1)} copy-done((bf16[128,2048]{1,0:T(8,128)(2,1)S(1)}, bf16[128,2048]{1,0:T(8,128)(2,1)}, u32[]{:S(2)}) %copy-start.7) | copy-done | bytes 524312
  80.9 6.3 %collide.4 = (f32[128,1024]{1,0:T(8,128)S(1)}, bf16[128,1024]{1,0:T(8,128)(2,1)S(1)}) custom-call(bf16[4,4,8,128]{3,2,1,0:T(8,128)(2,1)S(1)} %constant_dynamic-update-slice_fusion.refs_0_, bf16[4,4,8,128]{3,2,1,0:T(8,128)(2,1)S(1)} %collective-permute-done.6.refs_1_, bf16[4,4,8,128]{3,2,1,0:T(8,128)(2,1)S(1)} %collective-permute-done.7.refs_2_, ...), custom_call_target="tpu_custom_call" | custom-call | flops 4294967296 | bytes 6291456 | tf_op jit(solution)/shard_map/collide/pallas_call | solution.py:226
  87.5 6.3 %collide.5 = (f32[128,1024]{1,0:T(8,128)S(1)}, bf16[128,1024]{1,0:T(8,128)(2,1)S(1)}) custom-call(bf16[4,4,8,128]{3,2,1,0:T(8,128)(2,1)S(1)} %constant_dynamic-update-slice_fusion.refs_0_, bf16[4,4,8,128]{3,2,1,0:T(8,128)(2,1)S(1)} %collective-permute-done.6.refs_1_, bf16[4,4,8,128]{3,2,1,0:T(8,128)(2,1)S(1)} %collective-permute-done.7.refs_2_, ...), custom_call_target="tpu_custom_call" | custom-call | flops 4294967296 | bytes 6291456 | tf_op jit(solution)/shard_map/collide/pallas_call | solution.py:226
  93.9 0.8 copy-done.2
  94.7 2.0 %collective-permute-start.22 = (bf16[128,1024]{1,0:T(8,128)(2,1)S(1)}, bf16[128,1024]{1,0:T(8,128)(2,1)}, u32[]{:S(2)}, u32[]{:S(2)}) collective-permute-start(bf16[128,1024]{1,0:T(8,128)(2,1)S(1)} %get-tuple-element.56), channel_id=1, source_target_pairs={{0,16},{1,17},{2,18},{3,19},{4,20},{5,21},{6,22},{7,23},{8,24},{9,... | collective-permute-start | bytes 786440 | tf_op jit(solution)/shard_map/ppermute | solution.py:33
  96.7 1.9 %combine.4.refs_0_ = f32[128,4,8,128]{3,2,1,0:T(8,128)} custom-call(f32[128,1024]{1,0:T(8,128)} %copy-done.3, bf16[128,1024]{1,0:T(8,128)(2,1)} %collective-permute-done.18.b_ref), custom_call_target="tpu_custom_call" | custom-call | flops 131072 | bytes 1310720 | tf_op jit(solution)/shard_map/combine/pallas_call | solution.py:257
  98.5 2.7 %collective-permute-done.22.b_ref = bf16[128,1024]{1,0:T(8,128)(2,1)} collective-permute-done((bf16[128,1024]{1,0:T(8,128)(2,1)S(1)}, bf16[128,1024]{1,0:T(8,128)(2,1)}, u32[]{:S(2)}, u32[]{:S(2)}) %collective-permute-start.22) | collective-permute-done | bytes 262176 | tf_op jit(solution)/shard_map/ppermute | solution.py:33
  101.2 1.9 %combine.5.refs_0_ = f32[128,4,8,128]{3,2,1,0:T(8,128)} custom-call(f32[128,1024]{1,0:T(8,128)} %copy-done.2, bf16[128,1024]{1,0:T(8,128)(2,1)} %collective-permute-done.22.b_ref, f32[128,4,8,128]{3,2,1,0:T(8,128)} %combine.4.refs_0_), custom_call_target="tpu_custom_call", output_to_operand_aliasing={{}: (2, {})} | custom-call | flops 131072 | bytes 1310720 | tf_op jit(solution)/shard_map/combine/pallas_call | solution.py:257
  103.1 0.7 collective-permute-done.21.refs_15_
  103.9 1.0 copy-done.6
  104.9 1.0 copy-done.10
  106.0 1.0 copy-done.12
  107.0 7.0 %collide.6 = (f32[128,1024]{1,0:T(8,128)S(1)}, bf16[128,1024]{1,0:T(8,128)(2,1)S(1)}) custom-call(bf16[4,4,8,128]{3,2,1,0:T(8,128)(2,1)S(1)} %constant_dynamic-update-slice_fusion.refs_0_, bf16[4,4,8,128]{3,2,1,0:T(8,128)(2,1)S(1)} %collective-permute-done.6.refs_1_, bf16[4,4,8,128]{3,2,1,0:T(8,128)(2,1)S(1)} %collective-permute-done.7.refs_2_, ...), custom_call_target="tpu_custom_call" | custom-call | flops 4294967296 | bytes 6291456 | tf_op jit(solution)/shard_map/collide/pallas_call | solution.py:226
  114.1 0.8 copy-done
  114.9 1.2 collective-permute-start.24
  116.0 7.0 %collide.7 = (f32[128,1024]{1,0:T(8,128)S(1)}, bf16[128,1024]{1,0:T(8,128)(2,1)S(1)}) custom-call(bf16[4,4,8,128]{3,2,1,0:T(8,128)(2,1)S(1)} %constant_dynamic-update-slice_fusion.refs_0_, bf16[4,4,8,128]{3,2,1,0:T(8,128)(2,1)S(1)} %collective-permute-done.6.refs_1_, bf16[4,4,8,128]{3,2,1,0:T(8,128)(2,1)S(1)} %collective-permute-done.7.refs_2_, ...), custom_call_target="tpu_custom_call" | custom-call | flops 4294967296 | bytes 6291456 | tf_op jit(solution)/shard_map/collide/pallas_call | solution.py:226
  123.1 0.8 copy-done.1
  123.9 0.8 collective-permute-start.23
  124.7 1.9 %combine.6.refs_0_ = f32[128,4,8,128]{3,2,1,0:T(8,128)} custom-call(f32[128,1024]{1,0:T(8,128)} %copy-done, bf16[128,1024]{1,0:T(8,128)(2,1)} %collective-permute-done.24.b_ref, f32[128,4,8,128]{3,2,1,0:T(8,128)} %combine.5.refs_0_), custom_call_target="tpu_custom_call", output_to_operand_aliasing={{}: (2, {})} | custom-call | flops 131072 | bytes 1310720 | tf_op jit(solution)/shard_map/combine/pallas_call | solution.py:257
  126.6 4.5 %collective-permute-done.23.b_ref = bf16[128,1024]{1,0:T(8,128)(2,1)S(1)} collective-permute-done((bf16[128,1024]{1,0:T(8,128)(2,1)S(1)}, bf16[128,1024]{1,0:T(8,128)(2,1)S(1)}, u32[]{:S(2)}, u32[]{:S(2)}) %collective-permute-start.23) | collective-permute-done | bytes 262176 | tf_op jit(solution)/shard_map/ppermute | solution.py:33
  131.2 0.7 copy-done.15
  131.9 1.9 %combine.7 = f32[128,4,8,128]{3,2,1,0:T(8,128)} custom-call(f32[128,1024]{1,0:T(8,128)} %copy-done.1, bf16[128,1024]{1,0:T(8,128)(2,1)} %copy-done.15, f32[128,4,8,128]{3,2,1,0:T(8,128)} %combine.6.refs_0_), custom_call_target="tpu_custom_call", output_to_operand_aliasing={{}: (2, {})} | custom-call | flops 131072 | bytes 1310720 | tf_op jit(solution)/shard_map/combine/pallas_call | solution.py:257
  (51 shorter events, 0.6 us)
Async XLA Ops:
  2.4 4.7 %copy-start.14 = (bf16[256,512]{1,0:T(8,128)(2,1)S(1)}, bf16[256,512]{1,0:T(8,128)(2,1)}, u32[]{:S(2)}) copy-start(bf16[256,512]{1,0:T(8,128)(2,1)} %split_slice.1) | copy-start | bytes 786436
  2.4 8.6 %collective-permute-start.1 = (bf16[256,512]{1,0:T(8,128)(2,1)}, bf16[256,512]{1,0:T(8,128)(2,1)S(1)}, u32[]{:S(2)}, u32[]{:S(2)}) collective-permute-start(bf16[256,512]{1,0:T(8,128)(2,1)} %split_slice.1), channel_id=1, source_target_pairs={{0,16},{1,17},{2,18},{3,19},{4,20},{5,21},{6,22},{7,23},{8,24},{9,... | collective-permute-start | bytes 786440 | tf_op jit(solution)/shard_map/ppermute | solution.py:33
  7.1 23.8 %collective-permute-start.3 = (bf16[129,2,8,128]{3,2,1,0:T(8,128)(2,1)}, bf16[129,2,8,128]{3,2,1,0:T(8,128)(2,1)S(1)}, u32[]{:S(2)}, u32[]{:S(2)}) collective-permute-start(bf16[129,2,8,128]{3,2,1,0:T(8,128)(2,1)} %get-tuple-element.36), channel_id=1, source_target_pairs={{0,1},{1,0},{2,3},{3,2},{4,5},{5,4},{6,7},{7,6},{8,9},{9,8},{10,11... | collective-permute-start | bytes 1585160 | tf_op jit(solution)/shard_map/ppermute | solution.py:33
  11.1 19.9 %collective-permute-start.2 = (bf16[256,512]{1,0:T(8,128)(2,1)S(1)}, bf16[256,512]{1,0:T(8,128)(2,1)S(1)}, u32[]{:S(2)}, u32[]{:S(2)}) collective-permute-start(bf16[256,512]{1,0:T(8,128)(2,1)S(1)} %pad_maximum_fusion.1), channel_id=1, source_target_pairs={{0,18},{1,19},{2,16},{3,17},{4,22},{5,23},{6,20},{7,21},{8,26},{9,... | collective-permute-start | bytes 786440 | tf_op jit(solution)/shard_map/ppermute | solution.py:33
  14.9 21.3 %collective-permute-start = (bf16[129,2,8,128]{3,2,1,0:T(8,128)(2,1)}, bf16[129,2,8,128]{3,2,1,0:T(8,128)(2,1)}, u32[]{:S(2)}, u32[]{:S(2)}) collective-permute-start(bf16[129,2,8,128]{3,2,1,0:T(8,128)(2,1)} %get-tuple-element.34), channel_id=1, source_target_pairs={{1,2},{3,4},{5,6},{7,8},{9,10},{11,12},{13,14},{2,1},{4,3},{6,5},{... | collective-permute-start | bytes 1585160 | tf_op jit(solution)/shard_map/ppermute | solution.py:277
  31.0 5.3 %copy-start.13 = (bf16[129,2,8,128]{3,2,1,0:T(8,128)(2,1)}, bf16[129,2,8,128]{3,2,1,0:T(8,128)(2,1)S(1)}, u32[]{:S(2)}) copy-start(bf16[129,2,8,128]{3,2,1,0:T(8,128)(2,1)S(1)} %collective-permute-done.3.inner_ref.inner_code) | copy-start | bytes 1585156
  31.0 5.2 %collective-permute-start.4 = (bf16[512,512]{1,0:T(8,128)(2,1)S(1)}, bf16[512,512]{1,0:T(8,128)(2,1)S(1)}, u32[]{:S(2)}, u32[]{:S(2)}) collective-permute-start(bf16[512,512]{1,0:T(8,128)(2,1)S(1)} %pad_maximum_fusion.refs_4_), channel_id=1, source_target_pairs={{0,1},{1,0},{2,3},{3,2},{4,5},{5,4},{6,7},{7,6},{8,9},{9,8},{10,11... | collective-permute-start | bytes 1572872 | tf_op jit(solution)/shard_map/ppermute | solution.py:33
  31.1 15.8 %collective-permute-start.9 = (bf16[512,512]{1,0:T(8,128)(2,1)S(1)}, bf16[512,512]{1,0:T(8,128)(2,1)S(1)}, u32[]{:S(2)}, u32[]{:S(2)}) collective-permute-start(bf16[512,512]{1,0:T(8,128)(2,1)S(1)} %pad_maximum_fusion.refs_4_), channel_id=1, source_target_pairs={{0,4},{1,5},{2,6},{3,7},{4,8},{5,9},{6,10},{7,11},{8,12},{9,13},{1... | collective-permute-start | bytes 1572872 | tf_op jit(solution)/shard_map/ppermute | solution.py:33
  32.6 24.5 %collective-permute-start.10 = (bf16[512,512]{1,0:T(8,128)(2,1)S(1)}, bf16[512,512]{1,0:T(8,128)(2,1)S(1)}, u32[]{:S(2)}, u32[]{:S(2)}) collective-permute-start(bf16[512,512]{1,0:T(8,128)(2,1)S(1)} %pad_maximum_fusion.refs_4_), channel_id=1, source_target_pairs={{0,12},{1,13},{2,14},{3,15},{4,0},{5,1},{6,2},{7,3},{8,4},{9,5},{1... | collective-permute-start | bytes 1572872 | tf_op jit(solution)/shard_map/ppermute | solution.py:33
  34.4 25.8 %collective-permute-start.11 = (bf16[512,512]{1,0:T(8,128)(2,1)S(1)}, bf16[512,512]{1,0:T(8,128)(2,1)S(1)}, u32[]{:S(2)}, u32[]{:S(2)}) collective-permute-start(bf16[512,512]{1,0:T(8,128)(2,1)S(1)} %pad_maximum_fusion.refs_4_), channel_id=1, source_target_pairs={{0,8},{1,9},{2,10},{3,11},{4,12},{5,13},{6,14},{7,15},{8,0},{9,1},... | collective-permute-start | bytes 1572872 | tf_op jit(solution)/shard_map/ppermute | solution.py:33
  41.9 26.2 %collective-permute-start.15 = (bf16[128,2048]{1,0:T(8,128)(2,1)}, bf16[128,2048]{1,0:T(8,128)(2,1)S(1)}, u32[]{:S(2)}, u32[]{:S(2)}) collective-permute-start(bf16[128,2048]{1,0:T(8,128)(2,1)} %get-tuple-element.41.refs_12_), channel_id=1, source_target_pairs={{0,96},{1,97},{2,98},{3,99},{4,100},{5,101},{6,102},{7,103},{8,104... | collective-permute-start | bytes 1572872 | tf_op jit(solution)/shard_map/ppermute | solution.py:33
  45.0 5.1 %collective-permute-start.5 = (bf16[2,4,8,128]{3,2,1,0:T(8,128)(2,1)}, bf16[2,4,8,128]{3,2,1,0:T(8,128)(2,1)S(1)}, u32[]{:S(2)}, u32[]{:S(2)}) collective-permute-start(bf16[2,4,8,128]{3,2,1,0:T(8,128)(2,1)} %get-tuple-element.40), channel_id=1, source_target_pairs={{0,16},{1,17},{2,18},{3,19},{4,20},{5,21},{6,22},{7,23},{8,24},{9,... | collective-permute-start | bytes 49160 | tf_op jit(solution)/shard_map/ppermute | solution.py:33
  46.8 21.7 %collective-permute-start.16 = (bf16[128,2048]{1,0:T(8,128)(2,1)}, bf16[128,2048]{1,0:T(8,128)(2,1)S(1)}, u32[]{:S(2)}, u32[]{:S(2)}) collective-permute-start(bf16[128,2048]{1,0:T(8,128)(2,1)} %get-tuple-element.41.refs_12_), channel_id=1, source_target_pairs={{0,64},{1,65},{2,66},{3,67},{4,68},{5,69},{6,70},{7,71},{8,72},{9,... | collective-permute-start | bytes 1572872 | tf_op jit(solution)/shard_map/ppermute | solution.py:33
  50.0 23.3 %collective-permute-start.17 = (bf16[128,2048]{1,0:T(8,128)(2,1)}, bf16[128,2048]{1,0:T(8,128)(2,1)S(1)}, u32[]{:S(2)}, u32[]{:S(2)}) collective-permute-start(bf16[128,2048]{1,0:T(8,128)(2,1)} %get-tuple-element.41.refs_12_), channel_id=1, source_target_pairs={{0,32},{1,33},{2,34},{3,35},{4,36},{5,37},{6,38},{7,39},{8,40},{9,... | collective-permute-start | bytes 1572872 | tf_op jit(solution)/shard_map/ppermute | solution.py:33
  57.2 10.9 %collective-permute-start.6 = (bf16[4,4,8,128]{3,2,1,0:T(8,128)(2,1)S(1)}, bf16[4,4,8,128]{3,2,1,0:T(8,128)(2,1)S(1)}, u32[]{:S(2)}, u32[]{:S(2)}) collective-permute-start(bf16[4,4,8,128]{3,2,1,0:T(8,128)(2,1)S(1)} %constant_dynamic-update-slice_fusion.refs_0_), channel_id=1, source_target_pairs={{0,96},{1,97},{2,98},{3,99},{4,100},{5,101},{6,102},{7,103},{8,104... | collective-permute-start | bytes 98312 | tf_op jit(solution)/shard_map/ppermute | solution.py:33
  60.2 19.2 %collective-permute-start.12 = (bf16[512,512]{1,0:T(8,128)(2,1)S(1)}, bf16[512,512]{1,0:T(8,128)(2,1)S(1)}, u32[]{:S(2)}, u32[]{:S(2)}) collective-permute-start(bf16[512,512]{1,0:T(8,128)(2,1)S(1)} %collective-permute-done.9.refs_5_), channel_id=1, source_target_pairs={{0,1},{1,0},{2,3},{3,2},{4,5},{5,4},{6,7},{7,6},{8,9},{9,8},{10,11... | collective-permute-start | bytes 1572872 | tf_op jit(solution)/shard_map/ppermute | solution.py:33
  68.1 11.4 %collective-permute-start.13 = (bf16[512,512]{1,0:T(8,128)(2,1)S(1)}, bf16[512,512]{1,0:T(8,128)(2,1)S(1)}, u32[]{:S(2)}, u32[]{:S(2)}) collective-permute-start(bf16[512,512]{1,0:T(8,128)(2,1)S(1)} %collective-permute-done.10.refs_6_), channel_id=1, source_target_pairs={{0,1},{1,0},{2,3},{3,2},{4,5},{5,4},{6,7},{7,6},{8,9},{9,8},{10,11... | collective-permute-start | bytes 1572872 | tf_op jit(solution)/shard_map/ppermute | solution.py:33
  68.1 11.4 %collective-permute-start.14 = (bf16[512,512]{1,0:T(8,128)(2,1)S(1)}, bf16[512,512]{1,0:T(8,128)(2,1)S(1)}, u32[]{:S(2)}, u32[]{:S(2)}) collective-permute-start(bf16[512,512]{1,0:T(8,128)(2,1)S(1)} %collective-permute-done.11.refs_7_), channel_id=1, source_target_pairs={{0,1},{1,0},{2,3},{3,2},{4,5},{5,4},{6,7},{7,6},{8,9},{9,8},{10,11... | collective-permute-start | bytes 1572872 | tf_op jit(solution)/shard_map/ppermute | solution.py:33
  68.6 6.6 %collective-permute-start.7 = (bf16[4,4,8,128]{3,2,1,0:T(8,128)(2,1)S(1)}, bf16[4,4,8,128]{3,2,1,0:T(8,128)(2,1)S(1)}, u32[]{:S(2)}, u32[]{:S(2)}) collective-permute-start(bf16[4,4,8,128]{3,2,1,0:T(8,128)(2,1)S(1)} %constant_dynamic-update-slice_fusion.refs_0_), channel_id=1, source_target_pairs={{0,64},{1,65},{2,66},{3,67},{4,68},{5,69},{6,70},{7,71},{8,72},{9,... | collective-permute-start | bytes 98312 | tf_op jit(solution)/shard_map/ppermute | solution.py:33
  73.3 5.1 %collective-permute-start.8 = (bf16[4,4,8,128]{3,2,1,0:T(8,128)(2,1)S(1)}, bf16[4,4,8,128]{3,2,1,0:T(8,128)(2,1)S(1)}, u32[]{:S(2)}, u32[]{:S(2)}) collective-permute-start(bf16[4,4,8,128]{3,2,1,0:T(8,128)(2,1)S(1)} %constant_dynamic-update-slice_fusion.refs_0_), channel_id=1, source_target_pairs={{0,32},{1,33},{2,34},{3,35},{4,36},{5,37},{6,38},{7,39},{8,40},{9,... | collective-permute-start | bytes 98312 | tf_op jit(solution)/shard_map/ppermute | solution.py:33
  75.2 28.0 %collective-permute-start.19 = (bf16[128,2048]{1,0:T(8,128)(2,1)}, bf16[128,2048]{1,0:T(8,128)(2,1)}, u32[]{:S(2)}, u32[]{:S(2)}) collective-permute-start(bf16[128,2048]{1,0:T(8,128)(2,1)} %get-tuple-element.54.refs_12_), channel_id=1, source_target_pairs={{0,96},{1,97},{2,98},{3,99},{4,100},{5,101},{6,102},{7,103},{8,104... | collective-permute-start | bytes 1572872 | tf_op jit(solution)/shard_map/ppermute | solution.py:33
  78.4 24.7 %collective-permute-start.20 = (bf16[128,2048]{1,0:T(8,128)(2,1)}, bf16[128,2048]{1,0:T(8,128)(2,1)}, u32[]{:S(2)}, u32[]{:S(2)}) collective-permute-start(bf16[128,2048]{1,0:T(8,128)(2,1)} %get-tuple-element.54.refs_12_), channel_id=1, source_target_pairs={{0,64},{1,65},{2,66},{3,67},{4,68},{5,69},{6,70},{7,71},{8,72},{9,... | collective-permute-start | bytes 1572872 | tf_op jit(solution)/shard_map/ppermute | solution.py:33
  79.4 8.0 %copy-start.5 = (bf16[512,512]{1,0:T(8,128)(2,1)}, bf16[512,512]{1,0:T(8,128)(2,1)S(1)}, u32[]{:S(2)}) copy-start(bf16[512,512]{1,0:T(8,128)(2,1)S(1)} %collective-permute-done.12.refs_9_) | copy-start | bytes 1572868
  79.4 24.4 %collective-permute-start.21 = (bf16[128,2048]{1,0:T(8,128)(2,1)}, bf16[128,2048]{1,0:T(8,128)(2,1)}, u32[]{:S(2)}, u32[]{:S(2)}) collective-permute-start(bf16[128,2048]{1,0:T(8,128)(2,1)} %get-tuple-element.54.refs_12_), channel_id=1, source_target_pairs={{0,32},{1,33},{2,34},{3,35},{4,36},{5,37},{6,38},{7,39},{8,40},{9,... | collective-permute-start | bytes 1572872 | tf_op jit(solution)/shard_map/ppermute | solution.py:33
  79.5 8.0 %copy-start.9 = (bf16[512,512]{1,0:T(8,128)(2,1)}, bf16[512,512]{1,0:T(8,128)(2,1)S(1)}, u32[]{:S(2)}) copy-start(bf16[512,512]{1,0:T(8,128)(2,1)S(1)} %collective-permute-done.13.refs_10_) | copy-start | bytes 1572868
  79.5 1.4 %copy-start.7 = (bf16[128,2048]{1,0:T(8,128)(2,1)S(1)}, bf16[128,2048]{1,0:T(8,128)(2,1)}, u32[]{:S(2)}) copy-start(bf16[128,2048]{1,0:T(8,128)(2,1)} %get-tuple-element.41.refs_12_) | copy-start | bytes 1572868
  80.9 6.6 %copy-start.11 = (bf16[512,512]{1,0:T(8,128)(2,1)}, bf16[512,512]{1,0:T(8,128)(2,1)S(1)}, u32[]{:S(2)}) copy-start(bf16[512,512]{1,0:T(8,128)(2,1)S(1)} %collective-permute-done.14.refs_11_) | copy-start | bytes 1572868
  80.9 6.6 %copy-start.8 = (bf16[128,2048]{1,0:T(8,128)(2,1)S(1)}, bf16[128,2048]{1,0:T(8,128)(2,1)}, u32[]{:S(2)}) copy-start(bf16[128,2048]{1,0:T(8,128)(2,1)} %get-tuple-element.41.refs_12_) | copy-start | bytes 1572868
  87.2 6.7 %copy-start.3 = (f32[128,1024]{1,0:T(8,128)}, f32[128,1024]{1,0:T(8,128)S(1)}, u32[]{:S(2)}) copy-start(f32[128,1024]{1,0:T(8,128)S(1)} %get-tuple-element.42.a_ref) | copy-start | bytes 1572868
  87.2 9.5 %collective-permute-start.18 = (bf16[128,1024]{1,0:T(8,128)(2,1)S(1)}, bf16[128,1024]{1,0:T(8,128)(2,1)}, u32[]{:S(2)}, u32[]{:S(2)}) collective-permute-start(bf16[128,1024]{1,0:T(8,128)(2,1)S(1)} %get-tuple-element.48), channel_id=1, source_target_pairs={{0,16},{1,17},{2,18},{3,19},{4,20},{5,21},{6,22},{7,23},{8,24},{9,... | collective-permute-start | bytes 786440 | tf_op jit(solution)/shard_map/ppermute | solution.py:33
  93.9 0.8 copy-start.2
  94.7 6.6 %collective-permute-start.22 = (bf16[128,1024]{1,0:T(8,128)(2,1)S(1)}, bf16[128,1024]{1,0:T(8,128)(2,1)}, u32[]{:S(2)}, u32[]{:S(2)}) collective-permute-start(bf16[128,1024]{1,0:T(8,128)(2,1)S(1)} %get-tuple-element.56), channel_id=1, source_target_pairs={{0,16},{1,17},{2,18},{3,19},{4,20},{5,21},{6,22},{7,23},{8,24},{9,... | collective-permute-start | bytes 786440 | tf_op jit(solution)/shard_map/ppermute | solution.py:33
  98.5 5.3 %copy-start.4 = (bf16[128,2048]{1,0:T(8,128)(2,1)S(1)}, bf16[128,2048]{1,0:T(8,128)(2,1)}, u32[]{:S(2)}) copy-start(bf16[128,2048]{1,0:T(8,128)(2,1)} %get-tuple-element.54.refs_12_) | copy-start | bytes 1572868
  103.9 1.0 copy-start.6
  104.9 1.0 copy-start.10
  106.0 1.0 copy-start.12
  114.0 0.8 copy-start
  114.9 9.9 %collective-permute-start.24 = (bf16[128,1024]{1,0:T(8,128)(2,1)S(1)}, bf16[128,1024]{1,0:T(8,128)(2,1)}, u32[]{:S(2)}, u32[]{:S(2)}) collective-permute-start(bf16[128,1024]{1,0:T(8,128)(2,1)S(1)} %get-tuple-element.63), channel_id=1, source_target_pairs={{0,16},{1,17},{2,18},{3,19},{4,20},{5,21},{6,22},{7,23},{8,24},{9,... | collective-permute-start | bytes 786440 | tf_op jit(solution)/shard_map/ppermute | solution.py:33
  123.1 0.8 copy-start.1
  123.9 7.3 %collective-permute-start.23 = (bf16[128,1024]{1,0:T(8,128)(2,1)S(1)}, bf16[128,1024]{1,0:T(8,128)(2,1)S(1)}, u32[]{:S(2)}, u32[]{:S(2)}) collective-permute-start(bf16[128,1024]{1,0:T(8,128)(2,1)S(1)} %get-tuple-element.62), channel_id=1, source_target_pairs={{0,16},{1,17},{2,18},{3,19},{4,20},{5,21},{6,22},{7,23},{8,24},{9,... | collective-permute-start | bytes 786440 | tf_op jit(solution)/shard_map/ppermute | solution.py:33
  131.2 0.7 copy-start.15

commit v6 on v4

--- a/solution.py
+++ b/solution.py
@@ -304,7 +304,7 @@
             pltpu.SemaphoreType.DMA((10,)),
             pltpu.SemaphoreType.DMA((5,)),
         ],
-        compiler_params=pltpu.CompilerParams(vmem_limit_bytes=56 << 20),
+        compiler_params=pltpu.CompilerParams(vmem_limit_bytes=28 << 20),
         cost_estimate=pl.CostEstimate(
             flops=2 * SLICES * 256 * 512 * cells, bytes_accessed=6 << 20, transcendentals=0
         ),
@@ -368,7 +368,8 @@
     second = after(second, before)
     transported, block = transport(density, limiter, heading, courant, first, second, inner)
     before, behind = shift(block, dy=1), shift(block, dy=-1)
-    outside = [block, behind, before, shift(before[:64], dy=1), shift(behind[64:], dy=-1)]
+    across = shift(block, dy=2)
+    outside = [block, behind, before, across[:64], across[64:]]
 
     results, got = [None], []
     for layers, blocks in zip(BLOCKS, (inside, outside), strict=True):

time: 135 us -> 126 us (0.933)
  Pallas kernels: 62.8 us -> 52.3 us
  waiting for transfers between devices: 20 us -> 24.6 us
  starting transfers between devices: 42.7 us -> 39.1 us
  local copies, waits for them, and re-layouts: 6.69 us -> 8.13 us
    pallas_call x4, Pallas kernels: 41.1 us -> 30.5 us  [collide(): pl.pallas_call(kernel, out_shape=(shape((128, cells), F32), shape((128, c...]
    ppermute x28 -> x27, waiting for transfers between devices: 20 us -> 24.6 us  [shift(): return lax.ppermute(value, BOTH, pairs)]
    ppermute x28 -> x27, starting transfers between devices: 41.4 us -> 37.8 us  [shift(): return lax.ppermute(value, BOTH, pairs)]
    unnamed x50 -> x28, local copies, waits for them, and re-layouts: 6.54 us -> 7.28 us
  transfers between devices with their start and end apart: 30 -> 29, of which waited for: 9 -> 9; matrix products, arithmetic and copies ran while one was open for 1% -> 1% of each run, Pallas kernels for 36% -> 33%
where the time goes in v6:
time: 126 us
  Pallas kernels  52.3 us (42%)
  starting transfers between devices  39.1 us (31%)
  waiting for transfers between devices  24.6 us (20%)
  local copies, waits for them, and re-layouts  8.13 us (6%)
    ppermute x27, starting transfers between devices, shift(): return lax.ppermute(value, BOTH, pairs)  37.8 us
    pallas_call x4, Pallas kernels, collide(): pl.pallas_call(kernel, out_shape=(shape((128, cells), F32), shape((128, c...  30.5 us
    ppermute x27, waiting for transfers between devices, shift(): return lax.ppermute(value, BOTH, pairs)  24.6 us
    pallas_call x4, Pallas kernels, combine(): pl.pallas_call(kernel, grid=(128 // step,), out_shape=shape((128, 4, 8, 1...  7.59 us
    unnamed x28, local copies, waits for them, and re-layouts  7.28 us
    pallas_call x1, Pallas kernels, transport(): pl.pallas_call(kernel, grid=(rows // STEP,), out_shape=(shape(density.sha...  5.15 us
    pallas_call x1, Pallas kernels, transport_inner(): pl.pallas_call(kernel, grid=(rows // STEP,), out_shape=(shape((rows, 2048...  4.47 us
    pallas_call x1, Pallas kernels, pack(): pl.pallas_call(kernel, out_shape=(shape((rows + 3, *dims), BF16), shape((...  2.73 us
  transfers between devices with their start and end apart: 29, of which 9 were waited for; matrix products, arithmetic and copies ran while one was open for 1% of the time, Pallas kernels for 33%

profile of v6, /device:TPU:0, one launch (start us, length us, event | category | flops | bytes accessed | tf_op | source)
XLA Modules:
  0.0 125.7 jit_solution(3885346492262421760)
XLA Ops:
  0.6 1.8 %split_slice.1 = bf16[256,512]{1,0:T(8,128)(2,1)} custom-call(bf16[4,2,128,128]{3,2,1,0:T(8,128)(2,1)} %bitcast.1), custom_call_target="tpu_custom_call" | custom-call | tf_op jit(solution)/shard_map/split_slice/pallas_call | solution.py:89
  2.4 2.0 %collective-permute-start.1 = (bf16[256,512]{1,0:T(8,128)(2,1)}, bf16[256,512]{1,0:T(8,128)(2,1)S(1)}, u32[]{:S(2)}, u32[]{:S(2)}) collective-permute-start(bf16[256,512]{1,0:T(8,128)(2,1)} %split_slice.1), channel_id=1, source_target_pairs={{0,16},{1,17},{2,18},{3,19},{4,20},{5,21},{6,22},{7,23},{8,24},{9,... | collective-permute-start | bytes 786440 | tf_op jit(solution)/shard_map/ppermute | solution.py:33
  4.4 2.7 %pack.1 = (bf16[131,8,128]{2,1,0:T(8,128)(2,1)}, bf16[128,8,128]{2,1,0:T(8,128)(2,1)}, bf16[129,2,8,128]{3,2,1,0:T(8,128)(2,1)}) custom-call(f32[128,4,8,128]{3,2,1,0:T(8,128)} %d_ref.4, s32[4,8,128]{2,1,0:T(8,128)} %l_ref.5), custom_call_target="tpu_custom_call" | custom-call | tf_op jit(solution)/shard_map/pack/pallas_call | solution.py:68
  7.8 5.0 %collective-permute-start.2 = (bf16[129,2,8,128]{3,2,1,0:T(8,128)(2,1)}, bf16[129,2,8,128]{3,2,1,0:T(8,128)(2,1)S(1)}, u32[]{:S(2)}, u32[]{:S(2)}) collective-permute-start(bf16[129,2,8,128]{3,2,1,0:T(8,128)(2,1)} %get-tuple-element.43), channel_id=1, source_target_pairs={{0,1},{1,0},{2,3},{3,2},{4,5},{5,4},{6,7},{7,6},{8,9},{9,8},{10,11... | collective-permute-start | bytes 1585160 | tf_op jit(solution)/shard_map/ppermute | solution.py:33
  12.9 2.0 %collective-permute-start.4 = (bf16[256,512]{1,0:T(8,128)(2,1)S(1)}, bf16[256,512]{1,0:T(8,128)(2,1)S(1)}, u32[]{:S(2)}, u32[]{:S(2)}) collective-permute-start(bf16[256,512]{1,0:T(8,128)(2,1)S(1)} %pad_maximum_fusion.1), channel_id=1, source_target_pairs={{0,18},{1,19},{2,16},{3,17},{4,22},{5,23},{6,20},{7,21},{8,26},{9,... | collective-permute-start | bytes 786440 | tf_op jit(solution)/shard_map/ppermute | solution.py:33
  15.6 0.8 copy-done.9
  16.4 4.5 %transport_inner.1 = (bf16[128,2048]{1,0:T(8,128)(2,1)}, bf16[2,4,8,128]{3,2,1,0:T(8,128)(2,1)}) custom-call(s32[128]{0:T(128)} %h_ref.3, f32[128]{0:T(128)} %c_ref.3, f32[128,4,8,128]{3,2,1,0:T(8,128)} %d_ref.4, s32[4,8,128]{2,1,0:T(8,128)} %l_ref.5, bf16[131,8,128]{2,1,0:T(8,128)(2,1)} %copy-done.10, bf16[131,8,128]{2,1,0:T(8,128)(2,1)} %copy-done.10, ...), custom_call_target="tpu_custom_call" | custom-call | flops 2097152 | bytes 3145728 | tf_op jit(solution)/shard_map/transport_inner/pallas_call | solution.py:182
  20.9 3.0 %collective-permute-done.4 = bf16[256,512]{1,0:T(8,128)(2,1)S(1)} collective-permute-done((bf16[256,512]{1,0:T(8,128)(2,1)S(1)}, bf16[256,512]{1,0:T(8,128)(2,1)S(1)}, u32[]{:S(2)}, u32[]{:S(2)}) %collective-permute-start.4) | collective-permute-done | bytes 262176 | tf_op jit(solution)/shard_map/ppermute | solution.py:33
  24.0 1.5 %collective-permute-start.7 = (bf16[512,512]{1,0:T(8,128)(2,1)S(1)}, bf16[512,512]{1,0:T(8,128)(2,1)S(1)}, u32[]{:S(2)}, u32[]{:S(2)}) collective-permute-start(bf16[512,512]{1,0:T(8,128)(2,1)S(1)} %pad_maximum_fusion.refs_4_), channel_id=1, source_target_pairs={{0,1},{1,0},{2,3},{3,2},{4,5},{5,4},{6,7},{7,6},{8,9},{9,8},{10,11... | collective-permute-start | bytes 1572872 | tf_op jit(solution)/shard_map/ppermute | solution.py:33
  25.5 2.2 %collective-permute-start.5 = (bf16[512,512]{1,0:T(8,128)(2,1)S(1)}, bf16[512,512]{1,0:T(8,128)(2,1)S(1)}, u32[]{:S(2)}, u32[]{:S(2)}) collective-permute-start(bf16[512,512]{1,0:T(8,128)(2,1)S(1)} %pad_maximum_fusion.refs_4_), channel_id=1, source_target_pairs={{0,4},{1,5},{2,6},{3,7},{4,8},{5,9},{6,10},{7,11},{8,12},{9,13},{1... | collective-permute-start | bytes 1572872 | tf_op jit(solution)/shard_map/ppermute | solution.py:33
  27.6 1.3 %collective-permute-start.6 = (bf16[512,512]{1,0:T(8,128)(2,1)S(1)}, bf16[512,512]{1,0:T(8,128)(2,1)S(1)}, u32[]{:S(2)}, u32[]{:S(2)}) collective-permute-start(bf16[512,512]{1,0:T(8,128)(2,1)S(1)} %pad_maximum_fusion.refs_4_), channel_id=1, source_target_pairs={{0,12},{1,13},{2,14},{3,15},{4,0},{5,1},{6,2},{7,3},{8,4},{9,5},{1... | collective-permute-start | bytes 1572872 | tf_op jit(solution)/shard_map/ppermute | solution.py:33
  28.9 1.6 %collective-permute-start.8 = (bf16[128,2048]{1,0:T(8,128)(2,1)}, bf16[128,2048]{1,0:T(8,128)(2,1)S(1)}, u32[]{:S(2)}, u32[]{:S(2)}) collective-permute-start(bf16[128,2048]{1,0:T(8,128)(2,1)} %get-tuple-element.48.refs_14_), channel_id=1, source_target_pairs={{0,32},{1,33},{2,34},{3,35},{4,36},{5,37},{6,38},{7,39},{8,40},{9,... | collective-permute-start | bytes 1572872 | tf_op jit(solution)/shard_map/ppermute | solution.py:33
  30.5 1.7 %collective-permute-start.9 = (bf16[128,2048]{1,0:T(8,128)(2,1)}, bf16[128,2048]{1,0:T(8,128)(2,1)S(1)}, u32[]{:S(2)}, u32[]{:S(2)}) collective-permute-start(bf16[128,2048]{1,0:T(8,128)(2,1)} %get-tuple-element.48.refs_14_), channel_id=1, source_target_pairs={{0,96},{1,97},{2,98},{3,99},{4,100},{5,101},{6,102},{7,103},{8,104... | collective-permute-start | bytes 1572872 | tf_op jit(solution)/shard_map/ppermute | solution.py:33
  32.2 3.9 %collective-permute-done.10 = bf16[2,4,8,128]{3,2,1,0:T(8,128)(2,1)S(1)} collective-permute-done((bf16[2,4,8,128]{3,2,1,0:T(8,128)(2,1)}, bf16[2,4,8,128]{3,2,1,0:T(8,128)(2,1)S(1)}, u32[]{:S(2)}, u32[]{:S(2)}) %collective-permute-start.10) | collective-permute-done | bytes 16416 | tf_op jit(solution)/shard_map/ppermute | solution.py:33
  36.8 0.7 pad_maximum_fusion.2.refs_0_
  37.5 3.7 %collective-permute-done.5.refs_5_ = bf16[512,512]{1,0:T(8,128)(2,1)S(1)} collective-permute-done((bf16[512,512]{1,0:T(8,128)(2,1)S(1)}, bf16[512,512]{1,0:T(8,128)(2,1)S(1)}, u32[]{:S(2)}, u32[]{:S(2)}) %collective-permute-start.5) | collective-permute-done | bytes 524320 | tf_op jit(solution)/shard_map/ppermute | solution.py:33
  41.4 2.8 %collective-permute-done.8.refs_16_ = bf16[128,2048]{1,0:T(8,128)(2,1)S(1)} collective-permute-done((bf16[128,2048]{1,0:T(8,128)(2,1)}, bf16[128,2048]{1,0:T(8,128)(2,1)S(1)}, u32[]{:S(2)}, u32[]{:S(2)}) %collective-permute-start.8) | collective-permute-done | bytes 524320 | tf_op jit(solution)/shard_map/ppermute | solution.py:33
  44.2 2.9 %collective-permute-start.11 = (bf16[4,4,8,128]{3,2,1,0:T(8,128)(2,1)S(1)}, bf16[4,4,8,128]{3,2,1,0:T(8,128)(2,1)S(1)}, u32[]{:S(2)}, u32[]{:S(2)}) collective-permute-start(bf16[4,4,8,128]{3,2,1,0:T(8,128)(2,1)S(1)} %pad_maximum_fusion.2.refs_0_), channel_id=1, source_target_pairs={{0,96},{1,97},{2,98},{3,99},{4,100},{5,101},{6,102},{7,103},{8,104... | collective-permute-start | bytes 98312 | tf_op jit(solution)/shard_map/ppermute | solution.py:33
  47.1 0.7 collective-permute-start.12
  48.6 0.8 collective-permute-start.14
  49.4 2.6 %collective-permute-start.15 = (bf16[256,512]{1,0:T(8,128)(2,1)S(1)}, bf16[256,512]{1,0:T(8,128)(2,1)}, u32[]{:S(2)}, u32[]{:S(2)}) collective-permute-start(bf16[256,512]{1,0:T(8,128)(2,1)S(1)} %slice.35), channel_id=1, source_target_pairs={{0,12},{1,13},{2,14},{3,15},{4,0},{5,1},{6,2},{7,3},{8,4},{9,5},{1... | collective-permute-start | bytes 786440 | tf_op jit(solution)/shard_map/ppermute | solution.py:33
  52.0 2.1 %collective-permute-start.20 = (bf16[64,2048]{1,0:T(8,128)(2,1)S(1)}, bf16[64,2048]{1,0:T(8,128)(2,1)S(1)}, u32[]{:S(2)}, u32[]{:S(2)}) collective-permute-start(bf16[64,2048]{1,0:T(8,128)(2,1)S(1)} %slice.36), channel_id=1, source_target_pairs={{0,32},{1,33},{2,34},{3,35},{4,36},{5,37},{6,38},{7,39},{8,40},{9,... | collective-permute-start | bytes 786440 | tf_op jit(solution)/shard_map/ppermute | solution.py:33
  54.6 0.7 slice.37
  55.3 0.9 collective-permute-done.14.refs_7_
  56.2 2.6 %collective-permute-start.21 = (bf16[64,2048]{1,0:T(8,128)(2,1)}, bf16[64,2048]{1,0:T(8,128)(2,1)}, u32[]{:S(2)}, u32[]{:S(2)}) collective-permute-start(bf16[64,2048]{1,0:T(8,128)(2,1)} %slice.37), channel_id=1, source_target_pairs={{0,96},{1,97},{2,98},{3,99},{4,100},{5,101},{6,102},{7,103},{8,104... | collective-permute-start | bytes 786440 | tf_op jit(solution)/shard_map/ppermute | solution.py:33
  58.8 0.8 collective-permute-done.20.refs_17_
  59.6 0.7 copy-done.7
  60.3 5.2 %transport.1 = (f32[128,4,8,128]{3,2,1,0:T(8,128)}, bf16[128,2048]{1,0:T(8,128)(2,1)}) custom-call(s32[128]{0:T(128)} %h_ref.3, f32[128]{0:T(128)} %c_ref.3, f32[128,4,8,128]{3,2,1,0:T(8,128)} %d_ref.4, s32[4,8,128]{2,1,0:T(8,128)} %l_ref.5, bf16[131,8,128]{2,1,0:T(8,128)(2,1)} %copy-done.10, bf16[131,8,128]{2,1,0:T(8,128)(2,1)} %copy-done.10, ...), custom_call_target="tpu_custom_call" | custom-call | flops 4194304 | bytes 6291456 | tf_op jit(solution)/shard_map/transport/pallas_call | solution.py:219
  65.4 1.4 %collective-permute-start.25 = (bf16[128,2048]{1,0:T(8,128)(2,1)}, bf16[128,2048]{1,0:T(8,128)(2,1)S(1)}, u32[]{:S(2)}, u32[]{:S(2)}) collective-permute-start(bf16[128,2048]{1,0:T(8,128)(2,1)} %get-tuple-element.68.refs_14_), channel_id=1, source_target_pairs={{0,64},{1,65},{2,66},{3,67},{4,68},{5,69},{6,70},{7,71},{8,72},{9,... | collective-permute-start | bytes 1572872 | tf_op jit(solution)/shard_map/ppermute | solution.py:33
  66.8 2.2 %collective-permute-start.23 = (bf16[128,2048]{1,0:T(8,128)(2,1)}, bf16[128,2048]{1,0:T(8,128)(2,1)}, u32[]{:S(2)}, u32[]{:S(2)}) collective-permute-start(bf16[128,2048]{1,0:T(8,128)(2,1)} %get-tuple-element.68.refs_14_), channel_id=1, source_target_pairs={{0,96},{1,97},{2,98},{3,99},{4,100},{5,101},{6,102},{7,103},{8,104... | collective-permute-start | bytes 1572872 | tf_op jit(solution)/shard_map/ppermute | solution.py:33
  69.1 1.0 copy-done.4
  70.2 0.9 copy-done.8
  71.1 7.3 %collide.4 = (f32[128,1024]{1,0:T(8,128)S(1)}, bf16[128,1024]{1,0:T(8,128)(2,1)S(1)}) custom-call(bf16[4,4,8,128]{3,2,1,0:T(8,128)(2,1)S(1)} %pad_maximum_fusion.2.refs_0_, bf16[4,4,8,128]{3,2,1,0:T(8,128)(2,1)S(1)} %collective-permute-done.11.refs_1_, bf16[4,4,8,128]{3,2,1,0:T(8,128)(2,1)S(1)} %collective-permute-done.12.refs_2_, ...), custom_call_target="tpu_custom_call" | custom-call | flops 4294967296 | bytes 6291456 | tf_op jit(solution)/shard_map/collide/pallas_call | solution.py:295
  78.5 8.0 %collide.5 = (f32[128,1024]{1,0:T(8,128)S(1)}, bf16[128,1024]{1,0:T(8,128)(2,1)}) custom-call(bf16[4,4,8,128]{3,2,1,0:T(8,128)(2,1)S(1)} %pad_maximum_fusion.2.refs_0_, bf16[4,4,8,128]{3,2,1,0:T(8,128)(2,1)S(1)} %collective-permute-done.11.refs_1_, bf16[4,4,8,128]{3,2,1,0:T(8,128)(2,1)S(1)} %collective-permute-done.12.refs_2_, ...), custom_call_target="tpu_custom_call" | custom-call | flops 4294967296 | bytes 6291456 | tf_op jit(solution)/shard_map/collide/pallas_call | solution.py:295
  86.5 0.8 copy-done.2
  87.3 1.9 %collective-permute-start.26 = (bf16[128,1024]{1,0:T(8,128)(2,1)}, bf16[128,1024]{1,0:T(8,128)(2,1)}, u32[]{:S(2)}, u32[]{:S(2)}) collective-permute-start(bf16[128,1024]{1,0:T(8,128)(2,1)} %get-tuple-element.70), channel_id=1, source_target_pairs={{0,16},{1,17},{2,18},{3,19},{4,20},{5,21},{6,22},{7,23},{8,24},{9,... | collective-permute-start | bytes 786440 | tf_op jit(solution)/shard_map/ppermute | solution.py:33
  89.3 1.9 %combine.4.refs_0_ = f32[128,4,8,128]{3,2,1,0:T(8,128)} custom-call(f32[128,1024]{1,0:T(8,128)} %copy-done.3, bf16[128,1024]{1,0:T(8,128)(2,1)} %collective-permute-done.22.b_ref), custom_call_target="tpu_custom_call" | custom-call | flops 131072 | bytes 1310720 | tf_op jit(solution)/shard_map/combine/pallas_call | solution.py:326
  91.2 4.5 %collective-permute-done.26.b_ref = bf16[128,1024]{1,0:T(8,128)(2,1)} collective-permute-done((bf16[128,1024]{1,0:T(8,128)(2,1)}, bf16[128,1024]{1,0:T(8,128)(2,1)}, u32[]{:S(2)}, u32[]{:S(2)}) %collective-permute-start.26) | collective-permute-done | bytes 262176 | tf_op jit(solution)/shard_map/ppermute | solution.py:33
  95.7 1.9 %combine.5.refs_0_ = f32[128,4,8,128]{3,2,1,0:T(8,128)} custom-call(f32[128,1024]{1,0:T(8,128)} %copy-done.2, bf16[128,1024]{1,0:T(8,128)(2,1)} %collective-permute-done.26.b_ref, f32[128,4,8,128]{3,2,1,0:T(8,128)} %combine.4.refs_0_), custom_call_target="tpu_custom_call", output_to_operand_aliasing={{}: (2, {})} | custom-call | flops 131072 | bytes 1310720 | tf_op jit(solution)/shard_map/combine/pallas_call | solution.py:326
  97.6 7.3 %collide.6 = (f32[128,1024]{1,0:T(8,128)S(1)}, bf16[128,1024]{1,0:T(8,128)(2,1)S(1)}) custom-call(bf16[4,4,8,128]{3,2,1,0:T(8,128)(2,1)S(1)} %pad_maximum_fusion.2.refs_0_, bf16[4,4,8,128]{3,2,1,0:T(8,128)(2,1)S(1)} %collective-permute-done.11.refs_1_, bf16[4,4,8,128]{3,2,1,0:T(8,128)(2,1)S(1)} %collective-permute-done.12.refs_2_, ...), custom_call_target="tpu_custom_call" | custom-call | flops 4294967296 | bytes 6291456 | tf_op jit(solution)/shard_map/collide/pallas_call | solution.py:295
  105.0 0.8 copy-done
  105.8 1.7 %collective-permute-start.28 = (bf16[128,1024]{1,0:T(8,128)(2,1)S(1)}, bf16[128,1024]{1,0:T(8,128)(2,1)}, u32[]{:S(2)}, u32[]{:S(2)}) collective-permute-start(bf16[128,1024]{1,0:T(8,128)(2,1)S(1)} %get-tuple-element.77), channel_id=1, source_target_pairs={{0,16},{1,17},{2,18},{3,19},{4,20},{5,21},{6,22},{7,23},{8,24},{9,... | collective-permute-start | bytes 786440 | tf_op jit(solution)/shard_map/ppermute | solution.py:33
  107.5 8.0 %collide.7 = (f32[128,1024]{1,0:T(8,128)S(1)}, bf16[128,1024]{1,0:T(8,128)(2,1)}) custom-call(bf16[4,4,8,128]{3,2,1,0:T(8,128)(2,1)S(1)} %pad_maximum_fusion.2.refs_0_, bf16[4,4,8,128]{3,2,1,0:T(8,128)(2,1)S(1)} %collective-permute-done.11.refs_1_, bf16[4,4,8,128]{3,2,1,0:T(8,128)(2,1)S(1)} %collective-permute-done.12.refs_2_, ...), custom_call_target="tpu_custom_call" | custom-call | flops 4294967296 | bytes 6291456 | tf_op jit(solution)/shard_map/collide/pallas_call | solution.py:295
  115.5 0.8 copy-done.1
  116.6 1.9 %combine.6.refs_0_ = f32[128,4,8,128]{3,2,1,0:T(8,128)} custom-call(f32[128,1024]{1,0:T(8,128)} %copy-done, bf16[128,1024]{1,0:T(8,128)(2,1)} %collective-permute-done.28.b_ref, f32[128,4,8,128]{3,2,1,0:T(8,128)} %combine.5.refs_0_), custom_call_target="tpu_custom_call", output_to_operand_aliasing={{}: (2, {})} | custom-call | flops 131072 | bytes 1310720 | tf_op jit(solution)/shard_map/combine/pallas_call | solution.py:326
  118.5 4.6 %collective-permute-done.27.b_ref = bf16[128,1024]{1,0:T(8,128)(2,1)S(1)} collective-permute-done((bf16[128,1024]{1,0:T(8,128)(2,1)}, bf16[128,1024]{1,0:T(8,128)(2,1)S(1)}, u32[]{:S(2)}, u32[]{:S(2)}) %collective-permute-start.27) | collective-permute-done | bytes 262176 | tf_op jit(solution)/shard_map/ppermute | solution.py:33
  123.1 0.7 copy-done.13
  123.8 1.9 %combine.7 = f32[128,4,8,128]{3,2,1,0:T(8,128)} custom-call(f32[128,1024]{1,0:T(8,128)} %copy-done.1, bf16[128,1024]{1,0:T(8,128)(2,1)} %copy-done.13, f32[128,4,8,128]{3,2,1,0:T(8,128)} %combine.6.refs_0_), custom_call_target="tpu_custom_call", output_to_operand_aliasing={{}: (2, {})} | custom-call | flops 131072 | bytes 1310720 | tf_op jit(solution)/shard_map/combine/pallas_call | solution.py:326
  (60 shorter events, 4.2 us)
Async XLA Ops:
  2.4 10.4 %copy-start.11 = (bf16[256,512]{1,0:T(8,128)(2,1)S(1)}, bf16[256,512]{1,0:T(8,128)(2,1)}, u32[]{:S(2)}) copy-start(bf16[256,512]{1,0:T(8,128)(2,1)} %split_slice.1) | copy-start | bytes 786436
  2.4 10.4 %collective-permute-start.1 = (bf16[256,512]{1,0:T(8,128)(2,1)}, bf16[256,512]{1,0:T(8,128)(2,1)S(1)}, u32[]{:S(2)}, u32[]{:S(2)}) collective-permute-start(bf16[256,512]{1,0:T(8,128)(2,1)} %split_slice.1), channel_id=1, source_target_pairs={{0,16},{1,17},{2,18},{3,19},{4,20},{5,21},{6,22},{7,23},{8,24},{9,... | collective-permute-start | bytes 786440 | tf_op jit(solution)/shard_map/ppermute | solution.py:33
  7.2 7.8 %collective-permute-start = (bf16[131,8,128]{2,1,0:T(8,128)(2,1)}, bf16[131,8,128]{2,1,0:T(8,128)(2,1)S(1)}, u32[]{:S(2)}, u32[]{:S(2)}) collective-permute-start(bf16[131,8,128]{2,1,0:T(8,128)(2,1)} %get-tuple-element.41), channel_id=1, source_target_pairs={{1,2},{3,4},{5,6},{7,8},{9,10},{11,12},{13,14},{2,1},{4,3},{6,5},{... | collective-permute-start | bytes 804872 | tf_op jit(solution)/shard_map/ppermute | solution.py:346
  7.8 7.1 %collective-permute-start.2 = (bf16[129,2,8,128]{3,2,1,0:T(8,128)(2,1)}, bf16[129,2,8,128]{3,2,1,0:T(8,128)(2,1)S(1)}, u32[]{:S(2)}, u32[]{:S(2)}) collective-permute-start(bf16[129,2,8,128]{3,2,1,0:T(8,128)(2,1)} %get-tuple-element.43), channel_id=1, source_target_pairs={{0,1},{1,0},{2,3},{3,2},{4,5},{5,4},{6,7},{7,6},{8,9},{9,8},{10,11... | collective-permute-start | bytes 1585160 | tf_op jit(solution)/shard_map/ppermute | solution.py:33
  12.9 11.0 %collective-permute-start.4 = (bf16[256,512]{1,0:T(8,128)(2,1)S(1)}, bf16[256,512]{1,0:T(8,128)(2,1)S(1)}, u32[]{:S(2)}, u32[]{:S(2)}) collective-permute-start(bf16[256,512]{1,0:T(8,128)(2,1)S(1)} %pad_maximum_fusion.1), channel_id=1, source_target_pairs={{0,18},{1,19},{2,16},{3,17},{4,22},{5,23},{6,20},{7,21},{8,26},{9,... | collective-permute-start | bytes 786440 | tf_op jit(solution)/shard_map/ppermute | solution.py:33
  14.9 0.7 copy-start.10
  15.6 0.8 copy-start.9
  24.0 4.9 %collective-permute-start.7 = (bf16[512,512]{1,0:T(8,128)(2,1)S(1)}, bf16[512,512]{1,0:T(8,128)(2,1)S(1)}, u32[]{:S(2)}, u32[]{:S(2)}) collective-permute-start(bf16[512,512]{1,0:T(8,128)(2,1)S(1)} %pad_maximum_fusion.refs_4_), channel_id=1, source_target_pairs={{0,1},{1,0},{2,3},{3,2},{4,5},{5,4},{6,7},{7,6},{8,9},{9,8},{10,11... | collective-permute-start | bytes 1572872 | tf_op jit(solution)/shard_map/ppermute | solution.py:33
  25.5 15.8 %collective-permute-start.5 = (bf16[512,512]{1,0:T(8,128)(2,1)S(1)}, bf16[512,512]{1,0:T(8,128)(2,1)S(1)}, u32[]{:S(2)}, u32[]{:S(2)}) collective-permute-start(bf16[512,512]{1,0:T(8,128)(2,1)S(1)} %pad_maximum_fusion.refs_4_), channel_id=1, source_target_pairs={{0,4},{1,5},{2,6},{3,7},{4,8},{5,9},{6,10},{7,11},{8,12},{9,13},{1... | collective-permute-start | bytes 1572872 | tf_op jit(solution)/shard_map/ppermute | solution.py:33
  27.6 13.8 %collective-permute-start.6 = (bf16[512,512]{1,0:T(8,128)(2,1)S(1)}, bf16[512,512]{1,0:T(8,128)(2,1)S(1)}, u32[]{:S(2)}, u32[]{:S(2)}) collective-permute-start(bf16[512,512]{1,0:T(8,128)(2,1)S(1)} %pad_maximum_fusion.refs_4_), channel_id=1, source_target_pairs={{0,12},{1,13},{2,14},{3,15},{4,0},{5,1},{6,2},{7,3},{8,4},{9,5},{1... | collective-permute-start | bytes 1572872 | tf_op jit(solution)/shard_map/ppermute | solution.py:33
  28.9 15.3 %collective-permute-start.8 = (bf16[128,2048]{1,0:T(8,128)(2,1)}, bf16[128,2048]{1,0:T(8,128)(2,1)S(1)}, u32[]{:S(2)}, u32[]{:S(2)}) collective-permute-start(bf16[128,2048]{1,0:T(8,128)(2,1)} %get-tuple-element.48.refs_14_), channel_id=1, source_target_pairs={{0,32},{1,33},{2,34},{3,35},{4,36},{5,37},{6,38},{7,39},{8,40},{9,... | collective-permute-start | bytes 1572872 | tf_op jit(solution)/shard_map/ppermute | solution.py:33
  30.5 13.7 %collective-permute-start.9 = (bf16[128,2048]{1,0:T(8,128)(2,1)}, bf16[128,2048]{1,0:T(8,128)(2,1)S(1)}, u32[]{:S(2)}, u32[]{:S(2)}) collective-permute-start(bf16[128,2048]{1,0:T(8,128)(2,1)} %get-tuple-element.48.refs_14_), channel_id=1, source_target_pairs={{0,96},{1,97},{2,98},{3,99},{4,100},{5,101},{6,102},{7,103},{8,104... | collective-permute-start | bytes 1572872 | tf_op jit(solution)/shard_map/ppermute | solution.py:33
  32.2 3.9 %collective-permute-start.10 = (bf16[2,4,8,128]{3,2,1,0:T(8,128)(2,1)}, bf16[2,4,8,128]{3,2,1,0:T(8,128)(2,1)S(1)}, u32[]{:S(2)}, u32[]{:S(2)}) collective-permute-start(bf16[2,4,8,128]{3,2,1,0:T(8,128)(2,1)} %get-tuple-element.52), channel_id=1, source_target_pairs={{0,16},{1,17},{2,18},{3,19},{4,20},{5,21},{6,22},{7,23},{8,24},{9,... | collective-permute-start | bytes 49160 | tf_op jit(solution)/shard_map/ppermute | solution.py:33
  36.1 13.2 %collective-permute-start.3 = (bf16[128,8,128]{2,1,0:T(8,128)(2,1)}, bf16[128,8,128]{2,1,0:T(8,128)(2,1)S(1)}, u32[]{:S(2)}, u32[]{:S(2)}) collective-permute-start(bf16[128,8,128]{2,1,0:T(8,128)(2,1)} %get-tuple-element.45), channel_id=1, source_target_pairs={{1,2},{3,4},{5,6},{7,8},{9,10},{11,12},{13,14},{2,1},{4,3},{6,5},{... | collective-permute-start | bytes 786440 | tf_op jit(solution)/shard_map/ppermute | solution.py:352
  44.2 7.8 %collective-permute-start.11 = (bf16[4,4,8,128]{3,2,1,0:T(8,128)(2,1)S(1)}, bf16[4,4,8,128]{3,2,1,0:T(8,128)(2,1)S(1)}, u32[]{:S(2)}, u32[]{:S(2)}) collective-permute-start(bf16[4,4,8,128]{3,2,1,0:T(8,128)(2,1)S(1)} %pad_maximum_fusion.2.refs_0_), channel_id=1, source_target_pairs={{0,96},{1,97},{2,98},{3,99},{4,100},{5,101},{6,102},{7,103},{8,104... | collective-permute-start | bytes 98312 | tf_op jit(solution)/shard_map/ppermute | solution.py:33
  47.1 7.0 %collective-permute-start.12 = (bf16[4,4,8,128]{3,2,1,0:T(8,128)(2,1)S(1)}, bf16[4,4,8,128]{3,2,1,0:T(8,128)(2,1)S(1)}, u32[]{:S(2)}, u32[]{:S(2)}) collective-permute-start(bf16[4,4,8,128]{3,2,1,0:T(8,128)(2,1)S(1)} %pad_maximum_fusion.2.refs_0_), channel_id=1, source_target_pairs={{0,64},{1,65},{2,66},{3,67},{4,68},{5,69},{6,70},{7,71},{8,72},{9,... | collective-permute-start | bytes 98312 | tf_op jit(solution)/shard_map/ppermute | solution.py:33
  47.8 6.3 %collective-permute-start.13 = (bf16[4,4,8,128]{3,2,1,0:T(8,128)(2,1)S(1)}, bf16[4,4,8,128]{3,2,1,0:T(8,128)(2,1)S(1)}, u32[]{:S(2)}, u32[]{:S(2)}) collective-permute-start(bf16[4,4,8,128]{3,2,1,0:T(8,128)(2,1)S(1)} %pad_maximum_fusion.2.refs_0_), channel_id=1, source_target_pairs={{0,32},{1,33},{2,34},{3,35},{4,36},{5,37},{6,38},{7,39},{8,40},{9,... | collective-permute-start | bytes 98312 | tf_op jit(solution)/shard_map/ppermute | solution.py:33
  48.6 7.7 %collective-permute-start.14 = (bf16[256,512]{1,0:T(8,128)(2,1)S(1)}, bf16[256,512]{1,0:T(8,128)(2,1)S(1)}, u32[]{:S(2)}, u32[]{:S(2)}) collective-permute-start(bf16[256,512]{1,0:T(8,128)(2,1)S(1)} %slice.34), channel_id=1, source_target_pairs={{0,4},{1,5},{2,6},{3,7},{4,8},{5,9},{6,10},{7,11},{8,12},{9,13},{1... | collective-permute-start | bytes 786440 | tf_op jit(solution)/shard_map/ppermute | solution.py:33
  49.4 2.6 %copy-start.12 = (bf16[128,8,128]{2,1,0:T(8,128)(2,1)}, bf16[128,8,128]{2,1,0:T(8,128)(2,1)S(1)}, u32[]{:S(2)}) copy-start(bf16[128,8,128]{2,1,0:T(8,128)(2,1)S(1)} %collective-permute-done.3.next_ref) | copy-start | bytes 786436
  49.4 9.4 %collective-permute-start.15 = (bf16[256,512]{1,0:T(8,128)(2,1)S(1)}, bf16[256,512]{1,0:T(8,128)(2,1)}, u32[]{:S(2)}, u32[]{:S(2)}) collective-permute-start(bf16[256,512]{1,0:T(8,128)(2,1)S(1)} %slice.35), channel_id=1, source_target_pairs={{0,12},{1,13},{2,14},{3,15},{4,0},{5,1},{6,2},{7,3},{8,4},{9,5},{1... | collective-permute-start | bytes 786440 | tf_op jit(solution)/shard_map/ppermute | solution.py:33
  52.0 7.6 %collective-permute-start.20 = (bf16[64,2048]{1,0:T(8,128)(2,1)S(1)}, bf16[64,2048]{1,0:T(8,128)(2,1)S(1)}, u32[]{:S(2)}, u32[]{:S(2)}) collective-permute-start(bf16[64,2048]{1,0:T(8,128)(2,1)S(1)} %slice.36), channel_id=1, source_target_pairs={{0,32},{1,33},{2,34},{3,35},{4,36},{5,37},{6,38},{7,39},{8,40},{9,... | collective-permute-start | bytes 786440 | tf_op jit(solution)/shard_map/ppermute | solution.py:33
  54.1 15.0 %collective-permute-start.16 = (bf16[512,512]{1,0:T(8,128)(2,1)S(1)}, bf16[512,512]{1,0:T(8,128)(2,1)}, u32[]{:S(2)}, u32[]{:S(2)}) collective-permute-start(bf16[512,512]{1,0:T(8,128)(2,1)S(1)} %collective-permute-done.5.refs_5_), channel_id=1, source_target_pairs={{0,1},{1,0},{2,3},{3,2},{4,5},{5,4},{6,7},{7,6},{8,9},{9,8},{10,11... | collective-permute-start | bytes 1572872 | tf_op jit(solution)/shard_map/ppermute | solution.py:33
  54.1 15.0 %collective-permute-start.17 = (bf16[512,512]{1,0:T(8,128)(2,1)S(1)}, bf16[512,512]{1,0:T(8,128)(2,1)}, u32[]{:S(2)}, u32[]{:S(2)}) collective-permute-start(bf16[512,512]{1,0:T(8,128)(2,1)S(1)} %collective-permute-done.6.refs_6_), channel_id=1, source_target_pairs={{0,1},{1,0},{2,3},{3,2},{4,5},{5,4},{6,7},{7,6},{8,9},{9,8},{10,11... | collective-permute-start | bytes 1572872 | tf_op jit(solution)/shard_map/ppermute | solution.py:33
  56.2 9.2 %collective-permute-start.21 = (bf16[64,2048]{1,0:T(8,128)(2,1)}, bf16[64,2048]{1,0:T(8,128)(2,1)}, u32[]{:S(2)}, u32[]{:S(2)}) collective-permute-start(bf16[64,2048]{1,0:T(8,128)(2,1)} %slice.37), channel_id=1, source_target_pairs={{0,96},{1,97},{2,98},{3,99},{4,100},{5,101},{6,102},{7,103},{8,104... | collective-permute-start | bytes 786440 | tf_op jit(solution)/shard_map/ppermute | solution.py:33
  58.8 8.0 %collective-permute-start.18 = (bf16[256,512]{1,0:T(8,128)(2,1)S(1)}, bf16[256,512]{1,0:T(8,128)(2,1)}, u32[]{:S(2)}, u32[]{:S(2)}) collective-permute-start(bf16[256,512]{1,0:T(8,128)(2,1)S(1)} %collective-permute-done.14.refs_7_), channel_id=1, source_target_pairs={{0,1},{1,0},{2,3},{3,2},{4,5},{5,4},{6,7},{7,6},{8,9},{9,8},{10,11... | collective-permute-start | bytes 786440 | tf_op jit(solution)/shard_map/ppermute | solution.py:33
  59.6 0.7 copy-start.7
  60.3 8.8 %collective-permute-start.19 = (bf16[256,512]{1,0:T(8,128)(2,1)}, bf16[256,512]{1,0:T(8,128)(2,1)}, u32[]{:S(2)}, u32[]{:S(2)}) collective-permute-start(bf16[256,512]{1,0:T(8,128)(2,1)} %collective-permute-done.15.refs_8_), channel_id=1, source_target_pairs={{0,1},{1,0},{2,3},{3,2},{4,5},{5,4},{6,7},{7,6},{8,9},{9,8},{10,11... | collective-permute-start | bytes 786440 | tf_op jit(solution)/shard_map/ppermute | solution.py:33
  65.4 23.8 %collective-permute-start.25 = (bf16[128,2048]{1,0:T(8,128)(2,1)}, bf16[128,2048]{1,0:T(8,128)(2,1)S(1)}, u32[]{:S(2)}, u32[]{:S(2)}) collective-permute-start(bf16[128,2048]{1,0:T(8,128)(2,1)} %get-tuple-element.68.refs_14_), channel_id=1, source_target_pairs={{0,64},{1,65},{2,66},{3,67},{4,68},{5,69},{6,70},{7,71},{8,72},{9,... | collective-permute-start | bytes 1572872 | tf_op jit(solution)/shard_map/ppermute | solution.py:33
  66.8 30.8 %collective-permute-start.23 = (bf16[128,2048]{1,0:T(8,128)(2,1)}, bf16[128,2048]{1,0:T(8,128)(2,1)}, u32[]{:S(2)}, u32[]{:S(2)}) collective-permute-start(bf16[128,2048]{1,0:T(8,128)(2,1)} %get-tuple-element.68.refs_14_), channel_id=1, source_target_pairs={{0,96},{1,97},{2,98},{3,99},{4,100},{5,101},{6,102},{7,103},{8,104... | collective-permute-start | bytes 1572872 | tf_op jit(solution)/shard_map/ppermute | solution.py:33
  69.1 28.5 %collective-permute-start.24 = (bf16[128,2048]{1,0:T(8,128)(2,1)}, bf16[128,2048]{1,0:T(8,128)(2,1)}, u32[]{:S(2)}, u32[]{:S(2)}) collective-permute-start(bf16[128,2048]{1,0:T(8,128)(2,1)} %get-tuple-element.68.refs_14_), channel_id=1, source_target_pairs={{0,32},{1,33},{2,34},{3,35},{4,36},{5,37},{6,38},{7,39},{8,40},{9,... | collective-permute-start | bytes 1572872 | tf_op jit(solution)/shard_map/ppermute | solution.py:33
  69.1 1.0 copy-start.4
  70.2 0.9 copy-start.8
  71.1 7.4 %copy-start.5 = (bf16[128,2048]{1,0:T(8,128)(2,1)S(1)}, bf16[128,2048]{1,0:T(8,128)(2,1)}, u32[]{:S(2)}) copy-start(bf16[128,2048]{1,0:T(8,128)(2,1)} %get-tuple-element.48.refs_14_) | copy-start | bytes 1572868
  78.4 8.1 %copy-start.3 = (f32[128,1024]{1,0:T(8,128)}, f32[128,1024]{1,0:T(8,128)S(1)}, u32[]{:S(2)}) copy-start(f32[128,1024]{1,0:T(8,128)S(1)} %get-tuple-element.57.a_ref) | copy-start | bytes 1572868
  78.4 10.9 %collective-permute-start.22 = (bf16[128,1024]{1,0:T(8,128)(2,1)S(1)}, bf16[128,1024]{1,0:T(8,128)(2,1)}, u32[]{:S(2)}, u32[]{:S(2)}) collective-permute-start(bf16[128,1024]{1,0:T(8,128)(2,1)S(1)} %get-tuple-element.63), channel_id=1, source_target_pairs={{0,16},{1,17},{2,18},{3,19},{4,20},{5,21},{6,22},{7,23},{8,24},{9,... | collective-permute-start | bytes 786440 | tf_op jit(solution)/shard_map/ppermute | solution.py:33
  86.5 0.8 copy-start.2
  87.3 8.5 %collective-permute-start.26 = (bf16[128,1024]{1,0:T(8,128)(2,1)}, bf16[128,1024]{1,0:T(8,128)(2,1)}, u32[]{:S(2)}, u32[]{:S(2)}) collective-permute-start(bf16[128,1024]{1,0:T(8,128)(2,1)} %get-tuple-element.70), channel_id=1, source_target_pairs={{0,16},{1,17},{2,18},{3,19},{4,20},{5,21},{6,22},{7,23},{8,24},{9,... | collective-permute-start | bytes 786440 | tf_op jit(solution)/shard_map/ppermute | solution.py:33
  91.2 6.4 %copy-start.6 = (bf16[128,2048]{1,0:T(8,128)(2,1)S(1)}, bf16[128,2048]{1,0:T(8,128)(2,1)}, u32[]{:S(2)}) copy-start(bf16[128,2048]{1,0:T(8,128)(2,1)} %get-tuple-element.68.refs_14_) | copy-start | bytes 1572868
  105.0 0.8 copy-start
  105.8 10.8 %collective-permute-start.28 = (bf16[128,1024]{1,0:T(8,128)(2,1)S(1)}, bf16[128,1024]{1,0:T(8,128)(2,1)}, u32[]{:S(2)}, u32[]{:S(2)}) collective-permute-start(bf16[128,1024]{1,0:T(8,128)(2,1)S(1)} %get-tuple-element.77), channel_id=1, source_target_pairs={{0,16},{1,17},{2,18},{3,19},{4,20},{5,21},{6,22},{7,23},{8,24},{9,... | collective-permute-start | bytes 786440 | tf_op jit(solution)/shard_map/ppermute | solution.py:33
  115.4 0.8 copy-start.1
  116.2 6.9 %collective-permute-start.27 = (bf16[128,1024]{1,0:T(8,128)(2,1)}, bf16[128,1024]{1,0:T(8,128)(2,1)S(1)}, u32[]{:S(2)}, u32[]{:S(2)}) collective-permute-start(bf16[128,1024]{1,0:T(8,128)(2,1)} %get-tuple-element.76), channel_id=1, source_target_pairs={{0,16},{1,17},{2,18},{3,19},{4,20},{5,21},{6,22},{7,23},{8,24},{9,... | collective-permute-start | bytes 786440 | tf_op jit(solution)/shard_map/ppermute | solution.py:33
  123.1 0.7 copy-start.13

commit v7 on v6

--- a/solution.py
+++ b/solution.py
@@ -371,14 +371,15 @@
     across = shift(block, dy=2)
     outside = [block, behind, before, across[:64], across[64:]]
 
-    results, got = [None], []
+    waiting, result = [], None
     for layers, blocks in zip(BLOCKS, (inside, outside), strict=True):
         for place, layer in enumerate(layers):
             mine, other = collide(layer, place, pieces, blocks, weights)
-            weights = after(weights, mine, *got[-1:], *results[1:][-1:])
-            got.append(shift(other, dz=1))
-            results.append(combine(layer, mine, got[-1], results[-1]))
-    return transported, results[-1]
+            weights = after(weights, mine, *[got for _, _, got in waiting[:-1]])
+            if waiting:
+                result = combine(*waiting[-1][:2], after(waiting[-1][2], mine), result)
+            waiting.append((layer, mine, shift(other, dz=1)))
+    return transported, combine(*waiting[-1], result)
 
 
 def solution(mesh):

time: 126 us -> 123 us (0.976)
  starting transfers between devices: 39.1 us -> 35.9 us
  Pallas kernels: 52.3 us -> 50.2 us
  local copies, waits for them, and re-layouts: 8.13 us -> 10.2 us
    ppermute x27, starting transfers between devices: 37.8 us -> 34.5 us  [shift(): return lax.ppermute(value, BOTH, pairs)]
    unnamed x28 -> x32, local copies, waits for them, and re-layouts: 7.28 us -> 9.33 us
    pallas_call x4, Pallas kernels: 30.5 us -> 28.5 us  [collide(): pl.pallas_call(kernel, out_shape=(shape((128, cells), F32), shape((128, c...]
  transfers between devices with their start and end apart: 29 -> 29, of which waited for: 9 -> 10; matrix products, arithmetic and copies ran while one was open for 1% -> 1% of each run, Pallas kernels for 33% -> 38%
where the time goes in v7:
time: 123 us
  Pallas kernels  50.2 us (41%)
  starting transfers between devices  35.9 us (29%)
  waiting for transfers between devices  24.8 us (20%)
  local copies, waits for them, and re-layouts  10.2 us (8%)
    ppermute x27, starting transfers between devices, shift(): return lax.ppermute(value, BOTH, pairs)  34.5 us
    pallas_call x4, Pallas kernels, collide(): pl.pallas_call(kernel, out_shape=(shape((128, cells), F32), shape((128, c...  28.5 us
    ppermute x27, waiting for transfers between devices, shift(): return lax.ppermute(value, BOTH, pairs)  24.8 us
    unnamed x32, local copies, waits for them, and re-layouts  9.33 us
    pallas_call x4, Pallas kernels, combine(): pl.pallas_call(kernel, grid=(128 // step,), out_shape=shape((128, 4, 8, 1...  7.58 us
    pallas_call x1, Pallas kernels, transport(): pl.pallas_call(kernel, grid=(rows // STEP,), out_shape=(shape(density.sha...  5.15 us
    pallas_call x1, Pallas kernels, transport_inner(): pl.pallas_call(kernel, grid=(rows // STEP,), out_shape=(shape((rows, 2048...  4.48 us
    pallas_call x1, Pallas kernels, pack(): pl.pallas_call(kernel, out_shape=(shape((rows + 3, *dims), BF16), shape((...  2.73 us
  transfers between devices with their start and end apart: 29, of which 10 were waited for; matrix products, arithmetic and copies ran while one was open for 1% of the time, Pallas kernels for 38%

profile of v7, /device:TPU:0, one launch (start us, length us, event | category | flops | bytes accessed | tf_op | source)
XLA Modules:
  0.0 122.7 jit_solution(7235837944586513688)
XLA Ops:
  0.6 1.8 %split_slice.1 = bf16[256,512]{1,0:T(8,128)(2,1)} custom-call(bf16[4,2,128,128]{3,2,1,0:T(8,128)(2,1)} %bitcast.1), custom_call_target="tpu_custom_call" | custom-call | tf_op jit(solution)/shard_map/split_slice/pallas_call | solution.py:89
  2.4 2.0 %collective-permute-start.1 = (bf16[256,512]{1,0:T(8,128)(2,1)}, bf16[256,512]{1,0:T(8,128)(2,1)S(1)}, u32[]{:S(2)}, u32[]{:S(2)}) collective-permute-start(bf16[256,512]{1,0:T(8,128)(2,1)} %split_slice.1), channel_id=1, source_target_pairs={{0,16},{1,17},{2,18},{3,19},{4,20},{5,21},{6,22},{7,23},{8,24},{9,... | collective-permute-start | bytes 786440 | tf_op jit(solution)/shard_map/ppermute | solution.py:33
  4.4 2.7 %pack.1 = (bf16[131,8,128]{2,1,0:T(8,128)(2,1)}, bf16[128,8,128]{2,1,0:T(8,128)(2,1)}, bf16[129,2,8,128]{3,2,1,0:T(8,128)(2,1)}) custom-call(f32[128,4,8,128]{3,2,1,0:T(8,128)} %d_ref.4, s32[4,8,128]{2,1,0:T(8,128)} %l_ref.5), custom_call_target="tpu_custom_call" | custom-call | tf_op jit(solution)/shard_map/pack/pallas_call | solution.py:68
  7.8 5.0 %collective-permute-start.2 = (bf16[129,2,8,128]{3,2,1,0:T(8,128)(2,1)}, bf16[129,2,8,128]{3,2,1,0:T(8,128)(2,1)S(1)}, u32[]{:S(2)}, u32[]{:S(2)}) collective-permute-start(bf16[129,2,8,128]{3,2,1,0:T(8,128)(2,1)} %get-tuple-element.46), channel_id=1, source_target_pairs={{0,1},{1,0},{2,3},{3,2},{4,5},{5,4},{6,7},{7,6},{8,9},{9,8},{10,11... | collective-permute-start | bytes 1585160 | tf_op jit(solution)/shard_map/ppermute | solution.py:33
  12.9 2.0 %collective-permute-start.4 = (bf16[256,512]{1,0:T(8,128)(2,1)S(1)}, bf16[256,512]{1,0:T(8,128)(2,1)S(1)}, u32[]{:S(2)}, u32[]{:S(2)}) collective-permute-start(bf16[256,512]{1,0:T(8,128)(2,1)S(1)} %pad_maximum_fusion.1), channel_id=1, source_target_pairs={{0,18},{1,19},{2,16},{3,17},{4,22},{5,23},{6,20},{7,21},{8,26},{9,... | collective-permute-start | bytes 786440 | tf_op jit(solution)/shard_map/ppermute | solution.py:33
  14.9 0.7 copy-done.10
  15.7 0.8 copy-done.9
  16.4 4.5 %transport_inner.1 = (bf16[128,2048]{1,0:T(8,128)(2,1)}, bf16[2,4,8,128]{3,2,1,0:T(8,128)(2,1)}) custom-call(s32[128]{0:T(128)} %h_ref.3, f32[128]{0:T(128)} %c_ref.3, f32[128,4,8,128]{3,2,1,0:T(8,128)} %d_ref.4, s32[4,8,128]{2,1,0:T(8,128)} %l_ref.5, bf16[131,8,128]{2,1,0:T(8,128)(2,1)} %copy-done.10, bf16[131,8,128]{2,1,0:T(8,128)(2,1)} %copy-done.10, ...), custom_call_target="tpu_custom_call" | custom-call | flops 2097152 | bytes 3145728 | tf_op jit(solution)/shard_map/transport_inner/pallas_call | solution.py:182
  20.9 3.0 %collective-permute-done.4 = bf16[256,512]{1,0:T(8,128)(2,1)S(1)} collective-permute-done((bf16[256,512]{1,0:T(8,128)(2,1)S(1)}, bf16[256,512]{1,0:T(8,128)(2,1)S(1)}, u32[]{:S(2)}, u32[]{:S(2)}) %collective-permute-start.4) | collective-permute-done | bytes 262176 | tf_op jit(solution)/shard_map/ppermute | solution.py:33
  24.0 1.5 %collective-permute-start.7 = (bf16[512,512]{1,0:T(8,128)(2,1)S(1)}, bf16[512,512]{1,0:T(8,128)(2,1)S(1)}, u32[]{:S(2)}, u32[]{:S(2)}) collective-permute-start(bf16[512,512]{1,0:T(8,128)(2,1)S(1)} %pad_maximum_fusion.refs_4_), channel_id=1, source_target_pairs={{0,1},{1,0},{2,3},{3,2},{4,5},{5,4},{6,7},{7,6},{8,9},{9,8},{10,11... | collective-permute-start | bytes 1572872 | tf_op jit(solution)/shard_map/ppermute | solution.py:33
  25.5 3.5 %collective-permute-start.6 = (bf16[512,512]{1,0:T(8,128)(2,1)S(1)}, bf16[512,512]{1,0:T(8,128)(2,1)S(1)}, u32[]{:S(2)}, u32[]{:S(2)}) collective-permute-start(bf16[512,512]{1,0:T(8,128)(2,1)S(1)} %pad_maximum_fusion.refs_4_), channel_id=1, source_target_pairs={{0,12},{1,13},{2,14},{3,15},{4,0},{5,1},{6,2},{7,3},{8,4},{9,5},{1... | collective-permute-start | bytes 1572872 | tf_op jit(solution)/shard_map/ppermute | solution.py:33
  28.9 3.0 %collective-permute-start.9 = (bf16[128,2048]{1,0:T(8,128)(2,1)}, bf16[128,2048]{1,0:T(8,128)(2,1)S(1)}, u32[]{:S(2)}, u32[]{:S(2)}) collective-permute-start(bf16[128,2048]{1,0:T(8,128)(2,1)} %get-tuple-element.51.refs_14_), channel_id=1, source_target_pairs={{0,96},{1,97},{2,98},{3,99},{4,100},{5,101},{6,102},{7,103},{8,104... | collective-permute-start | bytes 1572872 | tf_op jit(solution)/shard_map/ppermute | solution.py:33
  32.0 3.9 %collective-permute-done.10 = bf16[2,4,8,128]{3,2,1,0:T(8,128)(2,1)S(1)} collective-permute-done((bf16[2,4,8,128]{3,2,1,0:T(8,128)(2,1)}, bf16[2,4,8,128]{3,2,1,0:T(8,128)(2,1)S(1)}, u32[]{:S(2)}, u32[]{:S(2)}) %collective-permute-start.10) | collective-permute-done | bytes 16416 | tf_op jit(solution)/shard_map/ppermute | solution.py:33
  36.6 0.7 pad_maximum_fusion.2.refs_0_
  37.3 3.2 %collective-permute-done.6.refs_6_ = bf16[512,512]{1,0:T(8,128)(2,1)S(1)} collective-permute-done((bf16[512,512]{1,0:T(8,128)(2,1)S(1)}, bf16[512,512]{1,0:T(8,128)(2,1)S(1)}, u32[]{:S(2)}, u32[]{:S(2)}) %collective-permute-start.6) | collective-permute-done | bytes 524320 | tf_op jit(solution)/shard_map/ppermute | solution.py:33
  40.5 3.4 %collective-permute-done.5.refs_5_ = bf16[512,512]{1,0:T(8,128)(2,1)S(1)} collective-permute-done((bf16[512,512]{1,0:T(8,128)(2,1)S(1)}, bf16[512,512]{1,0:T(8,128)(2,1)S(1)}, u32[]{:S(2)}, u32[]{:S(2)}) %collective-permute-start.5) | collective-permute-done | bytes 524320 | tf_op jit(solution)/shard_map/ppermute | solution.py:33
  43.9 2.9 %collective-permute-done.8.refs_16_ = bf16[128,2048]{1,0:T(8,128)(2,1)S(1)} collective-permute-done((bf16[128,2048]{1,0:T(8,128)(2,1)}, bf16[128,2048]{1,0:T(8,128)(2,1)S(1)}, u32[]{:S(2)}, u32[]{:S(2)}) %collective-permute-start.8) | collective-permute-done | bytes 524320 | tf_op jit(solution)/shard_map/ppermute | solution.py:33
  46.9 1.7 %collective-permute-start.12 = (bf16[4,4,8,128]{3,2,1,0:T(8,128)(2,1)S(1)}, bf16[4,4,8,128]{3,2,1,0:T(8,128)(2,1)S(1)}, u32[]{:S(2)}, u32[]{:S(2)}) collective-permute-start(bf16[4,4,8,128]{3,2,1,0:T(8,128)(2,1)S(1)} %pad_maximum_fusion.2.refs_0_), channel_id=1, source_target_pairs={{0,64},{1,65},{2,66},{3,67},{4,68},{5,69},{6,70},{7,71},{8,72},{9,... | collective-permute-start | bytes 98312 | tf_op jit(solution)/shard_map/ppermute | solution.py:33
  48.6 1.5 %collective-permute-start.11 = (bf16[4,4,8,128]{3,2,1,0:T(8,128)(2,1)S(1)}, bf16[4,4,8,128]{3,2,1,0:T(8,128)(2,1)S(1)}, u32[]{:S(2)}, u32[]{:S(2)}) collective-permute-start(bf16[4,4,8,128]{3,2,1,0:T(8,128)(2,1)S(1)} %pad_maximum_fusion.2.refs_0_), channel_id=1, source_target_pairs={{0,96},{1,97},{2,98},{3,99},{4,100},{5,101},{6,102},{7,103},{8,104... | collective-permute-start | bytes 98312 | tf_op jit(solution)/shard_map/ppermute | solution.py:33
  50.1 3.0 %collective-permute-start.15 = (bf16[256,512]{1,0:T(8,128)(2,1)S(1)}, bf16[256,512]{1,0:T(8,128)(2,1)S(1)}, u32[]{:S(2)}, u32[]{:S(2)}) collective-permute-start(bf16[256,512]{1,0:T(8,128)(2,1)S(1)} %slice.35), channel_id=1, source_target_pairs={{0,12},{1,13},{2,14},{3,15},{4,0},{5,1},{6,2},{7,3},{8,4},{9,5},{1... | collective-permute-start | bytes 786440 | tf_op jit(solution)/shard_map/ppermute | solution.py:33
  53.9 0.9 collective-permute-start.20
  55.3 0.7 slice.37
  56.0 1.0 collective-permute-done.15.refs_8_
  57.1 1.4 %collective-permute-start.21 = (bf16[64,2048]{1,0:T(8,128)(2,1)}, bf16[64,2048]{1,0:T(8,128)(2,1)}, u32[]{:S(2)}, u32[]{:S(2)}) collective-permute-start(bf16[64,2048]{1,0:T(8,128)(2,1)} %slice.37), channel_id=1, source_target_pairs={{0,96},{1,97},{2,98},{3,99},{4,100},{5,101},{6,102},{7,103},{8,104... | collective-permute-start | bytes 786440 | tf_op jit(solution)/shard_map/ppermute | solution.py:33
  58.4 2.6 %collective-permute-done.14.refs_7_ = bf16[256,512]{1,0:T(8,128)(2,1)} collective-permute-done((bf16[256,512]{1,0:T(8,128)(2,1)S(1)}, bf16[256,512]{1,0:T(8,128)(2,1)}, u32[]{:S(2)}, u32[]{:S(2)}) %collective-permute-start.14) | collective-permute-done | bytes 262176 | tf_op jit(solution)/shard_map/ppermute | solution.py:33
  61.5 0.7 copy-done.7
  62.2 5.1 %transport.1 = (f32[128,4,8,128]{3,2,1,0:T(8,128)}, bf16[128,2048]{1,0:T(8,128)(2,1)}) custom-call(s32[128]{0:T(128)} %h_ref.3, f32[128]{0:T(128)} %c_ref.3, f32[128,4,8,128]{3,2,1,0:T(8,128)} %d_ref.4, s32[4,8,128]{2,1,0:T(8,128)} %l_ref.5, bf16[131,8,128]{2,1,0:T(8,128)(2,1)} %copy-done.10, bf16[131,8,128]{2,1,0:T(8,128)(2,1)} %copy-done.10, ...), custom_call_target="tpu_custom_call" | custom-call | flops 4194304 | bytes 6291456 | tf_op jit(solution)/shard_map/transport/pallas_call | solution.py:219
  67.4 2.9 %collective-permute-start.24 = (bf16[128,2048]{1,0:T(8,128)(2,1)}, bf16[128,2048]{1,0:T(8,128)(2,1)S(1)}, u32[]{:S(2)}, u32[]{:S(2)}) collective-permute-start(bf16[128,2048]{1,0:T(8,128)(2,1)} %get-tuple-element.70.refs_14_), channel_id=1, source_target_pairs={{0,64},{1,65},{2,66},{3,67},{4,68},{5,69},{6,70},{7,71},{8,72},{9,... | collective-permute-start | bytes 1572872 | tf_op jit(solution)/shard_map/ppermute | solution.py:33
  70.3 3.2 %collective-permute-start.22 = (bf16[128,2048]{1,0:T(8,128)(2,1)}, bf16[128,2048]{1,0:T(8,128)(2,1)S(1)}, u32[]{:S(2)}, u32[]{:S(2)}) collective-permute-start(bf16[128,2048]{1,0:T(8,128)(2,1)} %get-tuple-element.70.refs_14_), channel_id=1, source_target_pairs={{0,96},{1,97},{2,98},{3,99},{4,100},{5,101},{6,102},{7,103},{8,104... | collective-permute-start | bytes 1572872 | tf_op jit(solution)/shard_map/ppermute | solution.py:33
  73.6 1.0 copy-done.4
  74.6 0.9 copy-done.8
  75.6 7.3 %collide.4 = (f32[128,1024]{1,0:T(8,128)S(1)}, bf16[128,1024]{1,0:T(8,128)(2,1)S(1)}) custom-call(bf16[4,4,8,128]{3,2,1,0:T(8,128)(2,1)S(1)} %pad_maximum_fusion.2.refs_0_, bf16[4,4,8,128]{3,2,1,0:T(8,128)(2,1)S(1)} %collective-permute-done.11.refs_1_, bf16[4,4,8,128]{3,2,1,0:T(8,128)(2,1)S(1)} %collective-permute-done.12.refs_2_, ...), custom_call_target="tpu_custom_call" | custom-call | flops 4294967296 | bytes 6291456 | tf_op jit(solution)/shard_map/collide/pallas_call | solution.py:295
  82.9 8.2 %collide.5 = (f32[128,1024]{1,0:T(8,128)S(1)}, bf16[128,1024]{1,0:T(8,128)(2,1)}) custom-call(bf16[4,4,8,128]{3,2,1,0:T(8,128)(2,1)S(1)} %pad_maximum_fusion.2.refs_0_, bf16[4,4,8,128]{3,2,1,0:T(8,128)(2,1)S(1)} %collective-permute-done.11.refs_1_, bf16[4,4,8,128]{3,2,1,0:T(8,128)(2,1)S(1)} %collective-permute-done.12.refs_2_, ...), custom_call_target="tpu_custom_call" | custom-call | flops 4294967296 | bytes 6291456 | tf_op jit(solution)/shard_map/collide/pallas_call | solution.py:295
  91.1 0.8 copy-done
  91.9 2.0 %collective-permute-start.25 = (bf16[128,1024]{1,0:T(8,128)(2,1)S(1)}, bf16[128,1024]{1,0:T(8,128)(2,1)S(1)}, u32[]{:S(2)}, u32[]{:S(2)}) collective-permute-start(bf16[128,1024]{1,0:T(8,128)(2,1)S(1)} %get-tuple-element.72), channel_id=1, source_target_pairs={{0,16},{1,17},{2,18},{3,19},{4,20},{5,21},{6,22},{7,23},{8,24},{9,... | collective-permute-start | bytes 786440 | tf_op jit(solution)/shard_map/ppermute | solution.py:33
  94.0 0.8 collective-permute-done.23.refs_16_
  94.7 6.5 %collide.6 = (f32[128,1024]{1,0:T(8,128)S(1)}, bf16[128,1024]{1,0:T(8,128)(2,1)S(1)}) custom-call(bf16[4,4,8,128]{3,2,1,0:T(8,128)(2,1)S(1)} %pad_maximum_fusion.2.refs_0_, bf16[4,4,8,128]{3,2,1,0:T(8,128)(2,1)S(1)} %collective-permute-done.11.refs_1_, bf16[4,4,8,128]{3,2,1,0:T(8,128)(2,1)S(1)} %collective-permute-done.12.refs_2_, ...), custom_call_target="tpu_custom_call" | custom-call | flops 4294967296 | bytes 6291456 | tf_op jit(solution)/shard_map/collide/pallas_call | solution.py:295
  101.3 0.8 copy-done.1
  102.1 3.3 %collective-permute-done.25.b_ref = bf16[128,1024]{1,0:T(8,128)(2,1)S(1)} collective-permute-done((bf16[128,1024]{1,0:T(8,128)(2,1)S(1)}, bf16[128,1024]{1,0:T(8,128)(2,1)S(1)}, u32[]{:S(2)}, u32[]{:S(2)}) %collective-permute-start.25) | collective-permute-done | bytes 262176 | tf_op jit(solution)/shard_map/ppermute | solution.py:33
  105.4 0.7 copy-done.15
  106.1 6.5 %collide.7 = (f32[128,1024]{1,0:T(8,128)S(1)}, bf16[128,1024]{1,0:T(8,128)(2,1)S(1)}) custom-call(bf16[4,4,8,128]{3,2,1,0:T(8,128)(2,1)S(1)} %pad_maximum_fusion.2.refs_0_, bf16[4,4,8,128]{3,2,1,0:T(8,128)(2,1)S(1)} %collective-permute-done.11.refs_1_, bf16[4,4,8,128]{3,2,1,0:T(8,128)(2,1)S(1)} %collective-permute-done.12.refs_2_, ...), custom_call_target="tpu_custom_call" | custom-call | flops 4294967296 | bytes 6291456 | tf_op jit(solution)/shard_map/collide/pallas_call | solution.py:295
  112.7 0.8 copy-done.2
  113.7 1.9 %combine.4.refs_0_ = f32[128,4,8,128]{3,2,1,0:T(8,128)} custom-call(f32[128,1024]{1,0:T(8,128)} %copy-done.3, bf16[128,1024]{1,0:T(8,128)(2,1)} %copy-done.15), custom_call_target="tpu_custom_call" | custom-call | flops 131072 | bytes 1310720 | tf_op jit(solution)/shard_map/combine/pallas_call | solution.py:326
  115.6 0.7 copy-done.13
  116.3 1.9 %combine.5.refs_0_ = f32[128,4,8,128]{3,2,1,0:T(8,128)} custom-call(f32[128,1024]{1,0:T(8,128)} %copy-done, bf16[128,1024]{1,0:T(8,128)(2,1)} %copy-done.13, f32[128,4,8,128]{3,2,1,0:T(8,128)} %combine.4.refs_0_), custom_call_target="tpu_custom_call", output_to_operand_aliasing={{}: (2, {})} | custom-call | flops 131072 | bytes 1310720 | tf_op jit(solution)/shard_map/combine/pallas_call | solution.py:326
  118.2 1.9 %combine.6.refs_0_ = f32[128,4,8,128]{3,2,1,0:T(8,128)} custom-call(f32[128,1024]{1,0:T(8,128)} %copy-done.1, bf16[128,1024]{1,0:T(8,128)(2,1)} %collective-permute-done.27.b_ref, f32[128,4,8,128]{3,2,1,0:T(8,128)} %combine.5.refs_0_), custom_call_target="tpu_custom_call", output_to_operand_aliasing={{}: (2, {})} | custom-call | flops 131072 | bytes 1310720 | tf_op jit(solution)/shard_map/combine/pallas_call | solution.py:326
  120.1 0.7 copy-done.14
  120.8 1.9 %combine.7 = f32[128,4,8,128]{3,2,1,0:T(8,128)} custom-call(f32[128,1024]{1,0:T(8,128)} %copy-done.2, bf16[128,1024]{1,0:T(8,128)(2,1)} %copy-done.14, f32[128,4,8,128]{3,2,1,0:T(8,128)} %combine.6.refs_0_), custom_call_target="tpu_custom_call", output_to_operand_aliasing={{}: (2, {})} | custom-call | flops 131072 | bytes 1310720 | tf_op jit(solution)/shard_map/combine/pallas_call | solution.py:326
  (64 shorter events, 3.7 us)
Async XLA Ops:
  2.4 10.4 %copy-start.11 = (bf16[256,512]{1,0:T(8,128)(2,1)S(1)}, bf16[256,512]{1,0:T(8,128)(2,1)}, u32[]{:S(2)}) copy-start(bf16[256,512]{1,0:T(8,128)(2,1)} %split_slice.1) | copy-start | bytes 786436
  2.4 10.4 %collective-permute-start.1 = (bf16[256,512]{1,0:T(8,128)(2,1)}, bf16[256,512]{1,0:T(8,128)(2,1)S(1)}, u32[]{:S(2)}, u32[]{:S(2)}) collective-permute-start(bf16[256,512]{1,0:T(8,128)(2,1)} %split_slice.1), channel_id=1, source_target_pairs={{0,16},{1,17},{2,18},{3,19},{4,20},{5,21},{6,22},{7,23},{8,24},{9,... | collective-permute-start | bytes 786440 | tf_op jit(solution)/shard_map/ppermute | solution.py:33
  7.2 7.8 %collective-permute-start = (bf16[131,8,128]{2,1,0:T(8,128)(2,1)}, bf16[131,8,128]{2,1,0:T(8,128)(2,1)S(1)}, u32[]{:S(2)}, u32[]{:S(2)}) collective-permute-start(bf16[131,8,128]{2,1,0:T(8,128)(2,1)} %get-tuple-element.44), channel_id=1, source_target_pairs={{1,2},{3,4},{5,6},{7,8},{9,10},{11,12},{13,14},{2,1},{4,3},{6,5},{... | collective-permute-start | bytes 804872 | tf_op jit(solution)/shard_map/ppermute | solution.py:346
  7.8 7.1 %collective-permute-start.2 = (bf16[129,2,8,128]{3,2,1,0:T(8,128)(2,1)}, bf16[129,2,8,128]{3,2,1,0:T(8,128)(2,1)S(1)}, u32[]{:S(2)}, u32[]{:S(2)}) collective-permute-start(bf16[129,2,8,128]{3,2,1,0:T(8,128)(2,1)} %get-tuple-element.46), channel_id=1, source_target_pairs={{0,1},{1,0},{2,3},{3,2},{4,5},{5,4},{6,7},{7,6},{8,9},{9,8},{10,11... | collective-permute-start | bytes 1585160 | tf_op jit(solution)/shard_map/ppermute | solution.py:33
  12.9 11.0 %collective-permute-start.4 = (bf16[256,512]{1,0:T(8,128)(2,1)S(1)}, bf16[256,512]{1,0:T(8,128)(2,1)S(1)}, u32[]{:S(2)}, u32[]{:S(2)}) collective-permute-start(bf16[256,512]{1,0:T(8,128)(2,1)S(1)} %pad_maximum_fusion.1), channel_id=1, source_target_pairs={{0,18},{1,19},{2,16},{3,17},{4,22},{5,23},{6,20},{7,21},{8,26},{9,... | collective-permute-start | bytes 786440 | tf_op jit(solution)/shard_map/ppermute | solution.py:33
  14.9 0.7 copy-start.10
  15.7 0.8 copy-start.9
  24.0 5.0 %collective-permute-start.7 = (bf16[512,512]{1,0:T(8,128)(2,1)S(1)}, bf16[512,512]{1,0:T(8,128)(2,1)S(1)}, u32[]{:S(2)}, u32[]{:S(2)}) collective-permute-start(bf16[512,512]{1,0:T(8,128)(2,1)S(1)} %pad_maximum_fusion.refs_4_), channel_id=1, source_target_pairs={{0,1},{1,0},{2,3},{3,2},{4,5},{5,4},{6,7},{7,6},{8,9},{9,8},{10,11... | collective-permute-start | bytes 1572872 | tf_op jit(solution)/shard_map/ppermute | solution.py:33
  25.5 15.0 %collective-permute-start.6 = (bf16[512,512]{1,0:T(8,128)(2,1)S(1)}, bf16[512,512]{1,0:T(8,128)(2,1)S(1)}, u32[]{:S(2)}, u32[]{:S(2)}) collective-permute-start(bf16[512,512]{1,0:T(8,128)(2,1)S(1)} %pad_maximum_fusion.refs_4_), channel_id=1, source_target_pairs={{0,12},{1,13},{2,14},{3,15},{4,0},{5,1},{6,2},{7,3},{8,4},{9,5},{1... | collective-permute-start | bytes 1572872 | tf_op jit(solution)/shard_map/ppermute | solution.py:33
  28.9 15.0 %collective-permute-start.5 = (bf16[512,512]{1,0:T(8,128)(2,1)S(1)}, bf16[512,512]{1,0:T(8,128)(2,1)S(1)}, u32[]{:S(2)}, u32[]{:S(2)}) collective-permute-start(bf16[512,512]{1,0:T(8,128)(2,1)S(1)} %pad_maximum_fusion.refs_4_), channel_id=1, source_target_pairs={{0,4},{1,5},{2,6},{3,7},{4,8},{5,9},{6,10},{7,11},{8,12},{9,13},{1... | collective-permute-start | bytes 1572872 | tf_op jit(solution)/shard_map/ppermute | solution.py:33
  28.9 15.0 %collective-permute-start.9 = (bf16[128,2048]{1,0:T(8,128)(2,1)}, bf16[128,2048]{1,0:T(8,128)(2,1)S(1)}, u32[]{:S(2)}, u32[]{:S(2)}) collective-permute-start(bf16[128,2048]{1,0:T(8,128)(2,1)} %get-tuple-element.51.refs_14_), channel_id=1, source_target_pairs={{0,96},{1,97},{2,98},{3,99},{4,100},{5,101},{6,102},{7,103},{8,104... | collective-permute-start | bytes 1572872 | tf_op jit(solution)/shard_map/ppermute | solution.py:33
  32.0 14.9 %collective-permute-start.8 = (bf16[128,2048]{1,0:T(8,128)(2,1)}, bf16[128,2048]{1,0:T(8,128)(2,1)S(1)}, u32[]{:S(2)}, u32[]{:S(2)}) collective-permute-start(bf16[128,2048]{1,0:T(8,128)(2,1)} %get-tuple-element.51.refs_14_), channel_id=1, source_target_pairs={{0,32},{1,33},{2,34},{3,35},{4,36},{5,37},{6,38},{7,39},{8,40},{9,... | collective-permute-start | bytes 1572872 | tf_op jit(solution)/shard_map/ppermute | solution.py:33
  32.0 3.9 %collective-permute-start.10 = (bf16[2,4,8,128]{3,2,1,0:T(8,128)(2,1)}, bf16[2,4,8,128]{3,2,1,0:T(8,128)(2,1)S(1)}, u32[]{:S(2)}, u32[]{:S(2)}) collective-permute-start(bf16[2,4,8,128]{3,2,1,0:T(8,128)(2,1)} %get-tuple-element.55), channel_id=1, source_target_pairs={{0,16},{1,17},{2,18},{3,19},{4,20},{5,21},{6,22},{7,23},{8,24},{9,... | collective-permute-start | bytes 49160 | tf_op jit(solution)/shard_map/ppermute | solution.py:33
  35.9 17.3 %collective-permute-start.3 = (bf16[128,8,128]{2,1,0:T(8,128)(2,1)}, bf16[128,8,128]{2,1,0:T(8,128)(2,1)S(1)}, u32[]{:S(2)}, u32[]{:S(2)}) collective-permute-start(bf16[128,8,128]{2,1,0:T(8,128)(2,1)} %get-tuple-element.48), channel_id=1, source_target_pairs={{1,2},{3,4},{5,6},{7,8},{9,10},{11,12},{13,14},{2,1},{4,3},{6,5},{... | collective-permute-start | bytes 786440 | tf_op jit(solution)/shard_map/ppermute | solution.py:352
  46.9 7.1 %collective-permute-start.13 = (bf16[4,4,8,128]{3,2,1,0:T(8,128)(2,1)S(1)}, bf16[4,4,8,128]{3,2,1,0:T(8,128)(2,1)S(1)}, u32[]{:S(2)}, u32[]{:S(2)}) collective-permute-start(bf16[4,4,8,128]{3,2,1,0:T(8,128)(2,1)S(1)} %pad_maximum_fusion.2.refs_0_), channel_id=1, source_target_pairs={{0,32},{1,33},{2,34},{3,35},{4,36},{5,37},{6,38},{7,39},{8,40},{9,... | collective-permute-start | bytes 98312 | tf_op jit(solution)/shard_map/ppermute | solution.py:33
  46.9 7.9 %collective-permute-start.12 = (bf16[4,4,8,128]{3,2,1,0:T(8,128)(2,1)S(1)}, bf16[4,4,8,128]{3,2,1,0:T(8,128)(2,1)S(1)}, u32[]{:S(2)}, u32[]{:S(2)}) collective-permute-start(bf16[4,4,8,128]{3,2,1,0:T(8,128)(2,1)S(1)} %pad_maximum_fusion.2.refs_0_), channel_id=1, source_target_pairs={{0,64},{1,65},{2,66},{3,67},{4,68},{5,69},{6,70},{7,71},{8,72},{9,... | collective-permute-start | bytes 98312 | tf_op jit(solution)/shard_map/ppermute | solution.py:33
  48.6 6.2 %collective-permute-start.11 = (bf16[4,4,8,128]{3,2,1,0:T(8,128)(2,1)S(1)}, bf16[4,4,8,128]{3,2,1,0:T(8,128)(2,1)S(1)}, u32[]{:S(2)}, u32[]{:S(2)}) collective-permute-start(bf16[4,4,8,128]{3,2,1,0:T(8,128)(2,1)S(1)} %pad_maximum_fusion.2.refs_0_), channel_id=1, source_target_pairs={{0,96},{1,97},{2,98},{3,99},{4,100},{5,101},{6,102},{7,103},{8,104... | collective-permute-start | bytes 98312 | tf_op jit(solution)/shard_map/ppermute | solution.py:33
  50.1 6.9 %collective-permute-start.15 = (bf16[256,512]{1,0:T(8,128)(2,1)S(1)}, bf16[256,512]{1,0:T(8,128)(2,1)S(1)}, u32[]{:S(2)}, u32[]{:S(2)}) collective-permute-start(bf16[256,512]{1,0:T(8,128)(2,1)S(1)} %slice.35), channel_id=1, source_target_pairs={{0,12},{1,13},{2,14},{3,15},{4,0},{5,1},{6,2},{7,3},{8,4},{9,5},{1... | collective-permute-start | bytes 786440 | tf_op jit(solution)/shard_map/ppermute | solution.py:33
  53.2 0.7 copy-start.12
  53.2 7.8 %collective-permute-start.14 = (bf16[256,512]{1,0:T(8,128)(2,1)S(1)}, bf16[256,512]{1,0:T(8,128)(2,1)}, u32[]{:S(2)}, u32[]{:S(2)}) collective-permute-start(bf16[256,512]{1,0:T(8,128)(2,1)S(1)} %slice.34), channel_id=1, source_target_pairs={{0,4},{1,5},{2,6},{3,7},{4,8},{5,9},{6,10},{7,11},{8,12},{9,13},{1... | collective-permute-start | bytes 786440 | tf_op jit(solution)/shard_map/ppermute | solution.py:33
  53.9 7.6 %collective-permute-start.20 = (bf16[64,2048]{1,0:T(8,128)(2,1)S(1)}, bf16[64,2048]{1,0:T(8,128)(2,1)S(1)}, u32[]{:S(2)}, u32[]{:S(2)}) collective-permute-start(bf16[64,2048]{1,0:T(8,128)(2,1)S(1)} %slice.36), channel_id=1, source_target_pairs={{0,32},{1,33},{2,34},{3,35},{4,36},{5,37},{6,38},{7,39},{8,40},{9,... | collective-permute-start | bytes 786440 | tf_op jit(solution)/shard_map/ppermute | solution.py:33
  54.8 18.8 %collective-permute-start.16 = (bf16[512,512]{1,0:T(8,128)(2,1)S(1)}, bf16[512,512]{1,0:T(8,128)(2,1)}, u32[]{:S(2)}, u32[]{:S(2)}) collective-permute-start(bf16[512,512]{1,0:T(8,128)(2,1)S(1)} %collective-permute-done.5.refs_5_), channel_id=1, source_target_pairs={{0,1},{1,0},{2,3},{3,2},{4,5},{5,4},{6,7},{7,6},{8,9},{9,8},{10,11... | collective-permute-start | bytes 1572872 | tf_op jit(solution)/shard_map/ppermute | solution.py:33
  54.8 18.8 %collective-permute-start.17 = (bf16[512,512]{1,0:T(8,128)(2,1)S(1)}, bf16[512,512]{1,0:T(8,128)(2,1)}, u32[]{:S(2)}, u32[]{:S(2)}) collective-permute-start(bf16[512,512]{1,0:T(8,128)(2,1)S(1)} %collective-permute-done.6.refs_6_), channel_id=1, source_target_pairs={{0,1},{1,0},{2,3},{3,2},{4,5},{5,4},{6,7},{7,6},{8,9},{9,8},{10,11... | collective-permute-start | bytes 1572872 | tf_op jit(solution)/shard_map/ppermute | solution.py:33
  57.1 10.3 %collective-permute-start.21 = (bf16[64,2048]{1,0:T(8,128)(2,1)}, bf16[64,2048]{1,0:T(8,128)(2,1)}, u32[]{:S(2)}, u32[]{:S(2)}) collective-permute-start(bf16[64,2048]{1,0:T(8,128)(2,1)} %slice.37), channel_id=1, source_target_pairs={{0,96},{1,97},{2,98},{3,99},{4,100},{5,101},{6,102},{7,103},{8,104... | collective-permute-start | bytes 786440 | tf_op jit(solution)/shard_map/ppermute | solution.py:33
  61.0 9.4 %collective-permute-start.19 = (bf16[256,512]{1,0:T(8,128)(2,1)S(1)}, bf16[256,512]{1,0:T(8,128)(2,1)}, u32[]{:S(2)}, u32[]{:S(2)}) collective-permute-start(bf16[256,512]{1,0:T(8,128)(2,1)S(1)} %collective-permute-done.15.refs_8_), channel_id=1, source_target_pairs={{0,1},{1,0},{2,3},{3,2},{4,5},{5,4},{6,7},{7,6},{8,9},{9,8},{10,11... | collective-permute-start | bytes 786440 | tf_op jit(solution)/shard_map/ppermute | solution.py:33
  61.5 0.7 copy-start.7
  62.2 8.1 %collective-permute-start.18 = (bf16[256,512]{1,0:T(8,128)(2,1)}, bf16[256,512]{1,0:T(8,128)(2,1)}, u32[]{:S(2)}, u32[]{:S(2)}) collective-permute-start(bf16[256,512]{1,0:T(8,128)(2,1)} %collective-permute-done.14.refs_7_), channel_id=1, source_target_pairs={{0,1},{1,0},{2,3},{3,2},{4,5},{5,4},{6,7},{7,6},{8,9},{9,8},{10,11... | collective-permute-start | bytes 786440 | tf_op jit(solution)/shard_map/ppermute | solution.py:33
  67.4 26.5 %collective-permute-start.24 = (bf16[128,2048]{1,0:T(8,128)(2,1)}, bf16[128,2048]{1,0:T(8,128)(2,1)S(1)}, u32[]{:S(2)}, u32[]{:S(2)}) collective-permute-start(bf16[128,2048]{1,0:T(8,128)(2,1)} %get-tuple-element.70.refs_14_), channel_id=1, source_target_pairs={{0,64},{1,65},{2,66},{3,67},{4,68},{5,69},{6,70},{7,71},{8,72},{9,... | collective-permute-start | bytes 1572872 | tf_op jit(solution)/shard_map/ppermute | solution.py:33
  70.3 24.4 %collective-permute-start.23 = (bf16[128,2048]{1,0:T(8,128)(2,1)}, bf16[128,2048]{1,0:T(8,128)(2,1)S(1)}, u32[]{:S(2)}, u32[]{:S(2)}) collective-permute-start(bf16[128,2048]{1,0:T(8,128)(2,1)} %get-tuple-element.70.refs_14_), channel_id=1, source_target_pairs={{0,32},{1,33},{2,34},{3,35},{4,36},{5,37},{6,38},{7,39},{8,40},{9,... | collective-permute-start | bytes 1572872 | tf_op jit(solution)/shard_map/ppermute | solution.py:33
  70.3 24.4 %collective-permute-start.22 = (bf16[128,2048]{1,0:T(8,128)(2,1)}, bf16[128,2048]{1,0:T(8,128)(2,1)S(1)}, u32[]{:S(2)}, u32[]{:S(2)}) collective-permute-start(bf16[128,2048]{1,0:T(8,128)(2,1)} %get-tuple-element.70.refs_14_), channel_id=1, source_target_pairs={{0,96},{1,97},{2,98},{3,99},{4,100},{5,101},{6,102},{7,103},{8,104... | collective-permute-start | bytes 1572872 | tf_op jit(solution)/shard_map/ppermute | solution.py:33
  73.6 1.0 copy-start.4
  74.6 0.9 copy-start.8
  75.6 7.3 %copy-start.5 = (bf16[128,2048]{1,0:T(8,128)(2,1)S(1)}, bf16[128,2048]{1,0:T(8,128)(2,1)}, u32[]{:S(2)}) copy-start(bf16[128,2048]{1,0:T(8,128)(2,1)} %get-tuple-element.51.refs_14_) | copy-start | bytes 1572868
  82.8 8.2 %copy-start.3 = (f32[128,1024]{1,0:T(8,128)}, f32[128,1024]{1,0:T(8,128)S(1)}, u32[]{:S(2)}) copy-start(f32[128,1024]{1,0:T(8,128)S(1)} %get-tuple-element.60.a_ref) | copy-start | bytes 1572868
  82.9 11.9 %copy-start.6 = (bf16[128,2048]{1,0:T(8,128)(2,1)S(1)}, bf16[128,2048]{1,0:T(8,128)(2,1)}, u32[]{:S(2)}) copy-start(bf16[128,2048]{1,0:T(8,128)(2,1)} %get-tuple-element.70.refs_14_) | copy-start | bytes 1572868
  91.1 0.8 copy-start
  91.9 23.8 %collective-permute-start.28 = (bf16[128,1024]{1,0:T(8,128)(2,1)}, bf16[128,1024]{1,0:T(8,128)(2,1)S(1)}, u32[]{:S(2)}, u32[]{:S(2)}) collective-permute-start(bf16[128,1024]{1,0:T(8,128)(2,1)} %get-tuple-element.81), channel_id=1, source_target_pairs={{0,16},{1,17},{2,18},{3,19},{4,20},{5,21},{6,22},{7,23},{8,24},{9,... | collective-permute-start | bytes 786440 | tf_op jit(solution)/shard_map/ppermute | solution.py:33
  91.9 13.5 %collective-permute-start.25 = (bf16[128,1024]{1,0:T(8,128)(2,1)S(1)}, bf16[128,1024]{1,0:T(8,128)(2,1)S(1)}, u32[]{:S(2)}, u32[]{:S(2)}) collective-permute-start(bf16[128,1024]{1,0:T(8,128)(2,1)S(1)} %get-tuple-element.72), channel_id=1, source_target_pairs={{0,16},{1,17},{2,18},{3,19},{4,20},{5,21},{6,22},{7,23},{8,24},{9,... | collective-permute-start | bytes 786440 | tf_op jit(solution)/shard_map/ppermute | solution.py:33
  101.3 0.8 copy-start.1
  102.1 16.2 %collective-permute-start.27 = (bf16[128,1024]{1,0:T(8,128)(2,1)S(1)}, bf16[128,1024]{1,0:T(8,128)(2,1)}, u32[]{:S(2)}, u32[]{:S(2)}) collective-permute-start(bf16[128,1024]{1,0:T(8,128)(2,1)S(1)} %get-tuple-element.79), channel_id=1, source_target_pairs={{0,16},{1,17},{2,18},{3,19},{4,20},{5,21},{6,22},{7,23},{8,24},{9,... | collective-permute-start | bytes 786440 | tf_op jit(solution)/shard_map/ppermute | solution.py:33
  105.4 0.7 copy-start.15
  112.7 0.8 copy-start.2
  113.5 6.7 %collective-permute-start.26 = (bf16[128,1024]{1,0:T(8,128)(2,1)S(1)}, bf16[128,1024]{1,0:T(8,128)(2,1)S(1)}, u32[]{:S(2)}, u32[]{:S(2)}) collective-permute-start(bf16[128,1024]{1,0:T(8,128)(2,1)S(1)} %get-tuple-element.78), channel_id=1, source_target_pairs={{0,16},{1,17},{2,18},{3,19},{4,20},{5,21},{6,22},{7,23},{8,24},{9,... | collective-permute-start | bytes 786440 | tf_op jit(solution)/shard_map/ppermute | solution.py:33
  115.6 0.7 copy-start.13
  120.1 0.7 copy-start.14

commit v8 on v7

--- a/solution.py
+++ b/solution.py
@@ -249,20 +249,20 @@
     cells = 1024
     tile = 512
     columns = pl.ds(place * cells, cells)
-    targets = [(0, 0, 128), (1, 0, 128), (3, 0, 128), (2, 0, 64), (2, 64, 64)]
+    targets = [0, 1, 3, 2]
 
     def kernel(*refs):
         w_parts = refs[:4]
         slabs = refs[4:14]
-        parts = refs[14:19]
-        mine_ref, other_ref, k_ref, m_ref, w_ref, sem_k, sem_m = refs[19:]
+        parts = refs[14:18]
+        mine_ref, other_ref, k_ref, m_ref, w_ref, sem_k, sem_m = refs[18:]
         y, places = weight_rows()
         loads = []
-        for i, (d, skip, n) in enumerate(targets):
-            at = pl.multiple_of(((y + d) & 3) * 128 + skip, 64)
+        for i, d in enumerate(targets):
+            at = pl.multiple_of(((y + d) & 3) * 128, 128)
             loads.append(
                 pltpu.make_async_copy(
-                    parts[i].at[:, columns], m_ref.at[pl.ds(at, n)], sem_m.at[i]
+                    parts[i].at[:, columns], m_ref.at[pl.ds(at, 128)], sem_m.at[i]
                 )
             )
         row, starts = 0, []
@@ -275,7 +275,7 @@
             load.start()
         for d in range(4):
             w_ref[4 * d : 4 * d + 4] = w_parts[d][:, layer].astype(F32)
-        for load in loads[:5]:
+        for load in loads[:4]:
             load.wait()
         for t in range(cells // tile):
             cols = pl.ds(t * tile, tile)
@@ -283,7 +283,7 @@
             total = jnp.zeros((256, tile), F32)
             for s in range(SLICES):
                 if t == 0 and s in starts:
-                    loads[5 + starts.index(s)].wait()
+                    loads[4 + starts.index(s)].wait()
                 product = jnp.dot(
                     k_ref[s * 256 : (s + 1) * 256], moved, preferred_element_type=F32
                 )
@@ -295,14 +295,14 @@
     return pl.pallas_call(
         kernel,
         out_shape=(shape((128, cells), F32), shape((128, cells), BF16)),
-        in_specs=[VMEM] * 4 + [ANY] * 15,
+        in_specs=[VMEM] * 4 + [ANY] * 14,
         out_specs=(VMEM, VMEM),
         scratch_shapes=[
             pltpu.VMEM((SLICES * 256, 512), BF16),
             pltpu.VMEM((512, cells), BF16),
             pltpu.VMEM((SLICES, 8, 128), F32),
             pltpu.SemaphoreType.DMA((10,)),
-            pltpu.SemaphoreType.DMA((5,)),
+            pltpu.SemaphoreType.DMA((4,)),
         ],
         compiler_params=pltpu.CompilerParams(vmem_limit_bytes=28 << 20),
         cost_estimate=pl.CostEstimate(
@@ -355,13 +355,13 @@
     base = jnp.concatenate([own_slice[128:], partner[:128], after(cross, block)], 0)
     swapped = [shift(base, dc=1)]
     block = after(block, swapped[0])
-    before, behind = shift(block, dy=1), shift(block, dy=-1)
+    before, behind, across = shift(block, dy=1), shift(block, dy=-1), shift(block, dy=2)
     one, three, before, behind = after(
         (shift(base, dx=1), shift(base, dx=-1), before, behind)
     )
     pieces = [base, one, three, shift(one[:256], dx=1), shift(three[256:], dx=-1)]
     pieces = pieces + swapped + [shift(p, dc=1) for p in pieces[1:]]
-    inside = [block, behind, before, shift(before[:64], dy=1), shift(behind[64:], dy=-1)]
+    inside = [block, behind, before, across]
 
     rows = after(jnp.concatenate([own, shift(own, dz=1)], 0), before)
     weights = [rows, shift(rows, dy=-1), shift(rows, dy=2), shift(rows, dy=1)]
@@ -369,7 +369,7 @@
     transported, block = transport(density, limiter, heading, courant, first, second, inner)
     before, behind = shift(block, dy=1), shift(block, dy=-1)
     across = shift(block, dy=2)
-    outside = [block, behind, before, across[:64], across[64:]]
+    outside = [block, behind, before, across]
 
     waiting, result = [], None
     for layers, blocks in zip(BLOCKS, (inside, outside), strict=True):

time: 123 us -> 137 us (1.11)
  waiting for transfers between devices: 24.8 us -> 45.6 us
  local copies, waits for them, and re-layouts: 10.2 us -> 7.52 us
  starting transfers between devices: 35.9 us -> 33.5 us
  Pallas kernels: 50.2 us -> 48.4 us
    ppermute x27 -> x26, waiting for transfers between devices: 24.8 us -> 45.6 us  [shift(): return lax.ppermute(value, BOTH, pairs)]
    ppermute x27 -> x26, starting transfers between devices: 34.5 us -> 32.2 us  [shift(): return lax.ppermute(value, BOTH, pairs)]
    unnamed x32 -> x34, local copies, waits for them, and re-layouts: 9.33 us -> 7.45 us
    pallas_call x4, Pallas kernels: 28.5 us -> 26.7 us  [collide(): pl.pallas_call(kernel, out_shape=(shape((128, cells), F32), shape((128, c...]
  transfers between devices with their start and end apart: 29 -> 28, of which waited for: 10 -> 11; matrix products, arithmetic and copies ran while one was open for 1% -> 0% of each run, Pallas kernels for 38% -> 33%
where the time goes in v8:
time: 137 us; the launch traced here: 136 us
  Pallas kernels  48.4 us (35%)
  waiting for transfers between devices  45.6 us (33%)
  starting transfers between devices  33.5 us (24%)
  local copies, waits for them, and re-layouts  7.52 us (5%)
    ppermute x26, waiting for transfers between devices, shift(): return lax.ppermute(value, BOTH, pairs)  45.6 us
    ppermute x26, starting transfers between devices, shift(): return lax.ppermute(value, BOTH, pairs)  32.2 us
    pallas_call x4, Pallas kernels, collide(): pl.pallas_call(kernel, out_shape=(shape((128, cells), F32), shape((128, c...  26.7 us
    pallas_call x4, Pallas kernels, combine(): pl.pallas_call(kernel, grid=(128 // step,), out_shape=shape((128, 4, 8, 1...  7.59 us
    unnamed x34, local copies, waits for them, and re-layouts  7.45 us
    pallas_call x1, Pallas kernels, transport(): pl.pallas_call(kernel, grid=(rows // STEP,), out_shape=(shape(density.sha...  5.15 us
    pallas_call x1, Pallas kernels, transport_inner(): pl.pallas_call(kernel, grid=(rows // STEP,), out_shape=(shape((rows, 2048...  4.47 us
  transfers between devices with their start and end apart: 28, of which 11 were waited for; matrix products, arithmetic and copies ran while one was open for 0% of the time, Pallas kernels for 33%

profile of v8, /device:TPU:0, one launch (start us, length us, event | category | flops | bytes accessed | tf_op | source)
XLA Modules:
  0.0 135.9 jit_solution(16992673544462160006)
XLA Ops:
  0.6 1.8 %split_slice.1 = bf16[256,512]{1,0:T(8,128)(2,1)} custom-call(bf16[4,2,128,128]{3,2,1,0:T(8,128)(2,1)} %bitcast.1), custom_call_target="tpu_custom_call" | custom-call | tf_op jit(solution)/shard_map/split_slice/pallas_call | solution.py:89
  2.4 2.0 %collective-permute-start.1 = (bf16[256,512]{1,0:T(8,128)(2,1)}, bf16[256,512]{1,0:T(8,128)(2,1)S(1)}, u32[]{:S(2)}, u32[]{:S(2)}) collective-permute-start(bf16[256,512]{1,0:T(8,128)(2,1)} %split_slice.1), channel_id=1, source_target_pairs={{0,16},{1,17},{2,18},{3,19},{4,20},{5,21},{6,22},{7,23},{8,24},{9,... | collective-permute-start | bytes 786440 | tf_op jit(solution)/shard_map/ppermute | solution.py:33
  4.4 2.7 %pack.1 = (bf16[131,8,128]{2,1,0:T(8,128)(2,1)}, bf16[128,8,128]{2,1,0:T(8,128)(2,1)}, bf16[129,2,8,128]{3,2,1,0:T(8,128)(2,1)}) custom-call(f32[128,4,8,128]{3,2,1,0:T(8,128)} %d_ref.4, s32[4,8,128]{2,1,0:T(8,128)} %l_ref.5), custom_call_target="tpu_custom_call" | custom-call | tf_op jit(solution)/shard_map/pack/pallas_call | solution.py:68
  7.1 0.7 collective-permute-start
  7.8 5.0 %collective-permute-start.2 = (bf16[129,2,8,128]{3,2,1,0:T(8,128)(2,1)}, bf16[129,2,8,128]{3,2,1,0:T(8,128)(2,1)S(1)}, u32[]{:S(2)}, u32[]{:S(2)}) collective-permute-start(bf16[129,2,8,128]{3,2,1,0:T(8,128)(2,1)} %get-tuple-element.46), channel_id=1, source_target_pairs={{0,1},{1,0},{2,3},{3,2},{4,5},{5,4},{6,7},{7,6},{8,9},{9,8},{10,11... | collective-permute-start | bytes 1585160 | tf_op jit(solution)/shard_map/ppermute | solution.py:33
  12.9 2.0 %collective-permute-start.4 = (bf16[256,512]{1,0:T(8,128)(2,1)S(1)}, bf16[256,512]{1,0:T(8,128)(2,1)S(1)}, u32[]{:S(2)}, u32[]{:S(2)}) collective-permute-start(bf16[256,512]{1,0:T(8,128)(2,1)S(1)} %pad_maximum_fusion.1), channel_id=1, source_target_pairs={{0,18},{1,19},{2,16},{3,17},{4,22},{5,23},{6,20},{7,21},{8,26},{9,... | collective-permute-start | bytes 786440 | tf_op jit(solution)/shard_map/ppermute | solution.py:33
  14.9 0.7 copy-done.11
  15.6 0.8 copy-done.10
  16.4 4.5 %transport_inner.1 = (bf16[128,2048]{1,0:T(8,128)(2,1)}, bf16[2,4,8,128]{3,2,1,0:T(8,128)(2,1)}) custom-call(s32[128]{0:T(128)} %h_ref.3, f32[128]{0:T(128)} %c_ref.3, f32[128,4,8,128]{3,2,1,0:T(8,128)} %d_ref.4, s32[4,8,128]{2,1,0:T(8,128)} %l_ref.5, bf16[131,8,128]{2,1,0:T(8,128)(2,1)} %copy-done.11, bf16[131,8,128]{2,1,0:T(8,128)(2,1)} %copy-done.11, ...), custom_call_target="tpu_custom_call" | custom-call | flops 2097152 | bytes 3145728 | tf_op jit(solution)/shard_map/transport_inner/pallas_call | solution.py:182
  20.9 3.0 %collective-permute-done.4 = bf16[256,512]{1,0:T(8,128)(2,1)S(1)} collective-permute-done((bf16[256,512]{1,0:T(8,128)(2,1)S(1)}, bf16[256,512]{1,0:T(8,128)(2,1)S(1)}, u32[]{:S(2)}, u32[]{:S(2)}) %collective-permute-start.4) | collective-permute-done | bytes 262176 | tf_op jit(solution)/shard_map/ppermute | solution.py:33
  24.0 1.5 %collective-permute-start.7 = (bf16[512,512]{1,0:T(8,128)(2,1)S(1)}, bf16[512,512]{1,0:T(8,128)(2,1)S(1)}, u32[]{:S(2)}, u32[]{:S(2)}) collective-permute-start(bf16[512,512]{1,0:T(8,128)(2,1)S(1)} %pad_maximum_fusion.refs_4_), channel_id=1, source_target_pairs={{0,1},{1,0},{2,3},{3,2},{4,5},{5,4},{6,7},{7,6},{8,9},{9,8},{10,11... | collective-permute-start | bytes 1572872 | tf_op jit(solution)/shard_map/ppermute | solution.py:33
  25.4 3.5 %collective-permute-start.6 = (bf16[512,512]{1,0:T(8,128)(2,1)S(1)}, bf16[512,512]{1,0:T(8,128)(2,1)S(1)}, u32[]{:S(2)}, u32[]{:S(2)}) collective-permute-start(bf16[512,512]{1,0:T(8,128)(2,1)S(1)} %pad_maximum_fusion.refs_4_), channel_id=1, source_target_pairs={{0,12},{1,13},{2,14},{3,15},{4,0},{5,1},{6,2},{7,3},{8,4},{9,5},{1... | collective-permute-start | bytes 1572872 | tf_op jit(solution)/shard_map/ppermute | solution.py:33
  28.9 3.0 %collective-permute-start.9 = (bf16[128,2048]{1,0:T(8,128)(2,1)}, bf16[128,2048]{1,0:T(8,128)(2,1)S(1)}, u32[]{:S(2)}, u32[]{:S(2)}) collective-permute-start(bf16[128,2048]{1,0:T(8,128)(2,1)} %get-tuple-element.51.refs_14_), channel_id=1, source_target_pairs={{0,96},{1,97},{2,98},{3,99},{4,100},{5,101},{6,102},{7,103},{8,104... | collective-permute-start | bytes 1572872 | tf_op jit(solution)/shard_map/ppermute | solution.py:33
  31.9 0.7 collective-permute-start.3
  32.6 7.9 %collective-permute-done.6.refs_6_ = bf16[512,512]{1,0:T(8,128)(2,1)S(1)} collective-permute-done((bf16[512,512]{1,0:T(8,128)(2,1)S(1)}, bf16[512,512]{1,0:T(8,128)(2,1)S(1)}, u32[]{:S(2)}, u32[]{:S(2)}) %collective-permute-start.6) | collective-permute-done | bytes 524320 | tf_op jit(solution)/shard_map/ppermute | solution.py:33
  40.5 3.2 %collective-permute-start.20 = (bf16[128,2048]{1,0:T(8,128)(2,1)}, bf16[128,2048]{1,0:T(8,128)(2,1)S(1)}, u32[]{:S(2)}, u32[]{:S(2)}) collective-permute-start(bf16[128,2048]{1,0:T(8,128)(2,1)} %get-tuple-element.51.refs_14_), channel_id=1, source_target_pairs={{0,64},{1,65},{2,66},{3,67},{4,68},{5,69},{6,70},{7,71},{8,72},{9,... | collective-permute-start | bytes 1572872 | tf_op jit(solution)/shard_map/ppermute | solution.py:33
  43.7 0.2 collective-permute-done.5.refs_5_
  43.9 14.2 %collective-permute-done.8.refs_16_ = bf16[128,2048]{1,0:T(8,128)(2,1)S(1)} collective-permute-done((bf16[128,2048]{1,0:T(8,128)(2,1)}, bf16[128,2048]{1,0:T(8,128)(2,1)S(1)}, u32[]{:S(2)}, u32[]{:S(2)}) %collective-permute-start.8) | collective-permute-done | bytes 524320 | tf_op jit(solution)/shard_map/ppermute | solution.py:33
  58.1 3.0 %collective-permute-start.15 = (bf16[256,512]{1,0:T(8,128)(2,1)S(1)}, bf16[256,512]{1,0:T(8,128)(2,1)S(1)}, u32[]{:S(2)}, u32[]{:S(2)}) collective-permute-start(bf16[256,512]{1,0:T(8,128)(2,1)S(1)} %slice.23), channel_id=1, source_target_pairs={{0,12},{1,13},{2,14},{3,15},{4,0},{5,1},{6,2},{7,3},{8,4},{9,5},{1... | collective-permute-start | bytes 786440 | tf_op jit(solution)/shard_map/ppermute | solution.py:33
  61.4 0.5 collective-permute-start.17
  61.9 3.2 %collective-permute-done.15.refs_8_ = bf16[256,512]{1,0:T(8,128)(2,1)S(1)} collective-permute-done((bf16[256,512]{1,0:T(8,128)(2,1)S(1)}, bf16[256,512]{1,0:T(8,128)(2,1)S(1)}, u32[]{:S(2)}, u32[]{:S(2)}) %collective-permute-start.15) | collective-permute-done | bytes 262176 | tf_op jit(solution)/shard_map/ppermute | solution.py:33
  65.0 3.9 %collective-permute-done.14.refs_7_ = bf16[256,512]{1,0:T(8,128)(2,1)} collective-permute-done((bf16[256,512]{1,0:T(8,128)(2,1)S(1)}, bf16[256,512]{1,0:T(8,128)(2,1)}, u32[]{:S(2)}, u32[]{:S(2)}) %collective-permute-start.14) | collective-permute-done | bytes 262176 | tf_op jit(solution)/shard_map/ppermute | solution.py:33
  68.9 0.8 copy-done.7
  69.7 5.1 %collective-permute-done.13.refs_3_ = bf16[4,4,8,128]{3,2,1,0:T(8,128)(2,1)S(1)} collective-permute-done((bf16[4,4,8,128]{3,2,1,0:T(8,128)(2,1)S(1)}, bf16[4,4,8,128]{3,2,1,0:T(8,128)(2,1)S(1)}, u32[]{:S(2)}, u32[]{:S(2)}) %collective-permute-start.13) | collective-permute-done | bytes 32800 | tf_op jit(solution)/shard_map/ppermute | solution.py:33
  74.9 5.4 %collective-permute-done.12.refs_2_ = bf16[4,4,8,128]{3,2,1,0:T(8,128)(2,1)S(1)} collective-permute-done((bf16[4,4,8,128]{3,2,1,0:T(8,128)(2,1)S(1)}, bf16[4,4,8,128]{3,2,1,0:T(8,128)(2,1)S(1)}, u32[]{:S(2)}, u32[]{:S(2)}) %collective-permute-start.12) | collective-permute-done | bytes 32800 | tf_op jit(solution)/shard_map/ppermute | solution.py:33
  80.3 5.2 %transport.1 = (f32[128,4,8,128]{3,2,1,0:T(8,128)}, bf16[128,2048]{1,0:T(8,128)(2,1)}) custom-call(s32[128]{0:T(128)} %h_ref.3, f32[128]{0:T(128)} %c_ref.3, f32[128,4,8,128]{3,2,1,0:T(8,128)} %d_ref.4, s32[4,8,128]{2,1,0:T(8,128)} %l_ref.5, bf16[131,8,128]{2,1,0:T(8,128)(2,1)} %copy-done.11, bf16[131,8,128]{2,1,0:T(8,128)(2,1)} %copy-done.11, ...), custom_call_target="tpu_custom_call" | custom-call | flops 4194304 | bytes 6291456 | tf_op jit(solution)/shard_map/transport/pallas_call | solution.py:219
  85.4 1.1 collective-permute-start.23
  86.5 1.1 collective-permute-start.22
  87.6 2.8 %collective-permute-start.21 = (bf16[128,2048]{1,0:T(8,128)(2,1)}, bf16[128,2048]{1,0:T(8,128)(2,1)S(1)}, u32[]{:S(2)}, u32[]{:S(2)}) collective-permute-start(bf16[128,2048]{1,0:T(8,128)(2,1)} %get-tuple-element.70.refs_14_), channel_id=1, source_target_pairs={{0,96},{1,97},{2,98},{3,99},{4,100},{5,101},{6,102},{7,103},{8,104... | collective-permute-start | bytes 1572872 | tf_op jit(solution)/shard_map/ppermute | solution.py:33
  90.5 1.0 copy-done.6
  91.5 1.0 copy-done.8
  92.6 6.5 %collide.4 = (f32[128,1024]{1,0:T(8,128)S(1)}, bf16[128,1024]{1,0:T(8,128)(2,1)S(1)}) custom-call(bf16[4,4,8,128]{3,2,1,0:T(8,128)(2,1)S(1)} %pad_maximum_fusion.2.refs_0_, bf16[4,4,8,128]{3,2,1,0:T(8,128)(2,1)S(1)} %collective-permute-done.11.refs_1_, bf16[4,4,8,128]{3,2,1,0:T(8,128)(2,1)S(1)} %collective-permute-done.12.refs_2_, ...), custom_call_target="tpu_custom_call" | custom-call | flops 4294967296 | bytes 6291456 | tf_op jit(solution)/shard_map/collide/pallas_call | solution.py:295
  99.1 7.2 %collide.5 = (f32[128,1024]{1,0:T(8,128)S(1)}, bf16[128,1024]{1,0:T(8,128)(2,1)}) custom-call(bf16[4,4,8,128]{3,2,1,0:T(8,128)(2,1)S(1)} %pad_maximum_fusion.2.refs_0_, bf16[4,4,8,128]{3,2,1,0:T(8,128)(2,1)S(1)} %collective-permute-done.11.refs_1_, bf16[4,4,8,128]{3,2,1,0:T(8,128)(2,1)S(1)} %collective-permute-done.12.refs_2_, ...), custom_call_target="tpu_custom_call" | custom-call | flops 4294967296 | bytes 6291456 | tf_op jit(solution)/shard_map/collide/pallas_call | solution.py:295
  106.3 0.8 copy-done
  107.1 2.0 %collective-permute-start.24 = (bf16[128,1024]{1,0:T(8,128)(2,1)S(1)}, bf16[128,1024]{1,0:T(8,128)(2,1)S(1)}, u32[]{:S(2)}, u32[]{:S(2)}) collective-permute-start(bf16[128,1024]{1,0:T(8,128)(2,1)S(1)} %get-tuple-element.72), channel_id=1, source_target_pairs={{0,16},{1,17},{2,18},{3,19},{4,20},{5,21},{6,22},{7,23},{8,24},{9,... | collective-permute-start | bytes 786440 | tf_op jit(solution)/shard_map/ppermute | solution.py:33
  109.2 1.3 collective-permute-done.22.refs_16_
  110.5 6.5 %collide.6 = (f32[128,1024]{1,0:T(8,128)S(1)}, bf16[128,1024]{1,0:T(8,128)(2,1)S(1)}) custom-call(bf16[4,4,8,128]{3,2,1,0:T(8,128)(2,1)S(1)} %pad_maximum_fusion.2.refs_0_, bf16[4,4,8,128]{3,2,1,0:T(8,128)(2,1)S(1)} %collective-permute-done.11.refs_1_, bf16[4,4,8,128]{3,2,1,0:T(8,128)(2,1)S(1)} %collective-permute-done.12.refs_2_, ...), custom_call_target="tpu_custom_call" | custom-call | flops 4294967296 | bytes 6291456 | tf_op jit(solution)/shard_map/collide/pallas_call | solution.py:295
  117.0 0.8 copy-done.1
  117.8 0.7 collective-permute-done.24.b_ref
  118.5 6.5 %collide.7 = (f32[128,1024]{1,0:T(8,128)S(1)}, bf16[128,1024]{1,0:T(8,128)(2,1)S(1)}) custom-call(bf16[4,4,8,128]{3,2,1,0:T(8,128)(2,1)S(1)} %pad_maximum_fusion.2.refs_0_, bf16[4,4,8,128]{3,2,1,0:T(8,128)(2,1)S(1)} %collective-permute-done.11.refs_1_, bf16[4,4,8,128]{3,2,1,0:T(8,128)(2,1)S(1)} %collective-permute-done.12.refs_2_, ...), custom_call_target="tpu_custom_call" | custom-call | flops 4294967296 | bytes 6291456 | tf_op jit(solution)/shard_map/collide/pallas_call | solution.py:295
  125.0 0.8 copy-done.2
  125.8 1.3 collective-permute-start.25
  127.1 1.9 %combine.4.refs_0_ = f32[128,4,8,128]{3,2,1,0:T(8,128)} custom-call(f32[128,1024]{1,0:T(8,128)} %copy-done.3, bf16[128,1024]{1,0:T(8,128)(2,1)} %copy-done.15), custom_call_target="tpu_custom_call" | custom-call | flops 131072 | bytes 1310720 | tf_op jit(solution)/shard_map/combine/pallas_call | solution.py:326
  129.0 1.9 %combine.5.refs_0_ = f32[128,4,8,128]{3,2,1,0:T(8,128)} custom-call(f32[128,1024]{1,0:T(8,128)} %copy-done, bf16[128,1024]{1,0:T(8,128)(2,1)} %collective-permute-done.27.b_ref, f32[128,4,8,128]{3,2,1,0:T(8,128)} %combine.4.refs_0_), custom_call_target="tpu_custom_call", output_to_operand_aliasing={{}: (2, {})} | custom-call | flops 131072 | bytes 1310720 | tf_op jit(solution)/shard_map/combine/pallas_call | solution.py:326
  130.9 1.9 %combine.6.refs_0_ = f32[128,4,8,128]{3,2,1,0:T(8,128)} custom-call(f32[128,1024]{1,0:T(8,128)} %copy-done.1, bf16[128,1024]{1,0:T(8,128)(2,1)} %collective-permute-done.26.b_ref, f32[128,4,8,128]{3,2,1,0:T(8,128)} %combine.5.refs_0_), custom_call_target="tpu_custom_call", output_to_operand_aliasing={{}: (2, {})} | custom-call | flops 131072 | bytes 1310720 | tf_op jit(solution)/shard_map/combine/pallas_call | solution.py:326
  132.8 0.5 collective-permute-done.25.b_ref
  133.3 0.7 copy-done.14
  134.0 1.9 %combine.7 = f32[128,4,8,128]{3,2,1,0:T(8,128)} custom-call(f32[128,1024]{1,0:T(8,128)} %copy-done.2, bf16[128,1024]{1,0:T(8,128)(2,1)} %copy-done.14, f32[128,4,8,128]{3,2,1,0:T(8,128)} %combine.6.refs_0_), custom_call_target="tpu_custom_call", output_to_operand_aliasing={{}: (2, {})} | custom-call | flops 131072 | bytes 1310720 | tf_op jit(solution)/shard_map/combine/pallas_call | solution.py:326
  (61 shorter events, 0.4 us)
Async XLA Ops:
  2.4 10.4 %copy-start.12 = (bf16[256,512]{1,0:T(8,128)(2,1)S(1)}, bf16[256,512]{1,0:T(8,128)(2,1)}, u32[]{:S(2)}) copy-start(bf16[256,512]{1,0:T(8,128)(2,1)} %split_slice.1) | copy-start | bytes 786436
  2.4 10.4 %collective-permute-start.1 = (bf16[256,512]{1,0:T(8,128)(2,1)}, bf16[256,512]{1,0:T(8,128)(2,1)S(1)}, u32[]{:S(2)}, u32[]{:S(2)}) collective-permute-start(bf16[256,512]{1,0:T(8,128)(2,1)} %split_slice.1), channel_id=1, source_target_pairs={{0,16},{1,17},{2,18},{3,19},{4,20},{5,21},{6,22},{7,23},{8,24},{9,... | collective-permute-start | bytes 786440 | tf_op jit(solution)/shard_map/ppermute | solution.py:33
  7.1 7.8 %collective-permute-start = (bf16[131,8,128]{2,1,0:T(8,128)(2,1)}, bf16[131,8,128]{2,1,0:T(8,128)(2,1)S(1)}, u32[]{:S(2)}, u32[]{:S(2)}) collective-permute-start(bf16[131,8,128]{2,1,0:T(8,128)(2,1)} %get-tuple-element.44), channel_id=1, source_target_pairs={{1,2},{3,4},{5,6},{7,8},{9,10},{11,12},{13,14},{2,1},{4,3},{6,5},{... | collective-permute-start | bytes 804872 | tf_op jit(solution)/shard_map/ppermute | solution.py:346
  7.8 7.1 %collective-permute-start.2 = (bf16[129,2,8,128]{3,2,1,0:T(8,128)(2,1)}, bf16[129,2,8,128]{3,2,1,0:T(8,128)(2,1)S(1)}, u32[]{:S(2)}, u32[]{:S(2)}) collective-permute-start(bf16[129,2,8,128]{3,2,1,0:T(8,128)(2,1)} %get-tuple-element.46), channel_id=1, source_target_pairs={{0,1},{1,0},{2,3},{3,2},{4,5},{5,4},{6,7},{7,6},{8,9},{9,8},{10,11... | collective-permute-start | bytes 1585160 | tf_op jit(solution)/shard_map/ppermute | solution.py:33
  12.9 11.0 %collective-permute-start.4 = (bf16[256,512]{1,0:T(8,128)(2,1)S(1)}, bf16[256,512]{1,0:T(8,128)(2,1)S(1)}, u32[]{:S(2)}, u32[]{:S(2)}) collective-permute-start(bf16[256,512]{1,0:T(8,128)(2,1)S(1)} %pad_maximum_fusion.1), channel_id=1, source_target_pairs={{0,18},{1,19},{2,16},{3,17},{4,22},{5,23},{6,20},{7,21},{8,26},{9,... | collective-permute-start | bytes 786440 | tf_op jit(solution)/shard_map/ppermute | solution.py:33
  14.9 0.7 copy-start.11
  15.6 0.8 copy-start.10
  20.9 48.0 %copy-start.16 = (bf16[2,4,8,128]{3,2,1,0:T(8,128)(2,1)S(1)}, bf16[2,4,8,128]{3,2,1,0:T(8,128)(2,1)}, u32[]{:S(2)}) copy-start(bf16[2,4,8,128]{3,2,1,0:T(8,128)(2,1)} %get-tuple-element.55) | copy-start | bytes 49156
  24.0 4.9 %collective-permute-start.7 = (bf16[512,512]{1,0:T(8,128)(2,1)S(1)}, bf16[512,512]{1,0:T(8,128)(2,1)S(1)}, u32[]{:S(2)}, u32[]{:S(2)}) collective-permute-start(bf16[512,512]{1,0:T(8,128)(2,1)S(1)} %pad_maximum_fusion.refs_4_), channel_id=1, source_target_pairs={{0,1},{1,0},{2,3},{3,2},{4,5},{5,4},{6,7},{7,6},{8,9},{9,8},{10,11... | collective-permute-start | bytes 1572872 | tf_op jit(solution)/shard_map/ppermute | solution.py:33
  25.4 15.0 %collective-permute-start.6 = (bf16[512,512]{1,0:T(8,128)(2,1)S(1)}, bf16[512,512]{1,0:T(8,128)(2,1)S(1)}, u32[]{:S(2)}, u32[]{:S(2)}) collective-permute-start(bf16[512,512]{1,0:T(8,128)(2,1)S(1)} %pad_maximum_fusion.refs_4_), channel_id=1, source_target_pairs={{0,12},{1,13},{2,14},{3,15},{4,0},{5,1},{6,2},{7,3},{8,4},{9,5},{1... | collective-permute-start | bytes 1572872 | tf_op jit(solution)/shard_map/ppermute | solution.py:33
  28.9 15.0 %collective-permute-start.5 = (bf16[512,512]{1,0:T(8,128)(2,1)S(1)}, bf16[512,512]{1,0:T(8,128)(2,1)S(1)}, u32[]{:S(2)}, u32[]{:S(2)}) collective-permute-start(bf16[512,512]{1,0:T(8,128)(2,1)S(1)} %pad_maximum_fusion.refs_4_), channel_id=1, source_target_pairs={{0,4},{1,5},{2,6},{3,7},{4,8},{5,9},{6,10},{7,11},{8,12},{9,13},{1... | collective-permute-start | bytes 1572872 | tf_op jit(solution)/shard_map/ppermute | solution.py:33
  28.9 15.0 %collective-permute-start.9 = (bf16[128,2048]{1,0:T(8,128)(2,1)}, bf16[128,2048]{1,0:T(8,128)(2,1)S(1)}, u32[]{:S(2)}, u32[]{:S(2)}) collective-permute-start(bf16[128,2048]{1,0:T(8,128)(2,1)} %get-tuple-element.51.refs_14_), channel_id=1, source_target_pairs={{0,96},{1,97},{2,98},{3,99},{4,100},{5,101},{6,102},{7,103},{8,104... | collective-permute-start | bytes 1572872 | tf_op jit(solution)/shard_map/ppermute | solution.py:33
  31.9 26.1 %collective-permute-start.8 = (bf16[128,2048]{1,0:T(8,128)(2,1)}, bf16[128,2048]{1,0:T(8,128)(2,1)S(1)}, u32[]{:S(2)}, u32[]{:S(2)}) collective-permute-start(bf16[128,2048]{1,0:T(8,128)(2,1)} %get-tuple-element.51.refs_14_), channel_id=1, source_target_pairs={{0,32},{1,33},{2,34},{3,35},{4,36},{5,37},{6,38},{7,39},{8,40},{9,... | collective-permute-start | bytes 1572872 | tf_op jit(solution)/shard_map/ppermute | solution.py:33
  31.9 29.3 %collective-permute-start.3 = (bf16[128,8,128]{2,1,0:T(8,128)(2,1)}, bf16[128,8,128]{2,1,0:T(8,128)(2,1)S(1)}, u32[]{:S(2)}, u32[]{:S(2)}) collective-permute-start(bf16[128,8,128]{2,1,0:T(8,128)(2,1)} %get-tuple-element.48), channel_id=1, source_target_pairs={{1,2},{3,4},{5,6},{7,8},{9,10},{11,12},{13,14},{2,1},{4,3},{6,5},{... | collective-permute-start | bytes 786440 | tf_op jit(solution)/shard_map/ppermute | solution.py:352
  40.5 28.5 %collective-permute-start.20 = (bf16[128,2048]{1,0:T(8,128)(2,1)}, bf16[128,2048]{1,0:T(8,128)(2,1)S(1)}, u32[]{:S(2)}, u32[]{:S(2)}) collective-permute-start(bf16[128,2048]{1,0:T(8,128)(2,1)} %get-tuple-element.51.refs_14_), channel_id=1, source_target_pairs={{0,64},{1,65},{2,66},{3,67},{4,68},{5,69},{6,70},{7,71},{8,72},{9,... | collective-permute-start | bytes 1572872 | tf_op jit(solution)/shard_map/ppermute | solution.py:33
  43.9 17.5 %collective-permute-start.10 = (bf16[2,4,8,128]{3,2,1,0:T(8,128)(2,1)}, bf16[2,4,8,128]{3,2,1,0:T(8,128)(2,1)S(1)}, u32[]{:S(2)}, u32[]{:S(2)}) collective-permute-start(bf16[2,4,8,128]{3,2,1,0:T(8,128)(2,1)} %get-tuple-element.55), channel_id=1, source_target_pairs={{0,16},{1,17},{2,18},{3,19},{4,20},{5,21},{6,22},{7,23},{8,24},{9,... | collective-permute-start | bytes 49160 | tf_op jit(solution)/shard_map/ppermute | solution.py:33
  58.1 3.0 %copy-start.5 = (bf16[128,2048]{1,0:T(8,128)(2,1)}, bf16[128,2048]{1,0:T(8,128)(2,1)S(1)}, u32[]{:S(2)}) copy-start(bf16[128,2048]{1,0:T(8,128)(2,1)S(1)} %collective-permute-done.8.refs_16_) | copy-start | bytes 1572868
  58.1 6.9 %collective-permute-start.15 = (bf16[256,512]{1,0:T(8,128)(2,1)S(1)}, bf16[256,512]{1,0:T(8,128)(2,1)S(1)}, u32[]{:S(2)}, u32[]{:S(2)}) collective-permute-start(bf16[256,512]{1,0:T(8,128)(2,1)S(1)} %slice.23), channel_id=1, source_target_pairs={{0,12},{1,13},{2,14},{3,15},{4,0},{5,1},{6,2},{7,3},{8,4},{9,5},{1... | collective-permute-start | bytes 786440 | tf_op jit(solution)/shard_map/ppermute | solution.py:33
  61.1 29.3 %copy-start.4 = (bf16[128,2048]{1,0:T(8,128)(2,1)S(1)}, bf16[128,2048]{1,0:T(8,128)(2,1)}, u32[]{:S(2)}) copy-start(bf16[128,2048]{1,0:T(8,128)(2,1)} %get-tuple-element.51.refs_14_) | copy-start | bytes 1572868
  61.2 7.8 %collective-permute-start.14 = (bf16[256,512]{1,0:T(8,128)(2,1)S(1)}, bf16[256,512]{1,0:T(8,128)(2,1)}, u32[]{:S(2)}, u32[]{:S(2)}) collective-permute-start(bf16[256,512]{1,0:T(8,128)(2,1)S(1)} %slice.22), channel_id=1, source_target_pairs={{0,4},{1,5},{2,6},{3,7},{4,8},{5,9},{6,10},{7,11},{8,12},{9,13},{1... | collective-permute-start | bytes 786440 | tf_op jit(solution)/shard_map/ppermute | solution.py:33
  61.2 19.0 %copy-start.13 = (bf16[128,8,128]{2,1,0:T(8,128)(2,1)}, bf16[128,8,128]{2,1,0:T(8,128)(2,1)S(1)}, u32[]{:S(2)}) copy-start(bf16[128,8,128]{2,1,0:T(8,128)(2,1)S(1)} %collective-permute-done.3.next_ref) | copy-start | bytes 786436
  61.3 29.2 %collective-permute-start.16 = (bf16[512,512]{1,0:T(8,128)(2,1)S(1)}, bf16[512,512]{1,0:T(8,128)(2,1)}, u32[]{:S(2)}, u32[]{:S(2)}) collective-permute-start(bf16[512,512]{1,0:T(8,128)(2,1)S(1)} %collective-permute-done.5.refs_5_), channel_id=1, source_target_pairs={{0,1},{1,0},{2,3},{3,2},{4,5},{5,4},{6,7},{7,6},{8,9},{9,8},{10,11... | collective-permute-start | bytes 1572872 | tf_op jit(solution)/shard_map/ppermute | solution.py:33
  61.4 29.1 %collective-permute-start.17 = (bf16[512,512]{1,0:T(8,128)(2,1)S(1)}, bf16[512,512]{1,0:T(8,128)(2,1)}, u32[]{:S(2)}, u32[]{:S(2)}) collective-permute-start(bf16[512,512]{1,0:T(8,128)(2,1)S(1)} %collective-permute-done.6.refs_6_), channel_id=1, source_target_pairs={{0,1},{1,0},{2,3},{3,2},{4,5},{5,4},{6,7},{7,6},{8,9},{9,8},{10,11... | collective-permute-start | bytes 1572872 | tf_op jit(solution)/shard_map/ppermute | solution.py:33
  65.0 21.5 %collective-permute-start.19 = (bf16[256,512]{1,0:T(8,128)(2,1)S(1)}, bf16[256,512]{1,0:T(8,128)(2,1)}, u32[]{:S(2)}, u32[]{:S(2)}) collective-permute-start(bf16[256,512]{1,0:T(8,128)(2,1)S(1)} %collective-permute-done.15.refs_8_), channel_id=1, source_target_pairs={{0,1},{1,0},{2,3},{3,2},{4,5},{5,4},{6,7},{7,6},{8,9},{9,8},{10,11... | collective-permute-start | bytes 786440 | tf_op jit(solution)/shard_map/ppermute | solution.py:33
  68.9 18.7 %collective-permute-start.18 = (bf16[256,512]{1,0:T(8,128)(2,1)}, bf16[256,512]{1,0:T(8,128)(2,1)}, u32[]{:S(2)}, u32[]{:S(2)}) collective-permute-start(bf16[256,512]{1,0:T(8,128)(2,1)} %collective-permute-done.14.refs_7_), channel_id=1, source_target_pairs={{0,1},{1,0},{2,3},{3,2},{4,5},{5,4},{6,7},{7,6},{8,9},{9,8},{10,11... | collective-permute-start | bytes 786440 | tf_op jit(solution)/shard_map/ppermute | solution.py:33
  68.9 0.8 copy-start.7
  69.7 5.1 %collective-permute-start.13 = (bf16[4,4,8,128]{3,2,1,0:T(8,128)(2,1)S(1)}, bf16[4,4,8,128]{3,2,1,0:T(8,128)(2,1)S(1)}, u32[]{:S(2)}, u32[]{:S(2)}) collective-permute-start(bf16[4,4,8,128]{3,2,1,0:T(8,128)(2,1)S(1)} %pad_maximum_fusion.2.refs_0_), channel_id=1, source_target_pairs={{0,32},{1,33},{2,34},{3,35},{4,36},{5,37},{6,38},{7,39},{8,40},{9,... | collective-permute-start | bytes 98312 | tf_op jit(solution)/shard_map/ppermute | solution.py:33
  74.9 5.4 %collective-permute-start.12 = (bf16[4,4,8,128]{3,2,1,0:T(8,128)(2,1)S(1)}, bf16[4,4,8,128]{3,2,1,0:T(8,128)(2,1)S(1)}, u32[]{:S(2)}, u32[]{:S(2)}) collective-permute-start(bf16[4,4,8,128]{3,2,1,0:T(8,128)(2,1)S(1)} %pad_maximum_fusion.2.refs_0_), channel_id=1, source_target_pairs={{0,64},{1,65},{2,66},{3,67},{4,68},{5,69},{6,70},{7,71},{8,72},{9,... | collective-permute-start | bytes 98312 | tf_op jit(solution)/shard_map/ppermute | solution.py:33
  80.3 5.2 %collective-permute-start.11 = (bf16[4,4,8,128]{3,2,1,0:T(8,128)(2,1)S(1)}, bf16[4,4,8,128]{3,2,1,0:T(8,128)(2,1)S(1)}, u32[]{:S(2)}, u32[]{:S(2)}) collective-permute-start(bf16[4,4,8,128]{3,2,1,0:T(8,128)(2,1)S(1)} %pad_maximum_fusion.2.refs_0_), channel_id=1, source_target_pairs={{0,96},{1,97},{2,98},{3,99},{4,100},{5,101},{6,102},{7,103},{8,104... | collective-permute-start | bytes 98312 | tf_op jit(solution)/shard_map/ppermute | solution.py:33
  85.4 23.7 %collective-permute-start.23 = (bf16[128,2048]{1,0:T(8,128)(2,1)}, bf16[128,2048]{1,0:T(8,128)(2,1)S(1)}, u32[]{:S(2)}, u32[]{:S(2)}) collective-permute-start(bf16[128,2048]{1,0:T(8,128)(2,1)} %get-tuple-element.70.refs_14_), channel_id=1, source_target_pairs={{0,64},{1,65},{2,66},{3,67},{4,68},{5,69},{6,70},{7,71},{8,72},{9,... | collective-permute-start | bytes 1572872 | tf_op jit(solution)/shard_map/ppermute | solution.py:33
  86.5 24.0 %collective-permute-start.22 = (bf16[128,2048]{1,0:T(8,128)(2,1)}, bf16[128,2048]{1,0:T(8,128)(2,1)S(1)}, u32[]{:S(2)}, u32[]{:S(2)}) collective-permute-start(bf16[128,2048]{1,0:T(8,128)(2,1)} %get-tuple-element.70.refs_14_), channel_id=1, source_target_pairs={{0,32},{1,33},{2,34},{3,35},{4,36},{5,37},{6,38},{7,39},{8,40},{9,... | collective-permute-start | bytes 1572872 | tf_op jit(solution)/shard_map/ppermute | solution.py:33
  87.6 22.9 %collective-permute-start.21 = (bf16[128,2048]{1,0:T(8,128)(2,1)}, bf16[128,2048]{1,0:T(8,128)(2,1)S(1)}, u32[]{:S(2)}, u32[]{:S(2)}) collective-permute-start(bf16[128,2048]{1,0:T(8,128)(2,1)} %get-tuple-element.70.refs_14_), channel_id=1, source_target_pairs={{0,96},{1,97},{2,98},{3,99},{4,100},{5,101},{6,102},{7,103},{8,104... | collective-permute-start | bytes 1572872 | tf_op jit(solution)/shard_map/ppermute | solution.py:33
  90.5 1.0 copy-start.6
  91.5 1.0 copy-start.8
  99.0 7.3 %copy-start.3 = (f32[128,1024]{1,0:T(8,128)}, f32[128,1024]{1,0:T(8,128)S(1)}, u32[]{:S(2)}) copy-start(f32[128,1024]{1,0:T(8,128)S(1)} %get-tuple-element.60.a_ref) | copy-start | bytes 1572868
  99.0 11.5 %copy-start.9 = (bf16[128,2048]{1,0:T(8,128)(2,1)S(1)}, bf16[128,2048]{1,0:T(8,128)(2,1)}, u32[]{:S(2)}) copy-start(bf16[128,2048]{1,0:T(8,128)(2,1)} %get-tuple-element.70.refs_14_) | copy-start | bytes 1572868
  106.3 0.8 copy-start
  107.1 21.9 %collective-permute-start.27 = (bf16[128,1024]{1,0:T(8,128)(2,1)}, bf16[128,1024]{1,0:T(8,128)(2,1)}, u32[]{:S(2)}, u32[]{:S(2)}) collective-permute-start(bf16[128,1024]{1,0:T(8,128)(2,1)} %get-tuple-element.81), channel_id=1, source_target_pairs={{0,16},{1,17},{2,18},{3,19},{4,20},{5,21},{6,22},{7,23},{8,24},{9,... | collective-permute-start | bytes 786440 | tf_op jit(solution)/shard_map/ppermute | solution.py:33
  107.1 11.4 %collective-permute-start.24 = (bf16[128,1024]{1,0:T(8,128)(2,1)S(1)}, bf16[128,1024]{1,0:T(8,128)(2,1)S(1)}, u32[]{:S(2)}, u32[]{:S(2)}) collective-permute-start(bf16[128,1024]{1,0:T(8,128)(2,1)S(1)} %get-tuple-element.72), channel_id=1, source_target_pairs={{0,16},{1,17},{2,18},{3,19},{4,20},{5,21},{6,22},{7,23},{8,24},{9,... | collective-permute-start | bytes 786440 | tf_op jit(solution)/shard_map/ppermute | solution.py:33
  117.0 0.8 copy-start.1
  117.8 13.1 %collective-permute-start.26 = (bf16[128,1024]{1,0:T(8,128)(2,1)S(1)}, bf16[128,1024]{1,0:T(8,128)(2,1)}, u32[]{:S(2)}, u32[]{:S(2)}) collective-permute-start(bf16[128,1024]{1,0:T(8,128)(2,1)S(1)} %get-tuple-element.79), channel_id=1, source_target_pairs={{0,16},{1,17},{2,18},{3,19},{4,20},{5,21},{6,22},{7,23},{8,24},{9,... | collective-permute-start | bytes 786440 | tf_op jit(solution)/shard_map/ppermute | solution.py:33
  118.5 6.5 %copy-start.15 = (bf16[128,1024]{1,0:T(8,128)(2,1)}, bf16[128,1024]{1,0:T(8,128)(2,1)S(1)}, u32[]{:S(2)}) copy-start(bf16[128,1024]{1,0:T(8,128)(2,1)S(1)} %collective-permute-done.24.b_ref) | copy-start | bytes 786436
  125.0 0.8 copy-start.2
  125.8 7.5 %collective-permute-start.25 = (bf16[128,1024]{1,0:T(8,128)(2,1)S(1)}, bf16[128,1024]{1,0:T(8,128)(2,1)S(1)}, u32[]{:S(2)}, u32[]{:S(2)}) collective-permute-start(bf16[128,1024]{1,0:T(8,128)(2,1)S(1)} %get-tuple-element.78), channel_id=1, source_target_pairs={{0,16},{1,17},{2,18},{3,19},{4,20},{5,21},{6,22},{7,23},{8,24},{9,... | collective-permute-start | bytes 786440 | tf_op jit(solution)/shard_map/ppermute | solution.py:33
  133.3 0.7 copy-start.14

commit v9 on v7

--- a/solution.py
+++ b/solution.py
@@ -289,12 +289,12 @@
                 )
                 lines = [w_ref[places[s], pl.ds(t * 4 + i, 1), :] for i in range(tile // 128)]
                 total = total + jnp.concatenate(lines, 1) * product
-            mine_ref[:, cols] = total[:128]
+            mine_ref[:, cols] = total[:128].astype(BF16)
             other_ref[:, cols] = total[128:].astype(BF16)
 
     return pl.pallas_call(
         kernel,
-        out_shape=(shape((128, cells), F32), shape((128, cells), BF16)),
+        out_shape=(shape((128, cells), BF16), shape((128, cells), BF16)),
         in_specs=[VMEM] * 4 + [ANY] * 15,
         out_specs=(VMEM, VMEM),
         scratch_shapes=[
@@ -317,7 +317,7 @@
 
     def kernel(a_ref, b_ref, *refs):
         o_ref = refs[-1]
-        total = a_ref[...] + b_ref[...].astype(F32)
+        total = a_ref[...].astype(F32) + b_ref[...].astype(F32)
         lines = jnp.stack([total[:, y * 128 : (y + 1) * 128] for y in range(8)], 0)
         o_ref[:, 0] = jnp.swapaxes(lines, 0, 1)
 

time: 123 us -> 124 us (level)
    unnamed x32 -> x30, local copies, waits for them, and re-layouts: 9.33 us -> 9.73 us
  transfers between devices with their start and end apart: 29 -> 29, of which waited for: 10 -> 10; matrix products, arithmetic and copies ran while one was open for 1% -> 1% of each run, Pallas kernels for 38% -> 37%
where the time goes in v9:
time: 124 us; the launch traced here: 123 us
  Pallas kernels  49.8 us (40%)
  starting transfers between devices  35.9 us (29%)
  waiting for transfers between devices  25.4 us (20%)
  local copies, waits for them, and re-layouts  10.6 us (9%)
    ppermute x27, starting transfers between devices, shift(): return lax.ppermute(value, BOTH, pairs)  34.6 us
    pallas_call x4, Pallas kernels, collide(): pl.pallas_call(kernel, out_shape=(shape((128, cells), BF16), shape((128,...  28.2 us
    ppermute x27, waiting for transfers between devices, shift(): return lax.ppermute(value, BOTH, pairs)  25.3 us
    unnamed x30, local copies, waits for them, and re-layouts  9.73 us
    pallas_call x4, Pallas kernels, combine(): pl.pallas_call(kernel, grid=(128 // step,), out_shape=shape((128, 4, 8, 1...  7.49 us
    pallas_call x1, Pallas kernels, transport(): pl.pallas_call(kernel, grid=(rows // STEP,), out_shape=(shape(density.sha...  5.14 us
    pallas_call x1, Pallas kernels, transport_inner(): pl.pallas_call(kernel, grid=(rows // STEP,), out_shape=(shape((rows, 2048...  4.47 us
    pallas_call x1, Pallas kernels, pack(): pl.pallas_call(kernel, out_shape=(shape((rows + 3, *dims), BF16), shape((...  2.73 us
  transfers between devices with their start and end apart: 29, of which 10 were waited for; matrix products, arithmetic and copies ran while one was open for 1% of the time, Pallas kernels for 37%

profile of v9, /device:TPU:0, one launch (start us, length us, event | category | flops | bytes accessed | tf_op | source)
XLA Modules:
  0.0 123.3 jit_solution(14396125645731817561)
XLA Ops:
  0.6 1.8 %split_slice.1 = bf16[256,512]{1,0:T(8,128)(2,1)} custom-call(bf16[4,2,128,128]{3,2,1,0:T(8,128)(2,1)} %bitcast.1), custom_call_target="tpu_custom_call" | custom-call | tf_op jit(solution)/shard_map/split_slice/pallas_call | solution.py:89
  2.4 2.0 %collective-permute-start.1 = (bf16[256,512]{1,0:T(8,128)(2,1)}, bf16[256,512]{1,0:T(8,128)(2,1)S(1)}, u32[]{:S(2)}, u32[]{:S(2)}) collective-permute-start(bf16[256,512]{1,0:T(8,128)(2,1)} %split_slice.1), channel_id=1, source_target_pairs={{0,16},{1,17},{2,18},{3,19},{4,20},{5,21},{6,22},{7,23},{8,24},{9,... | collective-permute-start | bytes 786440 | tf_op jit(solution)/shard_map/ppermute | solution.py:33
  4.4 2.7 %pack.1 = (bf16[131,8,128]{2,1,0:T(8,128)(2,1)}, bf16[128,8,128]{2,1,0:T(8,128)(2,1)}, bf16[129,2,8,128]{3,2,1,0:T(8,128)(2,1)}) custom-call(f32[128,4,8,128]{3,2,1,0:T(8,128)} %d_ref.4, s32[4,8,128]{2,1,0:T(8,128)} %l_ref.5), custom_call_target="tpu_custom_call" | custom-call | tf_op jit(solution)/shard_map/pack/pallas_call | solution.py:68
  7.8 5.0 %collective-permute-start.2 = (bf16[129,2,8,128]{3,2,1,0:T(8,128)(2,1)}, bf16[129,2,8,128]{3,2,1,0:T(8,128)(2,1)S(1)}, u32[]{:S(2)}, u32[]{:S(2)}) collective-permute-start(bf16[129,2,8,128]{3,2,1,0:T(8,128)(2,1)} %get-tuple-element.46), channel_id=1, source_target_pairs={{0,1},{1,0},{2,3},{3,2},{4,5},{5,4},{6,7},{7,6},{8,9},{9,8},{10,11... | collective-permute-start | bytes 1585160 | tf_op jit(solution)/shard_map/ppermute | solution.py:33
  12.9 2.0 %collective-permute-start.4 = (bf16[256,512]{1,0:T(8,128)(2,1)S(1)}, bf16[256,512]{1,0:T(8,128)(2,1)S(1)}, u32[]{:S(2)}, u32[]{:S(2)}) collective-permute-start(bf16[256,512]{1,0:T(8,128)(2,1)S(1)} %pad_maximum_fusion.1), channel_id=1, source_target_pairs={{0,18},{1,19},{2,16},{3,17},{4,22},{5,23},{6,20},{7,21},{8,26},{9,... | collective-permute-start | bytes 786440 | tf_op jit(solution)/shard_map/ppermute | solution.py:33
  14.9 0.7 copy-done.9
  15.7 0.8 copy-done.8
  16.5 4.5 %transport_inner.1 = (bf16[128,2048]{1,0:T(8,128)(2,1)}, bf16[2,4,8,128]{3,2,1,0:T(8,128)(2,1)}) custom-call(s32[128]{0:T(128)} %h_ref.3, f32[128]{0:T(128)} %c_ref.3, f32[128,4,8,128]{3,2,1,0:T(8,128)} %d_ref.4, s32[4,8,128]{2,1,0:T(8,128)} %l_ref.5, bf16[131,8,128]{2,1,0:T(8,128)(2,1)} %copy-done.9, bf16[131,8,128]{2,1,0:T(8,128)(2,1)} %copy-done.9, ...), custom_call_target="tpu_custom_call" | custom-call | flops 2097152 | bytes 3145728 | tf_op jit(solution)/shard_map/transport_inner/pallas_call | solution.py:182
  20.9 3.0 %collective-permute-done.4 = bf16[256,512]{1,0:T(8,128)(2,1)S(1)} collective-permute-done((bf16[256,512]{1,0:T(8,128)(2,1)S(1)}, bf16[256,512]{1,0:T(8,128)(2,1)S(1)}, u32[]{:S(2)}, u32[]{:S(2)}) %collective-permute-start.4) | collective-permute-done | bytes 262176 | tf_op jit(solution)/shard_map/ppermute | solution.py:33
  24.0 1.5 %collective-permute-start.7 = (bf16[512,512]{1,0:T(8,128)(2,1)S(1)}, bf16[512,512]{1,0:T(8,128)(2,1)S(1)}, u32[]{:S(2)}, u32[]{:S(2)}) collective-permute-start(bf16[512,512]{1,0:T(8,128)(2,1)S(1)} %pad_maximum_fusion.refs_4_), channel_id=1, source_target_pairs={{0,1},{1,0},{2,3},{3,2},{4,5},{5,4},{6,7},{7,6},{8,9},{9,8},{10,11... | collective-permute-start | bytes 1572872 | tf_op jit(solution)/shard_map/ppermute | solution.py:33
  25.5 3.5 %collective-permute-start.6 = (bf16[512,512]{1,0:T(8,128)(2,1)S(1)}, bf16[512,512]{1,0:T(8,128)(2,1)S(1)}, u32[]{:S(2)}, u32[]{:S(2)}) collective-permute-start(bf16[512,512]{1,0:T(8,128)(2,1)S(1)} %pad_maximum_fusion.refs_4_), channel_id=1, source_target_pairs={{0,12},{1,13},{2,14},{3,15},{4,0},{5,1},{6,2},{7,3},{8,4},{9,5},{1... | collective-permute-start | bytes 1572872 | tf_op jit(solution)/shard_map/ppermute | solution.py:33
  28.9 3.0 %collective-permute-start.9 = (bf16[128,2048]{1,0:T(8,128)(2,1)}, bf16[128,2048]{1,0:T(8,128)(2,1)S(1)}, u32[]{:S(2)}, u32[]{:S(2)}) collective-permute-start(bf16[128,2048]{1,0:T(8,128)(2,1)} %get-tuple-element.51.refs_14_), channel_id=1, source_target_pairs={{0,96},{1,97},{2,98},{3,99},{4,100},{5,101},{6,102},{7,103},{8,104... | collective-permute-start | bytes 1572872 | tf_op jit(solution)/shard_map/ppermute | solution.py:33
  32.0 3.9 %collective-permute-done.10 = bf16[2,4,8,128]{3,2,1,0:T(8,128)(2,1)S(1)} collective-permute-done((bf16[2,4,8,128]{3,2,1,0:T(8,128)(2,1)}, bf16[2,4,8,128]{3,2,1,0:T(8,128)(2,1)S(1)}, u32[]{:S(2)}, u32[]{:S(2)}) %collective-permute-start.10) | collective-permute-done | bytes 16416 | tf_op jit(solution)/shard_map/ppermute | solution.py:33
  36.6 0.7 pad_maximum_fusion.2.refs_0_
  37.3 3.2 %collective-permute-done.6.refs_6_ = bf16[512,512]{1,0:T(8,128)(2,1)S(1)} collective-permute-done((bf16[512,512]{1,0:T(8,128)(2,1)S(1)}, bf16[512,512]{1,0:T(8,128)(2,1)S(1)}, u32[]{:S(2)}, u32[]{:S(2)}) %collective-permute-start.6) | collective-permute-done | bytes 524320 | tf_op jit(solution)/shard_map/ppermute | solution.py:33
  40.5 3.4 %collective-permute-done.5.refs_5_ = bf16[512,512]{1,0:T(8,128)(2,1)S(1)} collective-permute-done((bf16[512,512]{1,0:T(8,128)(2,1)S(1)}, bf16[512,512]{1,0:T(8,128)(2,1)S(1)}, u32[]{:S(2)}, u32[]{:S(2)}) %collective-permute-start.5) | collective-permute-done | bytes 524320 | tf_op jit(solution)/shard_map/ppermute | solution.py:33
  43.9 2.9 %collective-permute-done.8.refs_16_ = bf16[128,2048]{1,0:T(8,128)(2,1)S(1)} collective-permute-done((bf16[128,2048]{1,0:T(8,128)(2,1)}, bf16[128,2048]{1,0:T(8,128)(2,1)S(1)}, u32[]{:S(2)}, u32[]{:S(2)}) %collective-permute-start.8) | collective-permute-done | bytes 524320 | tf_op jit(solution)/shard_map/ppermute | solution.py:33
  46.9 1.7 %collective-permute-start.12 = (bf16[4,4,8,128]{3,2,1,0:T(8,128)(2,1)S(1)}, bf16[4,4,8,128]{3,2,1,0:T(8,128)(2,1)S(1)}, u32[]{:S(2)}, u32[]{:S(2)}) collective-permute-start(bf16[4,4,8,128]{3,2,1,0:T(8,128)(2,1)S(1)} %pad_maximum_fusion.2.refs_0_), channel_id=1, source_target_pairs={{0,64},{1,65},{2,66},{3,67},{4,68},{5,69},{6,70},{7,71},{8,72},{9,... | collective-permute-start | bytes 98312 | tf_op jit(solution)/shard_map/ppermute | solution.py:33
  48.6 1.5 %collective-permute-start.11 = (bf16[4,4,8,128]{3,2,1,0:T(8,128)(2,1)S(1)}, bf16[4,4,8,128]{3,2,1,0:T(8,128)(2,1)S(1)}, u32[]{:S(2)}, u32[]{:S(2)}) collective-permute-start(bf16[4,4,8,128]{3,2,1,0:T(8,128)(2,1)S(1)} %pad_maximum_fusion.2.refs_0_), channel_id=1, source_target_pairs={{0,96},{1,97},{2,98},{3,99},{4,100},{5,101},{6,102},{7,103},{8,104... | collective-permute-start | bytes 98312 | tf_op jit(solution)/shard_map/ppermute | solution.py:33
  50.1 3.0 %collective-permute-start.15 = (bf16[256,512]{1,0:T(8,128)(2,1)S(1)}, bf16[256,512]{1,0:T(8,128)(2,1)S(1)}, u32[]{:S(2)}, u32[]{:S(2)}) collective-permute-start(bf16[256,512]{1,0:T(8,128)(2,1)S(1)} %slice.35), channel_id=1, source_target_pairs={{0,12},{1,13},{2,14},{3,15},{4,0},{5,1},{6,2},{7,3},{8,4},{9,5},{1... | collective-permute-start | bytes 786440 | tf_op jit(solution)/shard_map/ppermute | solution.py:33
  53.9 0.9 collective-permute-start.20
  55.3 0.7 slice.37
  56.0 1.0 collective-permute-done.15.refs_8_
  57.0 1.4 %collective-permute-start.21 = (bf16[64,2048]{1,0:T(8,128)(2,1)}, bf16[64,2048]{1,0:T(8,128)(2,1)}, u32[]{:S(2)}, u32[]{:S(2)}) collective-permute-start(bf16[64,2048]{1,0:T(8,128)(2,1)} %slice.37), channel_id=1, source_target_pairs={{0,96},{1,97},{2,98},{3,99},{4,100},{5,101},{6,102},{7,103},{8,104... | collective-permute-start | bytes 786440 | tf_op jit(solution)/shard_map/ppermute | solution.py:33
  58.4 2.6 %collective-permute-done.14.refs_7_ = bf16[256,512]{1,0:T(8,128)(2,1)} collective-permute-done((bf16[256,512]{1,0:T(8,128)(2,1)S(1)}, bf16[256,512]{1,0:T(8,128)(2,1)}, u32[]{:S(2)}, u32[]{:S(2)}) %collective-permute-start.14) | collective-permute-done | bytes 262176 | tf_op jit(solution)/shard_map/ppermute | solution.py:33
  61.5 0.7 copy-done.6
  62.2 5.1 %transport.1 = (f32[128,4,8,128]{3,2,1,0:T(8,128)}, bf16[128,2048]{1,0:T(8,128)(2,1)}) custom-call(s32[128]{0:T(128)} %h_ref.3, f32[128]{0:T(128)} %c_ref.3, f32[128,4,8,128]{3,2,1,0:T(8,128)} %d_ref.4, s32[4,8,128]{2,1,0:T(8,128)} %l_ref.5, bf16[131,8,128]{2,1,0:T(8,128)(2,1)} %copy-done.9, bf16[131,8,128]{2,1,0:T(8,128)(2,1)} %copy-done.9, ...), custom_call_target="tpu_custom_call" | custom-call | flops 4194304 | bytes 6291456 | tf_op jit(solution)/shard_map/transport/pallas_call | solution.py:219
  67.4 3.0 %collective-permute-start.24 = (bf16[128,2048]{1,0:T(8,128)(2,1)}, bf16[128,2048]{1,0:T(8,128)(2,1)S(1)}, u32[]{:S(2)}, u32[]{:S(2)}) collective-permute-start(bf16[128,2048]{1,0:T(8,128)(2,1)} %get-tuple-element.70.refs_14_), channel_id=1, source_target_pairs={{0,64},{1,65},{2,66},{3,67},{4,68},{5,69},{6,70},{7,71},{8,72},{9,... | collective-permute-start | bytes 1572872 | tf_op jit(solution)/shard_map/ppermute | solution.py:33
  70.3 3.2 %collective-permute-start.22 = (bf16[128,2048]{1,0:T(8,128)(2,1)}, bf16[128,2048]{1,0:T(8,128)(2,1)S(1)}, u32[]{:S(2)}, u32[]{:S(2)}) collective-permute-start(bf16[128,2048]{1,0:T(8,128)(2,1)} %get-tuple-element.70.refs_14_), channel_id=1, source_target_pairs={{0,96},{1,97},{2,98},{3,99},{4,100},{5,101},{6,102},{7,103},{8,104... | collective-permute-start | bytes 1572872 | tf_op jit(solution)/shard_map/ppermute | solution.py:33
  73.6 1.0 copy-done.4
  74.6 0.9 copy-done.7
  75.6 7.2 %collide.4 = (bf16[128,1024]{1,0:T(8,128)(2,1)S(1)}, bf16[128,1024]{1,0:T(8,128)(2,1)S(1)}) custom-call(bf16[4,4,8,128]{3,2,1,0:T(8,128)(2,1)S(1)} %pad_maximum_fusion.2.refs_0_, bf16[4,4,8,128]{3,2,1,0:T(8,128)(2,1)S(1)} %collective-permute-done.11.refs_1_, bf16[4,4,8,128]{3,2,1,0:T(8,128)(2,1)S(1)} %collective-permute-done.12.refs_2_, ...), custom_call_target="tpu_custom_call" | custom-call | flops 4294967296 | bytes 6291456 | tf_op jit(solution)/shard_map/collide/pallas_call | solution.py:295
  82.8 0.7 copy-done.1
  83.5 8.0 %collide.5 = (bf16[128,1024]{1,0:T(8,128)(2,1)S(1)}, bf16[128,1024]{1,0:T(8,128)(2,1)}) custom-call(bf16[4,4,8,128]{3,2,1,0:T(8,128)(2,1)S(1)} %pad_maximum_fusion.2.refs_0_, bf16[4,4,8,128]{3,2,1,0:T(8,128)(2,1)S(1)} %collective-permute-done.11.refs_1_, bf16[4,4,8,128]{3,2,1,0:T(8,128)(2,1)S(1)} %collective-permute-done.12.refs_2_, ...), custom_call_target="tpu_custom_call" | custom-call | flops 4294967296 | bytes 6291456 | tf_op jit(solution)/shard_map/collide/pallas_call | solution.py:295
  91.5 0.7 copy-done
  92.2 2.0 %collective-permute-start.25 = (bf16[128,1024]{1,0:T(8,128)(2,1)S(1)}, bf16[128,1024]{1,0:T(8,128)(2,1)S(1)}, u32[]{:S(2)}, u32[]{:S(2)}) collective-permute-start(bf16[128,1024]{1,0:T(8,128)(2,1)S(1)} %get-tuple-element.72), channel_id=1, source_target_pairs={{0,16},{1,17},{2,18},{3,19},{4,20},{5,21},{6,22},{7,23},{8,24},{9,... | collective-permute-start | bytes 786440 | tf_op jit(solution)/shard_map/ppermute | solution.py:33
  94.7 6.5 %collide.6 = (bf16[128,1024]{1,0:T(8,128)(2,1)S(1)}, bf16[128,1024]{1,0:T(8,128)(2,1)S(1)}) custom-call(bf16[4,4,8,128]{3,2,1,0:T(8,128)(2,1)S(1)} %pad_maximum_fusion.2.refs_0_, bf16[4,4,8,128]{3,2,1,0:T(8,128)(2,1)S(1)} %collective-permute-done.11.refs_1_, bf16[4,4,8,128]{3,2,1,0:T(8,128)(2,1)S(1)} %collective-permute-done.12.refs_2_, ...), custom_call_target="tpu_custom_call" | custom-call | flops 4294967296 | bytes 6291456 | tf_op jit(solution)/shard_map/collide/pallas_call | solution.py:295
  101.3 0.7 copy-done.2
  101.9 4.2 %collective-permute-done.25.b_ref = bf16[128,1024]{1,0:T(8,128)(2,1)S(1)} collective-permute-done((bf16[128,1024]{1,0:T(8,128)(2,1)S(1)}, bf16[128,1024]{1,0:T(8,128)(2,1)S(1)}, u32[]{:S(2)}, u32[]{:S(2)}) %collective-permute-start.25) | collective-permute-done | bytes 262176 | tf_op jit(solution)/shard_map/ppermute | solution.py:33
  106.2 0.7 copy-done.13
  106.9 6.5 %collide.7 = (bf16[128,1024]{1,0:T(8,128)(2,1)S(1)}, bf16[128,1024]{1,0:T(8,128)(2,1)S(1)}) custom-call(bf16[4,4,8,128]{3,2,1,0:T(8,128)(2,1)S(1)} %pad_maximum_fusion.2.refs_0_, bf16[4,4,8,128]{3,2,1,0:T(8,128)(2,1)S(1)} %collective-permute-done.11.refs_1_, bf16[4,4,8,128]{3,2,1,0:T(8,128)(2,1)S(1)} %collective-permute-done.12.refs_2_, ...), custom_call_target="tpu_custom_call" | custom-call | flops 4294967296 | bytes 6291456 | tf_op jit(solution)/shard_map/collide/pallas_call | solution.py:295
  113.4 0.7 copy-done.3
  114.4 1.9 %combine.4.refs_0_ = f32[128,4,8,128]{3,2,1,0:T(8,128)} custom-call(bf16[128,1024]{1,0:T(8,128)(2,1)} %copy-done.1, bf16[128,1024]{1,0:T(8,128)(2,1)} %copy-done.13), custom_call_target="tpu_custom_call" | custom-call | flops 131072 | bytes 1310720 | tf_op jit(solution)/shard_map/combine/pallas_call | solution.py:326
  116.3 0.7 copy-done.12
  117.0 1.9 %combine.5.refs_0_ = f32[128,4,8,128]{3,2,1,0:T(8,128)} custom-call(bf16[128,1024]{1,0:T(8,128)(2,1)} %copy-done, bf16[128,1024]{1,0:T(8,128)(2,1)} %copy-done.12, f32[128,4,8,128]{3,2,1,0:T(8,128)} %combine.4.refs_0_), custom_call_target="tpu_custom_call", output_to_operand_aliasing={{}: (2, {})} | custom-call | flops 131072 | bytes 1310720 | tf_op jit(solution)/shard_map/combine/pallas_call | solution.py:326
  118.8 1.9 %combine.6.refs_0_ = f32[128,4,8,128]{3,2,1,0:T(8,128)} custom-call(bf16[128,1024]{1,0:T(8,128)(2,1)} %copy-done.2, bf16[128,1024]{1,0:T(8,128)(2,1)} %collective-permute-done.27.b_ref, f32[128,4,8,128]{3,2,1,0:T(8,128)} %combine.5.refs_0_), custom_call_target="tpu_custom_call", output_to_operand_aliasing={{}: (2, {})} | custom-call | flops 131072 | bytes 1310720 | tf_op jit(solution)/shard_map/combine/pallas_call | solution.py:326
  120.7 0.7 copy-done.14
  121.4 1.9 %combine.7 = f32[128,4,8,128]{3,2,1,0:T(8,128)} custom-call(bf16[128,1024]{1,0:T(8,128)(2,1)} %copy-done.3, bf16[128,1024]{1,0:T(8,128)(2,1)} %copy-done.14, f32[128,4,8,128]{3,2,1,0:T(8,128)} %combine.6.refs_0_), custom_call_target="tpu_custom_call", output_to_operand_aliasing={{}: (2, {})} | custom-call | flops 131072 | bytes 1310720 | tf_op jit(solution)/shard_map/combine/pallas_call | solution.py:326
  (62 shorter events, 4.1 us)
Async XLA Ops:
  2.4 10.4 %copy-start.10 = (bf16[256,512]{1,0:T(8,128)(2,1)S(1)}, bf16[256,512]{1,0:T(8,128)(2,1)}, u32[]{:S(2)}) copy-start(bf16[256,512]{1,0:T(8,128)(2,1)} %split_slice.1) | copy-start | bytes 786436
  2.4 10.4 %collective-permute-start.1 = (bf16[256,512]{1,0:T(8,128)(2,1)}, bf16[256,512]{1,0:T(8,128)(2,1)S(1)}, u32[]{:S(2)}, u32[]{:S(2)}) collective-permute-start(bf16[256,512]{1,0:T(8,128)(2,1)} %split_slice.1), channel_id=1, source_target_pairs={{0,16},{1,17},{2,18},{3,19},{4,20},{5,21},{6,22},{7,23},{8,24},{9,... | collective-permute-start | bytes 786440 | tf_op jit(solution)/shard_map/ppermute | solution.py:33
  7.2 7.8 %collective-permute-start = (bf16[131,8,128]{2,1,0:T(8,128)(2,1)}, bf16[131,8,128]{2,1,0:T(8,128)(2,1)S(1)}, u32[]{:S(2)}, u32[]{:S(2)}) collective-permute-start(bf16[131,8,128]{2,1,0:T(8,128)(2,1)} %get-tuple-element.44), channel_id=1, source_target_pairs={{1,2},{3,4},{5,6},{7,8},{9,10},{11,12},{13,14},{2,1},{4,3},{6,5},{... | collective-permute-start | bytes 804872 | tf_op jit(solution)/shard_map/ppermute | solution.py:346
  7.8 7.1 %collective-permute-start.2 = (bf16[129,2,8,128]{3,2,1,0:T(8,128)(2,1)}, bf16[129,2,8,128]{3,2,1,0:T(8,128)(2,1)S(1)}, u32[]{:S(2)}, u32[]{:S(2)}) collective-permute-start(bf16[129,2,8,128]{3,2,1,0:T(8,128)(2,1)} %get-tuple-element.46), channel_id=1, source_target_pairs={{0,1},{1,0},{2,3},{3,2},{4,5},{5,4},{6,7},{7,6},{8,9},{9,8},{10,11... | collective-permute-start | bytes 1585160 | tf_op jit(solution)/shard_map/ppermute | solution.py:33
  12.9 11.0 %collective-permute-start.4 = (bf16[256,512]{1,0:T(8,128)(2,1)S(1)}, bf16[256,512]{1,0:T(8,128)(2,1)S(1)}, u32[]{:S(2)}, u32[]{:S(2)}) collective-permute-start(bf16[256,512]{1,0:T(8,128)(2,1)S(1)} %pad_maximum_fusion.1), channel_id=1, source_target_pairs={{0,18},{1,19},{2,16},{3,17},{4,22},{5,23},{6,20},{7,21},{8,26},{9,... | collective-permute-start | bytes 786440 | tf_op jit(solution)/shard_map/ppermute | solution.py:33
  14.9 0.7 copy-start.9
  15.7 0.8 copy-start.8
  24.0 5.0 %collective-permute-start.7 = (bf16[512,512]{1,0:T(8,128)(2,1)S(1)}, bf16[512,512]{1,0:T(8,128)(2,1)S(1)}, u32[]{:S(2)}, u32[]{:S(2)}) collective-permute-start(bf16[512,512]{1,0:T(8,128)(2,1)S(1)} %pad_maximum_fusion.refs_4_), channel_id=1, source_target_pairs={{0,1},{1,0},{2,3},{3,2},{4,5},{5,4},{6,7},{7,6},{8,9},{9,8},{10,11... | collective-permute-start | bytes 1572872 | tf_op jit(solution)/shard_map/ppermute | solution.py:33
  25.5 15.0 %collective-permute-start.6 = (bf16[512,512]{1,0:T(8,128)(2,1)S(1)}, bf16[512,512]{1,0:T(8,128)(2,1)S(1)}, u32[]{:S(2)}, u32[]{:S(2)}) collective-permute-start(bf16[512,512]{1,0:T(8,128)(2,1)S(1)} %pad_maximum_fusion.refs_4_), channel_id=1, source_target_pairs={{0,12},{1,13},{2,14},{3,15},{4,0},{5,1},{6,2},{7,3},{8,4},{9,5},{1... | collective-permute-start | bytes 1572872 | tf_op jit(solution)/shard_map/ppermute | solution.py:33
  28.9 15.0 %collective-permute-start.5 = (bf16[512,512]{1,0:T(8,128)(2,1)S(1)}, bf16[512,512]{1,0:T(8,128)(2,1)S(1)}, u32[]{:S(2)}, u32[]{:S(2)}) collective-permute-start(bf16[512,512]{1,0:T(8,128)(2,1)S(1)} %pad_maximum_fusion.refs_4_), channel_id=1, source_target_pairs={{0,4},{1,5},{2,6},{3,7},{4,8},{5,9},{6,10},{7,11},{8,12},{9,13},{1... | collective-permute-start | bytes 1572872 | tf_op jit(solution)/shard_map/ppermute | solution.py:33
  28.9 15.0 %collective-permute-start.9 = (bf16[128,2048]{1,0:T(8,128)(2,1)}, bf16[128,2048]{1,0:T(8,128)(2,1)S(1)}, u32[]{:S(2)}, u32[]{:S(2)}) collective-permute-start(bf16[128,2048]{1,0:T(8,128)(2,1)} %get-tuple-element.51.refs_14_), channel_id=1, source_target_pairs={{0,96},{1,97},{2,98},{3,99},{4,100},{5,101},{6,102},{7,103},{8,104... | collective-permute-start | bytes 1572872 | tf_op jit(solution)/shard_map/ppermute | solution.py:33
  32.0 14.9 %collective-permute-start.8 = (bf16[128,2048]{1,0:T(8,128)(2,1)}, bf16[128,2048]{1,0:T(8,128)(2,1)S(1)}, u32[]{:S(2)}, u32[]{:S(2)}) collective-permute-start(bf16[128,2048]{1,0:T(8,128)(2,1)} %get-tuple-element.51.refs_14_), channel_id=1, source_target_pairs={{0,32},{1,33},{2,34},{3,35},{4,36},{5,37},{6,38},{7,39},{8,40},{9,... | collective-permute-start | bytes 1572872 | tf_op jit(solution)/shard_map/ppermute | solution.py:33
  32.0 3.9 %collective-permute-start.10 = (bf16[2,4,8,128]{3,2,1,0:T(8,128)(2,1)}, bf16[2,4,8,128]{3,2,1,0:T(8,128)(2,1)S(1)}, u32[]{:S(2)}, u32[]{:S(2)}) collective-permute-start(bf16[2,4,8,128]{3,2,1,0:T(8,128)(2,1)} %get-tuple-element.55), channel_id=1, source_target_pairs={{0,16},{1,17},{2,18},{3,19},{4,20},{5,21},{6,22},{7,23},{8,24},{9,... | collective-permute-start | bytes 49160 | tf_op jit(solution)/shard_map/ppermute | solution.py:33
  35.9 17.3 %collective-permute-start.3 = (bf16[128,8,128]{2,1,0:T(8,128)(2,1)}, bf16[128,8,128]{2,1,0:T(8,128)(2,1)S(1)}, u32[]{:S(2)}, u32[]{:S(2)}) collective-permute-start(bf16[128,8,128]{2,1,0:T(8,128)(2,1)} %get-tuple-element.48), channel_id=1, source_target_pairs={{1,2},{3,4},{5,6},{7,8},{9,10},{11,12},{13,14},{2,1},{4,3},{6,5},{... | collective-permute-start | bytes 786440 | tf_op jit(solution)/shard_map/ppermute | solution.py:352
  46.8 7.1 %collective-permute-start.13 = (bf16[4,4,8,128]{3,2,1,0:T(8,128)(2,1)S(1)}, bf16[4,4,8,128]{3,2,1,0:T(8,128)(2,1)S(1)}, u32[]{:S(2)}, u32[]{:S(2)}) collective-permute-start(bf16[4,4,8,128]{3,2,1,0:T(8,128)(2,1)S(1)} %pad_maximum_fusion.2.refs_0_), channel_id=1, source_target_pairs={{0,32},{1,33},{2,34},{3,35},{4,36},{5,37},{6,38},{7,39},{8,40},{9,... | collective-permute-start | bytes 98312 | tf_op jit(solution)/shard_map/ppermute | solution.py:33
  46.9 7.9 %collective-permute-start.12 = (bf16[4,4,8,128]{3,2,1,0:T(8,128)(2,1)S(1)}, bf16[4,4,8,128]{3,2,1,0:T(8,128)(2,1)S(1)}, u32[]{:S(2)}, u32[]{:S(2)}) collective-permute-start(bf16[4,4,8,128]{3,2,1,0:T(8,128)(2,1)S(1)} %pad_maximum_fusion.2.refs_0_), channel_id=1, source_target_pairs={{0,64},{1,65},{2,66},{3,67},{4,68},{5,69},{6,70},{7,71},{8,72},{9,... | collective-permute-start | bytes 98312 | tf_op jit(solution)/shard_map/ppermute | solution.py:33
  48.6 6.2 %collective-permute-start.11 = (bf16[4,4,8,128]{3,2,1,0:T(8,128)(2,1)S(1)}, bf16[4,4,8,128]{3,2,1,0:T(8,128)(2,1)S(1)}, u32[]{:S(2)}, u32[]{:S(2)}) collective-permute-start(bf16[4,4,8,128]{3,2,1,0:T(8,128)(2,1)S(1)} %pad_maximum_fusion.2.refs_0_), channel_id=1, source_target_pairs={{0,96},{1,97},{2,98},{3,99},{4,100},{5,101},{6,102},{7,103},{8,104... | collective-permute-start | bytes 98312 | tf_op jit(solution)/shard_map/ppermute | solution.py:33
  50.1 6.9 %collective-permute-start.15 = (bf16[256,512]{1,0:T(8,128)(2,1)S(1)}, bf16[256,512]{1,0:T(8,128)(2,1)S(1)}, u32[]{:S(2)}, u32[]{:S(2)}) collective-permute-start(bf16[256,512]{1,0:T(8,128)(2,1)S(1)} %slice.35), channel_id=1, source_target_pairs={{0,12},{1,13},{2,14},{3,15},{4,0},{5,1},{6,2},{7,3},{8,4},{9,5},{1... | collective-permute-start | bytes 786440 | tf_op jit(solution)/shard_map/ppermute | solution.py:33
  53.2 0.7 copy-start.11
  53.2 7.8 %collective-permute-start.14 = (bf16[256,512]{1,0:T(8,128)(2,1)S(1)}, bf16[256,512]{1,0:T(8,128)(2,1)}, u32[]{:S(2)}, u32[]{:S(2)}) collective-permute-start(bf16[256,512]{1,0:T(8,128)(2,1)S(1)} %slice.34), channel_id=1, source_target_pairs={{0,4},{1,5},{2,6},{3,7},{4,8},{5,9},{6,10},{7,11},{8,12},{9,13},{1... | collective-permute-start | bytes 786440 | tf_op jit(solution)/shard_map/ppermute | solution.py:33
  53.9 7.6 %collective-permute-start.20 = (bf16[64,2048]{1,0:T(8,128)(2,1)S(1)}, bf16[64,2048]{1,0:T(8,128)(2,1)S(1)}, u32[]{:S(2)}, u32[]{:S(2)}) collective-permute-start(bf16[64,2048]{1,0:T(8,128)(2,1)S(1)} %slice.36), channel_id=1, source_target_pairs={{0,32},{1,33},{2,34},{3,35},{4,36},{5,37},{6,38},{7,39},{8,40},{9,... | collective-permute-start | bytes 786440 | tf_op jit(solution)/shard_map/ppermute | solution.py:33
  54.8 18.8 %collective-permute-start.16 = (bf16[512,512]{1,0:T(8,128)(2,1)S(1)}, bf16[512,512]{1,0:T(8,128)(2,1)}, u32[]{:S(2)}, u32[]{:S(2)}) collective-permute-start(bf16[512,512]{1,0:T(8,128)(2,1)S(1)} %collective-permute-done.5.refs_5_), channel_id=1, source_target_pairs={{0,1},{1,0},{2,3},{3,2},{4,5},{5,4},{6,7},{7,6},{8,9},{9,8},{10,11... | collective-permute-start | bytes 1572872 | tf_op jit(solution)/shard_map/ppermute | solution.py:33
  54.8 18.8 %collective-permute-start.17 = (bf16[512,512]{1,0:T(8,128)(2,1)S(1)}, bf16[512,512]{1,0:T(8,128)(2,1)}, u32[]{:S(2)}, u32[]{:S(2)}) collective-permute-start(bf16[512,512]{1,0:T(8,128)(2,1)S(1)} %collective-permute-done.6.refs_6_), channel_id=1, source_target_pairs={{0,1},{1,0},{2,3},{3,2},{4,5},{5,4},{6,7},{7,6},{8,9},{9,8},{10,11... | collective-permute-start | bytes 1572872 | tf_op jit(solution)/shard_map/ppermute | solution.py:33
  57.0 10.3 %collective-permute-start.21 = (bf16[64,2048]{1,0:T(8,128)(2,1)}, bf16[64,2048]{1,0:T(8,128)(2,1)}, u32[]{:S(2)}, u32[]{:S(2)}) collective-permute-start(bf16[64,2048]{1,0:T(8,128)(2,1)} %slice.37), channel_id=1, source_target_pairs={{0,96},{1,97},{2,98},{3,99},{4,100},{5,101},{6,102},{7,103},{8,104... | collective-permute-start | bytes 786440 | tf_op jit(solution)/shard_map/ppermute | solution.py:33
  61.0 9.4 %collective-permute-start.19 = (bf16[256,512]{1,0:T(8,128)(2,1)S(1)}, bf16[256,512]{1,0:T(8,128)(2,1)}, u32[]{:S(2)}, u32[]{:S(2)}) collective-permute-start(bf16[256,512]{1,0:T(8,128)(2,1)S(1)} %collective-permute-done.15.refs_8_), channel_id=1, source_target_pairs={{0,1},{1,0},{2,3},{3,2},{4,5},{5,4},{6,7},{7,6},{8,9},{9,8},{10,11... | collective-permute-start | bytes 786440 | tf_op jit(solution)/shard_map/ppermute | solution.py:33
  61.5 0.7 copy-start.6
  62.2 8.1 %collective-permute-start.18 = (bf16[256,512]{1,0:T(8,128)(2,1)}, bf16[256,512]{1,0:T(8,128)(2,1)}, u32[]{:S(2)}, u32[]{:S(2)}) collective-permute-start(bf16[256,512]{1,0:T(8,128)(2,1)} %collective-permute-done.14.refs_7_), channel_id=1, source_target_pairs={{0,1},{1,0},{2,3},{3,2},{4,5},{5,4},{6,7},{7,6},{8,9},{9,8},{10,11... | collective-permute-start | bytes 786440 | tf_op jit(solution)/shard_map/ppermute | solution.py:33
  67.4 26.8 %collective-permute-start.24 = (bf16[128,2048]{1,0:T(8,128)(2,1)}, bf16[128,2048]{1,0:T(8,128)(2,1)S(1)}, u32[]{:S(2)}, u32[]{:S(2)}) collective-permute-start(bf16[128,2048]{1,0:T(8,128)(2,1)} %get-tuple-element.70.refs_14_), channel_id=1, source_target_pairs={{0,64},{1,65},{2,66},{3,67},{4,68},{5,69},{6,70},{7,71},{8,72},{9,... | collective-permute-start | bytes 1572872 | tf_op jit(solution)/shard_map/ppermute | solution.py:33
  70.3 24.4 %collective-permute-start.23 = (bf16[128,2048]{1,0:T(8,128)(2,1)}, bf16[128,2048]{1,0:T(8,128)(2,1)S(1)}, u32[]{:S(2)}, u32[]{:S(2)}) collective-permute-start(bf16[128,2048]{1,0:T(8,128)(2,1)} %get-tuple-element.70.refs_14_), channel_id=1, source_target_pairs={{0,32},{1,33},{2,34},{3,35},{4,36},{5,37},{6,38},{7,39},{8,40},{9,... | collective-permute-start | bytes 1572872 | tf_op jit(solution)/shard_map/ppermute | solution.py:33
  70.3 24.4 %collective-permute-start.22 = (bf16[128,2048]{1,0:T(8,128)(2,1)}, bf16[128,2048]{1,0:T(8,128)(2,1)S(1)}, u32[]{:S(2)}, u32[]{:S(2)}) collective-permute-start(bf16[128,2048]{1,0:T(8,128)(2,1)} %get-tuple-element.70.refs_14_), channel_id=1, source_target_pairs={{0,96},{1,97},{2,98},{3,99},{4,100},{5,101},{6,102},{7,103},{8,104... | collective-permute-start | bytes 1572872 | tf_op jit(solution)/shard_map/ppermute | solution.py:33
  73.6 1.0 copy-start.4
  74.6 0.9 copy-start.7
  82.8 0.7 copy-start.1
  83.5 11.2 %copy-start.5 = (bf16[128,2048]{1,0:T(8,128)(2,1)S(1)}, bf16[128,2048]{1,0:T(8,128)(2,1)}, u32[]{:S(2)}) copy-start(bf16[128,2048]{1,0:T(8,128)(2,1)} %get-tuple-element.70.refs_14_) | copy-start | bytes 1572868
  91.5 0.7 copy-start
  92.2 24.1 %collective-permute-start.28 = (bf16[128,1024]{1,0:T(8,128)(2,1)}, bf16[128,1024]{1,0:T(8,128)(2,1)S(1)}, u32[]{:S(2)}, u32[]{:S(2)}) collective-permute-start(bf16[128,1024]{1,0:T(8,128)(2,1)} %get-tuple-element.81), channel_id=1, source_target_pairs={{0,16},{1,17},{2,18},{3,19},{4,20},{5,21},{6,22},{7,23},{8,24},{9,... | collective-permute-start | bytes 786440 | tf_op jit(solution)/shard_map/ppermute | solution.py:33
  92.2 14.0 %collective-permute-start.25 = (bf16[128,1024]{1,0:T(8,128)(2,1)S(1)}, bf16[128,1024]{1,0:T(8,128)(2,1)S(1)}, u32[]{:S(2)}, u32[]{:S(2)}) collective-permute-start(bf16[128,1024]{1,0:T(8,128)(2,1)S(1)} %get-tuple-element.72), channel_id=1, source_target_pairs={{0,16},{1,17},{2,18},{3,19},{4,20},{5,21},{6,22},{7,23},{8,24},{9,... | collective-permute-start | bytes 786440 | tf_op jit(solution)/shard_map/ppermute | solution.py:33
  101.3 0.7 copy-start.2
  101.9 16.9 %collective-permute-start.27 = (bf16[128,1024]{1,0:T(8,128)(2,1)S(1)}, bf16[128,1024]{1,0:T(8,128)(2,1)}, u32[]{:S(2)}, u32[]{:S(2)}) collective-permute-start(bf16[128,1024]{1,0:T(8,128)(2,1)S(1)} %get-tuple-element.79), channel_id=1, source_target_pairs={{0,16},{1,17},{2,18},{3,19},{4,20},{5,21},{6,22},{7,23},{8,24},{9,... | collective-permute-start | bytes 786440 | tf_op jit(solution)/shard_map/ppermute | solution.py:33
  106.2 0.7 copy-start.13
  113.4 0.7 copy-start.3
  114.1 6.6 %collective-permute-start.26 = (bf16[128,1024]{1,0:T(8,128)(2,1)S(1)}, bf16[128,1024]{1,0:T(8,128)(2,1)S(1)}, u32[]{:S(2)}, u32[]{:S(2)}) collective-permute-start(bf16[128,1024]{1,0:T(8,128)(2,1)S(1)} %get-tuple-element.78), channel_id=1, source_target_pairs={{0,16},{1,17},{2,18},{3,19},{4,20},{5,21},{6,22},{7,23},{8,24},{9,... | collective-permute-start | bytes 786440 | tf_op jit(solution)/shard_map/ppermute | solution.py:33
  116.3 0.7 copy-start.12
  120.7 0.7 copy-start.14
